TPU v7x, 32 devices: a whole 2x2x4 slice. The times are simulated.
32 devices in a mesh: ctx: 16 (over z, y, x), fsdp: 2 (over core).
Axes of the slice: x: 2, y: 2, z: 4, core: 2. Of those that a mesh axis runs over, the one named last changes fastest.
Arguments:
- block_input: bfloat16 [2, 2048, 768], P('fsdp', 'ctx'), may hold values from -6 to 6
- out_cotangent: float32 [2, 2048, 768], P('fsdp', 'ctx'), may hold values from -6 to 6
- block_position: int32 [2, 16], P('fsdp'), may hold values from 0 to 15, each once within a row
- first_gain: bfloat16 [768], P('fsdp'), may hold values from 0.25 to 1.75
- first_shift: bfloat16 [768], P('fsdp'), may hold values from -3 to 3
- qkv_weight: bfloat16 [768, 2304], P('fsdp'), may hold values from -1 to 1
- query_bias: bfloat16 [768], P('fsdp'), may hold values from -6 to 6
- value_bias: bfloat16 [768], P('fsdp'), may hold values from -3 to 3
- output_weight: bfloat16 [768, 768], P('fsdp'), may hold values from -1.25 to 1.25
- output_bias: bfloat16 [768], P('fsdp'), may hold values from -3 to 3
- second_gain: bfloat16 [768], P('fsdp'), may hold values from 0.25 to 1.75
- second_shift: bfloat16 [768], P('fsdp'), may hold values from -3 to 3
- expand_weight: bfloat16 [768, 3072], P('fsdp'), may hold values from -0.21875 to 0.21875
- expand_bias: bfloat16 [3072], P('fsdp'), may hold values from -3 to 3
- shrink_weight: bfloat16 [3072, 768], P('fsdp'), may hold values from -0.109375 to 0.109375
- shrink_bias: bfloat16 [768], P('fsdp'), may hold values from -3 to 3
Outputs:
- block_output: bfloat16 [2, 2048, 768], P('fsdp', 'ctx')
- input_grad: float32 [2, 2048, 768], P('fsdp', 'ctx')
- first_gain_grad: float32 [768], P('fsdp')
- first_shift_grad: float32 [768], P('fsdp')
- qkv_weight_grad: float32 [768, 2304], P('fsdp')
- query_bias_grad: float32 [768], P('fsdp')
- value_bias_grad: float32 [768], P('fsdp')
- output_weight_grad: float32 [768, 768], P('fsdp')
- output_bias_grad: float32 [768], P('fsdp')
- second_gain_grad: float32 [768], P('fsdp')
- second_shift_grad: float32 [768], P('fsdp')
- expand_weight_grad: float32 [768, 3072], P('fsdp')
- expand_bias_grad: float32 [3072], P('fsdp')
- shrink_weight_grad: float32 [3072, 768], P('fsdp')
- shrink_bias_grad: float32 [768], P('fsdp')
Inputs may be any that keep to these rules, and one draw needn't show every extreme that they name: Each row of block_position names every block once: the device at index c along ctx holds tokens block_position[s, c] * 128 to block_position[s, c] * 128 + 127 of sequence s.
All inputs are finite; a program needn't handle non-finite values.
Results may differ from a plain program's by a relative error of at most 0.019.
Values may be sent and summed in bfloat16 or wider, within the bound.
No kernel may reach another device: no remote copies, remote signals or barrier semaphores. Data moves between devices by JAX's collectives and lax.ppermute only.
A program may use at most 192 MiB of HBM per device.

v0:
```python
import jax
import jax.numpy as jnp
from jax import lax
from jax.sharding import PartitionSpec as P

H = 12
HD = 64


NORM_EPS = 1e-05
MASK_FLOOR = -1e30
GELU_COEF = 0.7978845608028654
GELU_CUBE = 0.044715


def layer_norm(inputs, norm_gain, norm_shift):
    middle = jnp.mean(inputs, axis=-1, keepdims=True)
    centred = inputs - middle
    inv_std = lax.rsqrt(jnp.mean(centred * centred, axis=-1, keepdims=True) + NORM_EPS)
    normed = centred * inv_std
    return (
        normed * norm_gain.astype(jnp.float32) + norm_shift.astype(jnp.float32),
        normed,
        inv_std,
    )


def norm_back(upstream, normed, inv_std, norm_gain):
    scaled = upstream * norm_gain.astype(jnp.float32)
    return inv_std * (
        scaled
        - jnp.mean(scaled, axis=-1, keepdims=True)
        - normed * jnp.mean(scaled * normed, axis=-1, keepdims=True)
    )


def gelu_value(inputs):
    tanh_part = jnp.tanh(GELU_COEF * (inputs + GELU_CUBE * inputs * inputs * inputs))
    return 0.5 * inputs * (1.0 + tanh_part)


def gelu_slope(inputs):
    tanh_part = jnp.tanh(GELU_COEF * (inputs + GELU_CUBE * inputs * inputs * inputs))
    return 0.5 * (1.0 + tanh_part) + 0.5 * inputs * (1.0 - tanh_part * tanh_part) * GELU_COEF * (
        1.0 + 3.0 * GELU_CUBE * inputs * inputs
    )


def contract_rows(left, right):
    return lax.dot_general(
        left, right, (((0,), (0,)), ((), ())), preferred_element_type=jnp.float32
    )


def contract_cols(left, right):
    return lax.dot_general(
        left, right, (((1,), (1,)), ((), ())), preferred_element_type=jnp.float32
    )


def positions_of(table, row_ids, block_rows):
    source = row_ids // block_rows
    slots = jnp.arange(table.shape[0], dtype=jnp.int32)
    owner = jnp.sum(jnp.where(source[:, None] == slots[None, :], table[None, :], 0), axis=1)
    return owner * block_rows + row_ids % block_rows


def group_rows(block_rows, devices):
    wanted = max(1, 512 // block_rows)
    while devices % wanted:
        wanted -= 1
    return wanted * block_rows


def body(
    block_input,
    out_cotangent,
    block_position,
    first_gain,
    first_shift,
    qkv_weight,
    query_bias,
    value_bias,
    output_weight,
    output_bias,
    second_gain,
    second_shift,
    expand_weight,
    expand_bias,
    shrink_weight,
    shrink_bias,
):
    (
        gain_one,
        shift_one,
        qkv_full,
        query_add,
        value_add,
        mix_full,
        mix_add,
        gain_two,
        shift_two,
        expand_full,
        expand_add,
        shrink_full,
        shrink_add,
    ) = (
        lax.all_gather(first_gain, "fsdp", axis=0, tiled=True),
        lax.all_gather(first_shift, "fsdp", axis=0, tiled=True),
        lax.all_gather(qkv_weight, "fsdp", axis=0, tiled=True),
        lax.all_gather(query_bias, "fsdp", axis=0, tiled=True),
        lax.all_gather(value_bias, "fsdp", axis=0, tiled=True),
        lax.all_gather(output_weight, "fsdp", axis=0, tiled=True),
        lax.all_gather(output_bias, "fsdp", axis=0, tiled=True),
        lax.all_gather(second_gain, "fsdp", axis=0, tiled=True),
        lax.all_gather(second_shift, "fsdp", axis=0, tiled=True),
        lax.all_gather(expand_weight, "fsdp", axis=0, tiled=True),
        lax.all_gather(expand_bias, "fsdp", axis=0, tiled=True),
        lax.all_gather(shrink_weight, "fsdp", axis=0, tiled=True),
        lax.all_gather(shrink_bias, "fsdp", axis=0, tiled=True),
    )
    block_rows = block_input.shape[1]
    width = block_input.shape[2]
    ctx_count = lax.axis_size("ctx")
    ctx_here = lax.axis_index("ctx")
    table = block_position[0]
    score_scale = HD ** (-0.5)
    group_span = group_rows(block_rows, ctx_count)
    group_count = ctx_count * block_rows // group_span
    own_rows = ctx_here * block_rows + jnp.arange(block_rows, dtype=jnp.int32)
    query_pos = positions_of(table, own_rows, block_rows)
    inputs_f = block_input[0].astype(jnp.float32)
    normed_a, unit_a, inv_a = layer_norm(inputs_f, gain_one, shift_one)
    hidden_a = normed_a.astype(jnp.bfloat16)
    joint = jnp.dot(hidden_a, qkv_full, preferred_element_type=jnp.float32)
    queries = (joint[:, :width] + query_add.astype(jnp.float32)).astype(jnp.bfloat16)
    key_rows = joint[:, width : 2 * width].astype(jnp.bfloat16)
    values = (joint[:, 2 * width :] + value_add.astype(jnp.float32)).astype(jnp.bfloat16)
    query_heads = queries.reshape(block_rows, H, HD)
    start_state = (
        jnp.full((H, block_rows), MASK_FLOOR, jnp.float32),
        jnp.zeros((H, block_rows), jnp.float32),
        jnp.zeros((block_rows, H, HD), jnp.float32),
    )
    part_keys = lax.all_gather(key_rows, "ctx", axis=0, tiled=True)
    part_values = lax.all_gather(values, "ctx", axis=0, tiled=True)
    key_count = part_keys.shape[0]
    key_pos = positions_of(table, jnp.arange(key_count, dtype=jnp.int32), block_rows)

    def visit(running_state):
        row_best, row_total, mixed_sum = running_state
        scores = (
            jnp.einsum(
                "qhd,khd->hqk",
                query_heads,
                part_keys.reshape(key_count, H, HD),
                preferred_element_type=jnp.float32,
            )
            * score_scale
        )
        visible = key_pos[None, None, :] <= query_pos[None, :, None]
        scores = jnp.where(visible, scores, MASK_FLOOR)
        new_best = jnp.maximum(row_best, jnp.max(scores, axis=2))
        weights = jnp.where(visible, jnp.exp(scores - new_best[:, :, None]), 0.0)
        factor = jnp.exp(row_best - new_best)
        row_total = jnp.sum(weights, axis=2)
        update = jnp.einsum(
            "hqk,khd->qhd",
            weights.astype(jnp.bfloat16),
            part_values.reshape(key_count, H, HD),
            preferred_element_type=jnp.float32,
        )
        mixed_sum = mixed_sum * factor.T[:, :, None] + update
        return (new_best, row_total, mixed_sum)

    row_best, row_total, mixed_sum = lax.cond(
        jnp.min(key_pos) > jnp.max(query_pos),
        lambda running_state: running_state,
        visit,
        start_state,
    )
    log_total = row_best + jnp.log(row_total)
    attended = (mixed_sum / row_total.T[:, :, None]).reshape(block_rows, width).astype(jnp.bfloat16)
    middle = (
        inputs_f
        + jnp.dot(attended, mix_full, preferred_element_type=jnp.float32)
        + mix_add.astype(jnp.float32)
    )
    normed_b, unit_b, inv_b = layer_norm(middle, gain_two, shift_two)
    hidden_b = normed_b.astype(jnp.bfloat16)
    expanded = jnp.dot(
        hidden_b, expand_full, preferred_element_type=jnp.float32
    ) + expand_add.astype(jnp.float32)
    active = gelu_value(expanded).astype(jnp.bfloat16)
    result = (
        middle
        + jnp.dot(active, shrink_full, preferred_element_type=jnp.float32)
        + shrink_add.astype(jnp.float32)
    )
    block_output = result.astype(jnp.bfloat16)[None]
    gain_one_back, qkv_back, mix_back, gain_two_back, expand_back, shrink_back = (
        lax.all_gather(first_gain, "fsdp", axis=0, tiled=True),
        lax.all_gather(qkv_weight, "fsdp", axis=0, tiled=True),
        lax.all_gather(output_weight, "fsdp", axis=0, tiled=True),
        lax.all_gather(second_gain, "fsdp", axis=0, tiled=True),
        lax.all_gather(expand_weight, "fsdp", axis=0, tiled=True),
        lax.all_gather(shrink_weight, "fsdp", axis=0, tiled=True),
    )
    upstream = out_cotangent[0]
    upstream_b = upstream.astype(jnp.bfloat16)
    grad_shrink = contract_rows(active, upstream_b)
    grad_shrink_add = jnp.sum(upstream, axis=0)
    grad_expanded = contract_cols(upstream_b, shrink_back) * gelu_slope(expanded)
    grad_expanded_b = grad_expanded.astype(jnp.bfloat16)
    grad_expand = contract_rows(hidden_b, grad_expanded_b)
    grad_expand_add = jnp.sum(grad_expanded, axis=0)
    grad_hidden_b = contract_cols(grad_expanded_b, expand_back)
    grad_gain_two = jnp.sum(grad_hidden_b * unit_b, axis=0)
    grad_shift_two = jnp.sum(grad_hidden_b, axis=0)
    grad_middle = upstream + norm_back(grad_hidden_b, unit_b, inv_b, gain_two_back)
    grad_middle_b = grad_middle.astype(jnp.bfloat16)
    grad_mix = contract_rows(attended, grad_middle_b)
    grad_mix_add = jnp.sum(grad_middle, axis=0)
    grad_attended = contract_cols(grad_middle_b, mix_back).astype(jnp.bfloat16)
    grad_heads = grad_attended.reshape(block_rows, H, HD)
    delta = jnp.sum(
        grad_attended.astype(jnp.float32).reshape(block_rows, H, HD)
        * attended.astype(jnp.float32).reshape(block_rows, H, HD),
        axis=2,
    )
    local_keys, local_values = (
        lax.all_gather(key_rows, "ctx", axis=0, tiled=True),
        lax.all_gather(values, "ctx", axis=0, tiled=True),
    )
    every_query, every_grad = (
        lax.all_gather(queries, "ctx", axis=0, tiled=True),
        lax.all_gather(grad_attended, "ctx", axis=0, tiled=True),
    )
    every_total, every_delta = (
        lax.all_gather(log_total.T, "ctx", axis=0, tiled=True),
        lax.all_gather(delta, "ctx", axis=0, tiled=True),
    )
    mine_keys = key_rows.reshape(block_rows, H, HD)
    mine_values = values.reshape(block_rows, H, HD)

    def scan_query_side(grad_query, group_index):
        first_row = group_index * group_span
        key_heads = lax.dynamic_slice_in_dim(local_keys, first_row, group_span, 0).reshape(
            group_span, H, HD
        )
        value_heads = lax.dynamic_slice_in_dim(local_values, first_row, group_span, 0).reshape(
            group_span, H, HD
        )
        key_pos = positions_of(
            table, first_row + jnp.arange(group_span, dtype=jnp.int32), block_rows
        )

        def visit():
            scores = (
                jnp.einsum(
                    "qhd,khd->hqk", query_heads, key_heads, preferred_element_type=jnp.float32
                )
                * score_scale
            )
            visible = key_pos[None, None, :] <= query_pos[None, :, None]
            scores = jnp.where(visible, scores, MASK_FLOOR)
            probs = jnp.where(visible, jnp.exp(scores - log_total[:, :, None]), 0.0)
            prob_grad = jnp.einsum(
                "qhd,khd->hqk", grad_heads, value_heads, preferred_element_type=jnp.float32
            )
            score_grad = probs * (prob_grad - delta.T[:, :, None])
            scaled_grad = (score_grad * score_scale).astype(jnp.bfloat16)
            return jnp.einsum(
                "hqk,khd->qhd", scaled_grad, key_heads, preferred_element_type=jnp.float32
            )

        def skipped():
            return jnp.zeros((block_rows, H, HD), jnp.float32)

        query_part = lax.cond(jnp.min(key_pos) > jnp.max(query_pos), skipped, visit)
        return (grad_query + query_part, None)

    def scan_key_side(sums, group_index):
        key_sum, value_sum = sums
        first_row = group_index * group_span
        part_queries = lax.dynamic_slice_in_dim(every_query, first_row, group_span, 0).reshape(
            group_span, H, HD
        )
        part_grads = lax.dynamic_slice_in_dim(every_grad, first_row, group_span, 0).reshape(
            group_span, H, HD
        )
        part_totals = lax.dynamic_slice_in_dim(every_total, first_row, group_span, 0)
        part_deltas = lax.dynamic_slice_in_dim(every_delta, first_row, group_span, 0)
        part_pos = positions_of(
            table, first_row + jnp.arange(group_span, dtype=jnp.int32), block_rows
        )

        def visit():
            scores = (
                jnp.einsum(
                    "qhd,khd->hqk", part_queries, mine_keys, preferred_element_type=jnp.float32
                )
                * score_scale
            )
            visible = query_pos[None, None, :] <= part_pos[None, :, None]
            scores = jnp.where(visible, scores, MASK_FLOOR)
            probs = jnp.where(visible, jnp.exp(scores - part_totals.T[:, :, None]), 0.0)
            prob_grad = jnp.einsum(
                "qhd,khd->hqk", part_grads, mine_values, preferred_element_type=jnp.float32
            )
            score_grad = probs * (prob_grad - part_deltas.T[:, :, None])
            value_part = jnp.einsum(
                "hqk,qhd->khd",
                probs.astype(jnp.bfloat16),
                part_grads,
                preferred_element_type=jnp.float32,
            )
            scaled_grad = (score_grad * score_scale).astype(jnp.bfloat16)
            key_part = jnp.einsum(
                "hqk,qhd->khd", scaled_grad, part_queries, preferred_element_type=jnp.float32
            )
            return (key_part, value_part)

        def skipped():
            return (
                jnp.zeros((block_rows, H, HD), jnp.float32),
                jnp.zeros((block_rows, H, HD), jnp.float32),
            )

        key_part, value_part = lax.cond(jnp.max(part_pos) < jnp.min(query_pos), skipped, visit)
        return ((key_sum + key_part, value_sum + value_part), None)

    grad_query, unused = lax.scan(
        scan_query_side,
        jnp.zeros((block_rows, H, HD), jnp.float32),
        jnp.arange(group_count, dtype=jnp.int32),
    )
    start_sums = (
        jnp.zeros((block_rows, H, HD), jnp.float32),
        jnp.zeros((block_rows, H, HD), jnp.float32),
    )
    (key_sum, value_sum), unused = lax.scan(
        scan_key_side, start_sums, jnp.arange(group_count, dtype=jnp.int32)
    )
    grad_queries = grad_query.reshape(block_rows, width)
    grad_keys = key_sum.reshape(block_rows, width)
    grad_values = value_sum.reshape(block_rows, width)
    grad_joint = jnp.concatenate([grad_queries, grad_keys, grad_values], axis=1).astype(
        jnp.bfloat16
    )
    grad_qkv = contract_rows(hidden_a, grad_joint)
    grad_query_add = jnp.sum(grad_queries, axis=0)
    grad_value_add = jnp.sum(grad_values, axis=0)
    grad_hidden_a = contract_cols(grad_joint, qkv_back)
    grad_gain_one = jnp.sum(grad_hidden_a * unit_a, axis=0)
    grad_shift_one = jnp.sum(grad_hidden_a, axis=0)
    input_grad = grad_middle + norm_back(grad_hidden_a, unit_a, inv_a, gain_one_back)
    shares = (
        lax.psum_scatter(grad_gain_one, "fsdp", scatter_dimension=0, tiled=True),
        lax.psum_scatter(grad_shift_one, "fsdp", scatter_dimension=0, tiled=True),
        lax.psum_scatter(grad_qkv, "fsdp", scatter_dimension=0, tiled=True),
        lax.psum_scatter(grad_query_add, "fsdp", scatter_dimension=0, tiled=True),
        lax.psum_scatter(grad_value_add, "fsdp", scatter_dimension=0, tiled=True),
        lax.psum_scatter(grad_mix, "fsdp", scatter_dimension=0, tiled=True),
        lax.psum_scatter(grad_mix_add, "fsdp", scatter_dimension=0, tiled=True),
        lax.psum_scatter(grad_gain_two, "fsdp", scatter_dimension=0, tiled=True),
        lax.psum_scatter(grad_shift_two, "fsdp", scatter_dimension=0, tiled=True),
        lax.psum_scatter(grad_expand, "fsdp", scatter_dimension=0, tiled=True),
        lax.psum_scatter(grad_expand_add, "fsdp", scatter_dimension=0, tiled=True),
        lax.psum_scatter(grad_shrink, "fsdp", scatter_dimension=0, tiled=True),
        lax.psum_scatter(grad_shrink_add, "fsdp", scatter_dimension=0, tiled=True),
    )
    totals = lax.psum(
        (
            shares[0],
            shares[1],
            shares[2],
            shares[3],
            shares[4],
            shares[5],
            shares[6],
            shares[7],
            shares[8],
            shares[9],
            shares[10],
            shares[11],
            shares[12],
        ),
        "ctx",
    )
    return (
        block_output,
        input_grad[None],
        totals[0],
        totals[1],
        totals[2],
        totals[3],
        totals[4],
        totals[5],
        totals[6],
        totals[7],
        totals[8],
        totals[9],
        totals[10],
        totals[11],
        totals[12],
    )


def solution(mesh):
    placed = (
        P("fsdp", "ctx", None),
        P("fsdp", "ctx", None),
        P("fsdp", None),
        P("fsdp"),
        P("fsdp"),
        P("fsdp", None),
        P("fsdp"),
        P("fsdp"),
        P("fsdp", None),
        P("fsdp"),
        P("fsdp"),
        P("fsdp"),
        P("fsdp", None),
        P("fsdp"),
        P("fsdp", None),
        P("fsdp"),
    )
    return jax.shard_map(
        body,
        mesh=mesh,
        in_specs=placed,
        out_specs=(
            P("fsdp", "ctx", None),
            P("fsdp", "ctx", None),
            P("fsdp"),
            P("fsdp"),
            P("fsdp", None),
            P("fsdp"),
            P("fsdp"),
            P("fsdp", None),
            P("fsdp"),
            P("fsdp"),
            P("fsdp"),
            P("fsdp", None),
            P("fsdp"),
            P("fsdp", None),
            P("fsdp"),
        ),
        check_vma=False,
    )
```

profile of v0, /device:TPU:0, one launch (start us, length us, event | category | flops | bytes accessed | tf_op | source)
XLA Modules:
  0.0 971.0 jit_solution(17017834458384710341)
XLA Ops:
  15.3 9.7 all-gather.18.cloned.1.call-done
  48.3 49.7 %all-gather.20.cloned.1.call-done = bf16[2048,768]{1,0:T(8,128)(2,1)} async-done(((bf16[128,768]{1,0:T(8,128)(2,1)}), bf16[2048,768]{1,0:T(8,128)(2,1)}) %all-gather.20.cloned.1.call-update) | async-done | bytes 3145744 | tf_op jit(solution)/shard_map/all_gather | solution.py:145
  98.0 70.0 %all-gather.22.cloned.1.call-done = bf16[2048,768]{1,0:T(8,128)(2,1)} async-done(((bf16[128,768]{1,0:T(8,128)(2,1)}), bf16[2048,768]{1,0:T(8,128)(2,1)}) %all-gather.22.cloned.1.call-update) | async-done | bytes 3145744 | tf_op jit(solution)/shard_map/all_gather | solution.py:146
  168.1 26.6 %conditional.3 = (f32[12,128]{1,0:T(8,128)S(1)}, f32[12,128]{1,0:T(8,128)S(1)}, f32[128,12,64]{0,2,1:T(8,128)S(1)}, f32[12,128]{1,0:T(8,128)S(1)}) conditional(s32[]{:T(128)} %convert_element_type.117, (s32[2048]{0:T(1024)S(1)}, s32[128]{0:T(128)}, bf16[2048,768]{1,0:T(8,128)(2,1)}, bf16[128,12,64]{0,2,1:T(8,128)(2,1)}, ...), branch_computations={%region_6.9_spmd, %region_9.10_spmd} | conditional | flops 846562816 | bytes 121246296 | solution.py:176
  183.6 10.8 %fusion.9 = f32[128,12,64]{0,2,1:T(8,128)S(1)} fusion(bf16[2048,12,64]{0,2,1:T(8,128)(2,1)} %bitcast.177, f32[12,128,2048]{2,1,0:T(8,128)} %copy-done.2, f32[12,128]{1,0:T(8,128)S(1)} %get-tuple-element.1069, pred[128,2048]{1,0:T(8,128)(4,1)S(1)} %broadcast_compare_fusion, f32[128,12]{0,1:T(8,128)S(1)} %get-tuple-element.860), kind=kOutput, calls=%fused_computation.8 | convolution fusion | flops 418480128 | bytes 16396288 | tf_op jit(solution)/shard_map/cond/branch_0_fun/hqk,khd->qhd/dot_general | solution.py:167
  200.6 10.7 %all-gather.28.cloned.1.call-done = bf16[3072,768]{1,0:T(8,128)(2,1)} async-done(((bf16[1536,768]{1,0:T(8,128)(2,1)}), bf16[3072,768]{1,0:T(8,128)(2,1)}) %all-gather.28.cloned.1.call-update) | async-done | bytes 4718608 | tf_op jit(solution)/shard_map/all_gather | solution.py:119
  211.3 4.9 fusion.113
  223.6 5.1 fusion.75
  229.7 5.2 fusion.81
  244.6 4.6 copy.70
  249.2 34.7 %all-gather.30.cloned.1.call-done = bf16[2048,768]{1,0:T(8,128)(2,1)} async-done(((bf16[128,768]{1,0:T(8,128)(2,1)}), bf16[2048,768]{1,0:T(8,128)(2,1)}) %all-gather.30.cloned.1.call-update) | async-done | bytes 3145744 | tf_op jit(solution)/shard_map/all_gather | solution.py:236
  284.0 4.6 copy.73
  288.6 41.7 %all_gather.81 = f32[2048,12]{0,1:T(8,128)} all-gather(f32[128,12]{0,1:T(8,128)} %bitcast.27), channel_id=1, replica_groups=mesh['ctx'=16,'fsdp'=2] {'ctx'}, dimensions={0}, use_global_device_ids=true | all-gather | bytes 104448 | tf_op jit(solution)/shard_map/all_gather | solution.py:240
  331.9 39.6 %all_gather.83 = f32[2048,12]{0,1:T(8,128)} all-gather(f32[128,12]{0,1:T(8,128)} %multiply_reduce_fusion.1), channel_id=1, replica_groups=mesh['ctx'=16,'fsdp'=2] {'ctx'}, dimensions={0}, use_global_device_ids=true | all-gather | bytes 104448 | tf_op jit(solution)/shard_map/all_gather | solution.py:241
  372.1 58.0 %while.28 = (s32[]{:T(128)}, f32[128,12,64]{0,2,1:T(8,128)}, s32[4]{0:T(128)}, s32[1,16]{1,0:T(1,128)S(1)}, s32[]{:T(128)}, /*index=5*/s32[128]{0:T(128)}, bf16[...) while((s32[]{:T(128)}, f32[128,12,64]{0,2,1:T(8,128)}, ...), condition=%wide.region_20.21_spmd.clone, body=%wide.region_15.20_spmd.clone.sunk | while | flops 308583424 | bytes 17064868 | solution.py:333
  376.0 11.5 %conditional.8 = (f32[128,12,64]{0,2,1:T(8,128)}) conditional(s32[]{:T(128)} %convert_element_type.251, (s32[512]{0:T(512)S(1)}, s32[128]{0:T(128)}, s32[]{:T(128)}, bf16[2048,768]{0,1:T(8,128)(2,1)}, bf16[128,12,64]{0,2,1:T(8,128)(2,1)}, /*index=5*/f32[12,128]{1,0:T(8,128)}, bf16[2048,768]{0,1:T(8,128)(2,1)}, bf16[128,12,64]{0,2,1:T(8,128)(2,1)}, ...), branch_computations={%region_18.18_spmd, %region_19.19_spmd} | conditional | flops 308346880 | bytes 15874634 | solution.py:280
  393.3 11.4 %conditional.8 = (f32[128,12,64]{0,2,1:T(8,128)}) conditional(s32[]{:T(128)} %convert_element_type.251, (s32[512]{0:T(512)S(1)}, s32[128]{0:T(128)}, s32[]{:T(128)}, bf16[2048,768]{0,1:T(8,128)(2,1)}, bf16[128,12,64]{0,2,1:T(8,128)(2,1)}, /*index=5*/f32[12,128]{1,0:T(8,128)}, bf16[2048,768]{0,1:T(8,128)(2,1)}, bf16[128,12,64]{0,2,1:T(8,128)(2,1)}, ...), branch_computations={%region_18.18_spmd, %region_19.19_spmd} | conditional | flops 308346880 | bytes 15874634 | solution.py:280
  410.7 10.8 %conditional.8 = (f32[128,12,64]{0,2,1:T(8,128)}) conditional(s32[]{:T(128)} %convert_element_type.251, (s32[512]{0:T(512)S(1)}, s32[128]{0:T(128)}, s32[]{:T(128)}, bf16[2048,768]{0,1:T(8,128)(2,1)}, bf16[128,12,64]{0,2,1:T(8,128)(2,1)}, /*index=5*/f32[12,128]{1,0:T(8,128)}, bf16[2048,768]{0,1:T(8,128)(2,1)}, bf16[128,12,64]{0,2,1:T(8,128)(2,1)}, ...), branch_computations={%region_18.18_spmd, %region_19.19_spmd} | conditional | flops 308346880 | bytes 15874634 | solution.py:280
  430.1 4.6 copy.74
  435.2 85.5 %while.29 = (s32[]{:T(128)}, f32[128,12,64]{0,2,1:T(8,128)}, f32[128,12,64]{0,2,1:T(8,128)}, s32[4]{0:T(128)}, s32[1,16]{1,0:T(1,128)S(1)}, /*index=5*/s32[]{:T(...) while((s32[]{:T(128)}, f32[128,12,64]{0,2,1:T(8,128)}, ...), condition=%wide.region_27.28_spmd.clone, body=%wide.region_22.27_spmd.clone.sunk | while | flops 413375488 | bytes 23581648 | solution.py:342
  439.2 15.1 %conditional.9 = (f32[128,12,64]{0,2,1:T(8,128)}, f32[128,12,64]{0,2,1:T(8,128)}) conditional(s32[]{:T(128)} %convert_element_type.252, (s32[128]{0:T(128)}, s32[512]{0:T(512)S(1)}, s32[]{:T(128)}, bf16[2048,768]{0,1:T(8,128)(2,1)}, bf16[128,12,64]{0,2,1:T(8,128)(2,1)}, /*index=5*/f32[2048,12]{0,1:T(8,128)}, bf16[2048,768]{0,1:T(8,128)(2,1)}, ...), branch_computations={%region_25.25_spmd, %region_26.26_spmd} | conditional | flops 412942336 | bytes 21211762 | solution.py:330
  446.8 4.5 fusion.30
  460.4 15.1 %conditional.9 = (f32[128,12,64]{0,2,1:T(8,128)}, f32[128,12,64]{0,2,1:T(8,128)}) conditional(s32[]{:T(128)} %convert_element_type.252, (s32[128]{0:T(128)}, s32[512]{0:T(512)S(1)}, s32[]{:T(128)}, bf16[2048,768]{0,1:T(8,128)(2,1)}, bf16[128,12,64]{0,2,1:T(8,128)(2,1)}, /*index=5*/f32[2048,12]{0,1:T(8,128)}, bf16[2048,768]{0,1:T(8,128)(2,1)}, ...), branch_computations={%region_25.25_spmd, %region_26.26_spmd} | conditional | flops 412942336 | bytes 21211762 | solution.py:330
  468.1 4.5 fusion.30
  481.9 15.1 %conditional.9 = (f32[128,12,64]{0,2,1:T(8,128)}, f32[128,12,64]{0,2,1:T(8,128)}) conditional(s32[]{:T(128)} %convert_element_type.252, (s32[128]{0:T(128)}, s32[512]{0:T(512)S(1)}, s32[]{:T(128)}, bf16[2048,768]{0,1:T(8,128)(2,1)}, bf16[128,12,64]{0,2,1:T(8,128)(2,1)}, /*index=5*/f32[2048,12]{0,1:T(8,128)}, bf16[2048,768]{0,1:T(8,128)(2,1)}, ...), branch_computations={%region_25.25_spmd, %region_26.26_spmd} | conditional | flops 412942336 | bytes 21211762 | solution.py:330
  489.5 4.5 fusion.30
  503.4 15.0 %conditional.9 = (f32[128,12,64]{0,2,1:T(8,128)}, f32[128,12,64]{0,2,1:T(8,128)}) conditional(s32[]{:T(128)} %convert_element_type.252, (s32[128]{0:T(128)}, s32[512]{0:T(512)S(1)}, s32[]{:T(128)}, bf16[2048,768]{0,1:T(8,128)(2,1)}, bf16[128,12,64]{0,2,1:T(8,128)(2,1)}, /*index=5*/f32[2048,12]{0,1:T(8,128)}, bf16[2048,768]{0,1:T(8,128)(2,1)}, ...), branch_computations={%region_25.25_spmd, %region_26.26_spmd} | conditional | flops 412942336 | bytes 21211762 | solution.py:330
  510.9 4.5 fusion.30
  523.5 5.1 fusion.79
  528.7 18.8 %reduce-scatter.5.cloned.1.call-done = f32[384,2304]{1,0:T(8,128)} async-done(((f32[768,2304]{1,0:T(8,128)}), f32[384,2304]{1,0:T(8,128)}) %reduce-scatter.5.cloned.1.call-update) | async-done | bytes 3538960 | tf_op jit(solution)/shard_map/reduce_scatter | solution.py:361
  564.3 81.7 %all-reduce.9 = (f32[384]{0:T(512)}, f32[384]{0:T(512)}, f32[384]{0:T(512)}, f32[384]{0:T(512)}, f32[384]{0:T(512)}, /*index=5*/f32[384]{0:T(512)}, f32[384]{0:T(512)}, f32[1536]{0:T(1024)}, f32[384]{0:T(512)}) all-reduce(f32[384]{0:T(512)S(1)} %dynamic-slice.1, ...), channel_id=1, replica_groups=mesh['ctx'=16,'fsdp'=2] {'ctx'}, use_global_device_ids=true, to_apply=%region_32.33 | all-reduce | flops 4608 | bytes 36864 | tf_op jit(solution)/shard_map/psum | solution.py:373
  646.9 306.8 %all-reduce.14.cloned.1.call-done = (f32[384,2304]{1,0:T(8,128)}, f32[384,768]{1,0:T(8,128)}, f32[384,3072]{1,0:T(8,128)}, f32[1536,768]{1,0:T(8,128)}) async-done(((f32[384,2304]{1,0:T(8,128)}, f32[384,768]{1,0:T(8,128)}, f32[384,3072]{1,0:T(8,128)}, f32[1536,768]{1,0:T(8,128)}), (f32[384,2304]{1,0:T(8,128)}, f32[384,768]{1,0:T(8,128)}, f32[384,3072]{1,0:T(8,128)}, ...) | async-done | bytes 14155792 | tf_op jit(solution)/shard_map/psum | solution.py:373
  (340 shorter events, 212.0 us)
Async XLA Ops:
  7.2 17.8 %all-gather.18.cloned.1.call-start = ((), (), s32[]{:S(2)}) async-start(), calls=%async_computation.4 | async-start | bytes 5308416 | tf_op jit(solution)/shard_map/all_gather | solution.py:110
  7.9 20.7 %copy-start.45 = (bf16[384]{0:T(512)(128)(2,1)S(1)}, bf16[384]{0:T(512)(128)(2,1)}, u32[]{:S(2)}) copy-start(bf16[384]{0:T(512)(128)(2,1)} %param.33) | copy-start | bytes 2308
  7.9 22.5 %copy-start.46 = (bf16[384]{0:T(512)(128)(2,1)S(1)}, bf16[384]{0:T(512)(128)(2,1)}, u32[]{:S(2)}) copy-start(bf16[384]{0:T(512)(128)(2,1)} %param.32) | copy-start | bytes 2308
  7.9 90.1 %all-gather.20.cloned.1.call-start = ((), (), s32[]{:S(2)}) async-start(), calls=%async_computation.5 | async-start | bytes 3342336 | tf_op jit(solution)/shard_map/all_gather | solution.py:145
  14.2 16.2 %copy-start.39 = (f32[128]{0:T(128)}, f32[128]{0:T(128)S(1)}, u32[]{:S(2)}) copy-start(f32[128]{0:T(128)S(1)} %broadcast_multiply_fusion.5) | copy-start | bytes 1540
  15.3 13.3 %copy-start.42 = (f32[128]{0:T(128)}, f32[128]{0:T(128)S(1)}, u32[]{:S(2)}) copy-start(f32[128]{0:T(128)S(1)} %add_rsqrt_fusion.1) | copy-start | bytes 1540
  28.5 139.5 %all-gather.22.cloned.1.call-start = ((), (), s32[]{:S(2)}) async-start(), calls=%async_computation.6 | async-start | bytes 3342336 | tf_op jit(solution)/shard_map/all_gather | solution.py:146
  33.1 8.3 copy-start.44
  33.1 10.8 %copy-start.48 = (bf16[384]{0:T(512)(128)(2,1)S(1)}, bf16[384]{0:T(512)(128)(2,1)}, u32[]{:S(2)}) copy-start(bf16[384]{0:T(512)(128)(2,1)} %param.37) | copy-start | bytes 2308
  33.1 12.6 %copy-start.49 = (bf16[384]{0:T(512)(128)(2,1)S(1)}, bf16[384]{0:T(512)(128)(2,1)}, u32[]{:S(2)}) copy-start(bf16[384]{0:T(512)(128)(2,1)} %param.36) | copy-start | bytes 2308
  33.1 14.4 %copy-start.19 = (bf16[128,768]{1,0:T(8,128)(2,1)S(1)}, bf16[128,768]{1,0:T(8,128)(2,1)}, u32[]{:S(2)}) copy-start(bf16[128,768]{1,0:T(8,128)(2,1)} %get-tuple-element.882) | copy-start | bytes 589828
  33.1 161.7 %all-gather.24.cloned.1.call-start = ((), (), s32[]{:S(2)}) async-start(), calls=%async_computation.7 | async-start | bytes 1769472 | tf_op jit(solution)/shard_map/all_gather | solution.py:113
  33.7 163.6 %all-gather.26.cloned.1.call-start = ((), (), s32[]{:S(2)}) async-start(), calls=%async_computation.8 | async-start | bytes 7077888 | tf_op jit(solution)/shard_map/all_gather | solution.py:117
  34.3 177.0 %all-gather.28.cloned.1.call-start = ((), (), s32[]{:S(2)}) async-start(), calls=%async_computation.9 | async-start | bytes 7077888 | tf_op jit(solution)/shard_map/all_gather | solution.py:119
  34.9 249.1 %all-gather.30.cloned.1.call-start = ((), (), s32[]{:S(2)}) async-start(), calls=%async_computation.10 | async-start | bytes 3342336 | tf_op jit(solution)/shard_map/all_gather | solution.py:236
  35.6 394.5 %all-gather.32.cloned.1.call-start = ((), (), s32[]{:S(2)}) async-start(), calls=%async_computation.11 | async-start | bytes 3342336 | tf_op jit(solution)/shard_map/all_gather | solution.py:237
  175.4 5.3 copy-start.2
  175.5 5.3 copy-start.5
  197.3 14.0 %copy-start.13 = (f32[1,128,768]{2,1,0:T(8,128)S(1)}, f32[1,128,768]{2,1,0:T(8,128)}, u32[]{:S(2)}) copy-start(f32[1,128,768]{2,1,0:T(8,128)} %param.27) | copy-start | bytes 1179652
  200.6 28.2 %copy-start.6 = (f32[128,3072]{1,0:T(8,128)}, f32[128,3072]{1,0:T(8,128)S(1)}, u32[]{:S(2)}) copy-start(f32[128,3072]{1,0:T(8,128)S(1)} %convolution_add_fusion) | copy-start | bytes 4718596
  220.6 308.0 %reduce-scatter.7.cloned.1.call-start = ((), (), s32[]{:S(2)}) async-start(), calls=%async_computation.13 | async-start | bytes 3538944 | tf_op jit(solution)/shard_map/reduce_scatter | solution.py:364
  223.5 305.2 %reduce-scatter.9.cloned.1.call-start = ((), (), s32[]{:S(2)}) async-start(), calls=%async_computation.14 | async-start | bytes 14155776 | tf_op jit(solution)/shard_map/reduce_scatter | solution.py:368
  228.8 299.9 %reduce-scatter.11.cloned.1.call-start = ((), (), s32[]{:S(2)}) async-start(), calls=%async_computation.15 | async-start | bytes 14155776 | tf_op jit(solution)/shard_map/reduce_scatter | solution.py:370
  235.0 6.8 copy-start.4
  235.0 312.5 %reduce-scatter.5.cloned.1.call-start = ((), (), s32[]{:S(2)}) async-start(), calls=%async_computation.12 | async-start | bytes 10616832 | tf_op jit(solution)/shard_map/reduce_scatter | solution.py:361
  249.2 81.0 %copy-start.22 = (f32[128,12,64]{0,2,1:T(8,128)S(1)}, f32[128,12,64]{0,2,1:T(8,128)}, u32[]{:S(2)}) copy-start(f32[128,12,64]{0,2,1:T(8,128)} %copy-done.21) | copy-start | bytes 1179652
  249.2 81.0 %copy-start.25 = (f32[12,128]{1,0:T(8,128)S(1)}, f32[12,128]{1,0:T(8,128)}, u32[]{:S(2)}) copy-start(f32[12,128]{1,0:T(8,128)} %copy-done.24) | copy-start | bytes 18436
  249.2 122.8 %copy-start.28 = (s32[1,16]{1,0:T(1,128)S(1)}, s32[1,16]{1,0:T(1,128)}, u32[]{:S(2)}) copy-start(s32[1,16]{1,0:T(1,128)} %param.28) | copy-start | bytes 196
  528.6 425.1 %all-reduce.14.cloned.1.call-start = ((), (), s32[]{:S(2)}) async-start(), calls=%async_computation.16 | async-start | bytes 28311552 | tf_op jit(solution)/shard_map/psum | solution.py:373
  556.4 89.6 %copy-start.11 = (f32[128,768]{1,0:T(8,128)S(1)}, f32[128,768]{1,0:T(8,128)}, u32[]{:S(2)}) copy-start(f32[128,768]{1,0:T(8,128)} %copy-done.10) | copy-start | bytes 1179652
  953.7 5.2 slice-start.2
  953.7 5.2 slice-start.3
  (45 other events, 130.5 us)
Sparse Core Ops, SparseCore 0:
  9.6 15.3 all-gather.17
  28.7 69.3 all-gather.19
  101.4 66.6 all-gather.21
  169.5 7.7 all-gather.23
  178.6 15.5 all-gather.25
  195.6 15.6 all-gather.27
  214.6 69.2 all-gather.29
  286.7 67.8 all-gather.31
  356.8 8.8 reduce-scatter.6
  368.0 18.9 reduce-scatter.8
  389.4 19.0 reduce-scatter.10
  528.7 18.7 reduce-scatter.4
  554.0 399.6 all-reduce.13
where the time goes:
time: 970 us; the launch traced here: 971 us
  waiting for transfers between devices  504 us (52%)
  blocking collectives  183 us (19%)
  matrix products  106 us (11%)
  local copies, waits for them, and re-layouts  93.5 us (10%)
  other arithmetic  51 us (5%)
  between operations  17.2 us (2%)
  loops' own time  16.2 us (2%)
    psum x1, waiting for transfers between devices, body(): lax.psum((shares[0], shares[1], shares[2], shares[3], shares[4], shares[5...  307 us
    psum x1, blocking collectives, body(): lax.psum((shares[0], shares[1], shares[2], shares[3], shares[4], shares[5...  81.7 us
    all_gather x1, waiting for transfers between devices, body(): part_values = lax.all_gather(values, 'ctx', axis=0, tiled=True)  70 us
    all_gather x1, waiting for transfers between devices, body(): part_keys = lax.all_gather(key_rows, 'ctx', axis=0, tiled=True)  49.7 us
    all_gather x1, blocking collectives, body(): lax.all_gather(log_total.T, 'ctx', axis=0, tiled=True)  41.7 us
    all_gather x1, blocking collectives, body(): lax.all_gather(delta, 'ctx', axis=0, tiled=True)  39.6 us
    all_gather x1, waiting for transfers between devices, body(): lax.all_gather(queries, 'ctx', axis=0, tiled=True)  34.7 us
    unnamed x129, local copies, waits for them, and re-layouts  32.5 us
  transfers between devices with their start and end apart: 13, of which 7 were waited for; matrix products, arithmetic and copies ran while one was open for 23% of the time, Pallas kernels for 0%

commit v1 on v0

v1 whole, which is shorter than its diff:
```python
import functools

import jax
import jax.numpy as jnp
from jax import lax
from jax.experimental import pallas as pl
from jax.experimental.pallas import tpu as pltpu
from jax.sharding import PartitionSpec as P

H = 12
HD = 64
NORM_EPS = 1e-05
MASK_FLOOR = -1e30
GELU_COEF = 0.7978845608028654
GELU_CUBE = 0.044715
SCALE = HD ** (-0.5)
F32 = jnp.float32
BF16 = jnp.bfloat16
VMEM_LIMIT = 56 * 1024 * 1024


def dot_nn(left, right):
    return lax.dot_general(left, right, (((1,), (0,)), ((), ())), preferred_element_type=F32)


def dot_nt(left, right):
    return lax.dot_general(left, right, (((1,), (1,)), ((), ())), preferred_element_type=F32)


def dot_tn(left, right):
    return lax.dot_general(left, right, (((0,), (0,)), ((), ())), preferred_element_type=F32)


def normalise(inputs):
    centred = inputs - jnp.mean(inputs, axis=-1, keepdims=True)
    inv_std = lax.rsqrt(jnp.mean(centred * centred, axis=-1, keepdims=True) + NORM_EPS)
    return centred * inv_std, inv_std


def norm_back(scaled, unit, inv_std):
    return inv_std * (
        scaled
        - jnp.mean(scaled, axis=-1, keepdims=True)
        - unit * jnp.mean(scaled * unit, axis=-1, keepdims=True)
    )


def halves(side_ref, size):
    side = side_ref[0]
    own = pl.ds(pl.multiple_of(side * size, 128), size)
    other = pl.ds(pl.multiple_of((1 - side) * size, 128), size)
    return own, other


def call(kernel, outs, scratch, name, flops, *args, smem=1):
    specs = [pl.BlockSpec(memory_space=pltpu.SMEM)] * smem
    specs += [pl.BlockSpec(memory_space=pltpu.VMEM)] * (len(args) - smem)
    moved = sum(a.size * a.dtype.itemsize for a in args)
    return pl.pallas_call(
        kernel,
        out_shape=[jax.ShapeDtypeStruct(s, d) for s, d in outs],
        in_specs=specs,
        out_specs=[pl.BlockSpec(memory_space=pltpu.VMEM)] * len(outs),
        scratch_shapes=[pltpu.VMEM(s, d) for s, d in scratch],
        compiler_params=pltpu.CompilerParams(vmem_limit_bytes=VMEM_LIMIT),
        cost_estimate=pl.CostEstimate(flops=flops, bytes_accessed=moved, transcendentals=0),
        name=name,
    )(*args)


def project_kernel(side_ref, x_ref, vec_ref, own_ref, other_ref, hid_ref, send_ref):
    rows, width = x_ref.shape
    own, other = halves(side_ref, width // 2)
    unit, _ = normalise(x_ref[...].astype(F32))
    vec = vec_ref[...].astype(F32)
    hid_ref[...] = (unit * vec[0:1] + vec[1:2]).astype(BF16)
    joint = dot_nn(hid_ref[:, own], own_ref[...]) + dot_nn(hid_ref[:, other], other_ref[...])
    three = (
        (joint[:, :width] + vec[2:3]).astype(BF16),
        joint[:, width : 2 * width].astype(BF16),
        (joint[:, 2 * width :] + vec[3:4]).astype(BF16),
    )
    for k, part in enumerate(three):
        turned = part.T
        for h in range(H):
            send_ref[h, k * HD : (k + 1) * HD, :] = turned[h * HD : (h + 1) * HD]
    for h in range(H, send_ref.shape[0]):
        send_ref[h] = jnp.zeros(send_ref.shape[1:], BF16)


def attend_kernel(slot_ref, in_ref, out_ref, total_ref, q_t, k_n, v_t, o_t):
    count, _, rows = in_ref.shape
    tile = 512
    for p in range(count):
        slot = slot_ref[p]
        where = slice(p * rows, (p + 1) * rows)
        q_t[:, where] = in_ref[slot, 0:HD, :] * jnp.asarray(SCALE, BF16)
        k_n[where, :] = in_ref[slot, HD : 2 * HD, :].T
        v_t[:, where] = in_ref[slot, 2 * HD : 3 * HD, :]
    length = count * rows
    below = lax.broadcasted_iota(jnp.int32, (tile, tile), 0) <= lax.broadcasted_iota(
        jnp.int32, (tile, tile), 1
    )
    for i in range(length // tile):
        here = slice(i * tile, (i + 1) * tile)
        query = q_t[:, here]
        scores = jnp.where(below, dot_nn(k_n[here, :], query), MASK_FLOOR)
        best = jnp.max(scores, axis=0, keepdims=True)
        weights = jnp.exp(scores - best)
        total = jnp.sum(weights, axis=0, keepdims=True)
        mixed = dot_nn(v_t[:, here], weights.astype(BF16))

        def step(j, state, query=query):
            best, total, mixed = state
            span = pl.ds(pl.multiple_of(j * tile, tile), tile)
            scores = dot_nn(k_n[span, :], query)
            new_best = jnp.maximum(best, jnp.max(scores, axis=0, keepdims=True))
            factor = jnp.exp(best - new_best)
            weights = jnp.exp(scores - new_best)
            total = total * factor + jnp.sum(weights, axis=0, keepdims=True)
            mixed = mixed * factor + dot_nn(v_t[:, span], weights.astype(BF16))
            return new_best, total, mixed

        if i:
            best, total, mixed = lax.fori_loop(0, i, step, (best, total, mixed))
        o_t[:, here] = (mixed / total).astype(BF16)
        total_ref[:, here] = best + jnp.log(total)
    for p in range(count):
        out_ref[slot_ref[p]] = o_t[:, p * rows : (p + 1) * rows]


def attend_back_kernel(
    slot_ref, in_ref, att_ref, grad_ref, total_ref, out_ref,
    q_t, q_n, k_t, k_n, v_n, g_t, g_n, delta, dq_t, dk_t, dv_t,
):
    count, _, rows = in_ref.shape
    tile = 512
    for p in range(count):
        slot = slot_ref[p]
        where = slice(p * rows, (p + 1) * rows)
        query = in_ref[slot, 0:HD, :] * jnp.asarray(SCALE, BF16)
        q_t[:, where] = query
        q_n[where, :] = query.T
        key = in_ref[slot, HD : 2 * HD, :]
        k_t[:, where] = key
        k_n[where, :] = key.T
        v_n[where, :] = in_ref[slot, 2 * HD : 3 * HD, :].T
        grad = grad_ref[slot]
        g_t[:, where] = grad
        g_n[where, :] = grad.T
        delta[:, where] = jnp.sum(
            grad.astype(F32) * att_ref[slot].astype(F32), axis=0, keepdims=True
        )
    length = count * rows
    tiles = length // tile
    below = lax.broadcasted_iota(jnp.int32, (tile, tile), 0) <= lax.broadcasted_iota(
        jnp.int32, (tile, tile), 1
    )
    dq_t[...] = jnp.zeros_like(dq_t)
    for j in range(tiles):
        here = slice(j * tile, (j + 1) * tile)

        def step(i, state, masked=False, here=here):
            key_sum, value_sum = state
            span = pl.ds(pl.multiple_of(i * tile, tile), tile)
            scores = dot_nn(k_n[here, :], q_t[:, span])
            probs = jnp.exp(scores - total_ref[:, span])
            if masked:
                probs = jnp.where(below, probs, 0.0)
            prob_grad = dot_nn(v_n[here, :], g_t[:, span])
            score_grad = (probs * (prob_grad - delta[:, span])).astype(BF16)
            value_sum = value_sum + dot_nn(probs.astype(BF16), g_n[span, :])
            key_sum = key_sum + dot_nn(score_grad, q_n[span, :])
            dq_t[:, span] = dq_t[:, span] + dot_nn(k_t[:, here], score_grad)
            return key_sum, value_sum

        zero = jnp.zeros((tile, HD), F32)
        state = step(j, (zero, zero), masked=True)
        if j + 1 < tiles:
            state = lax.fori_loop(j + 1, tiles, step, state)
        dk_t[:, here] = state[0].T
        dv_t[:, here] = state[1].T
    for p in range(count):
        slot = slot_ref[p]
        where = slice(p * rows, (p + 1) * rows)
        out_ref[slot, 0:HD, :] = (dq_t[:, where] * SCALE).astype(BF16)
        out_ref[slot, HD : 2 * HD, :] = dk_t[:, where].astype(BF16)
        out_ref[slot, 2 * HD : 3 * HD, :] = dv_t[:, where].astype(BF16)


def middle_kernel(
    side_ref, att_in, x_ref, cot_ref, vec_ref, ebias_ref,
    mix_own, mix_other, ex_own, ex_other, sh_own, sh_other,
    res_ref, gm_ref, gsend_ref, sums_ref, esum_ref,
    cotb_ref, act_keep, act_send, hid_keep, hid_send, ge_ref, att_keep, att_send, gmb_ref,
    wide, act_s, geb_s, hid_s, att_s, narrow,
):
    rows, width = x_ref.shape
    ff = wide.shape[1]
    own, other = halves(side_ref, width // 2)
    fown, fother = halves(side_ref, ff // 2)
    vec = vec_ref[...].astype(F32)
    att_s[...] = att_in[0:H].reshape(width, rows).T
    att_keep[...] = att_s[:, own]
    att_send[...] = att_s[:, other]
    middle = (
        x_ref[...].astype(F32)
        + (dot_nn(att_keep[...], mix_own[...]) + dot_nn(att_send[...], mix_other[...]))
        + vec[4:5]
    )
    unit, inv_std = normalise(middle)
    hid_s[...] = (unit * vec[5:6] + vec[6:7]).astype(BF16)
    hid_keep[...] = hid_s[:, own]
    hid_send[...] = hid_s[:, other]
    expanded = (
        dot_nn(hid_keep[...], ex_own[...])
        + dot_nn(hid_send[...], ex_other[...])
        + ebias_ref[...].astype(F32)
    )
    square = expanded * expanded
    bend = jnp.tanh(GELU_COEF * (expanded + GELU_CUBE * square * expanded))
    act_s[...] = (0.5 * expanded * (1.0 + bend)).astype(BF16)
    slope = 0.5 * (1.0 + bend) + 0.5 * expanded * (1.0 - bend * bend) * GELU_COEF * (
        1.0 + 3.0 * GELU_CUBE * square
    )
    act_keep[...] = act_s[:, fown]
    act_send[...] = act_s[:, fother]
    result = (
        middle
        + (dot_nn(act_keep[...], sh_own[...]) + dot_nn(act_send[...], sh_other[...]))
        + vec[7:8]
    )
    res_ref[...] = result.astype(BF16)
    upstream = cot_ref[...]
    cotb_ref[...] = upstream.astype(BF16)
    wide[:, fown] = dot_nt(cotb_ref[...], sh_own[...])
    wide[:, fother] = dot_nt(cotb_ref[...], sh_other[...])
    grad_expanded = wide[...] * slope
    esum_ref[...] = jnp.sum(grad_expanded, axis=0, keepdims=True)
    ge_ref[...] = grad_expanded.astype(BF16)
    narrow[:, own] = dot_nt(ge_ref[...], ex_own[...])
    narrow[:, other] = dot_nt(ge_ref[...], ex_other[...])
    grad_hidden = narrow[...]
    sums_ref[1:2] = jnp.sum(grad_hidden * unit, axis=0, keepdims=True)
    sums_ref[2:3] = jnp.sum(grad_hidden, axis=0, keepdims=True)
    grad_middle = upstream + norm_back(grad_hidden * vec[5:6], unit, inv_std)
    gm_ref[...] = grad_middle
    gmb_ref[...] = grad_middle.astype(BF16)
    sums_ref[0:1] = jnp.sum(grad_middle, axis=0, keepdims=True)
    sums_ref[3:4] = jnp.sum(upstream, axis=0, keepdims=True)
    narrow[:, own] = dot_nt(gmb_ref[...], mix_own[...])
    narrow[:, other] = dot_nt(gmb_ref[...], mix_other[...])
    gsend_ref[0:H] = narrow[...].astype(BF16).T.reshape(H, HD, rows)
    for h in range(H, gsend_ref.shape[0]):
        gsend_ref[h] = jnp.zeros(gsend_ref.shape[1:], BF16)


def finish_kernel(
    side_ref, in_ref, x_ref, gm_ref, vec_ref, hid_ref, own_ref, other_ref,
    grad_ref, sums_ref, gj_ref, hid_keep, hid_send, narrow,
):
    rows, width = x_ref.shape
    own, other = halves(side_ref, width // 2)
    vec = vec_ref[...].astype(F32)
    for k in range(3):
        gj_ref[:, k * width : (k + 1) * width] = (
            in_ref[0:H, k * HD : (k + 1) * HD, :].reshape(width, rows).T
        )
    hid_keep[...] = hid_ref[:, own]
    hid_send[...] = hid_ref[:, other]
    unit, inv_std = normalise(x_ref[...].astype(F32))
    narrow[:, own] = dot_nt(gj_ref[...], own_ref[...])
    narrow[:, other] = dot_nt(gj_ref[...], other_ref[...])
    grad_hidden = narrow[...]
    sums_ref[0:1] = jnp.sum(grad_hidden * unit, axis=0, keepdims=True)
    sums_ref[1:2] = jnp.sum(grad_hidden, axis=0, keepdims=True)
    sums_ref[2:3] = jnp.sum(gj_ref[:, :width].astype(F32), axis=0, keepdims=True)
    sums_ref[3:4] = jnp.sum(gj_ref[:, 2 * width :].astype(F32), axis=0, keepdims=True)
    grad_ref[...] = gm_ref[...] + norm_back(grad_hidden * vec[0:1], unit, inv_std)


SWAP = [(0, 1), (1, 0)]


def pieces(weight, group):
    if group == 2:
        return weight, lax.ppermute(weight, "fsdp", SWAP)
    full = lax.all_gather(weight, "fsdp", axis=0, tiled=True)
    half = full.shape[0] // 2
    return full[:half], full[half:]


def join_vector(vector, group, side):
    if group == 2:
        other = lax.ppermute(vector, "fsdp", SWAP)
        return jnp.where(
            side == 0,
            jnp.concatenate([vector, other], axis=1),
            jnp.concatenate([other, vector], axis=1),
        )
    return lax.all_gather(vector, "fsdp", axis=1, tiled=True)


def rows_over_pair(keep, send, right, group):
    if group == 2:
        left = jnp.concatenate([keep, lax.ppermute(send, "fsdp", SWAP)], axis=0)
        right = jnp.concatenate([right, lax.ppermute(right, "fsdp", SWAP)], axis=0)
    else:
        left = jnp.concatenate([keep, send], axis=1)
        left = lax.all_to_all(left, "fsdp", split_axis=1, concat_axis=0, tiled=True)
        right = lax.all_gather(right, "fsdp", axis=0, tiled=True)
    return dot_tn(left, right)


def own_columns(sums, group, side):
    if group == 2:
        half = sums.shape[1] // 2
        keep = lax.dynamic_slice_in_dim(sums, side * half, half, 1)
        send = lax.dynamic_slice_in_dim(sums, (1 - side) * half, half, 1)
        return keep + lax.ppermute(send, "fsdp", SWAP)
    return lax.psum_scatter(sums, "fsdp", scatter_dimension=1, tiled=True)


def vector_total(sums, count):
    spread = jnp.broadcast_to(sums[None], (count,) + sums.shape)
    return jnp.sum(lax.all_to_all(spread, "ctx", 0, 0, tiled=True), axis=0)


def bit_orders(count):
    bits = list(range(count.bit_length() - 1))
    turn, last = bits[:3], bits[3:]
    return [turn[k:] + turn[:k] + last for k in range(3)]


def swap_bit(part, bit, count):
    return lax.ppermute(part, "ctx", [(d, d ^ (1 << bit)) for d in range(count)])


def total_over_ctx(parts, count):
    index = lax.axis_index("ctx")
    orders = bit_orders(count)
    steps = len(orders[0])
    parts = list(parts)
    for s in range(steps):
        for k, part in enumerate(parts):
            bit = orders[k][s]
            high = (index >> bit) & 1
            half = part.shape[0] // 2
            keep = lax.dynamic_slice_in_dim(part, high * half, half, 0)
            send = lax.dynamic_slice_in_dim(part, (1 - high) * half, half, 0)
            came = swap_bit(send, bit, count)
            parts[k] = (keep.astype(F32) + came.astype(F32)).astype(BF16)
    for s in reversed(range(steps)):
        for k, part in enumerate(parts):
            bit = orders[k][s]
            high = (index >> bit) & 1
            came = swap_bit(part, bit, count)
            parts[k] = jnp.where(
                high == 0,
                jnp.concatenate([part, came], axis=0),
                jnp.concatenate([came, part], axis=0),
            )
    return parts


def stack_columns(weights, third, wide):
    blocks = []
    for weight in weights:
        span = weight.shape[1] // 3
        for c in range(span // wide):
            start = third * span + c * wide
            blocks.append(weight[:, start : start + wide])
    return jnp.concatenate(blocks, axis=0).astype(BF16)


def unstack_columns(parts, shapes, wide):
    outs = []
    first = 0
    for rows, cols in shapes:
        blocks = []
        each = cols // 3 // wide
        for part in parts:
            for c in range(each):
                blocks.append(part[first + c * rows : first + (c + 1) * rows])
        first += each * rows
        outs.append(jnp.concatenate(blocks, axis=1).astype(F32))
    return outs


def body(
    block_input, out_cotangent, block_position, first_gain, first_shift, qkv_weight, query_bias,
    value_bias, output_weight, output_bias, second_gain, second_shift, expand_weight, expand_bias,
    shrink_weight, shrink_bias,
):
    count = lax.axis_size("ctx")
    group = lax.axis_size("fsdp")
    rows, width = block_input.shape[1:]
    ff = expand_weight.shape[1]
    length = count * rows
    side = lax.axis_index("fsdp") if group == 2 else jnp.int32(0)
    sides = jnp.reshape(side, (1,)).astype(jnp.int32)
    table = block_position[0]
    places = jnp.arange(count, dtype=jnp.int32)
    slots = jnp.sum(
        jnp.where(table[None, :] == places[:, None], places[None, :], 0), axis=1
    ).astype(jnp.int32)
    x = block_input[0]
    vec = join_vector(
        jnp.stack(
            [first_gain, first_shift, query_bias, value_bias, output_bias, second_gain,
             second_shift, shrink_bias]
        ),
        group, side,
    )
    qkv = pieces(qkv_weight, group)
    ebias = join_vector(expand_bias[None], group, side)
    mix = pieces(output_weight, group)
    expand = pieces(expand_weight, group)
    shrink = pieces(shrink_weight, group)
    size = width * ff

    hidden_a, qkv_send = call(
        project_kernel,
        [((rows, width), BF16), ((count, 3 * HD, rows), BF16)],
        [], "project", 6 * rows * width * width,
        sides, x, vec, *qkv,
    )
    qkv_here = lax.all_to_all(qkv_send, "ctx", 0, 0, tiled=True)
    att_send, log_total = call(
        attend_kernel,
        [((count, HD, rows), BF16), ((1, length), F32)],
        [((HD, length), BF16), ((length, HD), BF16), ((HD, length), BF16), ((HD, length), BF16)],
        "attend", 2 * length * length * HD,
        slots, qkv_here,
    )
    att_here = lax.all_to_all(att_send, "ctx", 0, 0, tiled=True)
    half = width // 2
    (
        result, grad_middle, grad_send, sums, esum, cot_b, act_keep, act_out, hidb_keep, hidb_out,
        ge_b, att_keep, att_out, gm_b,
    ) = call(
        middle_kernel,
        [
            ((rows, width), BF16), ((rows, width), F32), ((count, HD, rows), BF16),
            ((4, width), F32), ((1, ff), F32), ((rows, width), BF16), ((rows, ff // 2), BF16),
            ((rows, ff // 2), BF16), ((rows, half), BF16), ((rows, half), BF16),
            ((rows, ff), BF16), ((rows, half), BF16), ((rows, half), BF16), ((rows, width), BF16),
        ],
        [
            ((rows, ff), F32), ((rows, ff), BF16), ((rows, ff), BF16), ((rows, width), BF16),
            ((rows, width), BF16), ((rows, width), F32),
        ],
        "middle", 8 * rows * size + 4 * rows * width * width,
        sides, att_here, x, out_cotangent[0], vec, ebias, *mix, *expand, *shrink,
    )
    grad_here = lax.all_to_all(grad_send, "ctx", 0, 0, tiled=True)
    (dqkv_send,) = call(
        attend_back_kernel,
        [((count, 3 * HD, rows), BF16)],
        [
            ((HD, length), BF16), ((length, HD), BF16), ((HD, length), BF16),
            ((length, HD), BF16), ((length, HD), BF16), ((HD, length), BF16),
            ((length, HD), BF16), ((1, length), F32), ((HD, length), F32), ((HD, length), F32),
            ((HD, length), F32),
        ],
        "attend_back", 5 * length * length * HD,
        slots, qkv_here, att_send, grad_here, log_total,
    )
    dqkv_here = lax.all_to_all(dqkv_send, "ctx", 0, 0, tiled=True)

    grad_shrink = rows_over_pair(act_keep, act_out, cot_b, group)
    grad_expand = rows_over_pair(hidb_keep, hidb_out, ge_b, group)
    grad_mix = rows_over_pair(att_keep, att_out, gm_b, group)
    early = (grad_shrink, grad_expand, grad_mix)
    early_sums = total_over_ctx([stack_columns(early, k, 256) for k in range(3)], count)
    grad_shrink, grad_expand, grad_mix = unstack_columns(
        early_sums, [g.shape for g in early], 256
    )
    each = width // group
    esum = esum.reshape(group, 4, each).swapaxes(0, 1).reshape(4, width)
    sums = own_columns(jnp.concatenate([sums, esum], axis=0), group, side)
    sums = vector_total(sums, count)

    input_grad, late, gj, hida_keep, hida_out = call(
        finish_kernel,
        [
            ((rows, width), F32), ((4, width), F32), ((rows, 3 * width), BF16),
            ((rows, half), BF16), ((rows, half), BF16),
        ],
        [((rows, width), F32)],
        "finish", 6 * rows * width * width,
        sides, dqkv_here, x, grad_middle, vec, hidden_a, *qkv,
    )
    grad_qkv = rows_over_pair(hida_keep, hida_out, gj, group)
    late_sums = total_over_ctx([stack_columns((grad_qkv,), k, 256) for k in range(3)], count)
    (grad_qkv,) = unstack_columns(late_sums, [grad_qkv.shape], 256)
    late = vector_total(own_columns(late, group, side), count)
    return (
        result[None], input_grad[None], late[0], late[1], grad_qkv, late[2], late[3],
        grad_mix, sums[0], sums[1], sums[2], grad_expand, sums[4:8].reshape(-1), grad_shrink,
        sums[3],
    )


def solution(mesh):
    block = P("fsdp", "ctx", None)
    vector, matrix = P("fsdp"), P("fsdp", None)
    return jax.shard_map(
        body,
        mesh=mesh,
        in_specs=(
            block, block, matrix, vector, vector, matrix, vector, vector, matrix, vector, vector,
            vector, matrix, vector, matrix, vector,
        ),
        out_specs=(
            block, block, vector, vector, matrix, vector, vector, matrix, vector, vector, vector,
            matrix, vector, matrix, vector,
        ),
        check_vma=False,
    )
```

time: 970 us -> 345 us (0.36)
  waiting for transfers between devices: 504 us -> 144 us
  blocking collectives: 183 us -> 0 us
  matrix products: 106 us -> 5.9 us
  starting transfers between devices: 0.52 us -> 97 us
  local copies, waits for them, and re-layouts: 93.5 us -> 27.5 us
  Pallas kernels: 0 us -> 39.2 us
  other arithmetic: 51 us -> 27.9 us
  loops' own time: 16.2 us -> 0 us
  between operations: 17.2 us -> 1.79 us
    psum x1 -> x0, waiting for transfers between devices: 307 us -> none  [body(): lax.psum((shares[0], shares[1], shares[2], shares[3], shares[4], shares[5...]
    all_gather x8 -> x0, waiting for transfers between devices: 175 us -> none  [the longest x1 70 us: body(): part_values = lax.all_gather(values, 'ctx', axis=0, tiled=True)]
    ppermute x0 -> x64, waiting for transfers between devices: none -> 107 us  [the longest x48 102 us: swap_bit(): return lax.ppermute(part, 'ctx', [(d, d ^ 1 << bit) for d in range(count)])]
    dot_general x32 -> x4, matrix products: 106 us -> 5.9 us  [dot_tn(): lax.dot_general(left, right, (((0,), (0,)), ((), ())), preferred_element_...]
    all_gather x11 -> x0, blocking collectives: 97.7 us -> none  [the longest x1 41.7 us: body(): lax.all_gather(log_total.T, 'ctx', axis=0, tiled=True)]
    psum x1 -> x0, blocking collectives: 81.7 us -> none  [body(): lax.psum((shares[0], shares[1], shares[2], shares[3], shares[4], shares[5...]
    ppermute x0 -> x64, starting transfers between devices: none -> 62.2 us  [the longest x48 58.6 us: swap_bit(): return lax.ppermute(part, 'ctx', [(d, d ^ 1 << bit) for d in range(count)])]
    pallas_call x0 -> x5, Pallas kernels: none -> 39.2 us  [call(): pl.pallas_call(kernel, out_shape=[jax.ShapeDtypeStruct(s, d) for s, d in...]
  transfers between devices with their start and end apart: 13 -> 70, of which waited for: 7 -> 29; matrix products, arithmetic and copies ran while one was open for 23% -> 13% of each run, Pallas kernels for 0% -> 8%
where the time goes in v1:
time: 345 us; the launch traced here: 344 us
  waiting for transfers between devices  144 us (42%)
  starting transfers between devices  97 us (28%)
  Pallas kernels  39.2 us (11%)
  other arithmetic  27.9 us (8%)
  local copies, waits for them, and re-layouts  27.5 us (8%)
  matrix products  5.9 us (2%)
    ppermute x48, waiting for transfers between devices, swap_bit(): return lax.ppermute(part, 'ctx', [(d, d ^ 1 << bit) for d in range(count)])  102 us
    ppermute x48, starting transfers between devices, swap_bit(): return lax.ppermute(part, 'ctx', [(d, d ^ 1 << bit) for d in range(count)])  58.6 us
    pallas_call x5, Pallas kernels, call(): pl.pallas_call(kernel, out_shape=[jax.ShapeDtypeStruct(s, d) for s, d in...  39.2 us
    all_to_all x1, waiting for transfers between devices, body(): qkv_here = lax.all_to_all(qkv_send, 'ctx', 0, 0, tiled=True)  19.3 us
    all_to_all x1, waiting for transfers between devices, body(): grad_here = lax.all_to_all(grad_send, 'ctx', 0, 0, tiled=True)  11.4 us
    all_to_all x2, starting transfers between devices, vector_total(): return jnp.sum(lax.all_to_all(spread, 'ctx', 0, 0, tiled=True), axis=0)  9.98 us
    unnamed x66, local copies, waits for them, and re-layouts  8.67 us
    convert_element_type x4, other arithmetic, unstack_columns(): outs.append(jnp.concatenate(blocks, axis=1).astype(F32))  8.41 us
  transfers between devices with their start and end apart: 70, of which 29 were waited for; matrix products, arithmetic and copies ran while one was open for 13% of the time, Pallas kernels for 8%

profile of v1, /device:TPU:0, one launch (start us, length us, event | category | flops | bytes accessed | tf_op | source)
XLA Modules:
  0.0 343.5 jit_solution(11479183942176280739)
XLA Ops:
  7.3 3.9 %collective-permute-done = bf16[8,384]{1,0:T(8,128)(2,1)S(1)} collective-permute-done((bf16[8,384]{1,0:T(8,128)(2,1)S(1)}, bf16[8,384]{1,0:T(8,128)(2,1)S(1)}, u32[]{:S(2)}, u32[]{:S(2)}) %collective-permute-start) | collective-permute-done | bytes 6176 | tf_op jit(solution)/shard_map/ppermute | solution.py:295
  13.1 4.1 %project.1 = (bf16[128,768]{1,0:T(8,128)(2,1)}, bf16[16,192,128]{2,1,0:T(8,128)(2,1)}) custom-call(s32[1]{0:T(128)} %bitcast.side_ref, bf16[128,768]{1,0:T(8,128)(2,1)} %bitcast.9, bf16[8,768]{1,0:T(8,128)(2,1)} %maximum_select_fusion.24.vec_ref, bf16[384,2304]{1,0:T(8,128)(2,1)} %own_ref.3, bf16[384,2304]{1,0:T(8,128)(2,1)} %copy-done), custom_call_target="tpu_custom_call" | custom-call | flops 452984832 | bytes 3747844 | tf_op jit(solution)/shard_map/project/pallas_call | solution.py:59
  17.2 8.4 %all-to-all-start = ((bf16[16,192,128]{2,1,0:T(8,128)(2,1)}), bf16[16,192,128]{2,1,0:T(8,128)(2,1)S(1)}, u32[]{:S(2)}, u32[]{:S(2)}) async-start(bf16[16,192,128]{2,1,0:T(8,128)(2,1)} %get-tuple-element.38), calls=%async_computation | async-start | bytes 1572864 | tf_op jit(solution)/shard_map/all_to_all | solution.py:428
  26.3 19.3 %all-to-all-done.in_ref = bf16[16,192,128]{2,1,0:T(8,128)(2,1)S(1)} async-done(((bf16[16,192,128]{2,1,0:T(8,128)(2,1)}), bf16[16,192,128]{2,1,0:T(8,128)(2,1)S(1)}, u32[]{:S(2)}, u32[]{:S(2)}) %all-to-all-start) | async-done | bytes 786464 | tf_op jit(solution)/shard_map/all_to_all | solution.py:428
  46.5 7.5 %attend.1 = (bf16[16,64,128]{2,1,0:T(8,128)(2,1)}, f32[1,2048]{1,0:T(1,128)}) custom-call(s32[16]{0:T(128)} %select_reduce_fusion.slot_ref, bf16[16,192,128]{2,1,0:T(8,128)(2,1)} %copy-done.10), custom_call_target="tpu_custom_call" | custom-call | flops 536870912 | bytes 786496 | tf_op jit(solution)/shard_map/attend/pallas_call | solution.py:59
  54.0 4.9 %all-to-all-start.1 = ((bf16[16,64,128]{2,1,0:T(8,128)(2,1)}), bf16[16,64,128]{2,1,0:T(8,128)(2,1)S(1)}, u32[]{:S(2)}, u32[]{:S(2)}) async-start(bf16[16,64,128]{2,1,0:T(8,128)(2,1)} %get-tuple-element.39.att_ref), calls=%async_computation.1 | async-start | bytes 524288 | tf_op jit(solution)/shard_map/all_to_all | solution.py:436
  60.9 6.6 %all-to-all-done.1.att_in = bf16[16,64,128]{2,1,0:T(8,128)(2,1)S(1)} async-done(((bf16[16,64,128]{2,1,0:T(8,128)(2,1)}), bf16[16,64,128]{2,1,0:T(8,128)(2,1)S(1)}, u32[]{:S(2)}, u32[]{:S(2)}) %all-to-all-start.1) | async-done | bytes 262176 | tf_op jit(solution)/shard_map/all_to_all | solution.py:436
  68.2 12.5 %middle.1 = (bf16[128,768]{1,0:T(8,128)(2,1)}, f32[128,768]{1,0:T(8,128)}, bf16[16,64,128]{2,1,0:T(8,128)(2,1)}, f32[4,768]{1,0:T(4,128)}, f32[1,3072]{1,0:T(1,1...) custom-call(s32[1]{0:T(128)} %bitcast.side_ref, ...), custom_call_target="tpu_custom_call" | custom-call | flops 2717908992 | bytes 11487236 | tf_op jit(solution)/shard_map/middle/pallas_call | solution.py:59
  86.6 4.4 %all-to-all-start.5 = ((f32[16,8,384]{2,1,0:T(8,128)}), f32[16,8,384]{2,1,0:T(8,128)}, u32[]{:S(2)}, u32[]{:S(2)}) async-start(f32[16,8,384]{2,1,0:T(8,128)} %broadcast_in_dim.38), calls=%async_computation.5 | async-start | bytes 393216 | tf_op jit(solution)/shard_map/all_to_all | solution.py:326
  100.5 5.7 %all-to-all-start.2 = ((bf16[16,64,128]{2,1,0:T(8,128)(2,1)}), bf16[16,64,128]{2,1,0:T(8,128)(2,1)}, u32[]{:S(2)}, u32[]{:S(2)}) async-start(bf16[16,64,128]{2,1,0:T(8,128)(2,1)} %get-tuple-element.41), calls=%async_computation.2 | async-start | bytes 524288 | tf_op jit(solution)/shard_map/all_to_all | solution.py:456
  113.7 11.4 %all-to-all-done.2.grad_ref = bf16[16,64,128]{2,1,0:T(8,128)(2,1)} async-done(((bf16[16,64,128]{2,1,0:T(8,128)(2,1)}), bf16[16,64,128]{2,1,0:T(8,128)(2,1)}, u32[]{:S(2)}, u32[]{:S(2)}) %all-to-all-start.2) | async-done | bytes 262176 | tf_op jit(solution)/shard_map/all_to_all | solution.py:456
  125.0 10.1 %attend_back.1 = bf16[16,192,128]{2,1,0:T(8,128)(2,1)} custom-call(s32[16]{0:T(128)} %select_reduce_fusion.slot_ref, bf16[16,192,128]{2,1,0:T(8,128)(2,1)} %copy-done.10, bf16[16,64,128]{2,1,0:T(8,128)(2,1)} %get-tuple-element.39.att_ref, bf16[16,64,128]{2,1,0:T(8,128)(2,1)} %all-to-all-done.2.grad_ref, f32[1,2048]{1,0:T(1,128)} %get-tuple-element.42.total_ref), custom_call_target="tpu_custom_call" | custom-call | flops 1342177280 | bytes 1318976 | tf_op jit(solution)/shard_map/attend_back/pallas_call | solution.py:59
  135.1 5.9 %all-to-all-start.3 = ((bf16[16,192,128]{2,1,0:T(8,128)(2,1)}), bf16[16,192,128]{2,1,0:T(8,128)(2,1)}, u32[]{:S(2)}, u32[]{:S(2)}) async-start(bf16[16,192,128]{2,1,0:T(8,128)(2,1)} %attend_back.1), calls=%async_computation.3 | async-start | bytes 1572864 | tf_op jit(solution)/shard_map/all_to_all | solution.py:469
  149.6 25.8 %collective-permute-done.55 = bf16[1728,256]{1,0:T(8,128)(2,1)S(1)} collective-permute-done((bf16[1728,256]{1,0:T(8,128)(2,1)S(1)}, bf16[1728,256]{1,0:T(8,128)(2,1)S(1)}, u32[]{:S(2)}, u32[]{:S(2)}) %collective-permute-start.55) | collective-permute-done | bytes 884768 | tf_op jit(solution)/shard_map/ppermute | solution.py:336
  176.6 5.0 %finish.1 = (f32[128,768]{1,0:T(8,128)}, f32[4,768]{1,0:T(4,128)}, bf16[128,2304]{1,0:T(8,128)(2,1)}, bf16[128,384]{1,0:T(8,128)(2,1)}, bf16[128,384]{1,0:T(8,128)(2,1)}) custom-call(s32[1]{0:T(128)} %bitcast.side_ref, bf16[16,192,128]{2,1,0:T(8,128)(2,1)} %all-to-all-done.3.in_ref, bf16[128,768]{1,0:T(8,128)(2,1)} %bitcast.11, ...), custom_call_target="tpu_custom_call" | custom-call | flops 452984832 | bytes 5124100 | tf_op jit(solution)/shard_map/finish/pallas_call | solution.py:59
  186.4 5.6 %all-to-all-start.4 = ((f32[16,4,384]{2,1,0:T(4,128)}), f32[16,4,384]{2,1,0:T(4,128)}, u32[]{:S(2)}, u32[]{:S(2)}) async-start(f32[16,4,384]{2,1,0:T(4,128)} %broadcast_in_dim.37), calls=%async_computation.4 | async-start | bytes 196608 | tf_op jit(solution)/shard_map/all_to_all | solution.py:326
  208.4 7.6 %collective-permute-done.42 = bf16[216,256]{1,0:T(8,128)(2,1)S(1)} collective-permute-done((bf16[216,256]{1,0:T(8,128)(2,1)S(1)}, bf16[216,256]{1,0:T(8,128)(2,1)S(1)}, u32[]{:S(2)}, u32[]{:S(2)}) %collective-permute-start.42) | collective-permute-done | bytes 110624 | tf_op jit(solution)/shard_map/ppermute | solution.py:336
  216.1 3.4 %collective-permute-done.50 = bf16[216,256]{1,0:T(8,128)(2,1)S(1)} collective-permute-done((bf16[216,256]{1,0:T(8,128)(2,1)S(1)}, bf16[216,256]{1,0:T(8,128)(2,1)S(1)}, u32[]{:S(2)}, u32[]{:S(2)}) %collective-permute-start.50) | collective-permute-done | bytes 110624 | tf_op jit(solution)/shard_map/ppermute | solution.py:336
  219.7 4.6 %collective-permute-done.58 = bf16[216,256]{1,0:T(8,128)(2,1)S(1)} collective-permute-done((bf16[216,256]{1,0:T(8,128)(2,1)S(1)}, bf16[216,256]{1,0:T(8,128)(2,1)S(1)}, u32[]{:S(2)}, u32[]{:S(2)}) %collective-permute-start.58) | collective-permute-done | bytes 110624 | tf_op jit(solution)/shard_map/ppermute | solution.py:336
  228.2 2.7 collective-permute-start.17
  231.0 3.7 %collective-permute-start.25 = (bf16[576,256]{1,0:T(8,128)(2,1)S(1)}, bf16[576,256]{1,0:T(8,128)(2,1)S(1)}, u32[]{:S(2)}, u32[]{:S(2)}) collective-permute-start(bf16[576,256]{1,0:T(8,128)(2,1)S(1)} %constant_dynamic-slice_fusion.15), channel_id=1, source_target_pairs={{0,8},{2,10},{4,12},{6,14},{8,0},{10,2},{12,4},{14,6},{16,24},{18,... | collective-permute-start | bytes 884744 | tf_op jit(solution)/shard_map/ppermute | solution.py:336
  235.9 9.4 %collective-permute-done.44 = bf16[432,256]{1,0:T(8,128)(2,1)S(1)} collective-permute-done((bf16[432,256]{1,0:T(8,128)(2,1)S(1)}, bf16[432,256]{1,0:T(8,128)(2,1)S(1)}, u32[]{:S(2)}, u32[]{:S(2)}) %collective-permute-start.44) | collective-permute-done | bytes 221216 | tf_op jit(solution)/shard_map/ppermute | solution.py:336
  247.8 5.9 %collective-permute-done.60 = bf16[432,256]{1,0:T(8,128)(2,1)S(1)} collective-permute-done((bf16[432,256]{1,0:T(8,128)(2,1)S(1)}, bf16[432,256]{1,0:T(8,128)(2,1)S(1)}, u32[]{:S(2)}, u32[]{:S(2)}) %collective-permute-start.60) | collective-permute-done | bytes 221216 | tf_op jit(solution)/shard_map/ppermute | solution.py:336
  259.3 4.5 %collective-permute-done.10 = bf16[288,256]{1,0:T(8,128)(2,1)S(1)} collective-permute-done((bf16[288,256]{1,0:T(8,128)(2,1)S(1)}, bf16[288,256]{1,0:T(8,128)(2,1)S(1)}, u32[]{:S(2)}, u32[]{:S(2)}) %collective-permute-start.10) | collective-permute-done | bytes 147488 | tf_op jit(solution)/shard_map/ppermute | solution.py:336
  263.9 2.6 collective-permute-start.26
  266.9 2.8 collective-permute-done.26
  277.1 2.7 collective-permute-done.12
  292.4 2.5 collective-permute-done.14
  309.8 13.0 %collective-permute-done.16 = bf16[576,256]{1,0:T(8,128)(2,1)S(1)} collective-permute-done((bf16[576,256]{1,0:T(8,128)(2,1)S(1)}, bf16[576,256]{1,0:T(8,128)(2,1)S(1)}, u32[]{:S(2)}, u32[]{:S(2)}) %collective-permute-start.16) | collective-permute-done | bytes 294944 | tf_op jit(solution)/shard_map/ppermute | solution.py:336
  325.1 4.5 %collective-permute-done.32 = bf16[576,256]{1,0:T(8,128)(2,1)S(1)} collective-permute-done((bf16[576,256]{1,0:T(8,128)(2,1)S(1)}, bf16[576,256]{1,0:T(8,128)(2,1)S(1)}, u32[]{:S(2)}, u32[]{:S(2)}) %collective-permute-start.32) | collective-permute-done | bytes 294944 | tf_op jit(solution)/shard_map/ppermute | solution.py:336
  336.4 2.8 convert_element_type.308
  341.0 2.5 maximum_convert_fusion
  (300 shorter events, 125.4 us)
Async XLA Ops:
  1.2 59.7 %collective-permute-start.4 = (bf16[384,3072]{1,0:T(8,128)(2,1)}, bf16[384,3072]{1,0:T(8,128)(2,1)}, u32[]{:S(2)}, u32[]{:S(2)}) collective-permute-start(bf16[384,3072]{1,0:T(8,128)(2,1)} %ex_own.1), channel_id=1, source_target_pairs={{0,1},{1,0},{2,3},{3,2},{4,5},{5,4},{6,7},{7,6},{8,9},{9,8},{10,11... | collective-permute-start | bytes 7077896 | tf_op jit(solution)/shard_map/ppermute | solution.py:287
  1.2 59.6 %collective-permute-start.5 = (bf16[1536,768]{1,0:T(8,128)(2,1)}, bf16[1536,768]{1,0:T(8,128)(2,1)}, u32[]{:S(2)}, u32[]{:S(2)}) collective-permute-start(bf16[1536,768]{1,0:T(8,128)(2,1)} %sh_own.1), channel_id=1, source_target_pairs={{0,1},{1,0},{2,3},{3,2},{4,5},{5,4},{6,7},{7,6},{8,9},{9,8},{10,11... | collective-permute-start | bytes 7077896 | tf_op jit(solution)/shard_map/ppermute | solution.py:287
  17.2 28.4 %all-to-all-start = ((bf16[16,192,128]{2,1,0:T(8,128)(2,1)}), bf16[16,192,128]{2,1,0:T(8,128)(2,1)S(1)}, u32[]{:S(2)}, u32[]{:S(2)}) async-start(bf16[16,192,128]{2,1,0:T(8,128)(2,1)} %get-tuple-element.38), calls=%async_computation | async-start | bytes 1572864 | tf_op jit(solution)/shard_map/all_to_all | solution.py:428
  25.6 35.2 %collective-permute-start.3 = (bf16[384,768]{1,0:T(8,128)(2,1)S(1)}, bf16[384,768]{1,0:T(8,128)(2,1)S(1)}, u32[]{:S(2)}, u32[]{:S(2)}) collective-permute-start(bf16[384,768]{1,0:T(8,128)(2,1)S(1)} %copy-done.11), channel_id=1, source_target_pairs={{0,1},{1,0},{2,3},{3,2},{4,5},{5,4},{6,7},{7,6},{8,9},{9,8},{10,11... | collective-permute-start | bytes 1769480 | tf_op jit(solution)/shard_map/ppermute | solution.py:287
  54.0 13.5 %all-to-all-start.1 = ((bf16[16,64,128]{2,1,0:T(8,128)(2,1)}), bf16[16,64,128]{2,1,0:T(8,128)(2,1)S(1)}, u32[]{:S(2)}, u32[]{:S(2)}) async-start(bf16[16,64,128]{2,1,0:T(8,128)(2,1)} %get-tuple-element.39.att_ref), calls=%async_computation.1 | async-start | bytes 524288 | tf_op jit(solution)/shard_map/all_to_all | solution.py:436
  86.6 13.9 %all-to-all-start.5 = ((f32[16,8,384]{2,1,0:T(8,128)}), f32[16,8,384]{2,1,0:T(8,128)}, u32[]{:S(2)}, u32[]{:S(2)}) async-start(f32[16,8,384]{2,1,0:T(8,128)} %broadcast_in_dim.38), calls=%async_computation.5 | async-start | bytes 393216 | tf_op jit(solution)/shard_map/all_to_all | solution.py:326
  99.1 43.9 %collective-permute-start.39 = (bf16[1728,256]{1,0:T(8,128)(2,1)}, bf16[1728,256]{1,0:T(8,128)(2,1)}, u32[]{:S(2)}, u32[]{:S(2)}) collective-permute-start(bf16[1728,256]{1,0:T(8,128)(2,1)} %constant_dynamic-slice_fusion.11), channel_id=1, source_target_pairs={{0,2},{2,0},{4,6},{6,4},{8,10},{10,8},{12,14},{14,12},{16,18},{18,... | collective-permute-start | bytes 2654216 | tf_op jit(solution)/shard_map/ppermute | solution.py:336
  100.5 24.5 %all-to-all-start.2 = ((bf16[16,64,128]{2,1,0:T(8,128)(2,1)}), bf16[16,64,128]{2,1,0:T(8,128)(2,1)}, u32[]{:S(2)}, u32[]{:S(2)}) async-start(bf16[16,64,128]{2,1,0:T(8,128)(2,1)} %get-tuple-element.41), calls=%async_computation.2 | async-start | bytes 524288 | tf_op jit(solution)/shard_map/all_to_all | solution.py:456
  111.8 35.0 %collective-permute-start.47 = (bf16[1728,256]{1,0:T(8,128)(2,1)}, bf16[1728,256]{1,0:T(8,128)(2,1)}, u32[]{:S(2)}, u32[]{:S(2)}) collective-permute-start(bf16[1728,256]{1,0:T(8,128)(2,1)} %constant_dynamic-slice_fusion.7), channel_id=1, source_target_pairs={{0,4},{2,6},{4,0},{6,2},{8,12},{10,14},{12,8},{14,10},{16,20},{18,... | collective-permute-start | bytes 2654216 | tf_op jit(solution)/shard_map/ppermute | solution.py:336
  135.1 41.4 %all-to-all-start.3 = ((bf16[16,192,128]{2,1,0:T(8,128)(2,1)}), bf16[16,192,128]{2,1,0:T(8,128)(2,1)}, u32[]{:S(2)}, u32[]{:S(2)}) async-start(bf16[16,192,128]{2,1,0:T(8,128)(2,1)} %attend_back.1), calls=%async_computation.3 | async-start | bytes 1572864 | tf_op jit(solution)/shard_map/all_to_all | solution.py:469
  141.1 34.3 %collective-permute-start.55 = (bf16[1728,256]{1,0:T(8,128)(2,1)S(1)}, bf16[1728,256]{1,0:T(8,128)(2,1)S(1)}, u32[]{:S(2)}, u32[]{:S(2)}) collective-permute-start(bf16[1728,256]{1,0:T(8,128)(2,1)S(1)} %constant_dynamic-slice_fusion.3), channel_id=1, source_target_pairs={{0,8},{2,10},{4,12},{6,14},{8,0},{10,2},{12,4},{14,6},{16,24},{18,... | collective-permute-start | bytes 2654216 | tf_op jit(solution)/shard_map/ppermute | solution.py:336
  145.3 46.7 %collective-permute-start.40 = (bf16[864,256]{1,0:T(8,128)(2,1)}, bf16[864,256]{1,0:T(8,128)(2,1)}, u32[]{:S(2)}, u32[]{:S(2)}) collective-permute-start(bf16[864,256]{1,0:T(8,128)(2,1)} %constant_dynamic-slice_fusion.10), channel_id=1, source_target_pairs={{0,4},{2,6},{4,0},{6,2},{8,12},{10,14},{12,8},{14,10},{16,20},{18,... | collective-permute-start | bytes 1327112 | tf_op jit(solution)/shard_map/ppermute | solution.py:336
  149.0 46.7 %collective-permute-start.48 = (bf16[864,256]{1,0:T(8,128)(2,1)}, bf16[864,256]{1,0:T(8,128)(2,1)}, u32[]{:S(2)}, u32[]{:S(2)}) collective-permute-start(bf16[864,256]{1,0:T(8,128)(2,1)} %constant_dynamic-slice_fusion.6), channel_id=1, source_target_pairs={{0,8},{2,10},{4,12},{6,14},{8,0},{10,2},{12,4},{14,6},{16,24},{18,... | collective-permute-start | bytes 1327112 | tf_op jit(solution)/shard_map/ppermute | solution.py:336
  183.0 15.4 %collective-permute-start.56 = (bf16[864,256]{1,0:T(8,128)(2,1)}, bf16[864,256]{1,0:T(8,128)(2,1)S(1)}, u32[]{:S(2)}, u32[]{:S(2)}) collective-permute-start(bf16[864,256]{1,0:T(8,128)(2,1)} %constant_dynamic-slice_fusion.2), channel_id=1, source_target_pairs={{0,2},{2,0},{4,6},{6,4},{8,10},{10,8},{12,14},{14,12},{16,18},{18,... | collective-permute-start | bytes 1327112 | tf_op jit(solution)/shard_map/ppermute | solution.py:336
  184.5 39.9 %collective-permute-start.8 = (bf16[128,2304]{1,0:T(8,128)(2,1)}, bf16[128,2304]{1,0:T(8,128)(2,1)}, u32[]{:S(2)}, u32[]{:S(2)}) collective-permute-start(bf16[128,2304]{1,0:T(8,128)(2,1)} %get-tuple-element.49), channel_id=1, source_target_pairs={{0,1},{1,0},{2,3},{3,2},{4,5},{5,4},{6,7},{7,6},{8,9},{9,8},{10,11... | collective-permute-start | bytes 1769480 | tf_op jit(solution)/shard_map/ppermute | solution.py:307
  184.7 39.7 %collective-permute-start.7 = (bf16[128,384]{1,0:T(8,128)(2,1)}, bf16[128,384]{1,0:T(8,128)(2,1)}, u32[]{:S(2)}, u32[]{:S(2)}) collective-permute-start(bf16[128,384]{1,0:T(8,128)(2,1)} %get-tuple-element.48), channel_id=1, source_target_pairs={{0,1},{1,0},{2,3},{3,2},{4,5},{5,4},{6,7},{7,6},{8,9},{9,8},{10,11... | collective-permute-start | bytes 294920 | tf_op jit(solution)/shard_map/ppermute | solution.py:306
  186.4 13.7 %all-to-all-start.4 = ((f32[16,4,384]{2,1,0:T(4,128)}), f32[16,4,384]{2,1,0:T(4,128)}, u32[]{:S(2)}, u32[]{:S(2)}) async-start(f32[16,4,384]{2,1,0:T(4,128)} %broadcast_in_dim.37), calls=%async_computation.4 | async-start | bytes 196608 | tf_op jit(solution)/shard_map/all_to_all | solution.py:326
  205.3 14.3 %collective-permute-start.50 = (bf16[216,256]{1,0:T(8,128)(2,1)S(1)}, bf16[216,256]{1,0:T(8,128)(2,1)S(1)}, u32[]{:S(2)}, u32[]{:S(2)}) collective-permute-start(bf16[216,256]{1,0:T(8,128)(2,1)S(1)} %constant_dynamic-slice_fusion.4), channel_id=1, source_target_pairs={{0,16},{2,18},{4,20},{6,22},{8,24},{10,26},{12,28},{14,30},{16,0},... | collective-permute-start | bytes 331784 | tf_op jit(solution)/shard_map/ppermute | solution.py:336
  206.4 17.9 %collective-permute-start.58 = (bf16[216,256]{1,0:T(8,128)(2,1)S(1)}, bf16[216,256]{1,0:T(8,128)(2,1)S(1)}, u32[]{:S(2)}, u32[]{:S(2)}) collective-permute-start(bf16[216,256]{1,0:T(8,128)(2,1)S(1)} %constant_dynamic-slice_fusion), channel_id=1, source_target_pairs={{0,16},{2,18},{4,20},{6,22},{8,24},{10,26},{12,28},{14,30},{16,0},... | collective-permute-start | bytes 331784 | tf_op jit(solution)/shard_map/ppermute | solution.py:336
  216.0 14.9 %collective-permute-start.43 = (bf16[216,256]{1,0:T(8,128)(2,1)S(1)}, bf16[216,256]{1,0:T(8,128)(2,1)S(1)}, u32[]{:S(2)}, u32[]{:S(2)}) collective-permute-start(bf16[216,256]{1,0:T(8,128)(2,1)S(1)} %add_convert_fusion.17), channel_id=1, source_target_pairs={{0,16},{2,18},{4,20},{6,22},{8,24},{10,26},{12,28},{14,30},{16,0},... | collective-permute-start | bytes 331784 | tf_op jit(solution)/shard_map/ppermute | solution.py:336
  219.6 15.2 %collective-permute-start.51 = (bf16[216,256]{1,0:T(8,128)(2,1)S(1)}, bf16[216,256]{1,0:T(8,128)(2,1)S(1)}, u32[]{:S(2)}, u32[]{:S(2)}) collective-permute-start(bf16[216,256]{1,0:T(8,128)(2,1)S(1)} %add_convert_fusion.16), channel_id=1, source_target_pairs={{0,16},{2,18},{4,20},{6,22},{8,24},{10,26},{12,28},{14,30},{16,0},... | collective-permute-start | bytes 331784 | tf_op jit(solution)/shard_map/ppermute | solution.py:336
  226.5 29.0 %collective-permute-start.9 = (bf16[576,256]{1,0:T(8,128)(2,1)S(1)}, bf16[576,256]{1,0:T(8,128)(2,1)S(1)}, u32[]{:S(2)}, u32[]{:S(2)}) collective-permute-start(bf16[576,256]{1,0:T(8,128)(2,1)S(1)} %constant_dynamic-slice_fusion.23), channel_id=1, source_target_pairs={{0,2},{2,0},{4,6},{6,4},{8,10},{10,8},{12,14},{14,12},{16,18},{18,... | collective-permute-start | bytes 884744 | tf_op jit(solution)/shard_map/ppermute | solution.py:336
  228.2 28.1 %collective-permute-start.17 = (bf16[576,256]{1,0:T(8,128)(2,1)S(1)}, bf16[576,256]{1,0:T(8,128)(2,1)S(1)}, u32[]{:S(2)}, u32[]{:S(2)}) collective-permute-start(bf16[576,256]{1,0:T(8,128)(2,1)S(1)} %constant_dynamic-slice_fusion.19), channel_id=1, source_target_pairs={{0,4},{2,6},{4,0},{6,2},{8,12},{10,14},{12,8},{14,10},{16,20},{18,... | collective-permute-start | bytes 884744 | tf_op jit(solution)/shard_map/ppermute | solution.py:336
  231.0 26.2 %collective-permute-start.25 = (bf16[576,256]{1,0:T(8,128)(2,1)S(1)}, bf16[576,256]{1,0:T(8,128)(2,1)S(1)}, u32[]{:S(2)}, u32[]{:S(2)}) collective-permute-start(bf16[576,256]{1,0:T(8,128)(2,1)S(1)} %constant_dynamic-slice_fusion.15), channel_id=1, source_target_pairs={{0,8},{2,10},{4,12},{6,14},{8,0},{10,2},{12,4},{14,6},{16,24},{18,... | collective-permute-start | bytes 884744 | tf_op jit(solution)/shard_map/ppermute | solution.py:336
  247.0 53.2 %collective-permute-start.45 = (bf16[864,256]{1,0:T(8,128)(2,1)S(1)}, bf16[864,256]{1,0:T(8,128)(2,1)S(1)}, u32[]{:S(2)}, u32[]{:S(2)}) collective-permute-start(bf16[864,256]{1,0:T(8,128)(2,1)S(1)} %maximum_select_fusion.9), channel_id=1, source_target_pairs={{0,4},{2,6},{4,0},{6,2},{8,12},{10,14},{12,8},{14,10},{16,20},{18,... | collective-permute-start | bytes 1327112 | tf_op jit(solution)/shard_map/ppermute | solution.py:336
  253.7 49.0 %collective-permute-start.53 = (bf16[864,256]{1,0:T(8,128)(2,1)S(1)}, bf16[864,256]{1,0:T(8,128)(2,1)S(1)}, u32[]{:S(2)}, u32[]{:S(2)}) collective-permute-start(bf16[864,256]{1,0:T(8,128)(2,1)S(1)} %maximum_select_fusion.10), channel_id=1, source_target_pairs={{0,8},{2,10},{4,12},{6,14},{8,0},{10,2},{12,4},{14,6},{16,24},{18,... | collective-permute-start | bytes 1327112 | tf_op jit(solution)/shard_map/ppermute | solution.py:336
  255.5 50.0 %collective-permute-start.61 = (bf16[864,256]{1,0:T(8,128)(2,1)S(1)}, bf16[864,256]{1,0:T(8,128)(2,1)S(1)}, u32[]{:S(2)}, u32[]{:S(2)}) collective-permute-start(bf16[864,256]{1,0:T(8,128)(2,1)S(1)} %maximum_select_fusion.11), channel_id=1, source_target_pairs={{0,2},{2,0},{4,6},{6,4},{8,10},{10,8},{12,14},{14,12},{16,18},{18,... | collective-permute-start | bytes 1327112 | tf_op jit(solution)/shard_map/ppermute | solution.py:336
  302.7 29.3 %collective-permute-start.46 = (bf16[1728,256]{1,0:T(8,128)(2,1)S(1)}, bf16[1728,256]{1,0:T(8,128)(2,1)S(1)}, u32[]{:S(2)}, u32[]{:S(2)}) collective-permute-start(bf16[1728,256]{1,0:T(8,128)(2,1)S(1)} %maximum_select_fusion.3), channel_id=1, source_target_pairs={{0,2},{2,0},{4,6},{6,4},{8,10},{10,8},{12,14},{14,12},{16,18},{18,... | collective-permute-start | bytes 2654216 | tf_op jit(solution)/shard_map/ppermute | solution.py:336
  303.8 28.7 %collective-permute-start.54 = (bf16[1728,256]{1,0:T(8,128)(2,1)S(1)}, bf16[1728,256]{1,0:T(8,128)(2,1)S(1)}, u32[]{:S(2)}, u32[]{:S(2)}) collective-permute-start(bf16[1728,256]{1,0:T(8,128)(2,1)S(1)} %maximum_select_fusion.4), channel_id=1, source_target_pairs={{0,4},{2,6},{4,0},{6,2},{8,12},{10,14},{12,8},{14,10},{16,20},{18,... | collective-permute-start | bytes 2654216 | tf_op jit(solution)/shard_map/ppermute | solution.py:336
  305.6 17.3 %collective-permute-start.16 = (bf16[576,256]{1,0:T(8,128)(2,1)S(1)}, bf16[576,256]{1,0:T(8,128)(2,1)S(1)}, u32[]{:S(2)}, u32[]{:S(2)}) collective-permute-start(bf16[576,256]{1,0:T(8,128)(2,1)S(1)} %maximum_select_fusion.12), channel_id=1, source_target_pairs={{0,2},{2,0},{4,6},{6,4},{8,10},{10,8},{12,14},{14,12},{16,18},{18,... | collective-permute-start | bytes 884744 | tf_op jit(solution)/shard_map/ppermute | solution.py:336
  307.4 27.4 %collective-permute-start.62 = (bf16[1728,256]{1,0:T(8,128)(2,1)S(1)}, bf16[1728,256]{1,0:T(8,128)(2,1)S(1)}, u32[]{:S(2)}, u32[]{:S(2)}) collective-permute-start(bf16[1728,256]{1,0:T(8,128)(2,1)S(1)} %maximum_select_fusion.5), channel_id=1, source_target_pairs={{0,8},{2,10},{4,12},{6,14},{8,0},{10,2},{12,4},{14,6},{16,24},{18,... | collective-permute-start | bytes 2654216 | tf_op jit(solution)/shard_map/ppermute | solution.py:336
  309.2 15.6 %collective-permute-start.24 = (bf16[576,256]{1,0:T(8,128)(2,1)S(1)}, bf16[576,256]{1,0:T(8,128)(2,1)S(1)}, u32[]{:S(2)}, u32[]{:S(2)}) collective-permute-start(bf16[576,256]{1,0:T(8,128)(2,1)S(1)} %maximum_select_fusion.13), channel_id=1, source_target_pairs={{0,4},{2,6},{4,0},{6,2},{8,12},{10,14},{12,8},{14,10},{16,20},{18,... | collective-permute-start | bytes 884744 | tf_op jit(solution)/shard_map/ppermute | solution.py:336
  (62 other events, 448.6 us)

commit v2 on v1

--- a/solution.py
+++ b/solution.py
@@ -16,7 +16,8 @@
 SCALE = HD ** (-0.5)
 F32 = jnp.float32
 BF16 = jnp.bfloat16
-VMEM_LIMIT = 56 * 1024 * 1024
+LANES = 128
+MIB = 1024 * 1024
 
 
 def dot_nn(left, right):
@@ -52,20 +53,42 @@
     return own, other
 
 
-def call(kernel, outs, scratch, name, flops, *args, smem=1):
+def call(kernel, outs, scratch, name, flops, *args, smem=1, away=0, away_outs=0):
+    vmem = pl.BlockSpec(memory_space=pltpu.VMEM)
+    anywhere = pl.BlockSpec(memory_space=pl.ANY)
     specs = [pl.BlockSpec(memory_space=pltpu.SMEM)] * smem
-    specs += [pl.BlockSpec(memory_space=pltpu.VMEM)] * (len(args) - smem)
+    specs += [vmem] * (len(args) - smem - away) + [anywhere] * away
     moved = sum(a.size * a.dtype.itemsize for a in args)
     return pl.pallas_call(
         kernel,
         out_shape=[jax.ShapeDtypeStruct(s, d) for s, d in outs],
         in_specs=specs,
-        out_specs=[pl.BlockSpec(memory_space=pltpu.VMEM)] * len(outs),
-        scratch_shapes=[pltpu.VMEM(s, d) for s, d in scratch],
-        compiler_params=pltpu.CompilerParams(vmem_limit_bytes=VMEM_LIMIT),
+        out_specs=[anywhere] * away_outs + [vmem] * (len(outs) - away_outs),
+        scratch_shapes=[pltpu.VMEM(*s) if isinstance(s, tuple) else s for s in scratch],
+        compiler_params=pltpu.CompilerParams(vmem_limit_bytes=56 * MIB),
         cost_estimate=pl.CostEstimate(flops=flops, bytes_accessed=moved, transcendentals=0),
         name=name,
     )(*args)
+
+
+def bits_of(count):
+    return list(range(count.bit_length() - 1))
+
+
+def sum_orders(count):
+    turn, last = bits_of(count)[:3], bits_of(count)[3:]
+    return [list(reversed(turn[k:] + turn[:k] + last)) for k in range(3)]
+
+
+def place_of(r, order):
+    place = 0
+    for s, bit in enumerate(order):
+        place = place | (((r >> bit) & 1) << s)
+    return place
+
+
+def relative_at(place, order):
+    return sum(((place >> s) & 1) << bit for s, bit in enumerate(order))
 
 
 def project_kernel(side_ref, x_ref, vec_ref, own_ref, other_ref, hid_ref, send_ref):
@@ -279,6 +302,97 @@
     grad_ref[...] = gm_ref[...] + norm_back(grad_hidden * vec[0:1], unit, inv_std)
 
 
+def block_spans(a, k, rows, cols, paired, count):
+    third = cols // 3
+    if paired:
+        tall, wide = 2 * rows // count, third // 2
+        first, start = a // 2 * tall, a % 2 * wide
+    else:
+        tall, wide = rows // count, third
+        first, start = a * tall, 0
+    return first, tall, [start + j * LANES for j in range(wide // LANES)]
+
+
+def pack_kernel(paired, meta_ref, *refs):
+    weights = len(paired)
+    ins, extra_ref = refs[: 4 * weights], refs[4 * weights]
+    outs = refs[4 * weights + 1 : 4 * weights + 7]
+    lefts = refs[4 * weights + 7 : -1 : 2]
+    rights = refs[4 * weights + 8 : -1 : 2]
+    pk = refs[-1]
+    count = extra_ref.shape[0]
+    for i, (left, right) in enumerate(zip(lefts, rights)):
+        rows = left.shape[0] // 2
+        for n, dst in enumerate((left, left, right, right)):
+            dst[(n % 2) * rows : (n % 2 + 1) * rows] = ins[4 * i + n][...]
+    for k, order in enumerate(sum_orders(count)):
+        keep_ref, send_ref = outs[2 * k : 2 * k + 2]
+        line = 0
+        for left, right, pair in zip(lefts, rights, paired):
+            third = right.shape[1] // 3
+            grad = dot_tn(left[...], right[:, k * third : (k + 1) * third]).astype(BF16)
+            for a in range(count):
+                first, tall, starts = block_spans(a, k, *grad.shape[:1], 3 * third, pair, count)
+                for j, start in enumerate(starts):
+                    pk[a, line + j * tall : line + (j + 1) * tall] = grad[
+                        first : first + tall, start : start + LANES
+                    ]
+            line += tall * len(starts)
+        for m in range(count):
+            dst = keep_ref if m < count // 2 else send_ref
+            a = relative_at(m, order) ^ meta_ref[1]
+            dst[m % (count // 2), 0:line] = pk[a]
+            if k == 0:
+                dst[m % (count // 2), line:] = extra_ref[a]
+
+
+def unpack_kernel(paired, meta_ref, *refs):
+    weights = len(paired)
+    near_far, outs = refs[:6], refs[6 : 6 + weights]
+    extra_ref = refs[6 + weights]
+    scratch, sem = refs[7 + weights : -1], refs[-1]
+    half = near_far[0].shape[0]
+    count = 2 * half
+    copies = []
+    for k, order in enumerate(sum_orders(count)):
+        for m in range(count):
+            a = relative_at(m, order) ^ meta_ref[1]
+            block = near_far[2 * k + m // half][m % half].astype(F32)
+            line = 0
+            for dst, pair in zip(scratch, paired):
+                rows, third = dst.shape[1:]
+                first, tall, starts = block_spans(a, k, rows, 3 * third, pair, count)
+                for start in starts:
+                    if pair:
+                        start = pl.ds(pl.multiple_of(start, LANES), LANES)
+                    else:
+                        start = slice(start, start + LANES)
+                    place = pl.ds(pl.multiple_of(first, 8), tall)
+                    dst[k, place, start] = block[line : line + tall]
+                    line += tall
+            if k == 0:
+                extra_ref[a] = block[line:]
+        for i, (src, dst) in enumerate(zip(scratch, outs)):
+            size = src.shape[2]
+            copy = pltpu.make_async_copy(
+                src.at[k], dst.at[:, k * size : (k + 1) * size], sem.at[k, i]
+            )
+            copy.start()
+            copies.append(copy)
+    for copy in copies:
+        copy.wait()
+
+
+def stack_kernel(*refs):
+    out_ref = refs[-1]
+    row = 0
+    for ref in refs[:-1]:
+        line = ref[...].reshape(1, -1)
+        for start in range(0, line.shape[1], out_ref.shape[1]):
+            out_ref[row : row + 1] = line[:, start : start + out_ref.shape[1]]
+            row += 1
+
+
 SWAP = [(0, 1), (1, 0)]
 
 
@@ -301,15 +415,14 @@
     return lax.all_gather(vector, "fsdp", axis=1, tiled=True)
 
 
-def rows_over_pair(keep, send, right, group):
-    if group == 2:
-        left = jnp.concatenate([keep, lax.ppermute(send, "fsdp", SWAP)], axis=0)
-        right = jnp.concatenate([right, lax.ppermute(right, "fsdp", SWAP)], axis=0)
-    else:
-        left = jnp.concatenate([keep, send], axis=1)
-        left = lax.all_to_all(left, "fsdp", split_axis=1, concat_axis=0, tiled=True)
-        right = lax.all_gather(right, "fsdp", axis=0, tiled=True)
-    return dot_tn(left, right)
+def swap_side(part):
+    return lax.ppermute(part, "fsdp", SWAP)
+
+
+def rows_over_group(keep, send, right):
+    left = jnp.concatenate([keep, send], axis=1)
+    left = lax.all_to_all(left, "fsdp", split_axis=1, concat_axis=0, tiled=True)
+    return dot_tn(left, lax.all_gather(right, "fsdp", axis=0, tiled=True))
 
 
 def own_columns(sums, group, side):
@@ -321,70 +434,142 @@
     return lax.psum_scatter(sums, "fsdp", scatter_dimension=1, tiled=True)
 
 
-def vector_total(sums, count):
-    spread = jnp.broadcast_to(sums[None], (count,) + sums.shape)
-    return jnp.sum(lax.all_to_all(spread, "ctx", 0, 0, tiled=True), axis=0)
-
-
-def bit_orders(count):
-    bits = list(range(count.bit_length() - 1))
-    turn, last = bits[:3], bits[3:]
-    return [turn[k:] + turn[:k] + last for k in range(3)]
-
-
 def swap_bit(part, bit, count):
     return lax.ppermute(part, "ctx", [(d, d ^ (1 << bit)) for d in range(count)])
 
 
-def total_over_ctx(parts, count):
-    index = lax.axis_index("ctx")
-    orders = bit_orders(count)
-    steps = len(orders[0])
-    parts = list(parts)
-    for s in range(steps):
-        for k, part in enumerate(parts):
-            bit = orders[k][s]
-            high = (index >> bit) & 1
-            half = part.shape[0] // 2
-            keep = lax.dynamic_slice_in_dim(part, high * half, half, 0)
-            send = lax.dynamic_slice_in_dim(part, (1 - high) * half, half, 0)
-            came = swap_bit(send, bit, count)
-            parts[k] = (keep.astype(F32) + came.astype(F32)).astype(BF16)
-    for s in reversed(range(steps)):
-        for k, part in enumerate(parts):
-            bit = orders[k][s]
-            high = (index >> bit) & 1
-            came = swap_bit(part, bit, count)
-            parts[k] = jnp.where(
-                high == 0,
-                jnp.concatenate([part, came], axis=0),
-                jnp.concatenate([came, part], axis=0),
-            )
-    return parts
-
-
-def stack_columns(weights, third, wide):
-    blocks = []
-    for weight in weights:
-        span = weight.shape[1] // 3
-        for c in range(span // wide):
-            start = third * span + c * wide
-            blocks.append(weight[:, start : start + wide])
-    return jnp.concatenate(blocks, axis=0).astype(BF16)
-
-
-def unstack_columns(parts, shapes, wide):
-    outs = []
-    first = 0
-    for rows, cols in shapes:
+def add_parts(left, right):
+    return (left.astype(F32) + right.astype(F32)).astype(BF16)
+
+
+class Flow:
+    def __init__(self, keeps, sends, count):
+        self.keeps, self.sends = list(keeps), list(sends)
+        self.orders = sum_orders(count)
+        self.bits = len(self.orders[0])
+        self.step = 0
+
+    def bit_row(self):
+        at = self.bits - 1 - self.step if self.step < self.bits else self.step - self.bits
+        return [order[at] for order in self.orders]
+
+    def pending(self):
+        parts = self.sends if self.step < self.bits else self.keeps
+        row = self.bit_row()
+        if len(set(row)) == 1:
+            return [(jnp.concatenate(parts, axis=1), row[0])]
+        return list(zip(parts, row))
+
+    def accept(self, cames):
+        if len(cames) == 1:
+            sizes = [part.shape[1] for part in self.keeps]
+            ends = [sum(sizes[: k + 1]) for k in range(3)]
+            cames = [cames[0][:, end - size : end] for end, size in zip(ends, sizes)]
+        half = cames[0].shape[0] // 2
+        if self.step < self.bits - 1:
+            self.sends = [add_parts(p[half:], c[half:]) for p, c in zip(self.keeps, cames)]
+            self.keeps = [add_parts(p[:half], c[:half]) for p, c in zip(self.keeps, cames)]
+        elif self.step == self.bits - 1:
+            self.keeps = [add_parts(p, c) for p, c in zip(self.keeps, cames)]
+        elif self.step == 2 * self.bits - 1:
+            self.fars = cames
+        else:
+            self.keeps = [jnp.concatenate(pair, axis=0) for pair in zip(self.keeps, cames)]
+        self.step += 1
+
+    def over(self):
+        return self.step == 2 * self.bits
+
+
+def advance(flows, count):
+    flows = [flow for flow in flows if not flow.over()]
+    waiting = [flow.pending() for flow in flows]
+    cames = lax.optimization_barrier(
+        [[swap_bit(part, bit, count) for part, bit in parts] for parts in waiting]
+    )
+    for flow, came in zip(flows, cames):
+        flow.accept(came)
+
+
+LINES = 16
+
+
+def pack(pairs, paired, sums, meta, index, group, count):
+    extra = sums.reshape(-1, LANES)
+    extra = jnp.pad(extra, ((0, LINES * count - extra.shape[0]), (0, 0))).astype(BF16)
+    extra = extra.reshape(count, LINES, LANES)
+    if group == 2 and count == 16:
+        args = []
+        for keep, send, right in pairs:
+            args += [keep, swap_side(send), right, swap_side(right)]
+        size = sum(keep.shape[1] * right.shape[1] for keep, _, right in pairs)
+        block = size // 3 // LANES // count
+        half = count // 2
+        tall = [block + LINES, block, block]
+        rows = pairs[0][0].shape[0]
+        parts = call(
+            functools.partial(pack_kernel, paired),
+            [((half, tall[k // 2], LANES), BF16) for k in range(6)],
+            [((2 * rows, a.shape[1]), BF16) for a in args[::2]] + [((count, block, LANES), BF16)],
+            "pack", 4 * rows * size, meta, *args, extra,
+        )
+        return Flow(parts[::2], parts[1::2], count)
+    weights = [rows_over_group(*pair) for pair in pairs]
+    return Flow(*plain_pack(weights, extra, index, count), count)
+
+
+def unpack(flow, shapes, paired, sums, meta, index, group, count):
+    if group == 2 and count == 16:
+        near_far = [part for pair in zip(flow.keeps, flow.fars) for part in pair]
+        *weights, extra = call(
+            functools.partial(unpack_kernel, paired),
+            [(s, F32) for s in shapes] + [((count, LINES, LANES), F32)],
+            [((3, r, c // 3), F32) for r, c in shapes]
+            + [pltpu.SemaphoreType.DMA((3, len(shapes)))],
+            "unpack", 0, meta, *near_far, away_outs=len(shapes),
+        )
+    else:
+        weights, extra = plain_unpack(flow.keeps, flow.fars, shapes, LINES, index, count)
+    sums = extra.reshape(-1, LANES)[: sums.size // LANES].reshape(sums.shape)
+    return weights, sums
+
+
+def plain_pack(weights, extra, index, count):
+    keeps, sends = [], []
+    for k, order in enumerate(sum_orders(count)):
         blocks = []
-        each = cols // 3 // wide
-        for part in parts:
-            for c in range(each):
-                blocks.append(part[first + c * rows : first + (c + 1) * rows])
-        first += each * rows
-        outs.append(jnp.concatenate(blocks, axis=1).astype(F32))
-    return outs
+        for weight in weights:
+            span = weight.shape[1] // 3
+            for start in range(k * span, (k + 1) * span, LANES):
+                blocks.append(weight[:, start : start + LANES].astype(BF16))
+        flat = jnp.concatenate(blocks, axis=0)
+        flat = flat.reshape(count, -1, LANES)
+        if k == 0:
+            flat = jnp.concatenate([flat, extra], axis=1)
+        turn = jnp.array([relative_at(m, order) for m in range(count)], jnp.int32) ^ index
+        flat = jnp.take(flat, turn, axis=0)
+        keeps.append(flat[: count // 2])
+        sends.append(flat[count // 2 :])
+    return keeps, sends
+
+
+def plain_unpack(keeps, fars, shapes, lines, index, count):
+    columns = [[] for _ in shapes]
+    extra = None
+    for k, order in enumerate(sum_orders(count)):
+        flat = jnp.concatenate([keeps[k], fars[k]], axis=0)
+        turn = place_of(jnp.arange(count, dtype=jnp.int32) ^ index, order)
+        flat = jnp.take(flat, turn, axis=0).astype(F32)
+        if k == 0:
+            extra = flat[:, flat.shape[1] - lines :]
+            flat = flat[:, : flat.shape[1] - lines]
+        flat = flat.reshape(-1, LANES)
+        first = 0
+        for i, (rows, cols) in enumerate(shapes):
+            for _ in range(cols // 3 // LANES):
+                columns[i].append(flat[first : first + rows])
+                first += rows
+    return [jnp.concatenate(c, axis=1) for c in columns], extra
 
 
 def body(
@@ -398,22 +583,34 @@
     ff = expand_weight.shape[1]
     length = count * rows
     side = lax.axis_index("fsdp") if group == 2 else jnp.int32(0)
-    sides = jnp.reshape(side, (1,)).astype(jnp.int32)
+    index = lax.axis_index("ctx")
+    half = width // 2
+    three = 3 * HD
+    each = width // group
+    meta = jnp.stack([side, index]).astype(jnp.int32)
     table = block_position[0]
     places = jnp.arange(count, dtype=jnp.int32)
     slots = jnp.sum(
         jnp.where(table[None, :] == places[:, None], places[None, :], 0), axis=1
     ).astype(jnp.int32)
     x = block_input[0]
-    vec = join_vector(
-        jnp.stack(
-            [first_gain, first_shift, query_bias, value_bias, output_bias, second_gain,
-             second_shift, shrink_bias]
-        ),
-        group, side,
-    )
     qkv = pieces(qkv_weight, group)
-    ebias = join_vector(expand_bias[None], group, side)
+    vectors = (
+        first_gain, first_shift, query_bias, value_bias, output_bias, second_gain, second_shift,
+        shrink_bias,
+    )
+    if group == 2:
+        (vec,) = call(
+            stack_kernel, [((12, each), BF16)], [], "stack", 0, *vectors, expand_bias, smem=0
+        )
+        vec = join_vector(vec, group, side)
+        ebias = vec[8:].reshape(4, group, each).swapaxes(0, 1).reshape(1, ff)
+    else:
+        vec = join_vector(jnp.stack(vectors), group, side)
+        ebias = join_vector(expand_bias[None], group, side)
+    qkv, output_weight, expand_weight, shrink_weight = lax.optimization_barrier(
+        (qkv, output_weight, expand_weight, shrink_weight)
+    )
     mix = pieces(output_weight, group)
     expand = pieces(expand_weight, group)
     shrink = pieces(shrink_weight, group)
@@ -421,9 +618,9 @@
 
     hidden_a, qkv_send = call(
         project_kernel,
-        [((rows, width), BF16), ((count, 3 * HD, rows), BF16)],
+        [((rows, width), BF16), ((count, three, rows), BF16)],
         [], "project", 6 * rows * width * width,
-        sides, x, vec, *qkv,
+        meta, x, vec, *qkv,
     )
     qkv_here = lax.all_to_all(qkv_send, "ctx", 0, 0, tiled=True)
     att_send, log_total = call(
@@ -434,9 +631,8 @@
         slots, qkv_here,
     )
     att_here = lax.all_to_all(att_send, "ctx", 0, 0, tiled=True)
-    half = width // 2
     (
-        result, grad_middle, grad_send, sums, esum, cot_b, act_keep, act_out, hidb_keep, hidb_out,
+        result, grad_middle, grad_send, sums, esum, cot_b, act_keep, act_out, hid_keep, hid_out,
         ge_b, att_keep, att_out, gm_b,
     ) = call(
         middle_kernel,
@@ -451,12 +647,24 @@
             ((rows, width), BF16), ((rows, width), F32),
         ],
         "middle", 8 * rows * size + 4 * rows * width * width,
-        sides, att_here, x, out_cotangent[0], vec, ebias, *mix, *expand, *shrink,
+        meta, att_here, x, out_cotangent[0], vec, ebias, *mix, *expand, *shrink,
     )
     grad_here = lax.all_to_all(grad_send, "ctx", 0, 0, tiled=True)
+
+    esum = esum.reshape(group, 4, each).swapaxes(0, 1).reshape(4, width)
+    sums = own_columns(jnp.concatenate([sums, esum], axis=0), group, side)
+    early_kinds = (False, True, True)
+    early = pack(
+        [(act_keep, act_out, cot_b), (hid_keep, hid_out, ge_b), (att_keep, att_out, gm_b)],
+        early_kinds, sums, meta, index, group, count,
+    )
+    early.keeps, early.sends, grad_here = lax.optimization_barrier(
+        (early.keeps, early.sends, grad_here)
+    )
+    advance([early], count)
     (dqkv_send,) = call(
         attend_back_kernel,
-        [((count, 3 * HD, rows), BF16)],
+        [((count, three, rows), BF16)],
         [
             ((HD, length), BF16), ((length, HD), BF16), ((HD, length), BF16),
             ((length, HD), BF16), ((length, HD), BF16), ((HD, length), BF16),
@@ -466,22 +674,16 @@
         "attend_back", 5 * length * length * HD,
         slots, qkv_here, att_send, grad_here, log_total,
     )
+    early.keeps, early.sends, dqkv_send = lax.optimization_barrier(
+        (early.keeps, early.sends, dqkv_send)
+    )
     dqkv_here = lax.all_to_all(dqkv_send, "ctx", 0, 0, tiled=True)
-
-    grad_shrink = rows_over_pair(act_keep, act_out, cot_b, group)
-    grad_expand = rows_over_pair(hidb_keep, hidb_out, ge_b, group)
-    grad_mix = rows_over_pair(att_keep, att_out, gm_b, group)
-    early = (grad_shrink, grad_expand, grad_mix)
-    early_sums = total_over_ctx([stack_columns(early, k, 256) for k in range(3)], count)
-    grad_shrink, grad_expand, grad_mix = unstack_columns(
-        early_sums, [g.shape for g in early], 256
-    )
-    each = width // group
-    esum = esum.reshape(group, 4, each).swapaxes(0, 1).reshape(4, width)
-    sums = own_columns(jnp.concatenate([sums, esum], axis=0), group, side)
-    sums = vector_total(sums, count)
-
-    input_grad, late, gj, hida_keep, hida_out = call(
+    advance([early], count)
+    early.keeps, early.sends, dqkv_here = lax.optimization_barrier(
+        (early.keeps, early.sends, dqkv_here)
+    )
+    advance([early], count)
+    input_grad, late_sums, gj, hida_keep, hida_out = call(
         finish_kernel,
         [
             ((rows, width), F32), ((4, width), F32), ((rows, 3 * width), BF16),
@@ -489,16 +691,25 @@
         ],
         [((rows, width), F32)],
         "finish", 6 * rows * width * width,
-        sides, dqkv_here, x, grad_middle, vec, hidden_a, *qkv,
-    )
-    grad_qkv = rows_over_pair(hida_keep, hida_out, gj, group)
-    late_sums = total_over_ctx([stack_columns((grad_qkv,), k, 256) for k in range(3)], count)
-    (grad_qkv,) = unstack_columns(late_sums, [grad_qkv.shape], 256)
-    late = vector_total(own_columns(late, group, side), count)
+        meta, dqkv_here, x, grad_middle, vec, hidden_a, *qkv,
+    )
+    late_sums = own_columns(late_sums, group, side)
+    late = pack([(hida_keep, hida_out, gj)], (True,), late_sums, meta, index, group, count)
+    while not early.over():
+        advance([early, late], count)
+    (grad_shrink, grad_expand, grad_mix), sums = unpack(
+        early, ((4 * each, width), (each, ff), (each, width)), early_kinds, sums, meta, index,
+        group, count,
+    )
+    while not late.over():
+        advance([late], count)
+    (grad_qkv,), late_sums = unpack(
+        late, ((each, 3 * width),), (True,), late_sums, meta, index, group, count
+    )
     return (
-        result[None], input_grad[None], late[0], late[1], grad_qkv, late[2], late[3],
-        grad_mix, sums[0], sums[1], sums[2], grad_expand, sums[4:8].reshape(-1), grad_shrink,
-        sums[3],
+        result[None], input_grad[None], late_sums[0], late_sums[1], grad_qkv, late_sums[2],
+        late_sums[3], grad_mix, sums[0], sums[1], sums[2], grad_expand, sums[4:8].reshape(-1),
+        grad_shrink, sums[3],
     )
 
 

time: 345 us -> 293 us (0.85)
  Pallas kernels: 39.2 us -> 62.3 us
  starting transfers between devices: 97 us -> 78.3 us
  other arithmetic: 27.9 us -> 10.5 us
  waiting for transfers between devices: 144 us -> 127 us
  local copies, waits for them, and re-layouts: 27.5 us -> 12.5 us
  matrix products: 5.9 us -> 0 us
    pallas_call x5 -> x10, Pallas kernels: 39.2 us -> 62.3 us  [call(): pl.pallas_call(kernel, out_shape=[jax.ShapeDtypeStruct(s, d) for s, d in...]
    convert_element_type x28 -> x21, other arithmetic: 16.5 us -> 3.57 us  [add_parts(): return (left.astype(F32) + right.astype(F32)).astype(BF16)]
    all_to_all x1, waiting for transfers between devices: 11.4 us -> 0.01 us  [body(): grad_here = lax.all_to_all(grad_send, 'ctx', 0, 0, tiled=True)]
    all_to_all x2 -> x0, starting transfers between devices: 9.98 us -> none  [vector_total(): return jnp.sum(lax.all_to_all(spread, 'ctx', 0, 0, tiled=True), axis=0)]
    ppermute x48 -> x40, waiting for transfers between devices: 102 us -> 93.9 us  [swap_bit(): return lax.ppermute(part, 'ctx', [(d, d ^ 1 << bit) for d in range(count)])]
    dynamic_slice x24 -> x0, local copies, waits for them, and re-layouts: 6.72 us -> none  [total_over_ctx(): send = lax.dynamic_slice_in_dim(part, (1 - high) * half, half, 0)]
    dot_general x4 -> x0, matrix products: 5.9 us -> none  [dot_tn(): lax.dot_general(left, right, (((0,), (0,)), ((), ())), preferred_element_...]
    ppermute x48 -> x40, starting transfers between devices: 58.6 us -> 52.7 us  [swap_bit(): return lax.ppermute(part, 'ctx', [(d, d ^ 1 << bit) for d in range(count)])]
  transfers between devices with their start and end apart: 70 -> 59, of which waited for: 29 -> 25; matrix products, arithmetic and copies ran while one was open for 13% -> 4% of each run, Pallas kernels for 8% -> 14%
where the time goes in v2:
time: 293 us; the launch traced here: 292 us
  waiting for transfers between devices  127 us (43%)
  starting transfers between devices  78.3 us (27%)
  Pallas kernels  62.3 us (21%)
  local copies, waits for them, and re-layouts  12.5 us (4%)
  other arithmetic  10.5 us (4%)
    ppermute x40, waiting for transfers between devices, swap_bit(): return lax.ppermute(part, 'ctx', [(d, d ^ 1 << bit) for d in range(count)])  93.9 us
    pallas_call x10, Pallas kernels, call(): pl.pallas_call(kernel, out_shape=[jax.ShapeDtypeStruct(s, d) for s, d in...  62.3 us
    ppermute x40, starting transfers between devices, swap_bit(): return lax.ppermute(part, 'ctx', [(d, d ^ 1 << bit) for d in range(count)])  52.7 us
    all_to_all x1, waiting for transfers between devices, body(): qkv_here = lax.all_to_all(qkv_send, 'ctx', 0, 0, tiled=True)  19.3 us
    all_to_all x1, starting transfers between devices, body(): qkv_here = lax.all_to_all(qkv_send, 'ctx', 0, 0, tiled=True)  8.36 us
    all_to_all x1, waiting for transfers between devices, body(): att_here = lax.all_to_all(att_send, 'ctx', 0, 0, tiled=True)  7.85 us
  transfers between devices with their start and end apart: 59, of which 25 were waited for; matrix products, arithmetic and copies ran while one was open for 4% of the time, Pallas kernels for 14%

profile of v2, /device:TPU:0, one launch (start us, length us, event | category | flops | bytes accessed | tf_op | source)
XLA Modules:
  0.0 292.1 jit_solution(9378157056354824373)
XLA Ops:
  1.2 3.5 %collective-permute-done.1.other_ref = bf16[384,2304]{1,0:T(8,128)(2,1)S(1)} collective-permute-done((bf16[384,2304]{1,0:T(8,128)(2,1)}, bf16[384,2304]{1,0:T(8,128)(2,1)S(1)}, u32[]{:S(2)}, u32[]{:S(2)}) %collective-permute-start.1) | collective-permute-done | bytes 1769504 | tf_op jit(solution)/shard_map/ppermute | solution.py:401
  10.9 4.2 %project.1 = (bf16[128,768]{1,0:T(8,128)(2,1)}, bf16[16,192,128]{2,1,0:T(8,128)(2,1)}) custom-call(s32[2]{0:T(128)} %pad_add_fusion.side_ref.meta_ref, bf16[128,768]{1,0:T(8,128)(2,1)} %bitcast.33, bf16[12,768]{1,0:T(8,128)(2,1)} %maximum_select_fusion.vec_ref, bf16[384,2304]{1,0:T(8,128)(2,1)} %own_ref.1, bf16[384,2304]{1,0:T(8,128)(2,1)} %copy-done), custom_call_target="tpu_custom_call" | custom-call | flops 452984832 | bytes 3753992 | tf_op jit(solution)/shard_map/project/pallas_call | solution.py:62
  15.0 8.4 %all-to-all-start = ((bf16[16,192,128]{2,1,0:T(8,128)(2,1)}), bf16[16,192,128]{2,1,0:T(8,128)(2,1)S(1)}, u32[]{:S(2)}, u32[]{:S(2)}) async-start(bf16[16,192,128]{2,1,0:T(8,128)(2,1)} %get-tuple-element.124), calls=%async_computation | async-start | bytes 1572864 | tf_op jit(solution)/shard_map/all_to_all | solution.py:625
  24.1 19.3 %all-to-all-done.in_ref = bf16[16,192,128]{2,1,0:T(8,128)(2,1)S(1)} async-done(((bf16[16,192,128]{2,1,0:T(8,128)(2,1)}), bf16[16,192,128]{2,1,0:T(8,128)(2,1)S(1)}, u32[]{:S(2)}, u32[]{:S(2)}) %all-to-all-start) | async-done | bytes 786464 | tf_op jit(solution)/shard_map/all_to_all | solution.py:625
  44.3 7.5 %attend.1 = (bf16[16,64,128]{2,1,0:T(8,128)(2,1)}, f32[1,2048]{1,0:T(1,128)}) custom-call(s32[16]{0:T(128)} %select_reduce_fusion.slot_ref, bf16[16,192,128]{2,1,0:T(8,128)(2,1)} %copy-done.15), custom_call_target="tpu_custom_call" | custom-call | flops 536870912 | bytes 786496 | tf_op jit(solution)/shard_map/attend/pallas_call | solution.py:62
  51.9 4.9 %all-to-all-start.1 = ((bf16[16,64,128]{2,1,0:T(8,128)(2,1)}), bf16[16,64,128]{2,1,0:T(8,128)(2,1)S(1)}, u32[]{:S(2)}, u32[]{:S(2)}) async-start(bf16[16,64,128]{2,1,0:T(8,128)(2,1)} %get-tuple-element.125.att_ref), calls=%async_computation.1 | async-start | bytes 524288 | tf_op jit(solution)/shard_map/all_to_all | solution.py:633
  57.5 7.9 %all-to-all-done.1.att_in = bf16[16,64,128]{2,1,0:T(8,128)(2,1)S(1)} async-done(((bf16[16,64,128]{2,1,0:T(8,128)(2,1)}), bf16[16,64,128]{2,1,0:T(8,128)(2,1)S(1)}, u32[]{:S(2)}, u32[]{:S(2)}) %all-to-all-start.1) | async-done | bytes 262176 | tf_op jit(solution)/shard_map/all_to_all | solution.py:633
  66.0 12.5 %middle.1 = (bf16[128,768]{1,0:T(8,128)(2,1)}, f32[128,768]{1,0:T(8,128)}, bf16[16,64,128]{2,1,0:T(8,128)(2,1)}, f32[4,768]{1,0:T(4,128)}, f32[1,3072]{1,0:T(1,1...) custom-call(s32[2]{0:T(128)} %pad_add_fusion.side_ref.meta_ref, ...), custom_call_target="tpu_custom_call" | custom-call | flops 2717908992 | bytes 11493384 | tf_op jit(solution)/shard_map/middle/pallas_call | solution.py:62
  79.1 3.8 %all-to-all-start.2 = ((bf16[16,64,128]{2,1,0:T(8,128)(2,1)}), bf16[16,64,128]{2,1,0:T(8,128)(2,1)S(1)}, u32[]{:S(2)}, u32[]{:S(2)}) async-start(bf16[16,64,128]{2,1,0:T(8,128)(2,1)} %get-tuple-element.147), calls=%async_computation.2 | async-start | bytes 524288 | tf_op jit(solution)/shard_map/all_to_all | solution.py:652
  90.2 6.5 %pack.2 = (bf16[8,448,128]{2,1,0:T(8,128)(2,1)}, bf16[8,448,128]{2,1,0:T(8,128)(2,1)}, bf16[8,432,128]{2,1,0:T(8,128)(2,1)}, bf16[8,432,128]{2,1,0:T(8,128)(2,1)...) custom-call(s32[2]{0:T(128)} %pad_add_fusion.side_ref.meta_ref, ...), custom_call_target="tpu_custom_call" | custom-call | flops 1358954496 | bytes 3604488 | tf_op jit(solution)/shard_map/pack/pallas_call | solution.py:62
  101.7 10.2 %attend_back.1 = bf16[16,192,128]{2,1,0:T(8,128)(2,1)} custom-call(s32[16]{0:T(128)} %select_reduce_fusion.slot_ref, bf16[16,192,128]{2,1,0:T(8,128)(2,1)} %copy-done.15, bf16[16,64,128]{2,1,0:T(8,128)(2,1)} %get-tuple-element.125.att_ref, bf16[16,64,128]{2,1,0:T(8,128)(2,1)} %copy-done.23, f32[1,2048]{1,0:T(1,128)} %get-tuple-element.158.total_ref), custom_call_target="tpu_custom_call" | custom-call | flops 1342177280 | bytes 1318976 | tf_op jit(solution)/shard_map/attend_back/pallas_call | solution.py:62
  111.9 8.7 %collective-permute-done.13 = bf16[8,432,128]{2,1,0:T(8,128)(2,1)S(1)} collective-permute-done((bf16[8,432,128]{2,1,0:T(8,128)(2,1)}, bf16[8,432,128]{2,1,0:T(8,128)(2,1)S(1)}, u32[]{:S(2)}, u32[]{:S(2)}) %collective-permute-start.13) | collective-permute-done | bytes 884768 | tf_op jit(solution)/shard_map/ppermute | solution.py:438
  123.3 4.8 %all-to-all-start.3 = ((bf16[16,192,128]{2,1,0:T(8,128)(2,1)}), bf16[16,192,128]{2,1,0:T(8,128)(2,1)S(1)}, u32[]{:S(2)}, u32[]{:S(2)}) async-start(bf16[16,192,128]{2,1,0:T(8,128)(2,1)} %attend_back.1), calls=%async_computation.3 | async-start | bytes 1572864 | tf_op jit(solution)/shard_map/all_to_all | solution.py:680
  128.0 2.0 collective-permute-start.15
  133.0 19.2 %collective-permute-done.16 = bf16[4,432,128]{2,1,0:T(8,128)(2,1)S(1)} collective-permute-done((bf16[4,432,128]{2,1,0:T(8,128)(2,1)}, bf16[4,432,128]{2,1,0:T(8,128)(2,1)S(1)}, u32[]{:S(2)}, u32[]{:S(2)}) %collective-permute-start.16) | collective-permute-done | bytes 442400 | tf_op jit(solution)/shard_map/ppermute | solution.py:438
  153.4 4.9 %finish.1 = (f32[128,768]{1,0:T(8,128)}, f32[4,768]{1,0:T(4,128)}, bf16[128,2304]{1,0:T(8,128)(2,1)}, bf16[128,384]{1,0:T(8,128)(2,1)}, bf16[128,384]{1,0:T(8,128)(2,1)}) custom-call(s32[2]{0:T(128)} %pad_add_fusion.side_ref.meta_ref, bf16[16,192,128]{2,1,0:T(8,128)(2,1)} %copy-done.4, bf16[128,768]{1,0:T(8,128)(2,1)} %bitcast.35, ...), custom_call_target="tpu_custom_call" | custom-call | flops 452984832 | bytes 5130248 | tf_op jit(solution)/shard_map/finish/pallas_call | solution.py:62
  164.4 3.0 %collective-permute-done.22 = bf16[2,432,128]{2,1,0:T(8,128)(2,1)S(1)} collective-permute-done((bf16[2,432,128]{2,1,0:T(8,128)(2,1)S(1)}, bf16[2,432,128]{2,1,0:T(8,128)(2,1)S(1)}, u32[]{:S(2)}, u32[]{:S(2)}) %collective-permute-start.22) | collective-permute-done | bytes 221216 | tf_op jit(solution)/shard_map/ppermute | solution.py:438
  169.0 2.4 collective-permute-start.24
  172.2 3.3 %pack.3 = (bf16[8,160,128]{2,1,0:T(8,128)(2,1)}, bf16[8,160,128]{2,1,0:T(8,128)(2,1)}, bf16[8,144,128]{2,1,0:T(8,128)(2,1)}, bf16[8,144,128]{2,1,0:T(8,128)(2,1)...) custom-call(s32[2]{0:T(128)} %pad_add_fusion.side_ref.meta_ref, ...), custom_call_target="tpu_custom_call" | custom-call | flops 452984832 | bytes 1441800 | tf_op jit(solution)/shard_map/pack/pallas_call | solution.py:62
  179.2 6.9 %collective-permute-done.24 = bf16[1,1312,128]{2,1,0:T(8,128)(2,1)S(1)} collective-permute-done((bf16[1,1312,128]{2,1,0:T(8,128)(2,1)S(1)}, bf16[1,1312,128]{2,1,0:T(8,128)(2,1)S(1)}, u32[]{:S(2)}, u32[]{:S(2)}) %collective-permute-start.24) | collective-permute-done | bytes 335904 | tf_op jit(solution)/shard_map/ppermute | solution.py:438
  186.1 5.2 %collective-permute-done.27 = bf16[8,144,128]{2,1,0:T(8,128)(2,1)S(1)} collective-permute-done((bf16[8,144,128]{2,1,0:T(8,128)(2,1)}, bf16[8,144,128]{2,1,0:T(8,128)(2,1)S(1)}, u32[]{:S(2)}, u32[]{:S(2)}) %collective-permute-start.27) | collective-permute-done | bytes 294944 | tf_op jit(solution)/shard_map/ppermute | solution.py:438
  195.4 2.4 collective-permute-start.30
  197.9 6.7 %collective-permute-done.30 = bf16[4,144,128]{2,1,0:T(8,128)(2,1)S(1)} collective-permute-done((bf16[4,144,128]{2,1,0:T(8,128)(2,1)S(1)}, bf16[4,144,128]{2,1,0:T(8,128)(2,1)S(1)}, u32[]{:S(2)}, u32[]{:S(2)}) %collective-permute-start.30) | collective-permute-done | bytes 147488 | tf_op jit(solution)/shard_map/ppermute | solution.py:438
  204.6 6.2 %collective-permute-done.28 = bf16[1,1312,128]{2,1,0:T(8,128)(2,1)S(1)} collective-permute-done((bf16[1,1312,128]{2,1,0:T(8,128)(2,1)S(1)}, bf16[1,1312,128]{2,1,0:T(8,128)(2,1)S(1)}, u32[]{:S(2)}, u32[]{:S(2)}) %collective-permute-start.28) | collective-permute-done | bytes 335904 | tf_op jit(solution)/shard_map/ppermute | solution.py:438
  213.6 2.1 collective-permute-start.32
  217.5 4.1 %collective-permute-done.36 = bf16[2,144,128]{2,1,0:T(8,128)(2,1)S(1)} collective-permute-done((bf16[2,144,128]{2,1,0:T(8,128)(2,1)S(1)}, bf16[2,144,128]{2,1,0:T(8,128)(2,1)S(1)}, u32[]{:S(2)}, u32[]{:S(2)}) %collective-permute-start.36) | collective-permute-done | bytes 73760 | tf_op jit(solution)/shard_map/ppermute | solution.py:438
  226.9 7.0 %collective-permute-done.41 = bf16[1,448,128]{2,1,0:T(8,128)(2,1)S(1)} collective-permute-done((bf16[1,448,128]{2,1,0:T(8,128)(2,1)S(1)}, bf16[1,448,128]{2,1,0:T(8,128)(2,1)S(1)}, u32[]{:S(2)}, u32[]{:S(2)}) %collective-permute-start.41) | collective-permute-done | bytes 114720 | tf_op jit(solution)/shard_map/ppermute | solution.py:438
  241.7 13.7 %collective-permute-done.45 = bf16[1,448,128]{2,1,0:T(8,128)(2,1)S(1)} collective-permute-done((bf16[1,448,128]{2,1,0:T(8,128)(2,1)S(1)}, bf16[1,448,128]{2,1,0:T(8,128)(2,1)S(1)}, u32[]{:S(2)}, u32[]{:S(2)}) %collective-permute-start.45) | collective-permute-done | bytes 114720 | tf_op jit(solution)/shard_map/ppermute | solution.py:438
  262.2 3.1 %collective-permute-done.47 = bf16[2,144,128]{2,1,0:T(8,128)(2,1)S(1)} collective-permute-done((bf16[2,144,128]{2,1,0:T(8,128)(2,1)S(1)}, bf16[2,144,128]{2,1,0:T(8,128)(2,1)S(1)}, u32[]{:S(2)}, u32[]{:S(2)}) %collective-permute-start.47) | collective-permute-done | bytes 73760 | tf_op jit(solution)/shard_map/ppermute | solution.py:438
  268.3 7.5 %unpack.3 = (f32[1536,768]{1,0:T(8,128)}, f32[384,3072]{1,0:T(8,128)}, f32[384,768]{1,0:T(8,128)}, f32[16,16,128]{2,1,0:T(8,128)}) custom-call(s32[2]{0:T(128)} %pad_add_fusion.side_ref.meta_ref, bf16[8,448,128]{2,1,0:T(8,128)(2,1)} %copy-done.1, bf16[8,448,128]{2,1,0:T(8,128)(2,1)} %copy-done.9, bf16[8,432,128]{2,1,0:T(8,128)(2,1)} %copy-done.3, ...), custom_call_target="tpu_custom_call" | custom-call | bytes 5373960 | tf_op jit(solution)/shard_map/unpack/pallas_call | solution.py:62
  283.7 2.2 collective-permute-done.52.refs_1_
  286.6 4.1 %unpack.2 = (f32[384,2304]{1,0:T(8,128)}, f32[16,16,128]{2,1,0:T(8,128)}) custom-call(s32[2]{0:T(128)} %pad_add_fusion.side_ref.meta_ref, bf16[8,160,128]{2,1,0:T(8,128)(2,1)} %copy-done.5, bf16[8,160,128]{2,1,0:T(8,128)(2,1)} %copy-done.19, bf16[8,144,128]{2,1,0:T(8,128)(2,1)} %copy-done.7, bf16[8,144,128]{2,1,0:T(8,128)(2,1)} %copy-done.22, ...), custom_call_target="tpu_custom_call" | custom-call | bytes 1835016 | tf_op jit(solution)/shard_map/unpack/pallas_call | solution.py:62
  (231 shorter events, 82.6 us)
Async XLA Ops:
  4.7 60.6 %collective-permute-start.3 = (bf16[384,3072]{1,0:T(8,128)(2,1)}, bf16[384,3072]{1,0:T(8,128)(2,1)}, u32[]{:S(2)}, u32[]{:S(2)}) collective-permute-start(bf16[384,3072]{1,0:T(8,128)(2,1)} %ex_own), channel_id=1, source_target_pairs={{0,1},{1,0},{2,3},{3,2},{4,5},{5,4},{6,7},{7,6},{8,9},{9,8},{10,11... | collective-permute-start | bytes 7077896 | tf_op jit(solution)/shard_map/ppermute | solution.py:401
  5.1 60.2 %collective-permute-start.4 = (bf16[1536,768]{1,0:T(8,128)(2,1)}, bf16[1536,768]{1,0:T(8,128)(2,1)}, u32[]{:S(2)}, u32[]{:S(2)}) collective-permute-start(bf16[1536,768]{1,0:T(8,128)(2,1)} %sh_own), channel_id=1, source_target_pairs={{0,1},{1,0},{2,3},{3,2},{4,5},{5,4},{6,7},{7,6},{8,9},{9,8},{10,11... | collective-permute-start | bytes 7077896 | tf_op jit(solution)/shard_map/ppermute | solution.py:401
  15.0 28.4 %all-to-all-start = ((bf16[16,192,128]{2,1,0:T(8,128)(2,1)}), bf16[16,192,128]{2,1,0:T(8,128)(2,1)S(1)}, u32[]{:S(2)}, u32[]{:S(2)}) async-start(bf16[16,192,128]{2,1,0:T(8,128)(2,1)} %get-tuple-element.124), calls=%async_computation | async-start | bytes 1572864 | tf_op jit(solution)/shard_map/all_to_all | solution.py:625
  23.4 34.0 %collective-permute-start.2 = (bf16[384,768]{1,0:T(8,128)(2,1)S(1)}, bf16[384,768]{1,0:T(8,128)(2,1)S(1)}, u32[]{:S(2)}, u32[]{:S(2)}) collective-permute-start(bf16[384,768]{1,0:T(8,128)(2,1)S(1)} %copy-done.16), channel_id=1, source_target_pairs={{0,1},{1,0},{2,3},{3,2},{4,5},{5,4},{6,7},{7,6},{8,9},{9,8},{10,11... | collective-permute-start | bytes 1769480 | tf_op jit(solution)/shard_map/ppermute | solution.py:401
  51.9 13.5 %all-to-all-start.1 = ((bf16[16,64,128]{2,1,0:T(8,128)(2,1)}), bf16[16,64,128]{2,1,0:T(8,128)(2,1)S(1)}, u32[]{:S(2)}, u32[]{:S(2)}) async-start(bf16[16,64,128]{2,1,0:T(8,128)(2,1)} %get-tuple-element.125.att_ref), calls=%async_computation.1 | async-start | bytes 524288 | tf_op jit(solution)/shard_map/all_to_all | solution.py:633
  78.6 10.5 %collective-permute-start.8 = (bf16[128,3072]{1,0:T(8,128)(2,1)}, bf16[128,3072]{1,0:T(8,128)(2,1)S(1)}, u32[]{:S(2)}, u32[]{:S(2)}) collective-permute-start(bf16[128,3072]{1,0:T(8,128)(2,1)} %get-tuple-element.135.refs_6_), channel_id=1, source_target_pairs={{0,1},{1,0},{2,3},{3,2},{4,5},{5,4},{6,7},{7,6},{8,9},{9,8},{10,11... | collective-permute-start | bytes 2359304 | tf_op jit(solution)/shard_map/ppermute | solution.py:419
  78.6 10.4 %collective-permute-start.5 = (bf16[128,1536]{1,0:T(8,128)(2,1)}, bf16[128,1536]{1,0:T(8,128)(2,1)S(1)}, u32[]{:S(2)}, u32[]{:S(2)}) collective-permute-start(bf16[128,1536]{1,0:T(8,128)(2,1)} %get-tuple-element.131), channel_id=1, source_target_pairs={{0,1},{1,0},{2,3},{3,2},{4,5},{5,4},{6,7},{7,6},{8,9},{9,8},{10,11... | collective-permute-start | bytes 1179656 | tf_op jit(solution)/shard_map/ppermute | solution.py:419
  79.1 17.6 %all-to-all-start.2 = ((bf16[16,64,128]{2,1,0:T(8,128)(2,1)}), bf16[16,64,128]{2,1,0:T(8,128)(2,1)S(1)}, u32[]{:S(2)}, u32[]{:S(2)}) async-start(bf16[16,64,128]{2,1,0:T(8,128)(2,1)} %get-tuple-element.147), calls=%async_computation.2 | async-start | bytes 524288 | tf_op jit(solution)/shard_map/all_to_all | solution.py:652
  96.8 25.0 %collective-permute-start.12 = (bf16[8,448,128]{2,1,0:T(8,128)(2,1)}, bf16[8,448,128]{2,1,0:T(8,128)(2,1)S(1)}, u32[]{:S(2)}, u32[]{:S(2)}) collective-permute-start(bf16[8,448,128]{2,1,0:T(8,128)(2,1)} %get-tuple-element.149), channel_id=1, source_target_pairs={{0,2},{2,0},{4,6},{6,4},{8,10},{10,8},{12,14},{14,12},{16,18},{18,... | collective-permute-start | bytes 2752520 | tf_op jit(solution)/shard_map/ppermute | solution.py:438
  98.7 21.8 %collective-permute-start.13 = (bf16[8,432,128]{2,1,0:T(8,128)(2,1)}, bf16[8,432,128]{2,1,0:T(8,128)(2,1)S(1)}, u32[]{:S(2)}, u32[]{:S(2)}) collective-permute-start(bf16[8,432,128]{2,1,0:T(8,128)(2,1)} %get-tuple-element.150), channel_id=1, source_target_pairs={{0,4},{2,6},{4,0},{6,2},{8,12},{10,14},{12,8},{14,10},{16,20},{18,... | collective-permute-start | bytes 2654216 | tf_op jit(solution)/shard_map/ppermute | solution.py:438
  100.2 21.5 %collective-permute-start.14 = (bf16[8,432,128]{2,1,0:T(8,128)(2,1)}, bf16[8,432,128]{2,1,0:T(8,128)(2,1)S(1)}, u32[]{:S(2)}, u32[]{:S(2)}) collective-permute-start(bf16[8,432,128]{2,1,0:T(8,128)(2,1)} %get-tuple-element.151), channel_id=1, source_target_pairs={{0,8},{2,10},{4,12},{6,14},{8,0},{10,2},{12,4},{14,6},{16,24},{18,... | collective-permute-start | bytes 2654216 | tf_op jit(solution)/shard_map/ppermute | solution.py:438
  123.3 29.3 %all-to-all-start.3 = ((bf16[16,192,128]{2,1,0:T(8,128)(2,1)}), bf16[16,192,128]{2,1,0:T(8,128)(2,1)S(1)}, u32[]{:S(2)}, u32[]{:S(2)}) async-start(bf16[16,192,128]{2,1,0:T(8,128)(2,1)} %attend_back.1), calls=%async_computation.3 | async-start | bytes 1572864 | tf_op jit(solution)/shard_map/all_to_all | solution.py:680
  128.0 24.1 %collective-permute-start.15 = (bf16[4,448,128]{2,1,0:T(8,128)(2,1)S(1)}, bf16[4,448,128]{2,1,0:T(8,128)(2,1)S(1)}, u32[]{:S(2)}, u32[]{:S(2)}) collective-permute-start(bf16[4,448,128]{2,1,0:T(8,128)(2,1)S(1)} %get-tuple-element.160), channel_id=1, source_target_pairs={{0,4},{2,6},{4,0},{6,2},{8,12},{10,14},{12,8},{14,10},{16,20},{18,... | collective-permute-start | bytes 1376264 | tf_op jit(solution)/shard_map/ppermute | solution.py:438
  130.0 22.1 %collective-permute-start.16 = (bf16[4,432,128]{2,1,0:T(8,128)(2,1)}, bf16[4,432,128]{2,1,0:T(8,128)(2,1)S(1)}, u32[]{:S(2)}, u32[]{:S(2)}) collective-permute-start(bf16[4,432,128]{2,1,0:T(8,128)(2,1)} %get-tuple-element.161), channel_id=1, source_target_pairs={{0,8},{2,10},{4,12},{6,14},{8,0},{10,2},{12,4},{14,6},{16,24},{18,... | collective-permute-start | bytes 1327112 | tf_op jit(solution)/shard_map/ppermute | solution.py:438
  131.5 20.6 %collective-permute-start.17 = (bf16[4,432,128]{2,1,0:T(8,128)(2,1)S(1)}, bf16[4,432,128]{2,1,0:T(8,128)(2,1)S(1)}, u32[]{:S(2)}, u32[]{:S(2)}) collective-permute-start(bf16[4,432,128]{2,1,0:T(8,128)(2,1)S(1)} %get-tuple-element.162), channel_id=1, source_target_pairs={{0,2},{2,0},{4,6},{6,4},{8,10},{10,8},{12,14},{14,12},{16,18},{18,... | collective-permute-start | bytes 1327112 | tf_op jit(solution)/shard_map/ppermute | solution.py:438
  159.0 9.8 %collective-permute-start.21 = (bf16[2,448,128]{2,1,0:T(8,128)(2,1)S(1)}, bf16[2,448,128]{2,1,0:T(8,128)(2,1)S(1)}, u32[]{:S(2)}, u32[]{:S(2)}) collective-permute-start(bf16[2,448,128]{2,1,0:T(8,128)(2,1)S(1)} %get-tuple-element.179), channel_id=1, source_target_pairs={{0,8},{2,10},{4,12},{6,14},{8,0},{10,2},{12,4},{14,6},{16,24},{18,... | collective-permute-start | bytes 688136 | tf_op jit(solution)/shard_map/ppermute | solution.py:438
  159.3 12.1 %collective-permute-start.19 = (bf16[128,2304]{1,0:T(8,128)(2,1)}, bf16[128,2304]{1,0:T(8,128)(2,1)S(1)}, u32[]{:S(2)}, u32[]{:S(2)}) collective-permute-start(bf16[128,2304]{1,0:T(8,128)(2,1)} %get-tuple-element.175.refs_2_), channel_id=1, source_target_pairs={{0,1},{1,0},{2,3},{3,2},{4,5},{5,4},{6,7},{7,6},{8,9},{9,8},{10,11... | collective-permute-start | bytes 1769480 | tf_op jit(solution)/shard_map/ppermute | solution.py:419
  159.5 11.9 %collective-permute-start.18 = (bf16[128,384]{1,0:T(8,128)(2,1)}, bf16[128,384]{1,0:T(8,128)(2,1)S(1)}, u32[]{:S(2)}, u32[]{:S(2)}) collective-permute-start(bf16[128,384]{1,0:T(8,128)(2,1)} %get-tuple-element.174), channel_id=1, source_target_pairs={{0,1},{1,0},{2,3},{3,2},{4,5},{5,4},{6,7},{7,6},{8,9},{9,8},{10,11... | collective-permute-start | bytes 294920 | tf_op jit(solution)/shard_map/ppermute | solution.py:419
  169.0 17.1 %collective-permute-start.24 = (bf16[1,1312,128]{2,1,0:T(8,128)(2,1)S(1)}, bf16[1,1312,128]{2,1,0:T(8,128)(2,1)S(1)}, u32[]{:S(2)}, u32[]{:S(2)}) collective-permute-start(bf16[1,1312,128]{2,1,0:T(8,128)(2,1)S(1)} %pad_maximum_fusion.6), channel_id=1, source_target_pairs={{0,16},{2,18},{4,20},{6,22},{8,24},{10,26},{12,28},{14,30},{16,0},... | collective-permute-start | bytes 1007624 | tf_op jit(solution)/shard_map/ppermute | solution.py:438
  175.6 15.7 %collective-permute-start.25 = (bf16[8,160,128]{2,1,0:T(8,128)(2,1)}, bf16[8,160,128]{2,1,0:T(8,128)(2,1)S(1)}, u32[]{:S(2)}, u32[]{:S(2)}) collective-permute-start(bf16[8,160,128]{2,1,0:T(8,128)(2,1)} %get-tuple-element.187), channel_id=1, source_target_pairs={{0,2},{2,0},{4,6},{6,4},{8,10},{10,8},{12,14},{14,12},{16,18},{18,... | collective-permute-start | bytes 983048 | tf_op jit(solution)/shard_map/ppermute | solution.py:438
  176.2 9.9 %collective-permute-start.26 = (bf16[8,144,128]{2,1,0:T(8,128)(2,1)}, bf16[8,144,128]{2,1,0:T(8,128)(2,1)S(1)}, u32[]{:S(2)}, u32[]{:S(2)}) collective-permute-start(bf16[8,144,128]{2,1,0:T(8,128)(2,1)} %get-tuple-element.188), channel_id=1, source_target_pairs={{0,4},{2,6},{4,0},{6,2},{8,12},{10,14},{12,8},{14,10},{16,20},{18,... | collective-permute-start | bytes 884744 | tf_op jit(solution)/shard_map/ppermute | solution.py:438
  177.7 13.6 %collective-permute-start.27 = (bf16[8,144,128]{2,1,0:T(8,128)(2,1)}, bf16[8,144,128]{2,1,0:T(8,128)(2,1)S(1)}, u32[]{:S(2)}, u32[]{:S(2)}) collective-permute-start(bf16[8,144,128]{2,1,0:T(8,128)(2,1)} %get-tuple-element.189), channel_id=1, source_target_pairs={{0,8},{2,10},{4,12},{6,14},{8,0},{10,2},{12,4},{14,6},{16,24},{18,... | collective-permute-start | bytes 884744 | tf_op jit(solution)/shard_map/ppermute | solution.py:438
  194.1 10.5 %collective-permute-start.29 = (bf16[4,160,128]{2,1,0:T(8,128)(2,1)S(1)}, bf16[4,160,128]{2,1,0:T(8,128)(2,1)S(1)}, u32[]{:S(2)}, u32[]{:S(2)}) collective-permute-start(bf16[4,160,128]{2,1,0:T(8,128)(2,1)S(1)} %get-tuple-element.242), channel_id=1, source_target_pairs={{0,4},{2,6},{4,0},{6,2},{8,12},{10,14},{12,8},{14,10},{16,20},{18,... | collective-permute-start | bytes 491528 | tf_op jit(solution)/shard_map/ppermute | solution.py:438
  194.8 15.9 %collective-permute-start.28 = (bf16[1,1312,128]{2,1,0:T(8,128)(2,1)S(1)}, bf16[1,1312,128]{2,1,0:T(8,128)(2,1)S(1)}, u32[]{:S(2)}, u32[]{:S(2)}) collective-permute-start(bf16[1,1312,128]{2,1,0:T(8,128)(2,1)S(1)} %pad_maximum_fusion.7), channel_id=1, source_target_pairs={{0,16},{2,18},{4,20},{6,22},{8,24},{10,26},{12,28},{14,30},{16,0},... | collective-permute-start | bytes 1007624 | tf_op jit(solution)/shard_map/ppermute | solution.py:438
  221.8 12.1 %collective-permute-start.40 = (bf16[4,432,128]{2,1,0:T(8,128)(2,1)S(1)}, bf16[4,432,128]{2,1,0:T(8,128)(2,1)S(1)}, u32[]{:S(2)}, u32[]{:S(2)}) collective-permute-start(bf16[4,432,128]{2,1,0:T(8,128)(2,1)S(1)} %pad_maximum_fusion.5), channel_id=1, source_target_pairs={{0,2},{2,0},{4,6},{6,4},{8,10},{10,8},{12,14},{14,12},{16,18},{18,... | collective-permute-start | bytes 1327112 | tf_op jit(solution)/shard_map/ppermute | solution.py:438
  222.6 12.9 %collective-permute-start.39 = (bf16[4,432,128]{2,1,0:T(8,128)(2,1)S(1)}, bf16[4,432,128]{2,1,0:T(8,128)(2,1)S(1)}, u32[]{:S(2)}, u32[]{:S(2)}) collective-permute-start(bf16[4,432,128]{2,1,0:T(8,128)(2,1)S(1)} %pad_maximum_fusion.4), channel_id=1, source_target_pairs={{0,8},{2,10},{4,12},{6,14},{8,0},{10,2},{12,4},{14,6},{16,24},{18,... | collective-permute-start | bytes 1327112 | tf_op jit(solution)/shard_map/ppermute | solution.py:438
  224.0 11.4 %collective-permute-start.38 = (bf16[4,448,128]{2,1,0:T(8,128)(2,1)S(1)}, bf16[4,448,128]{2,1,0:T(8,128)(2,1)S(1)}, u32[]{:S(2)}, u32[]{:S(2)}) collective-permute-start(bf16[4,448,128]{2,1,0:T(8,128)(2,1)S(1)} %pad_maximum_fusion.3), channel_id=1, source_target_pairs={{0,4},{2,6},{4,0},{6,2},{8,12},{10,14},{12,8},{14,10},{16,20},{18,... | collective-permute-start | bytes 1376264 | tf_op jit(solution)/shard_map/ppermute | solution.py:438
  235.6 21.5 %collective-permute-start.44 = (bf16[8,432,128]{2,1,0:T(8,128)(2,1)S(1)}, bf16[8,432,128]{2,1,0:T(8,128)(2,1)S(1)}, u32[]{:S(2)}, u32[]{:S(2)}) collective-permute-start(bf16[8,432,128]{2,1,0:T(8,128)(2,1)S(1)} %pad_maximum_fusion.2.refs_4_), channel_id=1, source_target_pairs={{0,8},{2,10},{4,12},{6,14},{8,0},{10,2},{12,4},{14,6},{16,24},{18,... | collective-permute-start | bytes 2654216 | tf_op jit(solution)/shard_map/ppermute | solution.py:438
  237.6 20.2 %collective-permute-start.42 = (bf16[8,448,128]{2,1,0:T(8,128)(2,1)S(1)}, bf16[8,448,128]{2,1,0:T(8,128)(2,1)S(1)}, u32[]{:S(2)}, u32[]{:S(2)}) collective-permute-start(bf16[8,448,128]{2,1,0:T(8,128)(2,1)S(1)} %pad_maximum_fusion.refs_0_), channel_id=1, source_target_pairs={{0,2},{2,0},{4,6},{6,4},{8,10},{10,8},{12,14},{14,12},{16,18},{18,... | collective-permute-start | bytes 2752520 | tf_op jit(solution)/shard_map/ppermute | solution.py:438
  239.3 18.4 %collective-permute-start.43 = (bf16[8,432,128]{2,1,0:T(8,128)(2,1)S(1)}, bf16[8,432,128]{2,1,0:T(8,128)(2,1)S(1)}, u32[]{:S(2)}, u32[]{:S(2)}) collective-permute-start(bf16[8,432,128]{2,1,0:T(8,128)(2,1)S(1)} %pad_maximum_fusion.1.refs_2_), channel_id=1, source_target_pairs={{0,4},{2,6},{4,0},{6,2},{8,12},{10,14},{12,8},{14,10},{16,20},{18,... | collective-permute-start | bytes 2654216 | tf_op jit(solution)/shard_map/ppermute | solution.py:438
  241.2 14.2 %collective-permute-start.45 = (bf16[1,448,128]{2,1,0:T(8,128)(2,1)S(1)}, bf16[1,448,128]{2,1,0:T(8,128)(2,1)S(1)}, u32[]{:S(2)}, u32[]{:S(2)}) collective-permute-start(bf16[1,448,128]{2,1,0:T(8,128)(2,1)S(1)} %pad_maximum_fusion.18), channel_id=1, source_target_pairs={{0,16},{2,18},{4,20},{6,22},{8,24},{10,26},{12,28},{14,30},{16,0},... | collective-permute-start | bytes 344072 | tf_op jit(solution)/shard_map/ppermute | solution.py:438
  265.4 10.5 %collective-permute-start.51 = (bf16[4,144,128]{2,1,0:T(8,128)(2,1)S(1)}, bf16[4,144,128]{2,1,0:T(8,128)(2,1)S(1)}, u32[]{:S(2)}, u32[]{:S(2)}) collective-permute-start(bf16[4,144,128]{2,1,0:T(8,128)(2,1)S(1)} %pad_maximum_fusion.16), channel_id=1, source_target_pairs={{0,2},{2,0},{4,6},{6,4},{8,10},{10,8},{12,14},{14,12},{16,18},{18,... | collective-permute-start | bytes 442376 | tf_op jit(solution)/shard_map/ppermute | solution.py:438
  (61 other events, 478.1 us)

commit v3 on v2

--- a/solution.py
+++ b/solution.py
@@ -17,6 +17,7 @@
 F32 = jnp.float32
 BF16 = jnp.bfloat16
 LANES = 128
+LINES = 16
 MIB = 1024 * 1024
 
 
@@ -44,6 +45,13 @@
         - jnp.mean(scaled, axis=-1, keepdims=True)
         - unit * jnp.mean(scaled * unit, axis=-1, keepdims=True)
     )
+
+
+def whole_vectors(side_ref, mine_ref, theirs_ref, rows):
+    mine, theirs = mine_ref[rows].astype(F32), theirs_ref[rows].astype(F32)
+    first = side_ref[0] == 0
+    left, right = jnp.where(first, mine, theirs), jnp.where(first, theirs, mine)
+    return jnp.concatenate([left, right], axis=1)
 
 
 def halves(side_ref, size):
@@ -75,9 +83,9 @@
     return list(range(count.bit_length() - 1))
 
 
-def sum_orders(count):
-    turn, last = bits_of(count)[:3], bits_of(count)[3:]
-    return [list(reversed(turn[k:] + turn[:k] + last)) for k in range(3)]
+def sum_orders(count, parts):
+    turn, last = bits_of(count)[:parts], bits_of(count)[parts:]
+    return [list(reversed(turn[k:] + turn[:k] + last)) for k in range(parts)]
 
 
 def place_of(r, order):
@@ -91,11 +99,11 @@
     return sum(((place >> s) & 1) << bit for s, bit in enumerate(order))
 
 
-def project_kernel(side_ref, x_ref, vec_ref, own_ref, other_ref, hid_ref, send_ref):
+def project_kernel(side_ref, x_ref, mine_ref, theirs_ref, own_ref, other_ref, hid_ref, send_ref):
     rows, width = x_ref.shape
     own, other = halves(side_ref, width // 2)
     unit, _ = normalise(x_ref[...].astype(F32))
-    vec = vec_ref[...].astype(F32)
+    vec = whole_vectors(side_ref, mine_ref, theirs_ref, slice(0, 8))
     hid_ref[...] = (unit * vec[0:1] + vec[1:2]).astype(BF16)
     joint = dot_nn(hid_ref[:, own], own_ref[...]) + dot_nn(hid_ref[:, other], other_ref[...])
     three = (
@@ -211,21 +219,50 @@
         out_ref[slot, 2 * HD : 3 * HD, :] = dv_t[:, where].astype(BF16)
 
 
+def split_sums(first, sums, keep_ref, send_ref):
+    for r, line in enumerate(sums):
+        half = line.shape[1] // 2
+        low, high = line[:, :half], line[:, half:]
+        keep_ref[r : r + 1] = jnp.where(first, low, high)
+        send_ref[r : r + 1] = jnp.where(first, high, low)
+
+
 def middle_kernel(
-    side_ref, att_in, x_ref, cot_ref, vec_ref, ebias_ref,
-    mix_own, mix_other, ex_own, ex_other, sh_own, sh_other,
-    res_ref, gm_ref, gsend_ref, sums_ref, esum_ref,
-    cotb_ref, act_keep, act_send, hid_keep, hid_send, ge_ref, att_keep, att_send, gmb_ref,
-    wide, act_s, geb_s, hid_s, att_s, narrow,
+    side_ref, att_in, x_ref, cot_ref, mine_ref, theirs_ref, *refs,
 ):
+    sources, refs = refs[:6], refs[6:]
+    (
+        res_ref, gm_ref, gsend_ref, sums_keep, sums_send,
+        cotb_ref, act_keep, act_send, hid_keep, hid_send, ge_ref, att_keep, att_send, gmb_ref,
+        wide, act_s, hid_s, att_s, narrow, *weights, sem,
+    ) = refs
+    mix_own, mix_other, ex_own, ex_other, sh_own, sh_other = weights
+    copies = [
+        pltpu.make_async_copy(src, dst, sem.at[i])
+        for i, (src, dst) in enumerate(zip(sources, weights))
+    ]
+    for copy in copies:
+        copy.start()
     rows, width = x_ref.shape
     ff = wide.shape[1]
+    part = ff // 8
     own, other = halves(side_ref, width // 2)
     fown, fother = halves(side_ref, ff // 2)
-    vec = vec_ref[...].astype(F32)
+    vec = whole_vectors(side_ref, mine_ref, theirs_ref, slice(0, 8))
+    first = side_ref[0] == 0
+    lines = [
+        [ref[8 + r : 9 + r].astype(F32) for r in range(4)] for ref in (mine_ref, theirs_ref)
+    ]
+    ebias = jnp.concatenate(
+        [jnp.where(first, a, b) for a, b in zip(*lines)]
+        + [jnp.where(first, b, a) for a, b in zip(*lines)],
+        axis=1,
+    )
     att_s[...] = att_in[0:H].reshape(width, rows).T
     att_keep[...] = att_s[:, own]
     att_send[...] = att_s[:, other]
+    copies[0].wait()
+    copies[1].wait()
     middle = (
         x_ref[...].astype(F32)
         + (dot_nn(att_keep[...], mix_own[...]) + dot_nn(att_send[...], mix_other[...]))
@@ -235,10 +272,12 @@
     hid_s[...] = (unit * vec[5:6] + vec[6:7]).astype(BF16)
     hid_keep[...] = hid_s[:, own]
     hid_send[...] = hid_s[:, other]
+    copies[2].wait()
+    copies[3].wait()
     expanded = (
         dot_nn(hid_keep[...], ex_own[...])
         + dot_nn(hid_send[...], ex_other[...])
-        + ebias_ref[...].astype(F32)
+        + ebias
     )
     square = expanded * expanded
     bend = jnp.tanh(GELU_COEF * (expanded + GELU_CUBE * square * expanded))
@@ -248,6 +287,8 @@
     )
     act_keep[...] = act_s[:, fown]
     act_send[...] = act_s[:, fother]
+    copies[4].wait()
+    copies[5].wait()
     result = (
         middle
         + (dot_nn(act_keep[...], sh_own[...]) + dot_nn(act_send[...], sh_other[...]))
@@ -259,18 +300,23 @@
     wide[:, fown] = dot_nt(cotb_ref[...], sh_own[...])
     wide[:, fother] = dot_nt(cotb_ref[...], sh_other[...])
     grad_expanded = wide[...] * slope
-    esum_ref[...] = jnp.sum(grad_expanded, axis=0, keepdims=True)
+    esum = jnp.sum(grad_expanded, axis=0, keepdims=True)
+    for r in range(4):
+        low = esum[:, r * part : (r + 1) * part]
+        high = esum[:, (4 + r) * part : (5 + r) * part]
+        sums_keep[4 + r : 5 + r] = jnp.where(first, low, high)
+        sums_send[4 + r : 5 + r] = jnp.where(first, high, low)
     ge_ref[...] = grad_expanded.astype(BF16)
     narrow[:, own] = dot_nt(ge_ref[...], ex_own[...])
     narrow[:, other] = dot_nt(ge_ref[...], ex_other[...])
     grad_hidden = narrow[...]
-    sums_ref[1:2] = jnp.sum(grad_hidden * unit, axis=0, keepdims=True)
-    sums_ref[2:3] = jnp.sum(grad_hidden, axis=0, keepdims=True)
+    sums = [jnp.sum(s, axis=0, keepdims=True) for s in (grad_hidden * unit, grad_hidden)]
     grad_middle = upstream + norm_back(grad_hidden * vec[5:6], unit, inv_std)
     gm_ref[...] = grad_middle
     gmb_ref[...] = grad_middle.astype(BF16)
-    sums_ref[0:1] = jnp.sum(grad_middle, axis=0, keepdims=True)
-    sums_ref[3:4] = jnp.sum(upstream, axis=0, keepdims=True)
+    sums = [jnp.sum(grad_middle, axis=0, keepdims=True)] + sums
+    sums += [jnp.sum(upstream, axis=0, keepdims=True)]
+    split_sums(first, sums, sums_keep, sums_send)
     narrow[:, own] = dot_nt(gmb_ref[...], mix_own[...])
     narrow[:, other] = dot_nt(gmb_ref[...], mix_other[...])
     gsend_ref[0:H] = narrow[...].astype(BF16).T.reshape(H, HD, rows)
@@ -279,12 +325,12 @@
 
 
 def finish_kernel(
-    side_ref, in_ref, x_ref, gm_ref, vec_ref, hid_ref, own_ref, other_ref,
-    grad_ref, sums_ref, gj_ref, hid_keep, hid_send, narrow,
+    side_ref, in_ref, x_ref, gm_ref, mine_ref, theirs_ref, hid_ref, own_ref, other_ref,
+    grad_ref, sums_keep, sums_send, gj_ref, hid_keep, hid_send, narrow,
 ):
     rows, width = x_ref.shape
     own, other = halves(side_ref, width // 2)
-    vec = vec_ref[...].astype(F32)
+    gain = whole_vectors(side_ref, mine_ref, theirs_ref, slice(0, 1))
     for k in range(3):
         gj_ref[:, k * width : (k + 1) * width] = (
             in_ref[0:H, k * HD : (k + 1) * HD, :].reshape(width, rows).T
@@ -295,44 +341,48 @@
     narrow[:, own] = dot_nt(gj_ref[...], own_ref[...])
     narrow[:, other] = dot_nt(gj_ref[...], other_ref[...])
     grad_hidden = narrow[...]
-    sums_ref[0:1] = jnp.sum(grad_hidden * unit, axis=0, keepdims=True)
-    sums_ref[1:2] = jnp.sum(grad_hidden, axis=0, keepdims=True)
-    sums_ref[2:3] = jnp.sum(gj_ref[:, :width].astype(F32), axis=0, keepdims=True)
-    sums_ref[3:4] = jnp.sum(gj_ref[:, 2 * width :].astype(F32), axis=0, keepdims=True)
-    grad_ref[...] = gm_ref[...] + norm_back(grad_hidden * vec[0:1], unit, inv_std)
-
-
-def block_spans(a, k, rows, cols, paired, count):
-    third = cols // 3
+    joint = gj_ref[...].astype(F32)
+    sums = (grad_hidden * unit, grad_hidden, joint[:, :width], joint[:, 2 * width :])
+    sums = [jnp.sum(s, axis=0, keepdims=True) for s in sums]
+    split_sums(side_ref[0] == 0, sums, sums_keep, sums_send)
+    grad_ref[...] = gm_ref[...] + norm_back(grad_hidden * gain, unit, inv_std)
+
+
+def block_spans(a, rows, wide, paired, count):
     if paired:
-        tall, wide = 2 * rows // count, third // 2
+        tall, wide = 2 * rows // count, wide // 2
         first, start = a // 2 * tall, a % 2 * wide
     else:
-        tall, wide = rows // count, third
+        tall = rows // count
         first, start = a * tall, 0
     return first, tall, [start + j * LANES for j in range(wide // LANES)]
 
 
-def pack_kernel(paired, meta_ref, *refs):
+def pack_kernel(paired, parts, meta_ref, *refs):
     weights = len(paired)
-    ins, extra_ref = refs[: 4 * weights], refs[4 * weights]
-    outs = refs[4 * weights + 1 : 4 * weights + 7]
-    lefts = refs[4 * weights + 7 : -1 : 2]
-    rights = refs[4 * weights + 8 : -1 : 2]
-    pk = refs[-1]
-    count = extra_ref.shape[0]
+    ins, (keep_sums, came_sums) = refs[: 4 * weights], refs[4 * weights : 4 * weights + 2]
+    outs, refs = refs[4 * weights + 2 :][: 2 * parts], refs[4 * weights + 2 + 2 * parts :]
+    lefts, rights, (pk, extra) = refs[:-2:2], refs[1:-2:2], refs[-2:]
+    count = pk.shape[0]
     for i, (left, right) in enumerate(zip(lefts, rights)):
         rows = left.shape[0] // 2
         for n, dst in enumerate((left, left, right, right)):
             dst[(n % 2) * rows : (n % 2 + 1) * rows] = ins[4 * i + n][...]
-    for k, order in enumerate(sum_orders(count)):
+    extra[...] = jnp.zeros_like(extra)
+    sums = keep_sums[...] + came_sums[...]
+    each = sums.shape[1] // LANES
+    for q in range(sums.shape[0] * each):
+        extra[q // LINES, q % LINES : q % LINES + 1] = sums[
+            q // each : q // each + 1, q % each * LANES : (q % each + 1) * LANES
+        ]
+    for k, order in enumerate(sum_orders(count, parts)):
         keep_ref, send_ref = outs[2 * k : 2 * k + 2]
         line = 0
         for left, right, pair in zip(lefts, rights, paired):
-            third = right.shape[1] // 3
-            grad = dot_tn(left[...], right[:, k * third : (k + 1) * third]).astype(BF16)
+            wide = right.shape[1] // parts
+            grad = dot_tn(left[...], right[:, k * wide : (k + 1) * wide]).astype(pk.dtype)
             for a in range(count):
-                first, tall, starts = block_spans(a, k, *grad.shape[:1], 3 * third, pair, count)
+                first, tall, starts = block_spans(a, grad.shape[0], wide, pair, count)
                 for j, start in enumerate(starts):
                     pk[a, line + j * tall : line + (j + 1) * tall] = grad[
                         first : first + tall, start : start + LANES
@@ -341,27 +391,28 @@
         for m in range(count):
             dst = keep_ref if m < count // 2 else send_ref
             a = relative_at(m, order) ^ meta_ref[1]
-            dst[m % (count // 2), 0:line] = pk[a]
+            dst[m % (count // 2), 0:line] = pk[a].astype(BF16)
             if k == 0:
-                dst[m % (count // 2), line:] = extra_ref[a]
-
-
-def unpack_kernel(paired, meta_ref, *refs):
+                dst[m % (count // 2), line:] = extra[a].astype(BF16)
+
+
+def unpack_kernel(paired, parts, meta_ref, *refs):
     weights = len(paired)
-    near_far, outs = refs[:6], refs[6 : 6 + weights]
-    extra_ref = refs[6 + weights]
-    scratch, sem = refs[7 + weights : -1], refs[-1]
+    near_far, refs = refs[: 2 * parts], refs[2 * parts :]
+    outs, sums_ref, scratch, (extra, sem) = (
+        refs[:weights], refs[weights], refs[weights + 1 : -2], refs[-2:],
+    )
     half = near_far[0].shape[0]
     count = 2 * half
     copies = []
-    for k, order in enumerate(sum_orders(count)):
+    for k, order in enumerate(sum_orders(count, parts)):
         for m in range(count):
             a = relative_at(m, order) ^ meta_ref[1]
             block = near_far[2 * k + m // half][m % half].astype(F32)
             line = 0
             for dst, pair in zip(scratch, paired):
-                rows, third = dst.shape[1:]
-                first, tall, starts = block_spans(a, k, rows, 3 * third, pair, count)
+                rows, wide = dst.shape[1:]
+                first, tall, starts = block_spans(a, rows, wide, pair, count)
                 for start in starts:
                     if pair:
                         start = pl.ds(pl.multiple_of(start, LANES), LANES)
@@ -371,7 +422,7 @@
                     dst[k, place, start] = block[line : line + tall]
                     line += tall
             if k == 0:
-                extra_ref[a] = block[line:]
+                extra[a] = block[line:]
         for i, (src, dst) in enumerate(zip(scratch, outs)):
             size = src.shape[2]
             copy = pltpu.make_async_copy(
@@ -379,6 +430,11 @@
             )
             copy.start()
             copies.append(copy)
+    each = sums_ref.shape[1] // LANES
+    for q in range(sums_ref.shape[0] * each):
+        sums_ref[q // each : q // each + 1, q % each * LANES : (q % each + 1) * LANES] = extra[
+            q // LINES, q % LINES : q % LINES + 1
+        ]
     for copy in copies:
         copy.wait()
 
@@ -425,12 +481,13 @@
     return dot_tn(left, lax.all_gather(right, "fsdp", axis=0, tiled=True))
 
 
-def own_columns(sums, group, side):
-    if group == 2:
-        half = sums.shape[1] // 2
-        keep = lax.dynamic_slice_in_dim(sums, side * half, half, 1)
-        send = lax.dynamic_slice_in_dim(sums, (1 - side) * half, half, 1)
-        return keep + lax.ppermute(send, "fsdp", SWAP)
+def sums_over_group(keep, send, group):
+    sums = jnp.concatenate([keep[:4], send[:4]], axis=1)
+    width = sums.shape[1]
+    if keep.shape[0] > 4:
+        wide = jnp.concatenate([keep[4:].reshape(-1), send[4:].reshape(-1)])
+        wide = wide.reshape(group, 4, width // group).swapaxes(0, 1).reshape(4, width)
+        sums = jnp.concatenate([sums, wide], axis=0)
     return lax.psum_scatter(sums, "fsdp", scatter_dimension=1, tiled=True)
 
 
@@ -445,7 +502,7 @@
 class Flow:
     def __init__(self, keeps, sends, count):
         self.keeps, self.sends = list(keeps), list(sends)
-        self.orders = sum_orders(count)
+        self.orders = sum_orders(count, len(self.keeps))
         self.bits = len(self.orders[0])
         self.step = 0
 
@@ -463,7 +520,7 @@
     def accept(self, cames):
         if len(cames) == 1:
             sizes = [part.shape[1] for part in self.keeps]
-            ends = [sum(sizes[: k + 1]) for k in range(3)]
+            ends = [sum(sizes[: k + 1]) for k in range(len(sizes))]
             cames = [cames[0][:, end - size : end] for end, size in zip(ends, sizes)]
         half = cames[0].shape[0] // 2
         if self.step < self.bits - 1:
@@ -489,9 +546,6 @@
     )
     for flow, came in zip(flows, cames):
         flow.accept(came)
-
-
-LINES = 16
 
 
 def pack(pairs, paired, sums, meta, index, group, count):
@@ -534,12 +588,12 @@
     return weights, sums
 
 
-def plain_pack(weights, extra, index, count):
+def plain_pack(weights, extra, index, count, parts):
     keeps, sends = [], []
-    for k, order in enumerate(sum_orders(count)):
+    for k, order in enumerate(sum_orders(count, parts)):
         blocks = []
         for weight in weights:
-            span = weight.shape[1] // 3
+            span = weight.shape[1] // parts
             for start in range(k * span, (k + 1) * span, LANES):
                 blocks.append(weight[:, start : start + LANES].astype(BF16))
         flat = jnp.concatenate(blocks, axis=0)
@@ -553,23 +607,68 @@
     return keeps, sends
 
 
-def plain_unpack(keeps, fars, shapes, lines, index, count):
+def plain_unpack(keeps, fars, shapes, index, count, parts):
     columns = [[] for _ in shapes]
     extra = None
-    for k, order in enumerate(sum_orders(count)):
+    for k, order in enumerate(sum_orders(count, parts)):
         flat = jnp.concatenate([keeps[k], fars[k]], axis=0)
         turn = place_of(jnp.arange(count, dtype=jnp.int32) ^ index, order)
         flat = jnp.take(flat, turn, axis=0).astype(F32)
         if k == 0:
-            extra = flat[:, flat.shape[1] - lines :]
-            flat = flat[:, : flat.shape[1] - lines]
+            extra = flat[:, flat.shape[1] - LINES :]
+            flat = flat[:, : flat.shape[1] - LINES]
         flat = flat.reshape(-1, LANES)
         first = 0
         for i, (rows, cols) in enumerate(shapes):
-            for _ in range(cols // 3 // LANES):
+            for _ in range(cols // parts // LANES):
                 columns[i].append(flat[first : first + rows])
                 first += rows
     return [jnp.concatenate(c, axis=1) for c in columns], extra
+
+
+def pack(pairs, paired, parts, sums, meta, index, group, count):
+    keep_sums, send_sums = sums
+    if group == 2 and count == 16:
+        args = []
+        for keep, send, right in pairs:
+            args += [keep, swap_side(send), right, swap_side(right)]
+        size = sum(keep.shape[1] * right.shape[1] for keep, _, right in pairs)
+        block = size // parts // LANES // count
+        half = count // 2
+        rows = pairs[0][0].shape[0]
+        kind = BF16 if block % 16 == 0 else F32
+        outs = [
+            ((half, block + (LINES if k // 2 == 0 else 0), LANES), BF16) for k in range(2 * parts)
+        ]
+        flows = call(
+            functools.partial(pack_kernel, paired, parts), outs,
+            [((2 * rows, a.shape[1]), BF16) for a in args[::2]]
+            + [((count, block, LANES), kind), ((count, LINES, LANES), F32)],
+            "pack", 4 * rows * size, meta, *args, keep_sums, swap_side(send_sums),
+        )
+        return Flow(flows[::2], flows[1::2], count)
+    extra = sums_over_group(keep_sums, send_sums, group).reshape(-1, LANES)
+    extra = jnp.pad(extra, ((0, LINES * count - extra.shape[0]), (0, 0))).astype(BF16)
+    extra = extra.reshape(count, LINES, LANES)
+    weights = [rows_over_group(*pair) for pair in pairs]
+    return Flow(*plain_pack(weights, extra, index, count, parts), count)
+
+
+def unpack(flow, shapes, paired, vectors, meta, index, group, count):
+    parts = len(flow.keeps)
+    each = shapes[-1][0]
+    if group == 2 and count == 16:
+        near_far = [part for pair in zip(flow.keeps, flow.fars) for part in pair]
+        *weights, sums = call(
+            functools.partial(unpack_kernel, paired, parts),
+            [(s, F32) for s in shapes] + [((vectors, each), F32)],
+            [((parts, r, c // parts), F32) for r, c in shapes]
+            + [((count, LINES, LANES), F32), pltpu.SemaphoreType.DMA((parts, len(shapes)))],
+            "unpack", 0, meta, *near_far, away_outs=len(shapes),
+        )
+        return weights, sums
+    weights, extra = plain_unpack(flow.keeps, flow.fars, shapes, index, count, parts)
+    return weights, extra.reshape(-1)[: vectors * each].reshape(vectors, each)
 
 
 def body(
@@ -594,20 +693,24 @@
         jnp.where(table[None, :] == places[:, None], places[None, :], 0), axis=1
     ).astype(jnp.int32)
     x = block_input[0]
-    qkv = pieces(qkv_weight, group)
     vectors = (
         first_gain, first_shift, query_bias, value_bias, output_bias, second_gain, second_shift,
         shrink_bias,
     )
     if group == 2:
-        (vec,) = call(
+        (mine,) = call(
             stack_kernel, [((12, each), BF16)], [], "stack", 0, *vectors, expand_bias, smem=0
         )
-        vec = join_vector(vec, group, side)
-        ebias = vec[8:].reshape(4, group, each).swapaxes(0, 1).reshape(1, ff)
+        mine, qkv_weight = lax.optimization_barrier((mine, qkv_weight))
+        vec = mine, swap_side(mine)
     else:
-        vec = join_vector(jnp.stack(vectors), group, side)
-        ebias = join_vector(expand_bias[None], group, side)
+        lines = lax.all_gather(jnp.stack(vectors), "fsdp", axis=1, tiled=True)
+        wide = lax.all_gather(expand_bias, "fsdp", axis=0, tiled=True).reshape(2, 4, half)
+        vec = [
+            jnp.concatenate([lines[:, i * half : (i + 1) * half], wide[i]], axis=0)
+            for i in range(2)
+        ]
+    qkv = pieces(qkv_weight, group)
     qkv, output_weight, expand_weight, shrink_weight = lax.optimization_barrier(
         (qkv, output_weight, expand_weight, shrink_weight)
     )
@@ -620,7 +723,7 @@
         project_kernel,
         [((rows, width), BF16), ((count, three, rows), BF16)],
         [], "project", 6 * rows * width * width,
-        meta, x, vec, *qkv,
+        meta, x, *vec, *qkv,
     )
     qkv_here = lax.all_to_all(qkv_send, "ctx", 0, 0, tiled=True)
     att_send, log_total = call(
@@ -632,31 +735,31 @@
     )
     att_here = lax.all_to_all(att_send, "ctx", 0, 0, tiled=True)
     (
-        result, grad_middle, grad_send, sums, esum, cot_b, act_keep, act_out, hid_keep, hid_out,
-        ge_b, att_keep, att_out, gm_b,
+        result, grad_middle, grad_send, keep_sums, send_sums, cot_b, act_keep, act_out, hid_keep,
+        hid_out, ge_b, att_keep, att_out, gm_b,
     ) = call(
         middle_kernel,
         [
             ((rows, width), BF16), ((rows, width), F32), ((count, HD, rows), BF16),
-            ((4, width), F32), ((1, ff), F32), ((rows, width), BF16), ((rows, ff // 2), BF16),
+            ((8, half), F32), ((8, half), F32), ((rows, width), BF16), ((rows, ff // 2), BF16),
             ((rows, ff // 2), BF16), ((rows, half), BF16), ((rows, half), BF16),
             ((rows, ff), BF16), ((rows, half), BF16), ((rows, half), BF16), ((rows, width), BF16),
         ],
         [
-            ((rows, ff), F32), ((rows, ff), BF16), ((rows, ff), BF16), ((rows, width), BF16),
-            ((rows, width), BF16), ((rows, width), F32),
-        ],
+            ((rows, ff), F32), ((rows, ff), BF16), ((rows, width), BF16), ((rows, width), BF16),
+            ((rows, width), F32),
+        ]
+        + [(w.shape, BF16) for w in (*mix, *expand, *shrink)]
+        + [pltpu.SemaphoreType.DMA((6,))],
         "middle", 8 * rows * size + 4 * rows * width * width,
-        meta, att_here, x, out_cotangent[0], vec, ebias, *mix, *expand, *shrink,
+        meta, att_here, x, out_cotangent[0], *vec, *mix, *expand, *shrink, away=6,
     )
     grad_here = lax.all_to_all(grad_send, "ctx", 0, 0, tiled=True)
 
-    esum = esum.reshape(group, 4, each).swapaxes(0, 1).reshape(4, width)
-    sums = own_columns(jnp.concatenate([sums, esum], axis=0), group, side)
     early_kinds = (False, True, True)
     early = pack(
         [(act_keep, act_out, cot_b), (hid_keep, hid_out, ge_b), (att_keep, att_out, gm_b)],
-        early_kinds, sums, meta, index, group, count,
+        early_kinds, 3, (keep_sums, send_sums), meta, index, group, count,
     )
     early.keeps, early.sends, grad_here = lax.optimization_barrier(
         (early.keeps, early.sends, grad_here)
@@ -674,37 +777,36 @@
         "attend_back", 5 * length * length * HD,
         slots, qkv_here, att_send, grad_here, log_total,
     )
-    early.keeps, early.sends, dqkv_send = lax.optimization_barrier(
+    dqkv_here = lax.all_to_all(dqkv_send, "ctx", 0, 0, tiled=True)
+    early.keeps, early.sends, _ = lax.optimization_barrier(
         (early.keeps, early.sends, dqkv_send)
     )
-    dqkv_here = lax.all_to_all(dqkv_send, "ctx", 0, 0, tiled=True)
     advance([early], count)
-    early.keeps, early.sends, dqkv_here = lax.optimization_barrier(
-        (early.keeps, early.sends, dqkv_here)
-    )
     advance([early], count)
-    input_grad, late_sums, gj, hida_keep, hida_out = call(
+    input_grad, keep_sums, send_sums, gj, hida_keep, hida_out = call(
         finish_kernel,
         [
-            ((rows, width), F32), ((4, width), F32), ((rows, 3 * width), BF16),
+            ((rows, width), F32), ((4, half), F32), ((4, half), F32), ((rows, 3 * width), BF16),
             ((rows, half), BF16), ((rows, half), BF16),
         ],
         [((rows, width), F32)],
         "finish", 6 * rows * width * width,
-        meta, dqkv_here, x, grad_middle, vec, hidden_a, *qkv,
-    )
-    late_sums = own_columns(late_sums, group, side)
-    late = pack([(hida_keep, hida_out, gj)], (True,), late_sums, meta, index, group, count)
+        meta, dqkv_here, x, grad_middle, *vec, hidden_a, *qkv,
+    )
+    late = pack(
+        [(hida_keep, hida_out, gj)], (False,), 2, (keep_sums, send_sums), meta, index, group,
+        count,
+    )
     while not early.over():
         advance([early, late], count)
     (grad_shrink, grad_expand, grad_mix), sums = unpack(
-        early, ((4 * each, width), (each, ff), (each, width)), early_kinds, sums, meta, index,
+        early, ((4 * each, width), (each, ff), (each, width)), early_kinds, 8, meta, index,
         group, count,
     )
     while not late.over():
         advance([late], count)
     (grad_qkv,), late_sums = unpack(
-        late, ((each, 3 * width),), (True,), late_sums, meta, index, group, count
+        late, ((each, 3 * width),), (False,), 4, meta, index, group, count
     )
     return (
         result[None], input_grad[None], late_sums[0], late_sums[1], grad_qkv, late_sums[2],

time: 293 us -> 280 us (0.956)
  starting transfers between devices: 78.3 us -> 61.6 us
  waiting for transfers between devices: 127 us -> 139 us
  other arithmetic: 10.5 us -> 6.25 us
    ppermute x40 -> x32, starting transfers between devices: 52.7 us -> 37 us  [swap_bit(): return lax.ppermute(part, 'ctx', [(d, d ^ 1 << bit) for d in range(count)])]
    ppermute x8 -> x11, waiting for transfers between devices: 0.02 us -> 7.04 us  [swap_side(): return lax.ppermute(part, 'fsdp', SWAP)]
    ppermute x40 -> x32, waiting for transfers between devices: 93.9 us -> 100 us  [swap_bit(): return lax.ppermute(part, 'ctx', [(d, d ^ 1 << bit) for d in range(count)])]
    slice x2 -> x3, local copies, waits for them, and re-layouts: 0.01 us -> 3.63 us  [the longest x1 1.47 us: body(): sums[3]]
  transfers between devices with their start and end apart: 59 -> 51, of which waited for: 25 -> 24; matrix products, arithmetic and copies ran while one was open for 4% -> 3% of each run, Pallas kernels for 14% -> 14%
where the time goes in v3:
time: 280 us; the launch traced here: 279 us
  waiting for transfers between devices  139 us (50%)
  starting transfers between devices  61.6 us (22%)
  Pallas kernels  60.4 us (22%)
  local copies, waits for them, and re-layouts  11 us (4%)
  other arithmetic  6.25 us (2%)
    ppermute x32, waiting for transfers between devices, swap_bit(): return lax.ppermute(part, 'ctx', [(d, d ^ 1 << bit) for d in range(count)])  100 us
    pallas_call x10, Pallas kernels, call(): pl.pallas_call(kernel, out_shape=[jax.ShapeDtypeStruct(s, d) for s, d in...  60.4 us
    ppermute x32, starting transfers between devices, swap_bit(): return lax.ppermute(part, 'ctx', [(d, d ^ 1 << bit) for d in range(count)])  37 us
    all_to_all x1, waiting for transfers between devices, body(): qkv_here = lax.all_to_all(qkv_send, 'ctx', 0, 0, tiled=True)  19.3 us
    all_to_all x1, waiting for transfers between devices, body(): att_here = lax.all_to_all(att_send, 'ctx', 0, 0, tiled=True)  8.48 us
    all_to_all x1, starting transfers between devices, body(): qkv_here = lax.all_to_all(qkv_send, 'ctx', 0, 0, tiled=True)  8.23 us
    ppermute x11, waiting for transfers between devices, swap_side(): return lax.ppermute(part, 'fsdp', SWAP)  7.04 us
    unnamed x66, local copies, waits for them, and re-layouts  6.67 us
  transfers between devices with their start and end apart: 51, of which 24 were waited for; matrix products, arithmetic and copies ran while one was open for 3% of the time, Pallas kernels for 14%

profile of v3, /device:TPU:0, one launch (start us, length us, event | category | flops | bytes accessed | tf_op | source)
XLA Modules:
  0.0 279.3 jit_solution(7377719610015327231)
XLA Ops:
  2.5 3.5 %collective-permute-done.1.other_ref = bf16[384,2304]{1,0:T(8,128)(2,1)S(1)} collective-permute-done((bf16[384,2304]{1,0:T(8,128)(2,1)}, bf16[384,2304]{1,0:T(8,128)(2,1)S(1)}, u32[]{:S(2)}, u32[]{:S(2)}) %collective-permute-start.1) | collective-permute-done | bytes 1769504 | tf_op jit(solution)/shard_map/ppermute | solution.py:457
  7.5 3.3 %collective-permute-done.theirs_ref = bf16[12,384]{1,0:T(8,128)(2,1)S(1)} collective-permute-done((bf16[12,384]{1,0:T(8,128)(2,1)}, bf16[12,384]{1,0:T(8,128)(2,1)S(1)}, u32[]{:S(2)}, u32[]{:S(2)}) %collective-permute-start) | collective-permute-done | bytes 9248 | tf_op jit(solution)/shard_map/ppermute | solution.py:475
  11.5 4.1 %project.1 = (bf16[128,768]{1,0:T(8,128)(2,1)}, bf16[16,192,128]{2,1,0:T(8,128)(2,1)}) custom-call(s32[2]{0:T(128)} %pad_add_fusion.side_ref.meta_ref, bf16[128,768]{1,0:T(8,128)(2,1)} %bitcast.7, bf16[12,384]{1,0:T(8,128)(2,1)} %stack.13.mine_ref, bf16[12,384]{1,0:T(8,128)(2,1)} %copy-done.21, bf16[384,2304]{1,0:T(8,128)(2,1)} %own_ref.1, ...), custom_call_target="tpu_custom_call" | custom-call | flops 452984832 | bytes 3753992 | tf_op jit(solution)/shard_map/project/pallas_call | solution.py:70
  15.6 8.2 %all-to-all-start = ((bf16[16,192,128]{2,1,0:T(8,128)(2,1)}), bf16[16,192,128]{2,1,0:T(8,128)(2,1)S(1)}, u32[]{:S(2)}, u32[]{:S(2)}) async-start(bf16[16,192,128]{2,1,0:T(8,128)(2,1)} %get-tuple-element.110), calls=%async_computation | async-start | bytes 1572864 | tf_op jit(solution)/shard_map/all_to_all | solution.py:728
  24.6 19.3 %all-to-all-done.in_ref = bf16[16,192,128]{2,1,0:T(8,128)(2,1)S(1)} async-done(((bf16[16,192,128]{2,1,0:T(8,128)(2,1)}), bf16[16,192,128]{2,1,0:T(8,128)(2,1)S(1)}, u32[]{:S(2)}, u32[]{:S(2)}) %all-to-all-start) | async-done | bytes 786464 | tf_op jit(solution)/shard_map/all_to_all | solution.py:728
  44.7 7.5 %attend.1 = (bf16[16,64,128]{2,1,0:T(8,128)(2,1)}, f32[1,2048]{1,0:T(1,128)}) custom-call(s32[16]{0:T(128)} %select_reduce_fusion.slot_ref, bf16[16,192,128]{2,1,0:T(8,128)(2,1)} %copy-done.14), custom_call_target="tpu_custom_call" | custom-call | flops 536870912 | bytes 786496 | tf_op jit(solution)/shard_map/attend/pallas_call | solution.py:70
  52.2 4.9 %all-to-all-start.1 = ((bf16[16,64,128]{2,1,0:T(8,128)(2,1)}), bf16[16,64,128]{2,1,0:T(8,128)(2,1)S(1)}, u32[]{:S(2)}, u32[]{:S(2)}) async-start(bf16[16,64,128]{2,1,0:T(8,128)(2,1)} %get-tuple-element.111.att_ref), calls=%async_computation.1 | async-start | bytes 524288 | tf_op jit(solution)/shard_map/all_to_all | solution.py:736
  57.2 8.5 %all-to-all-done.1.att_in = bf16[16,64,128]{2,1,0:T(8,128)(2,1)S(1)} async-done(((bf16[16,64,128]{2,1,0:T(8,128)(2,1)}), bf16[16,64,128]{2,1,0:T(8,128)(2,1)S(1)}, u32[]{:S(2)}, u32[]{:S(2)}) %all-to-all-start.1) | async-done | bytes 262176 | tf_op jit(solution)/shard_map/all_to_all | solution.py:736
  66.4 11.2 %middle.1 = (bf16[128,768]{1,0:T(8,128)(2,1)}, f32[128,768]{1,0:T(8,128)}, bf16[16,64,128]{2,1,0:T(8,128)(2,1)}, f32[8,384]{1,0:T(8,128)}, f32[8,384]{1,0:T(8,12...) custom-call(s32[2]{0:T(128)} %pad_add_fusion.side_ref.meta_ref, ...), custom_call_target="tpu_custom_call" | custom-call | flops 2717908992 | bytes 11487240 | tf_op jit(solution)/shard_map/middle/pallas_call | solution.py:70
  78.2 3.8 %all-to-all-start.2 = ((bf16[16,64,128]{2,1,0:T(8,128)(2,1)}), bf16[16,64,128]{2,1,0:T(8,128)(2,1)S(1)}, u32[]{:S(2)}, u32[]{:S(2)}) async-start(bf16[16,64,128]{2,1,0:T(8,128)(2,1)} %get-tuple-element.133), calls=%async_computation.2 | async-start | bytes 524288 | tf_op jit(solution)/shard_map/all_to_all | solution.py:757
  86.5 6.4 %pack.2 = (bf16[8,448,128]{2,1,0:T(8,128)(2,1)}, bf16[8,448,128]{2,1,0:T(8,128)(2,1)}, bf16[8,432,128]{2,1,0:T(8,128)(2,1)}, bf16[8,432,128]{2,1,0:T(8,128)(2,1)...) custom-call(s32[2]{0:T(128)} %pad_add_fusion.side_ref.meta_ref, ...), custom_call_target="tpu_custom_call" | custom-call | flops 1358954496 | bytes 3563528 | tf_op jit(solution)/shard_map/pack/pallas_call | solution.py:70
  97.8 10.2 %attend_back.1 = bf16[16,192,128]{2,1,0:T(8,128)(2,1)} custom-call(s32[16]{0:T(128)} %select_reduce_fusion.slot_ref, bf16[16,192,128]{2,1,0:T(8,128)(2,1)} %copy-done.14, bf16[16,64,128]{2,1,0:T(8,128)(2,1)} %get-tuple-element.111.att_ref, bf16[16,64,128]{2,1,0:T(8,128)(2,1)} %copy-done.20, f32[1,2048]{1,0:T(1,128)} %get-tuple-element.135.total_ref), custom_call_target="tpu_custom_call" | custom-call | flops 1342177280 | bytes 1318976 | tf_op jit(solution)/shard_map/attend_back/pallas_call | solution.py:70
  108.1 3.9 %all-to-all-start.3 = ((bf16[16,192,128]{2,1,0:T(8,128)(2,1)}), bf16[16,192,128]{2,1,0:T(8,128)(2,1)S(1)}, u32[]{:S(2)}, u32[]{:S(2)}) async-start(bf16[16,192,128]{2,1,0:T(8,128)(2,1)} %attend_back.1), calls=%async_computation.3 | async-start | bytes 1572864 | tf_op jit(solution)/shard_map/all_to_all | solution.py:780
  111.9 7.6 %collective-permute-done.16 = bf16[8,432,128]{2,1,0:T(8,128)(2,1)} collective-permute-done((bf16[8,432,128]{2,1,0:T(8,128)(2,1)}, bf16[8,432,128]{2,1,0:T(8,128)(2,1)}, u32[]{:S(2)}, u32[]{:S(2)}) %collective-permute-start.16) | collective-permute-done | bytes 884768 | tf_op jit(solution)/shard_map/ppermute | solution.py:495
  119.5 5.0 %collective-permute-done.17 = bf16[8,432,128]{2,1,0:T(8,128)(2,1)} collective-permute-done((bf16[8,432,128]{2,1,0:T(8,128)(2,1)}, bf16[8,432,128]{2,1,0:T(8,128)(2,1)}, u32[]{:S(2)}, u32[]{:S(2)}) %collective-permute-start.17) | collective-permute-done | bytes 884768 | tf_op jit(solution)/shard_map/ppermute | solution.py:495
  127.4 12.6 %collective-permute-done.19 = bf16[4,432,128]{2,1,0:T(8,128)(2,1)S(1)} collective-permute-done((bf16[4,432,128]{2,1,0:T(8,128)(2,1)S(1)}, bf16[4,432,128]{2,1,0:T(8,128)(2,1)S(1)}, u32[]{:S(2)}, u32[]{:S(2)}) %collective-permute-start.19) | collective-permute-done | bytes 442400 | tf_op jit(solution)/shard_map/ppermute | solution.py:495
  144.1 4.8 %finish.1 = (f32[128,768]{1,0:T(8,128)}, f32[4,384]{1,0:T(4,128)}, f32[4,384]{1,0:T(4,128)}, bf16[128,2304]{1,0:T(8,128)(2,1)}, bf16[128,384]{1,0:T(8,128)(2,1)}, /*index=5*/bf16[128,384]{1,0:T(8,128)(2,1)}) custom-call(s32[2]{0:T(128)} %pad_add_fusion.side_ref.meta_ref, bf16[16,192,128]{2,1,0:T(8,128)(2,1)} %copy-done.4, bf16[128,768]{1,0:T(8,128)(2,1)} %bitcast.9, ...), custom_call_target="tpu_custom_call" | custom-call | flops 452984832 | bytes 5130248 | tf_op jit(solution)/shard_map/finish/pallas_call | solution.py:70
  152.2 3.3 %pack.3 = (bf16[8,232,128]{2,1,0:T(8,128)(2,1)}, bf16[8,232,128]{2,1,0:T(8,128)(2,1)}, bf16[8,216,128]{2,1,0:T(8,128)(2,1)}, bf16[8,216,128]{2,1,0:T(8,128)(2,1)}) custom-call(s32[2]{0:T(128)} %pad_add_fusion.side_ref.meta_ref, bf16[128,384]{1,0:T(8,128)(2,1)} %get-tuple-element.139.refs_0_, bf16[128,384]{1,0:T(8,128)(2,1)} %copy-done.28, ...), custom_call_target="tpu_custom_call" | custom-call | flops 452984832 | bytes 1388552 | tf_op jit(solution)/shard_map/pack/pallas_call | solution.py:70
  158.4 2.4 collective-permute-start.24
  160.8 15.1 %collective-permute-done.24 = bf16[1,1312,128]{2,1,0:T(8,128)(2,1)S(1)} collective-permute-done((bf16[1,1312,128]{2,1,0:T(8,128)(2,1)S(1)}, bf16[1,1312,128]{2,1,0:T(8,128)(2,1)S(1)}, u32[]{:S(2)}, u32[]{:S(2)}) %collective-permute-start.24) | collective-permute-done | bytes 335904 | tf_op jit(solution)/shard_map/ppermute | solution.py:495
  178.6 6.7 %collective-permute-done.29 = bf16[4,216,128]{2,1,0:T(8,128)(2,1)S(1)} collective-permute-done((bf16[4,216,128]{2,1,0:T(8,128)(2,1)S(1)}, bf16[4,216,128]{2,1,0:T(8,128)(2,1)S(1)}, u32[]{:S(2)}, u32[]{:S(2)}) %collective-permute-start.29) | collective-permute-done | bytes 221216 | tf_op jit(solution)/shard_map/ppermute | solution.py:495
  185.3 9.1 %collective-permute-done.27 = bf16[1,1312,128]{2,1,0:T(8,128)(2,1)S(1)} collective-permute-done((bf16[1,1312,128]{2,1,0:T(8,128)(2,1)S(1)}, bf16[1,1312,128]{2,1,0:T(8,128)(2,1)S(1)}, u32[]{:S(2)}, u32[]{:S(2)}) %collective-permute-start.27) | collective-permute-done | bytes 335904 | tf_op jit(solution)/shard_map/ppermute | solution.py:495
  196.4 2.1 collective-permute-start.30
  199.0 3.1 %collective-permute-done.32 = bf16[2,432,128]{2,1,0:T(8,128)(2,1)S(1)} collective-permute-done((bf16[2,432,128]{2,1,0:T(8,128)(2,1)S(1)}, bf16[2,432,128]{2,1,0:T(8,128)(2,1)S(1)}, u32[]{:S(2)}, u32[]{:S(2)}) %collective-permute-start.32) | collective-permute-done | bytes 221216 | tf_op jit(solution)/shard_map/ppermute | solution.py:495
  202.1 2.9 %collective-permute-done.31 = bf16[2,432,128]{2,1,0:T(8,128)(2,1)S(1)} collective-permute-done((bf16[2,432,128]{2,1,0:T(8,128)(2,1)S(1)}, bf16[2,432,128]{2,1,0:T(8,128)(2,1)S(1)}, u32[]{:S(2)}, u32[]{:S(2)}) %collective-permute-start.31) | collective-permute-done | bytes 221216 | tf_op jit(solution)/shard_map/ppermute | solution.py:495
  209.8 2.8 collective-permute-start.37
  212.6 6.8 %collective-permute-done.37 = bf16[1,448,128]{2,1,0:T(8,128)(2,1)S(1)} collective-permute-done((bf16[1,448,128]{2,1,0:T(8,128)(2,1)S(1)}, bf16[1,448,128]{2,1,0:T(8,128)(2,1)S(1)}, u32[]{:S(2)}, u32[]{:S(2)}) %collective-permute-start.37) | collective-permute-done | bytes 114720 | tf_op jit(solution)/shard_map/ppermute | solution.py:495
  227.9 14.8 %collective-permute-done.41 = bf16[1,448,128]{2,1,0:T(8,128)(2,1)S(1)} collective-permute-done((bf16[1,448,128]{2,1,0:T(8,128)(2,1)S(1)}, bf16[1,448,128]{2,1,0:T(8,128)(2,1)S(1)}, u32[]{:S(2)}, u32[]{:S(2)}) %collective-permute-start.41) | collective-permute-done | bytes 114720 | tf_op jit(solution)/shard_map/ppermute | solution.py:495
  245.2 4.8 %collective-permute-done.42 = bf16[2,448,128]{2,1,0:T(8,128)(2,1)S(1)} collective-permute-done((bf16[2,448,128]{2,1,0:T(8,128)(2,1)S(1)}, bf16[2,448,128]{2,1,0:T(8,128)(2,1)S(1)}, u32[]{:S(2)}, u32[]{:S(2)}) %collective-permute-start.42) | collective-permute-done | bytes 229408 | tf_op jit(solution)/shard_map/ppermute | solution.py:495
  253.2 6.8 %collective-permute-done.44 = bf16[4,216,128]{2,1,0:T(8,128)(2,1)S(1)} collective-permute-done((bf16[4,216,128]{2,1,0:T(8,128)(2,1)S(1)}, bf16[4,216,128]{2,1,0:T(8,128)(2,1)S(1)}, u32[]{:S(2)}, u32[]{:S(2)}) %collective-permute-start.44) | collective-permute-done | bytes 221216 | tf_op jit(solution)/shard_map/ppermute | solution.py:495
  262.1 7.4 %unpack.3 = (f32[1536,768]{1,0:T(8,128)}, f32[384,3072]{1,0:T(8,128)}, f32[384,768]{1,0:T(8,128)}, f32[8,384]{1,0:T(8,128)}) custom-call(s32[2]{0:T(128)} %pad_add_fusion.side_ref.meta_ref, bf16[8,448,128]{2,1,0:T(8,128)(2,1)} %copy-done.1, bf16[8,448,128]{2,1,0:T(8,128)(2,1)} %copy-done.8, bf16[8,432,128]{2,1,0:T(8,128)(2,1)} %copy-done.3, ...), custom_call_target="tpu_custom_call" | custom-call | bytes 5373960 | tf_op jit(solution)/shard_map/unpack/pallas_call | solution.py:70
  273.9 4.0 %unpack.2 = (f32[384,2304]{1,0:T(8,128)}, f32[4,384]{1,0:T(4,128)}) custom-call(s32[2]{0:T(128)} %pad_add_fusion.side_ref.meta_ref, bf16[8,232,128]{2,1,0:T(8,128)(2,1)} %copy-done.5, bf16[8,232,128]{2,1,0:T(8,128)(2,1)} %copy-done.17, bf16[8,216,128]{2,1,0:T(8,128)(2,1)} %copy-done.6, bf16[8,216,128]{2,1,0:T(8,128)(2,1)} %copy-done.19), custom_call_target="tpu_custom_call" | custom-call | bytes 1835016 | tf_op jit(solution)/shard_map/unpack/pallas_call | solution.py:70
  (195 shorter events, 61.1 us)
Async XLA Ops:
  6.1 59.6 %collective-permute-start.3 = (bf16[384,3072]{1,0:T(8,128)(2,1)}, bf16[384,3072]{1,0:T(8,128)(2,1)}, u32[]{:S(2)}, u32[]{:S(2)}) collective-permute-start(bf16[384,3072]{1,0:T(8,128)(2,1)} %refs_2_.2), channel_id=1, source_target_pairs={{0,1},{1,0},{2,3},{3,2},{4,5},{5,4},{6,7},{7,6},{8,9},{9,8},{10,11... | collective-permute-start | bytes 7077896 | tf_op jit(solution)/shard_map/ppermute | solution.py:457
  6.5 59.2 %collective-permute-start.4 = (bf16[1536,768]{1,0:T(8,128)(2,1)}, bf16[1536,768]{1,0:T(8,128)(2,1)}, u32[]{:S(2)}, u32[]{:S(2)}) collective-permute-start(bf16[1536,768]{1,0:T(8,128)(2,1)} %refs_4_.2), channel_id=1, source_target_pairs={{0,1},{1,0},{2,3},{3,2},{4,5},{5,4},{6,7},{7,6},{8,9},{9,8},{10,11... | collective-permute-start | bytes 7077896 | tf_op jit(solution)/shard_map/ppermute | solution.py:457
  15.6 28.2 %all-to-all-start = ((bf16[16,192,128]{2,1,0:T(8,128)(2,1)}), bf16[16,192,128]{2,1,0:T(8,128)(2,1)S(1)}, u32[]{:S(2)}, u32[]{:S(2)}) async-start(bf16[16,192,128]{2,1,0:T(8,128)(2,1)} %get-tuple-element.110), calls=%async_computation | async-start | bytes 1572864 | tf_op jit(solution)/shard_map/all_to_all | solution.py:728
  23.8 33.3 %collective-permute-start.2 = (bf16[384,768]{1,0:T(8,128)(2,1)S(1)}, bf16[384,768]{1,0:T(8,128)(2,1)S(1)}, u32[]{:S(2)}, u32[]{:S(2)}) collective-permute-start(bf16[384,768]{1,0:T(8,128)(2,1)S(1)} %copy-done.15), channel_id=1, source_target_pairs={{0,1},{1,0},{2,3},{3,2},{4,5},{5,4},{6,7},{7,6},{8,9},{9,8},{10,11... | collective-permute-start | bytes 1769480 | tf_op jit(solution)/shard_map/ppermute | solution.py:457
  52.2 13.4 %all-to-all-start.1 = ((bf16[16,64,128]{2,1,0:T(8,128)(2,1)}), bf16[16,64,128]{2,1,0:T(8,128)(2,1)S(1)}, u32[]{:S(2)}, u32[]{:S(2)}) async-start(bf16[16,64,128]{2,1,0:T(8,128)(2,1)} %get-tuple-element.111.att_ref), calls=%async_computation.1 | async-start | bytes 524288 | tf_op jit(solution)/shard_map/all_to_all | solution.py:736
  78.2 14.7 %all-to-all-start.2 = ((bf16[16,64,128]{2,1,0:T(8,128)(2,1)}), bf16[16,64,128]{2,1,0:T(8,128)(2,1)S(1)}, u32[]{:S(2)}, u32[]{:S(2)}) async-start(bf16[16,64,128]{2,1,0:T(8,128)(2,1)} %get-tuple-element.133), calls=%async_computation.2 | async-start | bytes 524288 | tf_op jit(solution)/shard_map/all_to_all | solution.py:757
  92.9 31.6 %collective-permute-start.15 = (bf16[8,448,128]{2,1,0:T(8,128)(2,1)}, bf16[8,448,128]{2,1,0:T(8,128)(2,1)S(1)}, u32[]{:S(2)}, u32[]{:S(2)}) collective-permute-start(bf16[8,448,128]{2,1,0:T(8,128)(2,1)} %get-tuple-element.146), channel_id=1, source_target_pairs={{0,2},{2,0},{4,6},{6,4},{8,10},{10,8},{12,14},{14,12},{16,18},{18,... | collective-permute-start | bytes 2752520 | tf_op jit(solution)/shard_map/ppermute | solution.py:495
  94.9 24.6 %collective-permute-start.16 = (bf16[8,432,128]{2,1,0:T(8,128)(2,1)}, bf16[8,432,128]{2,1,0:T(8,128)(2,1)}, u32[]{:S(2)}, u32[]{:S(2)}) collective-permute-start(bf16[8,432,128]{2,1,0:T(8,128)(2,1)} %get-tuple-element.147), channel_id=1, source_target_pairs={{0,4},{2,6},{4,0},{6,2},{8,12},{10,14},{12,8},{14,10},{16,20},{18,... | collective-permute-start | bytes 2654216 | tf_op jit(solution)/shard_map/ppermute | solution.py:495
  96.4 28.1 %collective-permute-start.17 = (bf16[8,432,128]{2,1,0:T(8,128)(2,1)}, bf16[8,432,128]{2,1,0:T(8,128)(2,1)}, u32[]{:S(2)}, u32[]{:S(2)}) collective-permute-start(bf16[8,432,128]{2,1,0:T(8,128)(2,1)} %get-tuple-element.148), channel_id=1, source_target_pairs={{0,8},{2,10},{4,12},{6,14},{8,0},{10,2},{12,4},{14,6},{16,24},{18,... | collective-permute-start | bytes 2654216 | tf_op jit(solution)/shard_map/ppermute | solution.py:495
  108.1 35.2 %all-to-all-start.3 = ((bf16[16,192,128]{2,1,0:T(8,128)(2,1)}), bf16[16,192,128]{2,1,0:T(8,128)(2,1)S(1)}, u32[]{:S(2)}, u32[]{:S(2)}) async-start(bf16[16,192,128]{2,1,0:T(8,128)(2,1)} %attend_back.1), calls=%async_computation.3 | async-start | bytes 1572864 | tf_op jit(solution)/shard_map/all_to_all | solution.py:780
  126.6 13.4 %collective-permute-start.18 = (bf16[4,448,128]{2,1,0:T(8,128)(2,1)S(1)}, bf16[4,448,128]{2,1,0:T(8,128)(2,1)S(1)}, u32[]{:S(2)}, u32[]{:S(2)}) collective-permute-start(bf16[4,448,128]{2,1,0:T(8,128)(2,1)S(1)} %get-tuple-element.155), channel_id=1, source_target_pairs={{0,4},{2,6},{4,0},{6,2},{8,12},{10,14},{12,8},{14,10},{16,20},{18,... | collective-permute-start | bytes 1376264 | tf_op jit(solution)/shard_map/ppermute | solution.py:495
  126.7 13.3 %collective-permute-start.19 = (bf16[4,432,128]{2,1,0:T(8,128)(2,1)S(1)}, bf16[4,432,128]{2,1,0:T(8,128)(2,1)S(1)}, u32[]{:S(2)}, u32[]{:S(2)}) collective-permute-start(bf16[4,432,128]{2,1,0:T(8,128)(2,1)S(1)} %get-tuple-element.156), channel_id=1, source_target_pairs={{0,8},{2,10},{4,12},{6,14},{8,0},{10,2},{12,4},{14,6},{16,24},{18,... | collective-permute-start | bytes 1327112 | tf_op jit(solution)/shard_map/ppermute | solution.py:495
  126.8 13.2 %collective-permute-start.20 = (bf16[4,432,128]{2,1,0:T(8,128)(2,1)S(1)}, bf16[4,432,128]{2,1,0:T(8,128)(2,1)S(1)}, u32[]{:S(2)}, u32[]{:S(2)}) collective-permute-start(bf16[4,432,128]{2,1,0:T(8,128)(2,1)S(1)} %get-tuple-element.157), channel_id=1, source_target_pairs={{0,2},{2,0},{4,6},{6,4},{8,10},{10,8},{12,14},{14,12},{16,18},{18,... | collective-permute-start | bytes 1327112 | tf_op jit(solution)/shard_map/ppermute | solution.py:495
  140.2 9.4 %collective-permute-start.21 = (bf16[2,448,128]{2,1,0:T(8,128)(2,1)S(1)}, bf16[2,448,128]{2,1,0:T(8,128)(2,1)S(1)}, u32[]{:S(2)}, u32[]{:S(2)}) collective-permute-start(bf16[2,448,128]{2,1,0:T(8,128)(2,1)S(1)} %get-tuple-element.214), channel_id=1, source_target_pairs={{0,8},{2,10},{4,12},{6,14},{8,0},{10,2},{12,4},{14,6},{16,24},{18,... | collective-permute-start | bytes 688136 | tf_op jit(solution)/shard_map/ppermute | solution.py:495
  155.5 20.4 %collective-permute-start.25 = (bf16[8,232,128]{2,1,0:T(8,128)(2,1)}, bf16[8,232,128]{2,1,0:T(8,128)(2,1)S(1)}, u32[]{:S(2)}, u32[]{:S(2)}) collective-permute-start(bf16[8,232,128]{2,1,0:T(8,128)(2,1)} %get-tuple-element.166), channel_id=1, source_target_pairs={{0,2},{2,0},{4,6},{6,4},{8,10},{10,8},{12,14},{14,12},{16,18},{18,... | collective-permute-start | bytes 1425416 | tf_op jit(solution)/shard_map/ppermute | solution.py:495
  157.0 19.0 %collective-permute-start.26 = (bf16[8,216,128]{2,1,0:T(8,128)(2,1)}, bf16[8,216,128]{2,1,0:T(8,128)(2,1)S(1)}, u32[]{:S(2)}, u32[]{:S(2)}) collective-permute-start(bf16[8,216,128]{2,1,0:T(8,128)(2,1)} %get-tuple-element.167), channel_id=1, source_target_pairs={{0,4},{2,6},{4,0},{6,2},{8,12},{10,14},{12,8},{14,10},{16,20},{18,... | collective-permute-start | bytes 1327112 | tf_op jit(solution)/shard_map/ppermute | solution.py:495
  158.4 17.5 %collective-permute-start.24 = (bf16[1,1312,128]{2,1,0:T(8,128)(2,1)S(1)}, bf16[1,1312,128]{2,1,0:T(8,128)(2,1)S(1)}, u32[]{:S(2)}, u32[]{:S(2)}) collective-permute-start(bf16[1,1312,128]{2,1,0:T(8,128)(2,1)S(1)} %pad_maximum_fusion.8), channel_id=1, source_target_pairs={{0,16},{2,18},{4,20},{6,22},{8,24},{10,26},{12,28},{14,30},{16,0},... | collective-permute-start | bytes 1007624 | tf_op jit(solution)/shard_map/ppermute | solution.py:495
  177.9 16.5 %collective-permute-start.27 = (bf16[1,1312,128]{2,1,0:T(8,128)(2,1)S(1)}, bf16[1,1312,128]{2,1,0:T(8,128)(2,1)S(1)}, u32[]{:S(2)}, u32[]{:S(2)}) collective-permute-start(bf16[1,1312,128]{2,1,0:T(8,128)(2,1)S(1)} %pad_maximum_fusion.9), channel_id=1, source_target_pairs={{0,16},{2,18},{4,20},{6,22},{8,24},{10,26},{12,28},{14,30},{16,0},... | collective-permute-start | bytes 1007624 | tf_op jit(solution)/shard_map/ppermute | solution.py:495
  194.6 10.4 %collective-permute-start.33 = (bf16[2,448,128]{2,1,0:T(8,128)(2,1)S(1)}, bf16[2,448,128]{2,1,0:T(8,128)(2,1)S(1)}, u32[]{:S(2)}, u32[]{:S(2)}) collective-permute-start(bf16[2,448,128]{2,1,0:T(8,128)(2,1)S(1)} %pad_maximum_fusion.12), channel_id=1, source_target_pairs={{0,8},{2,10},{4,12},{6,14},{8,0},{10,2},{12,4},{14,6},{16,24},{18,... | collective-permute-start | bytes 688136 | tf_op jit(solution)/shard_map/ppermute | solution.py:495
  196.4 10.7 %collective-permute-start.30 = (bf16[2,448,128]{2,1,0:T(8,128)(2,1)S(1)}, bf16[2,448,128]{2,1,0:T(8,128)(2,1)S(1)}, u32[]{:S(2)}, u32[]{:S(2)}) collective-permute-start(bf16[2,448,128]{2,1,0:T(8,128)(2,1)S(1)} %pad_maximum_fusion.11), channel_id=1, source_target_pairs={{0,8},{2,10},{4,12},{6,14},{8,0},{10,2},{12,4},{14,6},{16,24},{18,... | collective-permute-start | bytes 688136 | tf_op jit(solution)/shard_map/ppermute | solution.py:495
  207.2 12.3 %collective-permute-start.36 = (bf16[4,432,128]{2,1,0:T(8,128)(2,1)S(1)}, bf16[4,432,128]{2,1,0:T(8,128)(2,1)S(1)}, u32[]{:S(2)}, u32[]{:S(2)}) collective-permute-start(bf16[4,432,128]{2,1,0:T(8,128)(2,1)S(1)} %pad_maximum_fusion.6), channel_id=1, source_target_pairs={{0,2},{2,0},{4,6},{6,4},{8,10},{10,8},{12,14},{14,12},{16,18},{18,... | collective-permute-start | bytes 1327112 | tf_op jit(solution)/shard_map/ppermute | solution.py:495
  207.8 13.5 %collective-permute-start.35 = (bf16[4,432,128]{2,1,0:T(8,128)(2,1)S(1)}, bf16[4,432,128]{2,1,0:T(8,128)(2,1)S(1)}, u32[]{:S(2)}, u32[]{:S(2)}) collective-permute-start(bf16[4,432,128]{2,1,0:T(8,128)(2,1)S(1)} %pad_maximum_fusion.5), channel_id=1, source_target_pairs={{0,8},{2,10},{4,12},{6,14},{8,0},{10,2},{12,4},{14,6},{16,24},{18,... | collective-permute-start | bytes 1327112 | tf_op jit(solution)/shard_map/ppermute | solution.py:495
  208.2 13.1 %collective-permute-start.34 = (bf16[4,448,128]{2,1,0:T(8,128)(2,1)S(1)}, bf16[4,448,128]{2,1,0:T(8,128)(2,1)S(1)}, u32[]{:S(2)}, u32[]{:S(2)}) collective-permute-start(bf16[4,448,128]{2,1,0:T(8,128)(2,1)S(1)} %pad_maximum_fusion.4), channel_id=1, source_target_pairs={{0,4},{2,6},{4,0},{6,2},{8,12},{10,14},{12,8},{14,10},{16,20},{18,... | collective-permute-start | bytes 1376264 | tf_op jit(solution)/shard_map/ppermute | solution.py:495
  209.8 9.6 %collective-permute-start.37 = (bf16[1,448,128]{2,1,0:T(8,128)(2,1)S(1)}, bf16[1,448,128]{2,1,0:T(8,128)(2,1)S(1)}, u32[]{:S(2)}, u32[]{:S(2)}) collective-permute-start(bf16[1,448,128]{2,1,0:T(8,128)(2,1)S(1)} %pad_maximum_fusion.16), channel_id=1, source_target_pairs={{0,16},{2,18},{4,20},{6,22},{8,24},{10,26},{12,28},{14,30},{16,0},... | collective-permute-start | bytes 344072 | tf_op jit(solution)/shard_map/ppermute | solution.py:495
  221.4 22.2 %collective-permute-start.40 = (bf16[8,432,128]{2,1,0:T(8,128)(2,1)S(1)}, bf16[8,432,128]{2,1,0:T(8,128)(2,1)S(1)}, u32[]{:S(2)}, u32[]{:S(2)}) collective-permute-start(bf16[8,432,128]{2,1,0:T(8,128)(2,1)S(1)} %pad_maximum_fusion.2.refs_4_), channel_id=1, source_target_pairs={{0,8},{2,10},{4,12},{6,14},{8,0},{10,2},{12,4},{14,6},{16,24},{18,... | collective-permute-start | bytes 2654216 | tf_op jit(solution)/shard_map/ppermute | solution.py:495
  223.0 20.9 %collective-permute-start.38 = (bf16[8,448,128]{2,1,0:T(8,128)(2,1)S(1)}, bf16[8,448,128]{2,1,0:T(8,128)(2,1)S(1)}, u32[]{:S(2)}, u32[]{:S(2)}) collective-permute-start(bf16[8,448,128]{2,1,0:T(8,128)(2,1)S(1)} %pad_maximum_fusion.refs_0_), channel_id=1, source_target_pairs={{0,2},{2,0},{4,6},{6,4},{8,10},{10,8},{12,14},{14,12},{16,18},{18,... | collective-permute-start | bytes 2752520 | tf_op jit(solution)/shard_map/ppermute | solution.py:495
  224.8 19.1 %collective-permute-start.39 = (bf16[8,432,128]{2,1,0:T(8,128)(2,1)S(1)}, bf16[8,432,128]{2,1,0:T(8,128)(2,1)S(1)}, u32[]{:S(2)}, u32[]{:S(2)}) collective-permute-start(bf16[8,432,128]{2,1,0:T(8,128)(2,1)S(1)} %pad_maximum_fusion.1.refs_2_), channel_id=1, source_target_pairs={{0,4},{2,6},{4,0},{6,2},{8,12},{10,14},{12,8},{14,10},{16,20},{18,... | collective-permute-start | bytes 2654216 | tf_op jit(solution)/shard_map/ppermute | solution.py:495
  226.4 16.2 %collective-permute-start.41 = (bf16[1,448,128]{2,1,0:T(8,128)(2,1)S(1)}, bf16[1,448,128]{2,1,0:T(8,128)(2,1)S(1)}, u32[]{:S(2)}, u32[]{:S(2)}) collective-permute-start(bf16[1,448,128]{2,1,0:T(8,128)(2,1)S(1)} %pad_maximum_fusion.17), channel_id=1, source_target_pairs={{0,16},{2,18},{4,20},{6,22},{8,24},{10,26},{12,28},{14,30},{16,0},... | collective-permute-start | bytes 344072 | tf_op jit(solution)/shard_map/ppermute | solution.py:495
  250.1 9.9 %collective-permute-start.43 = (bf16[4,232,128]{2,1,0:T(8,128)(2,1)S(1)}, bf16[4,232,128]{2,1,0:T(8,128)(2,1)S(1)}, u32[]{:S(2)}, u32[]{:S(2)}) collective-permute-start(bf16[4,232,128]{2,1,0:T(8,128)(2,1)S(1)} %pad_maximum_fusion.10), channel_id=1, source_target_pairs={{0,4},{2,6},{4,0},{6,2},{8,12},{10,14},{12,8},{14,10},{16,20},{18,... | collective-permute-start | bytes 712712 | tf_op jit(solution)/shard_map/ppermute | solution.py:495
  251.6 8.4 %collective-permute-start.44 = (bf16[4,216,128]{2,1,0:T(8,128)(2,1)S(1)}, bf16[4,216,128]{2,1,0:T(8,128)(2,1)S(1)}, u32[]{:S(2)}, u32[]{:S(2)}) collective-permute-start(bf16[4,216,128]{2,1,0:T(8,128)(2,1)S(1)} %pad_maximum_fusion.15), channel_id=1, source_target_pairs={{0,2},{2,0},{4,6},{6,4},{8,10},{10,8},{12,14},{14,12},{16,18},{18,... | collective-permute-start | bytes 663560 | tf_op jit(solution)/shard_map/ppermute | solution.py:495
  260.1 12.2 %collective-permute-start.45 = (bf16[8,232,128]{2,1,0:T(8,128)(2,1)S(1)}, bf16[8,232,128]{2,1,0:T(8,128)(2,1)S(1)}, u32[]{:S(2)}, u32[]{:S(2)}) collective-permute-start(bf16[8,232,128]{2,1,0:T(8,128)(2,1)S(1)} %pad_maximum_fusion.3.refs_0_), channel_id=1, source_target_pairs={{0,2},{2,0},{4,6},{6,4},{8,10},{10,8},{12,14},{14,12},{16,18},{18,... | collective-permute-start | bytes 1425416 | tf_op jit(solution)/shard_map/ppermute | solution.py:495
  261.7 10.6 %collective-permute-start.46 = (bf16[8,216,128]{2,1,0:T(8,128)(2,1)S(1)}, bf16[8,216,128]{2,1,0:T(8,128)(2,1)S(1)}, u32[]{:S(2)}, u32[]{:S(2)}) collective-permute-start(bf16[8,216,128]{2,1,0:T(8,128)(2,1)S(1)} %pad_maximum_fusion.7.refs_2_), channel_id=1, source_target_pairs={{0,4},{2,6},{4,0},{6,2},{8,12},{10,14},{12,8},{14,10},{16,20},{18,... | collective-permute-start | bytes 1327112 | tf_op jit(solution)/shard_map/ppermute | solution.py:495
  (52 other events, 405.8 us)

commit v4 on v3

--- a/solution.py
+++ b/solution.py
@@ -99,7 +99,19 @@
     return sum(((place >> s) & 1) << bit for s, bit in enumerate(order))
 
 
-def project_kernel(side_ref, x_ref, mine_ref, theirs_ref, own_ref, other_ref, hid_ref, send_ref):
+def fetch(sources, targets, sem):
+    copies = [
+        pltpu.make_async_copy(src, dst, sem.at[i])
+        for i, (src, dst) in enumerate(zip(sources, targets))
+    ]
+    for copy in copies:
+        copy.start()
+    return copies
+
+
+def project_kernel(
+    side_ref, x_ref, mine_ref, theirs_ref, own_ref, other_ref, hid_ref, send_ref
+):
     rows, width = x_ref.shape
     own, other = halves(side_ref, width // 2)
     unit, _ = normalise(x_ref[...].astype(F32))
@@ -133,27 +145,17 @@
         jnp.int32, (tile, tile), 1
     )
     for i in range(length // tile):
-        here = slice(i * tile, (i + 1) * tile)
+        front, here = slice(0, i * tile), slice(i * tile, (i + 1) * tile)
         query = q_t[:, here]
-        scores = jnp.where(below, dot_nn(k_n[here, :], query), MASK_FLOOR)
-        best = jnp.max(scores, axis=0, keepdims=True)
-        weights = jnp.exp(scores - best)
-        total = jnp.sum(weights, axis=0, keepdims=True)
-        mixed = dot_nn(v_t[:, here], weights.astype(BF16))
-
-        def step(j, state, query=query):
-            best, total, mixed = state
-            span = pl.ds(pl.multiple_of(j * tile, tile), tile)
-            scores = dot_nn(k_n[span, :], query)
-            new_best = jnp.maximum(best, jnp.max(scores, axis=0, keepdims=True))
-            factor = jnp.exp(best - new_best)
-            weights = jnp.exp(scores - new_best)
-            total = total * factor + jnp.sum(weights, axis=0, keepdims=True)
-            mixed = mixed * factor + dot_nn(v_t[:, span], weights.astype(BF16))
-            return new_best, total, mixed
-
-        if i:
-            best, total, mixed = lax.fori_loop(0, i, step, (best, total, mixed))
+        spans = [here] + [front] * (i > 0)
+        scores = [dot_nn(k_n[span, :], query) for span in spans]
+        scores[0] = jnp.where(below, scores[0], MASK_FLOOR)
+        best = jnp.max(scores[0], axis=0, keepdims=True)
+        for part in scores[1:]:
+            best = jnp.maximum(best, jnp.max(part, axis=0, keepdims=True))
+        weights = [jnp.exp(part - best) for part in scores]
+        total = sum(jnp.sum(part, axis=0, keepdims=True) for part in weights)
+        mixed = sum(dot_nn(v_t[:, s], w.astype(BF16)) for s, w in zip(spans, weights))
         o_t[:, here] = (mixed / total).astype(BF16)
         total_ref[:, here] = best + jnp.log(total)
     for p in range(count):
@@ -193,7 +195,7 @@
 
         def step(i, state, masked=False, here=here):
             key_sum, value_sum = state
-            span = pl.ds(pl.multiple_of(i * tile, tile), tile)
+            span = slice(i * tile, (i + 1) * tile)
             scores = dot_nn(k_n[here, :], q_t[:, span])
             probs = jnp.exp(scores - total_ref[:, span])
             if masked:
@@ -207,8 +209,8 @@
 
         zero = jnp.zeros((tile, HD), F32)
         state = step(j, (zero, zero), masked=True)
-        if j + 1 < tiles:
-            state = lax.fori_loop(j + 1, tiles, step, state)
+        for i in range(j + 1, tiles):
+            state = step(i, state)
         dk_t[:, here] = state[0].T
         dv_t[:, here] = state[1].T
     for p in range(count):
@@ -237,12 +239,7 @@
         wide, act_s, hid_s, att_s, narrow, *weights, sem,
     ) = refs
     mix_own, mix_other, ex_own, ex_other, sh_own, sh_other = weights
-    copies = [
-        pltpu.make_async_copy(src, dst, sem.at[i])
-        for i, (src, dst) in enumerate(zip(sources, weights))
-    ]
-    for copy in copies:
-        copy.start()
+    copies = fetch(sources, weights, sem)
     rows, width = x_ref.shape
     ff = wide.shape[1]
     part = ff // 8
@@ -399,9 +396,8 @@
 def unpack_kernel(paired, parts, meta_ref, *refs):
     weights = len(paired)
     near_far, refs = refs[: 2 * parts], refs[2 * parts :]
-    outs, sums_ref, scratch, (extra, sem) = (
-        refs[:weights], refs[weights], refs[weights + 1 : -2], refs[-2:],
-    )
+    outs, refs, (extra, sem) = refs[:weights], refs[weights:-2], refs[-2:]
+    lines, scratch = refs[:-weights], refs[-weights:]
     half = near_far[0].shape[0]
     count = 2 * half
     copies = []
@@ -430,10 +426,10 @@
             )
             copy.start()
             copies.append(copy)
-    each = sums_ref.shape[1] // LANES
-    for q in range(sums_ref.shape[0] * each):
-        sums_ref[q // each : q // each + 1, q % each * LANES : (q % each + 1) * LANES] = extra[
-            q // LINES, q % LINES : q % LINES + 1
+    each = lines[0].shape[0] // LANES
+    for q in range(len(lines) * each):
+        lines[q // each][q % each * LANES : (q % each + 1) * LANES] = extra[
+            q // LINES, q % LINES, :
         ]
     for copy in copies:
         copy.wait()
@@ -659,16 +655,16 @@
     each = shapes[-1][0]
     if group == 2 and count == 16:
         near_far = [part for pair in zip(flow.keeps, flow.fars) for part in pair]
-        *weights, sums = call(
+        outs = call(
             functools.partial(unpack_kernel, paired, parts),
-            [(s, F32) for s in shapes] + [((vectors, each), F32)],
+            [(s, F32) for s in shapes] + [((each,), F32)] * vectors,
             [((parts, r, c // parts), F32) for r, c in shapes]
             + [((count, LINES, LANES), F32), pltpu.SemaphoreType.DMA((parts, len(shapes)))],
             "unpack", 0, meta, *near_far, away_outs=len(shapes),
         )
-        return weights, sums
+        return outs[: len(shapes)], outs[len(shapes) :]
     weights, extra = plain_unpack(flow.keeps, flow.fars, shapes, index, count, parts)
-    return weights, extra.reshape(-1)[: vectors * each].reshape(vectors, each)
+    return weights, list(extra.reshape(-1)[: vectors * each].reshape(vectors, each))
 
 
 def body(
@@ -711,8 +707,8 @@
             for i in range(2)
         ]
     qkv = pieces(qkv_weight, group)
-    qkv, output_weight, expand_weight, shrink_weight = lax.optimization_barrier(
-        (qkv, output_weight, expand_weight, shrink_weight)
+    vec, qkv, output_weight, expand_weight, shrink_weight = lax.optimization_barrier(
+        (vec, qkv, output_weight, expand_weight, shrink_weight)
     )
     mix = pieces(output_weight, group)
     expand = pieces(expand_weight, group)
@@ -810,7 +806,7 @@
     )
     return (
         result[None], input_grad[None], late_sums[0], late_sums[1], grad_qkv, late_sums[2],
-        late_sums[3], grad_mix, sums[0], sums[1], sums[2], grad_expand, sums[4:8].reshape(-1),
+        late_sums[3], grad_mix, sums[0], sums[1], sums[2], grad_expand, jnp.concatenate(sums[4:8]),
         grad_shrink, sums[3],
     )
 

time: 280 us -> 271 us (0.968)
  local copies, waits for them, and re-layouts: 11 us -> 6.16 us
  Pallas kernels: 60.4 us -> 57.5 us
    slice x3 -> x0, local copies, waits for them, and re-layouts: 3.63 us -> none  [the longest x1 1.47 us: body(): sums[3]]
    ppermute x4, waiting for transfers between devices: 3.54 us -> 0.01 us  [pieces(): return (weight, lax.ppermute(weight, 'fsdp', SWAP))]
    pallas_call x10, Pallas kernels: 60.4 us -> 57.5 us  [call(): pl.pallas_call(kernel, out_shape=[jax.ShapeDtypeStruct(s, d) for s, d in...]
  transfers between devices with their start and end apart: 51 -> 51, of which waited for: 24 -> 23; matrix products, arithmetic and copies ran while one was open for 3% -> 2% of each run, Pallas kernels for 14% -> 14%
where the time goes in v4:
time: 271 us
  waiting for transfers between devices  137 us (51%)
  starting transfers between devices  60.8 us (22%)
  Pallas kernels  57.5 us (21%)
  other arithmetic  7.58 us (3%)
  local copies, waits for them, and re-layouts  6.16 us (2%)
    ppermute x32, waiting for transfers between devices, swap_bit(): return lax.ppermute(part, 'ctx', [(d, d ^ 1 << bit) for d in range(count)])  102 us
    pallas_call x10, Pallas kernels, call(): pl.pallas_call(kernel, out_shape=[jax.ShapeDtypeStruct(s, d) for s, d in...  57.5 us
    ppermute x32, starting transfers between devices, swap_bit(): return lax.ppermute(part, 'ctx', [(d, d ^ 1 << bit) for d in range(count)])  36.5 us
    all_to_all x1, waiting for transfers between devices, body(): qkv_here = lax.all_to_all(qkv_send, 'ctx', 0, 0, tiled=True)  19.3 us
    all_to_all x1, waiting for transfers between devices, body(): att_here = lax.all_to_all(att_send, 'ctx', 0, 0, tiled=True)  8.48 us
    all_to_all x1, starting transfers between devices, body(): qkv_here = lax.all_to_all(qkv_send, 'ctx', 0, 0, tiled=True)  8.23 us
    ppermute x11, waiting for transfers between devices, swap_side(): return lax.ppermute(part, 'fsdp', SWAP)  7.21 us
    unnamed x66, local copies, waits for them, and re-layouts  6.1 us
  transfers between devices with their start and end apart: 51, of which 23 were waited for; matrix products, arithmetic and copies ran while one was open for 2% of the time, Pallas kernels for 14%

profile of v4, /device:TPU:0, one launch (start us, length us, event | category | flops | bytes accessed | tf_op | source)
XLA Modules:
  0.0 270.5 jit_solution(2591796540665549369)
XLA Ops:
  2.6 3.5 %collective-permute-done.theirs_ref = bf16[12,384]{1,0:T(8,128)(2,1)S(1)} collective-permute-done((bf16[12,384]{1,0:T(8,128)(2,1)}, bf16[12,384]{1,0:T(8,128)(2,1)S(1)}, u32[]{:S(2)}, u32[]{:S(2)}) %collective-permute-start) | collective-permute-done | bytes 9248 | tf_op jit(solution)/shard_map/ppermute | solution.py:471
  7.3 4.1 %project.1 = (bf16[128,768]{1,0:T(8,128)(2,1)}, bf16[16,192,128]{2,1,0:T(8,128)(2,1)}) custom-call(s32[2]{0:T(128)} %pad_add_fusion.side_ref.meta_ref, bf16[128,768]{1,0:T(8,128)(2,1)} %bitcast.7, bf16[12,384]{1,0:T(8,128)(2,1)} %stack.13.mine_ref, bf16[12,384]{1,0:T(8,128)(2,1)} %copy-done.21, bf16[384,2304]{1,0:T(8,128)(2,1)} %own_ref.1, ...), custom_call_target="tpu_custom_call" | custom-call | flops 452984832 | bytes 3753992 | tf_op jit(solution)/shard_map/project/pallas_call | solution.py:70
  11.4 8.2 %all-to-all-start = ((bf16[16,192,128]{2,1,0:T(8,128)(2,1)}), bf16[16,192,128]{2,1,0:T(8,128)(2,1)S(1)}, u32[]{:S(2)}, u32[]{:S(2)}) async-start(bf16[16,192,128]{2,1,0:T(8,128)(2,1)} %get-tuple-element.124), calls=%async_computation | async-start | bytes 1572864 | tf_op jit(solution)/shard_map/all_to_all | solution.py:724
  20.4 19.3 %all-to-all-done.in_ref = bf16[16,192,128]{2,1,0:T(8,128)(2,1)S(1)} async-done(((bf16[16,192,128]{2,1,0:T(8,128)(2,1)}), bf16[16,192,128]{2,1,0:T(8,128)(2,1)S(1)}, u32[]{:S(2)}, u32[]{:S(2)}) %all-to-all-start) | async-done | bytes 786464 | tf_op jit(solution)/shard_map/all_to_all | solution.py:724
  40.6 5.7 %attend.1 = (bf16[16,64,128]{2,1,0:T(8,128)(2,1)}, f32[1,2048]{1,0:T(1,128)}) custom-call(s32[16]{0:T(128)} %select_reduce_fusion.slot_ref, bf16[16,192,128]{2,1,0:T(8,128)(2,1)} %copy-done.14), custom_call_target="tpu_custom_call" | custom-call | flops 536870912 | bytes 786496 | tf_op jit(solution)/shard_map/attend/pallas_call | solution.py:70
  46.2 5.0 %all-to-all-start.1 = ((bf16[16,64,128]{2,1,0:T(8,128)(2,1)}), bf16[16,64,128]{2,1,0:T(8,128)(2,1)S(1)}, u32[]{:S(2)}, u32[]{:S(2)}) async-start(bf16[16,64,128]{2,1,0:T(8,128)(2,1)} %get-tuple-element.125.att_ref), calls=%async_computation.1 | async-start | bytes 524288 | tf_op jit(solution)/shard_map/all_to_all | solution.py:732
  51.2 8.5 %all-to-all-done.1.att_in = bf16[16,64,128]{2,1,0:T(8,128)(2,1)S(1)} async-done(((bf16[16,64,128]{2,1,0:T(8,128)(2,1)}), bf16[16,64,128]{2,1,0:T(8,128)(2,1)S(1)}, u32[]{:S(2)}, u32[]{:S(2)}) %all-to-all-start.1) | async-done | bytes 262176 | tf_op jit(solution)/shard_map/all_to_all | solution.py:732
  60.4 11.2 %middle.1 = (bf16[128,768]{1,0:T(8,128)(2,1)}, f32[128,768]{1,0:T(8,128)}, bf16[16,64,128]{2,1,0:T(8,128)(2,1)}, f32[8,384]{1,0:T(8,128)}, f32[8,384]{1,0:T(8,12...) custom-call(s32[2]{0:T(128)} %pad_add_fusion.side_ref.meta_ref, ...), custom_call_target="tpu_custom_call" | custom-call | flops 2717908992 | bytes 11487240 | tf_op jit(solution)/shard_map/middle/pallas_call | solution.py:70
  72.2 3.8 %all-to-all-start.2 = ((bf16[16,64,128]{2,1,0:T(8,128)(2,1)}), bf16[16,64,128]{2,1,0:T(8,128)(2,1)S(1)}, u32[]{:S(2)}, u32[]{:S(2)}) async-start(bf16[16,64,128]{2,1,0:T(8,128)(2,1)} %get-tuple-element.147), calls=%async_computation.2 | async-start | bytes 524288 | tf_op jit(solution)/shard_map/all_to_all | solution.py:753
  80.4 6.4 %pack.2 = (bf16[8,448,128]{2,1,0:T(8,128)(2,1)}, bf16[8,448,128]{2,1,0:T(8,128)(2,1)}, bf16[8,432,128]{2,1,0:T(8,128)(2,1)}, bf16[8,432,128]{2,1,0:T(8,128)(2,1)...) custom-call(s32[2]{0:T(128)} %pad_add_fusion.side_ref.meta_ref, ...), custom_call_target="tpu_custom_call" | custom-call | flops 1358954496 | bytes 3563528 | tf_op jit(solution)/shard_map/pack/pallas_call | solution.py:70
  91.8 9.3 %attend_back.1 = bf16[16,192,128]{2,1,0:T(8,128)(2,1)} custom-call(s32[16]{0:T(128)} %select_reduce_fusion.slot_ref, bf16[16,192,128]{2,1,0:T(8,128)(2,1)} %copy-done.14, bf16[16,64,128]{2,1,0:T(8,128)(2,1)} %get-tuple-element.125.att_ref, bf16[16,64,128]{2,1,0:T(8,128)(2,1)} %copy-done.20, f32[1,2048]{1,0:T(1,128)} %get-tuple-element.149.total_ref), custom_call_target="tpu_custom_call" | custom-call | flops 1342177280 | bytes 1318976 | tf_op jit(solution)/shard_map/attend_back/pallas_call | solution.py:70
  101.1 3.9 %all-to-all-start.3 = ((bf16[16,192,128]{2,1,0:T(8,128)(2,1)}), bf16[16,192,128]{2,1,0:T(8,128)(2,1)S(1)}, u32[]{:S(2)}, u32[]{:S(2)}) async-start(bf16[16,192,128]{2,1,0:T(8,128)(2,1)} %attend_back.1), calls=%async_computation.3 | async-start | bytes 1572864 | tf_op jit(solution)/shard_map/all_to_all | solution.py:776
  104.9 9.0 %collective-permute-done.16 = bf16[8,432,128]{2,1,0:T(8,128)(2,1)} collective-permute-done((bf16[8,432,128]{2,1,0:T(8,128)(2,1)}, bf16[8,432,128]{2,1,0:T(8,128)(2,1)}, u32[]{:S(2)}, u32[]{:S(2)}) %collective-permute-start.16) | collective-permute-done | bytes 884768 | tf_op jit(solution)/shard_map/ppermute | solution.py:491
  113.9 6.1 %collective-permute-done.17 = bf16[8,432,128]{2,1,0:T(8,128)(2,1)} collective-permute-done((bf16[8,432,128]{2,1,0:T(8,128)(2,1)}, bf16[8,432,128]{2,1,0:T(8,128)(2,1)}, u32[]{:S(2)}, u32[]{:S(2)}) %collective-permute-start.17) | collective-permute-done | bytes 884768 | tf_op jit(solution)/shard_map/ppermute | solution.py:491
  122.4 11.6 %collective-permute-done.19 = bf16[4,432,128]{2,1,0:T(8,128)(2,1)S(1)} collective-permute-done((bf16[4,432,128]{2,1,0:T(8,128)(2,1)S(1)}, bf16[4,432,128]{2,1,0:T(8,128)(2,1)S(1)}, u32[]{:S(2)}, u32[]{:S(2)}) %collective-permute-start.19) | collective-permute-done | bytes 442400 | tf_op jit(solution)/shard_map/ppermute | solution.py:491
  138.1 4.8 %finish.1 = (f32[128,768]{1,0:T(8,128)}, f32[4,384]{1,0:T(4,128)}, f32[4,384]{1,0:T(4,128)}, bf16[128,2304]{1,0:T(8,128)(2,1)}, bf16[128,384]{1,0:T(8,128)(2,1)}, /*index=5*/bf16[128,384]{1,0:T(8,128)(2,1)}) custom-call(s32[2]{0:T(128)} %pad_add_fusion.side_ref.meta_ref, bf16[16,192,128]{2,1,0:T(8,128)(2,1)} %copy-done.4, bf16[128,768]{1,0:T(8,128)(2,1)} %bitcast.9, ...), custom_call_target="tpu_custom_call" | custom-call | flops 452984832 | bytes 5130248 | tf_op jit(solution)/shard_map/finish/pallas_call | solution.py:70
  146.2 3.3 %pack.3 = (bf16[8,232,128]{2,1,0:T(8,128)(2,1)}, bf16[8,232,128]{2,1,0:T(8,128)(2,1)}, bf16[8,216,128]{2,1,0:T(8,128)(2,1)}, bf16[8,216,128]{2,1,0:T(8,128)(2,1)}) custom-call(s32[2]{0:T(128)} %pad_add_fusion.side_ref.meta_ref, bf16[128,384]{1,0:T(8,128)(2,1)} %get-tuple-element.153.refs_0_, bf16[128,384]{1,0:T(8,128)(2,1)} %copy-done.28, ...), custom_call_target="tpu_custom_call" | custom-call | flops 452984832 | bytes 1388552 | tf_op jit(solution)/shard_map/pack/pallas_call | solution.py:70
  152.4 2.4 collective-permute-start.24
  154.8 15.1 %collective-permute-done.24 = bf16[1,1312,128]{2,1,0:T(8,128)(2,1)S(1)} collective-permute-done((bf16[1,1312,128]{2,1,0:T(8,128)(2,1)S(1)}, bf16[1,1312,128]{2,1,0:T(8,128)(2,1)S(1)}, u32[]{:S(2)}, u32[]{:S(2)}) %collective-permute-start.24) | collective-permute-done | bytes 335904 | tf_op jit(solution)/shard_map/ppermute | solution.py:491
  172.6 6.7 %collective-permute-done.29 = bf16[4,216,128]{2,1,0:T(8,128)(2,1)S(1)} collective-permute-done((bf16[4,216,128]{2,1,0:T(8,128)(2,1)S(1)}, bf16[4,216,128]{2,1,0:T(8,128)(2,1)S(1)}, u32[]{:S(2)}, u32[]{:S(2)}) %collective-permute-start.29) | collective-permute-done | bytes 221216 | tf_op jit(solution)/shard_map/ppermute | solution.py:491
  179.3 9.1 %collective-permute-done.27 = bf16[1,1312,128]{2,1,0:T(8,128)(2,1)S(1)} collective-permute-done((bf16[1,1312,128]{2,1,0:T(8,128)(2,1)S(1)}, bf16[1,1312,128]{2,1,0:T(8,128)(2,1)S(1)}, u32[]{:S(2)}, u32[]{:S(2)}) %collective-permute-start.27) | collective-permute-done | bytes 335904 | tf_op jit(solution)/shard_map/ppermute | solution.py:491
  190.3 2.1 collective-permute-start.30
  193.1 3.0 %collective-permute-done.32 = bf16[2,432,128]{2,1,0:T(8,128)(2,1)S(1)} collective-permute-done((bf16[2,432,128]{2,1,0:T(8,128)(2,1)S(1)}, bf16[2,432,128]{2,1,0:T(8,128)(2,1)S(1)}, u32[]{:S(2)}, u32[]{:S(2)}) %collective-permute-start.32) | collective-permute-done | bytes 221216 | tf_op jit(solution)/shard_map/ppermute | solution.py:491
  196.1 2.9 %collective-permute-done.31 = bf16[2,432,128]{2,1,0:T(8,128)(2,1)S(1)} collective-permute-done((bf16[2,432,128]{2,1,0:T(8,128)(2,1)S(1)}, bf16[2,432,128]{2,1,0:T(8,128)(2,1)S(1)}, u32[]{:S(2)}, u32[]{:S(2)}) %collective-permute-start.31) | collective-permute-done | bytes 221216 | tf_op jit(solution)/shard_map/ppermute | solution.py:491
  199.0 2.1 collective-permute-done.30
  203.9 2.6 collective-permute-start.37
  206.6 6.9 %collective-permute-done.37 = bf16[1,448,128]{2,1,0:T(8,128)(2,1)S(1)} collective-permute-done((bf16[1,448,128]{2,1,0:T(8,128)(2,1)S(1)}, bf16[1,448,128]{2,1,0:T(8,128)(2,1)S(1)}, u32[]{:S(2)}, u32[]{:S(2)}) %collective-permute-start.37) | collective-permute-done | bytes 114720 | tf_op jit(solution)/shard_map/ppermute | solution.py:491
  221.9 14.7 %collective-permute-done.41 = bf16[1,448,128]{2,1,0:T(8,128)(2,1)S(1)} collective-permute-done((bf16[1,448,128]{2,1,0:T(8,128)(2,1)S(1)}, bf16[1,448,128]{2,1,0:T(8,128)(2,1)S(1)}, u32[]{:S(2)}, u32[]{:S(2)}) %collective-permute-start.41) | collective-permute-done | bytes 114720 | tf_op jit(solution)/shard_map/ppermute | solution.py:491
  239.2 4.8 %collective-permute-done.42 = bf16[2,448,128]{2,1,0:T(8,128)(2,1)S(1)} collective-permute-done((bf16[2,448,128]{2,1,0:T(8,128)(2,1)S(1)}, bf16[2,448,128]{2,1,0:T(8,128)(2,1)S(1)}, u32[]{:S(2)}, u32[]{:S(2)}) %collective-permute-start.42) | collective-permute-done | bytes 229408 | tf_op jit(solution)/shard_map/ppermute | solution.py:491
  247.1 6.9 %collective-permute-done.44 = bf16[4,216,128]{2,1,0:T(8,128)(2,1)S(1)} collective-permute-done((bf16[4,216,128]{2,1,0:T(8,128)(2,1)S(1)}, bf16[4,216,128]{2,1,0:T(8,128)(2,1)S(1)}, u32[]{:S(2)}, u32[]{:S(2)}) %collective-permute-start.44) | collective-permute-done | bytes 221216 | tf_op jit(solution)/shard_map/ppermute | solution.py:491
  256.1 7.4 %unpack.3 = (f32[1536,768]{1,0:T(8,128)}, f32[384,3072]{1,0:T(8,128)}, f32[384,768]{1,0:T(8,128)}, f32[384]{0:T(512)}, f32[384]{0:T(512)}, /*index=5*/f32[384]{0...) custom-call(s32[2]{0:T(128)} %pad_add_fusion.side_ref.meta_ref, ...), custom_call_target="tpu_custom_call" | custom-call | bytes 5373960 | tf_op jit(solution)/shard_map/unpack/pallas_call | solution.py:70
  266.4 3.9 %unpack.2 = (f32[384,2304]{1,0:T(8,128)}, f32[384]{0:T(512)}, f32[384]{0:T(512)}, f32[384]{0:T(512)}, f32[384]{0:T(512)}) custom-call(s32[2]{0:T(128)} %pad_add_fusion.side_ref.meta_ref, bf16[8,232,128]{2,1,0:T(8,128)(2,1)} %copy-done.5, bf16[8,232,128]{2,1,0:T(8,128)(2,1)} %copy-done.17, bf16[8,216,128]{2,1,0:T(8,128)(2,1)} %copy-done.6, ...), custom_call_target="tpu_custom_call" | custom-call | bytes 1835016 | tf_op jit(solution)/shard_map/unpack/pallas_call | solution.py:70
  (192 shorter events, 54.9 us)
Async XLA Ops:
  6.1 53.6 %collective-permute-start.3 = (bf16[384,3072]{1,0:T(8,128)(2,1)}, bf16[384,3072]{1,0:T(8,128)(2,1)}, u32[]{:S(2)}, u32[]{:S(2)}) collective-permute-start(bf16[384,3072]{1,0:T(8,128)(2,1)} %refs_2_.2), channel_id=1, source_target_pairs={{0,1},{1,0},{2,3},{3,2},{4,5},{5,4},{6,7},{7,6},{8,9},{9,8},{10,11... | collective-permute-start | bytes 7077896 | tf_op jit(solution)/shard_map/ppermute | solution.py:453
  6.5 53.2 %collective-permute-start.4 = (bf16[1536,768]{1,0:T(8,128)(2,1)}, bf16[1536,768]{1,0:T(8,128)(2,1)}, u32[]{:S(2)}, u32[]{:S(2)}) collective-permute-start(bf16[1536,768]{1,0:T(8,128)(2,1)} %refs_4_.2), channel_id=1, source_target_pairs={{0,1},{1,0},{2,3},{3,2},{4,5},{5,4},{6,7},{7,6},{8,9},{9,8},{10,11... | collective-permute-start | bytes 7077896 | tf_op jit(solution)/shard_map/ppermute | solution.py:453
  11.4 28.2 %all-to-all-start = ((bf16[16,192,128]{2,1,0:T(8,128)(2,1)}), bf16[16,192,128]{2,1,0:T(8,128)(2,1)S(1)}, u32[]{:S(2)}, u32[]{:S(2)}) async-start(bf16[16,192,128]{2,1,0:T(8,128)(2,1)} %get-tuple-element.124), calls=%async_computation | async-start | bytes 1572864 | tf_op jit(solution)/shard_map/all_to_all | solution.py:724
  19.7 31.5 %collective-permute-start.2 = (bf16[384,768]{1,0:T(8,128)(2,1)S(1)}, bf16[384,768]{1,0:T(8,128)(2,1)S(1)}, u32[]{:S(2)}, u32[]{:S(2)}) collective-permute-start(bf16[384,768]{1,0:T(8,128)(2,1)S(1)} %copy-done.15), channel_id=1, source_target_pairs={{0,1},{1,0},{2,3},{3,2},{4,5},{5,4},{6,7},{7,6},{8,9},{9,8},{10,11... | collective-permute-start | bytes 1769480 | tf_op jit(solution)/shard_map/ppermute | solution.py:453
  46.2 13.5 %all-to-all-start.1 = ((bf16[16,64,128]{2,1,0:T(8,128)(2,1)}), bf16[16,64,128]{2,1,0:T(8,128)(2,1)S(1)}, u32[]{:S(2)}, u32[]{:S(2)}) async-start(bf16[16,64,128]{2,1,0:T(8,128)(2,1)} %get-tuple-element.125.att_ref), calls=%async_computation.1 | async-start | bytes 524288 | tf_op jit(solution)/shard_map/all_to_all | solution.py:732
  72.2 14.7 %all-to-all-start.2 = ((bf16[16,64,128]{2,1,0:T(8,128)(2,1)}), bf16[16,64,128]{2,1,0:T(8,128)(2,1)S(1)}, u32[]{:S(2)}, u32[]{:S(2)}) async-start(bf16[16,64,128]{2,1,0:T(8,128)(2,1)} %get-tuple-element.147), calls=%async_computation.2 | async-start | bytes 524288 | tf_op jit(solution)/shard_map/all_to_all | solution.py:753
  86.9 33.2 %collective-permute-start.15 = (bf16[8,448,128]{2,1,0:T(8,128)(2,1)}, bf16[8,448,128]{2,1,0:T(8,128)(2,1)S(1)}, u32[]{:S(2)}, u32[]{:S(2)}) collective-permute-start(bf16[8,448,128]{2,1,0:T(8,128)(2,1)} %get-tuple-element.160), channel_id=1, source_target_pairs={{0,2},{2,0},{4,6},{6,4},{8,10},{10,8},{12,14},{14,12},{16,18},{18,... | collective-permute-start | bytes 2752520 | tf_op jit(solution)/shard_map/ppermute | solution.py:491
  88.9 25.1 %collective-permute-start.16 = (bf16[8,432,128]{2,1,0:T(8,128)(2,1)}, bf16[8,432,128]{2,1,0:T(8,128)(2,1)}, u32[]{:S(2)}, u32[]{:S(2)}) collective-permute-start(bf16[8,432,128]{2,1,0:T(8,128)(2,1)} %get-tuple-element.161), channel_id=1, source_target_pairs={{0,4},{2,6},{4,0},{6,2},{8,12},{10,14},{12,8},{14,10},{16,20},{18,... | collective-permute-start | bytes 2654216 | tf_op jit(solution)/shard_map/ppermute | solution.py:491
  90.3 29.7 %collective-permute-start.17 = (bf16[8,432,128]{2,1,0:T(8,128)(2,1)}, bf16[8,432,128]{2,1,0:T(8,128)(2,1)}, u32[]{:S(2)}, u32[]{:S(2)}) collective-permute-start(bf16[8,432,128]{2,1,0:T(8,128)(2,1)} %get-tuple-element.162), channel_id=1, source_target_pairs={{0,8},{2,10},{4,12},{6,14},{8,0},{10,2},{12,4},{14,6},{16,24},{18,... | collective-permute-start | bytes 2654216 | tf_op jit(solution)/shard_map/ppermute | solution.py:491
  101.1 36.2 %all-to-all-start.3 = ((bf16[16,192,128]{2,1,0:T(8,128)(2,1)}), bf16[16,192,128]{2,1,0:T(8,128)(2,1)S(1)}, u32[]{:S(2)}, u32[]{:S(2)}) async-start(bf16[16,192,128]{2,1,0:T(8,128)(2,1)} %attend_back.1), calls=%async_computation.3 | async-start | bytes 1572864 | tf_op jit(solution)/shard_map/all_to_all | solution.py:776
  122.2 11.8 %collective-permute-start.18 = (bf16[4,448,128]{2,1,0:T(8,128)(2,1)S(1)}, bf16[4,448,128]{2,1,0:T(8,128)(2,1)S(1)}, u32[]{:S(2)}, u32[]{:S(2)}) collective-permute-start(bf16[4,448,128]{2,1,0:T(8,128)(2,1)S(1)} %get-tuple-element.169), channel_id=1, source_target_pairs={{0,4},{2,6},{4,0},{6,2},{8,12},{10,14},{12,8},{14,10},{16,20},{18,... | collective-permute-start | bytes 1376264 | tf_op jit(solution)/shard_map/ppermute | solution.py:491
  122.3 11.7 %collective-permute-start.19 = (bf16[4,432,128]{2,1,0:T(8,128)(2,1)S(1)}, bf16[4,432,128]{2,1,0:T(8,128)(2,1)S(1)}, u32[]{:S(2)}, u32[]{:S(2)}) collective-permute-start(bf16[4,432,128]{2,1,0:T(8,128)(2,1)S(1)} %get-tuple-element.170), channel_id=1, source_target_pairs={{0,8},{2,10},{4,12},{6,14},{8,0},{10,2},{12,4},{14,6},{16,24},{18,... | collective-permute-start | bytes 1327112 | tf_op jit(solution)/shard_map/ppermute | solution.py:491
  122.4 11.6 %collective-permute-start.20 = (bf16[4,432,128]{2,1,0:T(8,128)(2,1)S(1)}, bf16[4,432,128]{2,1,0:T(8,128)(2,1)S(1)}, u32[]{:S(2)}, u32[]{:S(2)}) collective-permute-start(bf16[4,432,128]{2,1,0:T(8,128)(2,1)S(1)} %get-tuple-element.171), channel_id=1, source_target_pairs={{0,2},{2,0},{4,6},{6,4},{8,10},{10,8},{12,14},{14,12},{16,18},{18,... | collective-permute-start | bytes 1327112 | tf_op jit(solution)/shard_map/ppermute | solution.py:491
  134.1 9.4 %collective-permute-start.21 = (bf16[2,448,128]{2,1,0:T(8,128)(2,1)S(1)}, bf16[2,448,128]{2,1,0:T(8,128)(2,1)S(1)}, u32[]{:S(2)}, u32[]{:S(2)}) collective-permute-start(bf16[2,448,128]{2,1,0:T(8,128)(2,1)S(1)} %get-tuple-element.230), channel_id=1, source_target_pairs={{0,8},{2,10},{4,12},{6,14},{8,0},{10,2},{12,4},{14,6},{16,24},{18,... | collective-permute-start | bytes 688136 | tf_op jit(solution)/shard_map/ppermute | solution.py:491
  149.5 20.4 %collective-permute-start.25 = (bf16[8,232,128]{2,1,0:T(8,128)(2,1)}, bf16[8,232,128]{2,1,0:T(8,128)(2,1)S(1)}, u32[]{:S(2)}, u32[]{:S(2)}) collective-permute-start(bf16[8,232,128]{2,1,0:T(8,128)(2,1)} %get-tuple-element.180), channel_id=1, source_target_pairs={{0,2},{2,0},{4,6},{6,4},{8,10},{10,8},{12,14},{14,12},{16,18},{18,... | collective-permute-start | bytes 1425416 | tf_op jit(solution)/shard_map/ppermute | solution.py:491
  150.9 19.0 %collective-permute-start.26 = (bf16[8,216,128]{2,1,0:T(8,128)(2,1)}, bf16[8,216,128]{2,1,0:T(8,128)(2,1)S(1)}, u32[]{:S(2)}, u32[]{:S(2)}) collective-permute-start(bf16[8,216,128]{2,1,0:T(8,128)(2,1)} %get-tuple-element.181), channel_id=1, source_target_pairs={{0,4},{2,6},{4,0},{6,2},{8,12},{10,14},{12,8},{14,10},{16,20},{18,... | collective-permute-start | bytes 1327112 | tf_op jit(solution)/shard_map/ppermute | solution.py:491
  152.4 17.5 %collective-permute-start.24 = (bf16[1,1312,128]{2,1,0:T(8,128)(2,1)S(1)}, bf16[1,1312,128]{2,1,0:T(8,128)(2,1)S(1)}, u32[]{:S(2)}, u32[]{:S(2)}) collective-permute-start(bf16[1,1312,128]{2,1,0:T(8,128)(2,1)S(1)} %pad_maximum_fusion.8), channel_id=1, source_target_pairs={{0,16},{2,18},{4,20},{6,22},{8,24},{10,26},{12,28},{14,30},{16,0},... | collective-permute-start | bytes 1007624 | tf_op jit(solution)/shard_map/ppermute | solution.py:491
  171.9 16.4 %collective-permute-start.27 = (bf16[1,1312,128]{2,1,0:T(8,128)(2,1)S(1)}, bf16[1,1312,128]{2,1,0:T(8,128)(2,1)S(1)}, u32[]{:S(2)}, u32[]{:S(2)}) collective-permute-start(bf16[1,1312,128]{2,1,0:T(8,128)(2,1)S(1)} %pad_maximum_fusion.9), channel_id=1, source_target_pairs={{0,16},{2,18},{4,20},{6,22},{8,24},{10,26},{12,28},{14,30},{16,0},... | collective-permute-start | bytes 1007624 | tf_op jit(solution)/shard_map/ppermute | solution.py:491
  188.6 10.4 %collective-permute-start.33 = (bf16[2,448,128]{2,1,0:T(8,128)(2,1)S(1)}, bf16[2,448,128]{2,1,0:T(8,128)(2,1)S(1)}, u32[]{:S(2)}, u32[]{:S(2)}) collective-permute-start(bf16[2,448,128]{2,1,0:T(8,128)(2,1)S(1)} %pad_maximum_fusion.12), channel_id=1, source_target_pairs={{0,8},{2,10},{4,12},{6,14},{8,0},{10,2},{12,4},{14,6},{16,24},{18,... | collective-permute-start | bytes 688136 | tf_op jit(solution)/shard_map/ppermute | solution.py:491
  190.3 10.7 %collective-permute-start.30 = (bf16[2,448,128]{2,1,0:T(8,128)(2,1)S(1)}, bf16[2,448,128]{2,1,0:T(8,128)(2,1)S(1)}, u32[]{:S(2)}, u32[]{:S(2)}) collective-permute-start(bf16[2,448,128]{2,1,0:T(8,128)(2,1)S(1)} %pad_maximum_fusion.11), channel_id=1, source_target_pairs={{0,8},{2,10},{4,12},{6,14},{8,0},{10,2},{12,4},{14,6},{16,24},{18,... | collective-permute-start | bytes 688136 | tf_op jit(solution)/shard_map/ppermute | solution.py:491
  201.1 12.3 %collective-permute-start.36 = (bf16[4,432,128]{2,1,0:T(8,128)(2,1)S(1)}, bf16[4,432,128]{2,1,0:T(8,128)(2,1)S(1)}, u32[]{:S(2)}, u32[]{:S(2)}) collective-permute-start(bf16[4,432,128]{2,1,0:T(8,128)(2,1)S(1)} %pad_maximum_fusion.6), channel_id=1, source_target_pairs={{0,2},{2,0},{4,6},{6,4},{8,10},{10,8},{12,14},{14,12},{16,18},{18,... | collective-permute-start | bytes 1327112 | tf_op jit(solution)/shard_map/ppermute | solution.py:491
  201.8 13.5 %collective-permute-start.35 = (bf16[4,432,128]{2,1,0:T(8,128)(2,1)S(1)}, bf16[4,432,128]{2,1,0:T(8,128)(2,1)S(1)}, u32[]{:S(2)}, u32[]{:S(2)}) collective-permute-start(bf16[4,432,128]{2,1,0:T(8,128)(2,1)S(1)} %pad_maximum_fusion.5), channel_id=1, source_target_pairs={{0,8},{2,10},{4,12},{6,14},{8,0},{10,2},{12,4},{14,6},{16,24},{18,... | collective-permute-start | bytes 1327112 | tf_op jit(solution)/shard_map/ppermute | solution.py:491
  202.2 13.1 %collective-permute-start.34 = (bf16[4,448,128]{2,1,0:T(8,128)(2,1)S(1)}, bf16[4,448,128]{2,1,0:T(8,128)(2,1)S(1)}, u32[]{:S(2)}, u32[]{:S(2)}) collective-permute-start(bf16[4,448,128]{2,1,0:T(8,128)(2,1)S(1)} %pad_maximum_fusion.4), channel_id=1, source_target_pairs={{0,4},{2,6},{4,0},{6,2},{8,12},{10,14},{12,8},{14,10},{16,20},{18,... | collective-permute-start | bytes 1376264 | tf_op jit(solution)/shard_map/ppermute | solution.py:491
  203.9 9.5 %collective-permute-start.37 = (bf16[1,448,128]{2,1,0:T(8,128)(2,1)S(1)}, bf16[1,448,128]{2,1,0:T(8,128)(2,1)S(1)}, u32[]{:S(2)}, u32[]{:S(2)}) collective-permute-start(bf16[1,448,128]{2,1,0:T(8,128)(2,1)S(1)} %pad_maximum_fusion.16), channel_id=1, source_target_pairs={{0,16},{2,18},{4,20},{6,22},{8,24},{10,26},{12,28},{14,30},{16,0},... | collective-permute-start | bytes 344072 | tf_op jit(solution)/shard_map/ppermute | solution.py:491
  215.4 22.2 %collective-permute-start.40 = (bf16[8,432,128]{2,1,0:T(8,128)(2,1)S(1)}, bf16[8,432,128]{2,1,0:T(8,128)(2,1)S(1)}, u32[]{:S(2)}, u32[]{:S(2)}) collective-permute-start(bf16[8,432,128]{2,1,0:T(8,128)(2,1)S(1)} %pad_maximum_fusion.2.refs_4_), channel_id=1, source_target_pairs={{0,8},{2,10},{4,12},{6,14},{8,0},{10,2},{12,4},{14,6},{16,24},{18,... | collective-permute-start | bytes 2654216 | tf_op jit(solution)/shard_map/ppermute | solution.py:491
  216.9 20.9 %collective-permute-start.38 = (bf16[8,448,128]{2,1,0:T(8,128)(2,1)S(1)}, bf16[8,448,128]{2,1,0:T(8,128)(2,1)S(1)}, u32[]{:S(2)}, u32[]{:S(2)}) collective-permute-start(bf16[8,448,128]{2,1,0:T(8,128)(2,1)S(1)} %pad_maximum_fusion.refs_0_), channel_id=1, source_target_pairs={{0,2},{2,0},{4,6},{6,4},{8,10},{10,8},{12,14},{14,12},{16,18},{18,... | collective-permute-start | bytes 2752520 | tf_op jit(solution)/shard_map/ppermute | solution.py:491
  218.8 19.1 %collective-permute-start.39 = (bf16[8,432,128]{2,1,0:T(8,128)(2,1)S(1)}, bf16[8,432,128]{2,1,0:T(8,128)(2,1)S(1)}, u32[]{:S(2)}, u32[]{:S(2)}) collective-permute-start(bf16[8,432,128]{2,1,0:T(8,128)(2,1)S(1)} %pad_maximum_fusion.1.refs_2_), channel_id=1, source_target_pairs={{0,4},{2,6},{4,0},{6,2},{8,12},{10,14},{12,8},{14,10},{16,20},{18,... | collective-permute-start | bytes 2654216 | tf_op jit(solution)/shard_map/ppermute | solution.py:491
  220.4 16.2 %collective-permute-start.41 = (bf16[1,448,128]{2,1,0:T(8,128)(2,1)S(1)}, bf16[1,448,128]{2,1,0:T(8,128)(2,1)S(1)}, u32[]{:S(2)}, u32[]{:S(2)}) collective-permute-start(bf16[1,448,128]{2,1,0:T(8,128)(2,1)S(1)} %pad_maximum_fusion.17), channel_id=1, source_target_pairs={{0,16},{2,18},{4,20},{6,22},{8,24},{10,26},{12,28},{14,30},{16,0},... | collective-permute-start | bytes 344072 | tf_op jit(solution)/shard_map/ppermute | solution.py:491
  244.1 9.9 %collective-permute-start.43 = (bf16[4,232,128]{2,1,0:T(8,128)(2,1)S(1)}, bf16[4,232,128]{2,1,0:T(8,128)(2,1)S(1)}, u32[]{:S(2)}, u32[]{:S(2)}) collective-permute-start(bf16[4,232,128]{2,1,0:T(8,128)(2,1)S(1)} %pad_maximum_fusion.10), channel_id=1, source_target_pairs={{0,4},{2,6},{4,0},{6,2},{8,12},{10,14},{12,8},{14,10},{16,20},{18,... | collective-permute-start | bytes 712712 | tf_op jit(solution)/shard_map/ppermute | solution.py:491
  245.6 8.4 %collective-permute-start.44 = (bf16[4,216,128]{2,1,0:T(8,128)(2,1)S(1)}, bf16[4,216,128]{2,1,0:T(8,128)(2,1)S(1)}, u32[]{:S(2)}, u32[]{:S(2)}) collective-permute-start(bf16[4,216,128]{2,1,0:T(8,128)(2,1)S(1)} %pad_maximum_fusion.15), channel_id=1, source_target_pairs={{0,2},{2,0},{4,6},{6,4},{8,10},{10,8},{12,14},{14,12},{16,18},{18,... | collective-permute-start | bytes 663560 | tf_op jit(solution)/shard_map/ppermute | solution.py:491
  254.1 10.8 %collective-permute-start.45 = (bf16[8,232,128]{2,1,0:T(8,128)(2,1)S(1)}, bf16[8,232,128]{2,1,0:T(8,128)(2,1)S(1)}, u32[]{:S(2)}, u32[]{:S(2)}) collective-permute-start(bf16[8,232,128]{2,1,0:T(8,128)(2,1)S(1)} %pad_maximum_fusion.3.refs_0_), channel_id=1, source_target_pairs={{0,2},{2,0},{4,6},{6,4},{8,10},{10,8},{12,14},{14,12},{16,18},{18,... | collective-permute-start | bytes 1425416 | tf_op jit(solution)/shard_map/ppermute | solution.py:491
  255.6 9.2 %collective-permute-start.46 = (bf16[8,216,128]{2,1,0:T(8,128)(2,1)S(1)}, bf16[8,216,128]{2,1,0:T(8,128)(2,1)S(1)}, u32[]{:S(2)}, u32[]{:S(2)}) collective-permute-start(bf16[8,216,128]{2,1,0:T(8,128)(2,1)S(1)} %pad_maximum_fusion.7.refs_2_), channel_id=1, source_target_pairs={{0,4},{2,6},{4,0},{6,2},{8,12},{10,14},{12,8},{14,10},{16,20},{18,... | collective-permute-start | bytes 1327112 | tf_op jit(solution)/shard_map/ppermute | solution.py:491
  (52 other events, 407.9 us)

commit v5 on v4

--- a/solution.py
+++ b/solution.py
@@ -534,54 +534,18 @@
         return self.step == 2 * self.bits
 
 
-def advance(flows, count):
-    flows = [flow for flow in flows if not flow.over()]
-    waiting = [flow.pending() for flow in flows]
-    cames = lax.optimization_barrier(
-        [[swap_bit(part, bit, count) for part, bit in parts] for parts in waiting]
-    )
-    for flow, came in zip(flows, cames):
-        flow.accept(came)
-
-
-def pack(pairs, paired, sums, meta, index, group, count):
-    extra = sums.reshape(-1, LANES)
-    extra = jnp.pad(extra, ((0, LINES * count - extra.shape[0]), (0, 0))).astype(BF16)
-    extra = extra.reshape(count, LINES, LANES)
-    if group == 2 and count == 16:
-        args = []
-        for keep, send, right in pairs:
-            args += [keep, swap_side(send), right, swap_side(right)]
-        size = sum(keep.shape[1] * right.shape[1] for keep, _, right in pairs)
-        block = size // 3 // LANES // count
-        half = count // 2
-        tall = [block + LINES, block, block]
-        rows = pairs[0][0].shape[0]
-        parts = call(
-            functools.partial(pack_kernel, paired),
-            [((half, tall[k // 2], LANES), BF16) for k in range(6)],
-            [((2 * rows, a.shape[1]), BF16) for a in args[::2]] + [((count, block, LANES), BF16)],
-            "pack", 4 * rows * size, meta, *args, extra,
-        )
-        return Flow(parts[::2], parts[1::2], count)
-    weights = [rows_over_group(*pair) for pair in pairs]
-    return Flow(*plain_pack(weights, extra, index, count), count)
-
-
-def unpack(flow, shapes, paired, sums, meta, index, group, count):
-    if group == 2 and count == 16:
-        near_far = [part for pair in zip(flow.keeps, flow.fars) for part in pair]
-        *weights, extra = call(
-            functools.partial(unpack_kernel, paired),
-            [(s, F32) for s in shapes] + [((count, LINES, LANES), F32)],
-            [((3, r, c // 3), F32) for r, c in shapes]
-            + [pltpu.SemaphoreType.DMA((3, len(shapes)))],
-            "unpack", 0, meta, *near_far, away_outs=len(shapes),
-        )
-    else:
-        weights, extra = plain_unpack(flow.keeps, flow.fars, shapes, LINES, index, count)
-    sums = extra.reshape(-1, LANES)[: sums.size // LANES].reshape(sums.shape)
-    return weights, sums
+def send_all(flow, count):
+    return [swap_bit(part, bit, count) for part, bit in flow.pending()]
+
+
+def advance(flow, count, inner=None, steps=0):
+    cames = send_all(flow, count)
+    for _ in range(steps - 1):
+        inner.accept(lax.optimization_barrier(send_all(inner, count)))
+    both = lax.optimization_barrier((cames, send_all(inner, count) if steps else []))
+    flow.accept(both[0])
+    if steps:
+        inner.accept(both[1])
 
 
 def plain_pack(weights, extra, index, count, parts):
@@ -622,12 +586,18 @@
     return [jnp.concatenate(c, axis=1) for c in columns], extra
 
 
-def pack(pairs, paired, parts, sums, meta, index, group, count):
+def exchange(pairs, sums, group, count):
+    if group != 2 or count != 16:
+        return []
+    args = []
+    for keep, send, right in pairs:
+        args += [keep, swap_side(send), right, swap_side(right)]
+    return args + [sums[0], swap_side(sums[1])]
+
+
+def pack(pairs, sums, args, paired, parts, meta, index, group, count):
     keep_sums, send_sums = sums
-    if group == 2 and count == 16:
-        args = []
-        for keep, send, right in pairs:
-            args += [keep, swap_side(send), right, swap_side(right)]
+    if args:
         size = sum(keep.shape[1] * right.shape[1] for keep, _, right in pairs)
         block = size // parts // LANES // count
         half = count // 2
@@ -638,9 +608,9 @@
         ]
         flows = call(
             functools.partial(pack_kernel, paired, parts), outs,
-            [((2 * rows, a.shape[1]), BF16) for a in args[::2]]
+            [((2 * rows, a.shape[1]), BF16) for a in args[:-2:2]]
             + [((count, block, LANES), kind), ((count, LINES, LANES), F32)],
-            "pack", 4 * rows * size, meta, *args, keep_sums, swap_side(send_sums),
+            "pack", 4 * rows * size, meta, *args,
         )
         return Flow(flows[::2], flows[1::2], count)
     extra = sums_over_group(keep_sums, send_sums, group).reshape(-1, LANES)
@@ -753,14 +723,14 @@
     grad_here = lax.all_to_all(grad_send, "ctx", 0, 0, tiled=True)
 
     early_kinds = (False, True, True)
-    early = pack(
-        [(act_keep, act_out, cot_b), (hid_keep, hid_out, ge_b), (att_keep, att_out, gm_b)],
-        early_kinds, 3, (keep_sums, send_sums), meta, index, group, count,
-    )
+    pairs = [(act_keep, act_out, cot_b), (hid_keep, hid_out, ge_b), (att_keep, att_out, gm_b)]
+    sums = keep_sums, send_sums
+    args = exchange(pairs, sums, group, count)
+    early = pack(pairs, sums, args, early_kinds, 3, meta, index, group, count)
     early.keeps, early.sends, grad_here = lax.optimization_barrier(
         (early.keeps, early.sends, grad_here)
     )
-    advance([early], count)
+    advance(early, count)
     (dqkv_send,) = call(
         attend_back_kernel,
         [((count, three, rows), BF16)],
@@ -777,8 +747,7 @@
     early.keeps, early.sends, _ = lax.optimization_barrier(
         (early.keeps, early.sends, dqkv_send)
     )
-    advance([early], count)
-    advance([early], count)
+    advance(early, count)
     input_grad, keep_sums, send_sums, gj, hida_keep, hida_out = call(
         finish_kernel,
         [
@@ -789,18 +758,20 @@
         "finish", 6 * rows * width * width,
         meta, dqkv_here, x, grad_middle, *vec, hidden_a, *qkv,
     )
-    late = pack(
-        [(hida_keep, hida_out, gj)], (False,), 2, (keep_sums, send_sums), meta, index, group,
-        count,
-    )
+    pairs = [(hida_keep, hida_out, gj)]
+    sums = keep_sums, send_sums
+    args = exchange(pairs, sums, group, count)
+    early.keeps, early.sends, args = lax.optimization_barrier((early.keeps, early.sends, args))
+    advance(early, count)
+    late = pack(pairs, sums, args, (False,), 2, meta, index, group, count)
     while not early.over():
-        advance([early, late], count)
+        advance(early, count, late, 1 + (2 * early.bits - 1 > early.step >= 2 * early.bits - 3))
     (grad_shrink, grad_expand, grad_mix), sums = unpack(
         early, ((4 * each, width), (each, ff), (each, width)), early_kinds, 8, meta, index,
         group, count,
     )
     while not late.over():
-        advance([late], count)
+        advance(late, count)
     (grad_qkv,), late_sums = unpack(
         late, ((each, 3 * width),), (False,), 4, meta, index, group, count
     )

time: 271 us -> 265 us (0.978)
  starting transfers between devices: 60.8 us -> 56.3 us
    ppermute x32, starting transfers between devices: 36.5 us -> 32 us  [swap_bit(): return lax.ppermute(part, 'ctx', [(d, d ^ 1 << bit) for d in range(count)])]
    unnamed x66 -> x72, local copies, waits for them, and re-layouts: 6.1 us -> 5.77 us
  transfers between devices with their start and end apart: 51 -> 51, of which waited for: 23 -> 24; matrix products, arithmetic and copies ran while one was open for 2% -> 2% of each run, Pallas kernels for 14% -> 14%
where the time goes in v5:
time: 265 us
  waiting for transfers between devices  137 us (52%)
  Pallas kernels  57.5 us (22%)
  starting transfers between devices  56.3 us (21%)
  other arithmetic  6.56 us (2%)
  local copies, waits for them, and re-layouts  5.82 us (2%)
    ppermute x32, waiting for transfers between devices, swap_bit(): return lax.ppermute(part, 'ctx', [(d, d ^ 1 << bit) for d in range(count)])  103 us
    pallas_call x10, Pallas kernels, call(): pl.pallas_call(kernel, out_shape=[jax.ShapeDtypeStruct(s, d) for s, d in...  57.5 us
    ppermute x32, starting transfers between devices, swap_bit(): return lax.ppermute(part, 'ctx', [(d, d ^ 1 << bit) for d in range(count)])  32 us
    all_to_all x1, waiting for transfers between devices, body(): qkv_here = lax.all_to_all(qkv_send, 'ctx', 0, 0, tiled=True)  19.3 us
    all_to_all x1, waiting for transfers between devices, body(): att_here = lax.all_to_all(att_send, 'ctx', 0, 0, tiled=True)  8.48 us
    all_to_all x1, starting transfers between devices, body(): qkv_here = lax.all_to_all(qkv_send, 'ctx', 0, 0, tiled=True)  8.26 us
    ppermute x11, waiting for transfers between devices, swap_side(): return lax.ppermute(part, 'fsdp', SWAP)  6.33 us
    unnamed x72, local copies, waits for them, and re-layouts  5.77 us
  transfers between devices with their start and end apart: 51, of which 24 were waited for; matrix products, arithmetic and copies ran while one was open for 2% of the time, Pallas kernels for 14%

profile of v5, /device:TPU:0, one launch (start us, length us, event | category | flops | bytes accessed | tf_op | source)
XLA Modules:
  0.0 264.6 jit_solution(3020318597376110639)
XLA Ops:
  2.6 3.5 %collective-permute-done.theirs_ref = bf16[12,384]{1,0:T(8,128)(2,1)S(1)} collective-permute-done((bf16[12,384]{1,0:T(8,128)(2,1)}, bf16[12,384]{1,0:T(8,128)(2,1)S(1)}, u32[]{:S(2)}, u32[]{:S(2)}) %collective-permute-start) | collective-permute-done | bytes 9248 | tf_op jit(solution)/shard_map/ppermute | solution.py:471
  7.3 4.1 %project.1 = (bf16[128,768]{1,0:T(8,128)(2,1)}, bf16[16,192,128]{2,1,0:T(8,128)(2,1)}) custom-call(s32[2]{0:T(128)} %pad_add_fusion.side_ref.meta_ref, bf16[128,768]{1,0:T(8,128)(2,1)} %bitcast.7, bf16[12,384]{1,0:T(8,128)(2,1)} %stack.13.mine_ref, bf16[12,384]{1,0:T(8,128)(2,1)} %copy-done.22, bf16[384,2304]{1,0:T(8,128)(2,1)} %own_ref.1, ...), custom_call_target="tpu_custom_call" | custom-call | flops 452984832 | bytes 3753992 | tf_op jit(solution)/shard_map/project/pallas_call | solution.py:70
  11.4 8.3 %all-to-all-start = ((bf16[16,192,128]{2,1,0:T(8,128)(2,1)}), bf16[16,192,128]{2,1,0:T(8,128)(2,1)S(1)}, u32[]{:S(2)}, u32[]{:S(2)}) async-start(bf16[16,192,128]{2,1,0:T(8,128)(2,1)} %get-tuple-element.135), calls=%async_computation | async-start | bytes 1572864 | tf_op jit(solution)/shard_map/all_to_all | solution.py:694
  20.4 19.3 %all-to-all-done.in_ref = bf16[16,192,128]{2,1,0:T(8,128)(2,1)S(1)} async-done(((bf16[16,192,128]{2,1,0:T(8,128)(2,1)}), bf16[16,192,128]{2,1,0:T(8,128)(2,1)S(1)}, u32[]{:S(2)}, u32[]{:S(2)}) %all-to-all-start) | async-done | bytes 786464 | tf_op jit(solution)/shard_map/all_to_all | solution.py:694
  40.6 5.7 %attend.1 = (bf16[16,64,128]{2,1,0:T(8,128)(2,1)}, f32[1,2048]{1,0:T(1,128)}) custom-call(s32[16]{0:T(128)} %select_reduce_fusion.slot_ref, bf16[16,192,128]{2,1,0:T(8,128)(2,1)} %copy-done.14), custom_call_target="tpu_custom_call" | custom-call | flops 536870912 | bytes 786496 | tf_op jit(solution)/shard_map/attend/pallas_call | solution.py:70
  46.3 4.9 %all-to-all-start.1 = ((bf16[16,64,128]{2,1,0:T(8,128)(2,1)}), bf16[16,64,128]{2,1,0:T(8,128)(2,1)S(1)}, u32[]{:S(2)}, u32[]{:S(2)}) async-start(bf16[16,64,128]{2,1,0:T(8,128)(2,1)} %get-tuple-element.136.att_ref), calls=%async_computation.1 | async-start | bytes 524288 | tf_op jit(solution)/shard_map/all_to_all | solution.py:702
  51.2 8.5 %all-to-all-done.1.att_in = bf16[16,64,128]{2,1,0:T(8,128)(2,1)S(1)} async-done(((bf16[16,64,128]{2,1,0:T(8,128)(2,1)}), bf16[16,64,128]{2,1,0:T(8,128)(2,1)S(1)}, u32[]{:S(2)}, u32[]{:S(2)}) %all-to-all-start.1) | async-done | bytes 262176 | tf_op jit(solution)/shard_map/all_to_all | solution.py:702
  60.4 11.2 %middle.1 = (bf16[128,768]{1,0:T(8,128)(2,1)}, f32[128,768]{1,0:T(8,128)}, bf16[16,64,128]{2,1,0:T(8,128)(2,1)}, f32[8,384]{1,0:T(8,128)}, f32[8,384]{1,0:T(8,12...) custom-call(s32[2]{0:T(128)} %pad_add_fusion.side_ref.meta_ref, ...), custom_call_target="tpu_custom_call" | custom-call | flops 2717908992 | bytes 11487240 | tf_op jit(solution)/shard_map/middle/pallas_call | solution.py:70
  72.2 3.8 %all-to-all-start.2 = ((bf16[16,64,128]{2,1,0:T(8,128)(2,1)}), bf16[16,64,128]{2,1,0:T(8,128)(2,1)S(1)}, u32[]{:S(2)}, u32[]{:S(2)}) async-start(bf16[16,64,128]{2,1,0:T(8,128)(2,1)} %get-tuple-element.158), calls=%async_computation.2 | async-start | bytes 524288 | tf_op jit(solution)/shard_map/all_to_all | solution.py:723
  80.4 6.4 %pack.2 = (bf16[8,448,128]{2,1,0:T(8,128)(2,1)}, bf16[8,448,128]{2,1,0:T(8,128)(2,1)}, bf16[8,432,128]{2,1,0:T(8,128)(2,1)}, bf16[8,432,128]{2,1,0:T(8,128)(2,1)...) custom-call(s32[2]{0:T(128)} %pad_add_fusion.side_ref.meta_ref, ...), custom_call_target="tpu_custom_call" | custom-call | flops 1358954496 | bytes 3563528 | tf_op jit(solution)/shard_map/pack/pallas_call | solution.py:70
  86.9 2.0 collective-permute-start.12
  91.8 9.2 %attend_back.1 = bf16[16,192,128]{2,1,0:T(8,128)(2,1)} custom-call(s32[16]{0:T(128)} %select_reduce_fusion.slot_ref, bf16[16,192,128]{2,1,0:T(8,128)(2,1)} %copy-done.14, bf16[16,64,128]{2,1,0:T(8,128)(2,1)} %get-tuple-element.136.att_ref, bf16[16,64,128]{2,1,0:T(8,128)(2,1)} %copy-done.21, f32[1,2048]{1,0:T(1,128)} %get-tuple-element.160.total_ref), custom_call_target="tpu_custom_call" | custom-call | flops 1342177280 | bytes 1318976 | tf_op jit(solution)/shard_map/attend_back/pallas_call | solution.py:70
  101.0 3.9 %all-to-all-start.3 = ((bf16[16,192,128]{2,1,0:T(8,128)(2,1)}), bf16[16,192,128]{2,1,0:T(8,128)(2,1)S(1)}, u32[]{:S(2)}, u32[]{:S(2)}) async-start(bf16[16,192,128]{2,1,0:T(8,128)(2,1)} %attend_back.1), calls=%async_computation.3 | async-start | bytes 1572864 | tf_op jit(solution)/shard_map/all_to_all | solution.py:746
  104.9 9.1 %collective-permute-done.13 = bf16[8,432,128]{2,1,0:T(8,128)(2,1)} collective-permute-done((bf16[8,432,128]{2,1,0:T(8,128)(2,1)}, bf16[8,432,128]{2,1,0:T(8,128)(2,1)}, u32[]{:S(2)}, u32[]{:S(2)}) %collective-permute-start.13) | collective-permute-done | bytes 884768 | tf_op jit(solution)/shard_map/ppermute | solution.py:491
  113.9 6.1 %collective-permute-done.14 = bf16[8,432,128]{2,1,0:T(8,128)(2,1)} collective-permute-done((bf16[8,432,128]{2,1,0:T(8,128)(2,1)}, bf16[8,432,128]{2,1,0:T(8,128)(2,1)}, u32[]{:S(2)}, u32[]{:S(2)}) %collective-permute-start.14) | collective-permute-done | bytes 884768 | tf_op jit(solution)/shard_map/ppermute | solution.py:491
  120.3 1.9 add_convert_fusion.2
  122.4 11.6 %collective-permute-done.16 = bf16[4,432,128]{2,1,0:T(8,128)(2,1)S(1)} collective-permute-done((bf16[4,432,128]{2,1,0:T(8,128)(2,1)S(1)}, bf16[4,432,128]{2,1,0:T(8,128)(2,1)S(1)}, u32[]{:S(2)}, u32[]{:S(2)}) %collective-permute-start.16) | collective-permute-done | bytes 442400 | tf_op jit(solution)/shard_map/ppermute | solution.py:491
  134.9 4.8 %finish.1 = (f32[128,768]{1,0:T(8,128)}, f32[4,384]{1,0:T(4,128)}, f32[4,384]{1,0:T(4,128)}, bf16[128,2304]{1,0:T(8,128)(2,1)}, bf16[128,384]{1,0:T(8,128)(2,1)}, /*index=5*/bf16[128,384]{1,0:T(8,128)(2,1)}) custom-call(s32[2]{0:T(128)} %pad_add_fusion.side_ref.meta_ref, bf16[16,192,128]{2,1,0:T(8,128)(2,1)} %copy-done.4, bf16[128,768]{1,0:T(8,128)(2,1)} %bitcast.9, ...), custom_call_target="tpu_custom_call" | custom-call | flops 452984832 | bytes 5130248 | tf_op jit(solution)/shard_map/finish/pallas_call | solution.py:70
  144.6 3.3 %pack.3 = (bf16[8,232,128]{2,1,0:T(8,128)(2,1)}, bf16[8,232,128]{2,1,0:T(8,128)(2,1)}, bf16[8,216,128]{2,1,0:T(8,128)(2,1)}, bf16[8,216,128]{2,1,0:T(8,128)(2,1)}) custom-call(s32[2]{0:T(128)} %pad_add_fusion.side_ref.meta_ref, bf16[128,384]{1,0:T(8,128)(2,1)} %get-tuple-element.187.refs_0_, bf16[128,384]{1,0:T(8,128)(2,1)} %copy-done.29, ...), custom_call_target="tpu_custom_call" | custom-call | flops 452984832 | bytes 1388552 | tf_op jit(solution)/shard_map/pack/pallas_call | solution.py:70
  151.6 2.4 collective-permute-start.24
  154.0 6.9 %collective-permute-done.26 = bf16[8,216,128]{2,1,0:T(8,128)(2,1)S(1)} collective-permute-done((bf16[8,216,128]{2,1,0:T(8,128)(2,1)}, bf16[8,216,128]{2,1,0:T(8,128)(2,1)S(1)}, u32[]{:S(2)}, u32[]{:S(2)}) %collective-permute-start.26) | collective-permute-done | bytes 442400 | tf_op jit(solution)/shard_map/ppermute | solution.py:491
  161.0 7.2 %collective-permute-done.24 = bf16[1,1312,128]{2,1,0:T(8,128)(2,1)S(1)} collective-permute-done((bf16[1,1312,128]{2,1,0:T(8,128)(2,1)S(1)}, bf16[1,1312,128]{2,1,0:T(8,128)(2,1)S(1)}, u32[]{:S(2)}, u32[]{:S(2)}) %collective-permute-start.24) | collective-permute-done | bytes 335904 | tf_op jit(solution)/shard_map/ppermute | solution.py:491
  170.8 5.5 %collective-permute-done.29 = bf16[4,216,128]{2,1,0:T(8,128)(2,1)S(1)} collective-permute-done((bf16[4,216,128]{2,1,0:T(8,128)(2,1)S(1)}, bf16[4,216,128]{2,1,0:T(8,128)(2,1)S(1)}, u32[]{:S(2)}, u32[]{:S(2)}) %collective-permute-start.29) | collective-permute-done | bytes 221216 | tf_op jit(solution)/shard_map/ppermute | solution.py:491
  176.3 9.6 %collective-permute-done.27 = bf16[1,1312,128]{2,1,0:T(8,128)(2,1)S(1)} collective-permute-done((bf16[1,1312,128]{2,1,0:T(8,128)(2,1)S(1)}, bf16[1,1312,128]{2,1,0:T(8,128)(2,1)S(1)}, u32[]{:S(2)}, u32[]{:S(2)}) %collective-permute-start.27) | collective-permute-done | bytes 335904 | tf_op jit(solution)/shard_map/ppermute | solution.py:491
  189.0 2.1 collective-permute-start.31
  191.1 3.6 %collective-permute-done.30 = bf16[2,448,128]{2,1,0:T(8,128)(2,1)S(1)} collective-permute-done((bf16[2,448,128]{2,1,0:T(8,128)(2,1)S(1)}, bf16[2,448,128]{2,1,0:T(8,128)(2,1)S(1)}, u32[]{:S(2)}, u32[]{:S(2)}) %collective-permute-start.30) | collective-permute-done | bytes 229408 | tf_op jit(solution)/shard_map/ppermute | solution.py:491
  195.2 5.1 %collective-permute-done.31 = bf16[2,448,128]{2,1,0:T(8,128)(2,1)S(1)} collective-permute-done((bf16[2,448,128]{2,1,0:T(8,128)(2,1)S(1)}, bf16[2,448,128]{2,1,0:T(8,128)(2,1)S(1)}, u32[]{:S(2)}, u32[]{:S(2)}) %collective-permute-start.31) | collective-permute-done | bytes 229408 | tf_op jit(solution)/shard_map/ppermute | solution.py:491
  205.7 2.4 collective-permute-start.37
  208.7 13.6 %collective-permute-done.39 = bf16[2,448,128]{2,1,0:T(8,128)(2,1)S(1)} collective-permute-done((bf16[2,448,128]{2,1,0:T(8,128)(2,1)S(1)}, bf16[2,448,128]{2,1,0:T(8,128)(2,1)S(1)}, u32[]{:S(2)}, u32[]{:S(2)}) %collective-permute-start.39) | collective-permute-done | bytes 229408 | tf_op jit(solution)/shard_map/ppermute | solution.py:491
  227.1 20.8 %collective-permute-done.44 = bf16[4,216,128]{2,1,0:T(8,128)(2,1)S(1)} collective-permute-done((bf16[4,216,128]{2,1,0:T(8,128)(2,1)S(1)}, bf16[4,216,128]{2,1,0:T(8,128)(2,1)S(1)}, u32[]{:S(2)}, u32[]{:S(2)}) %collective-permute-start.44) | collective-permute-done | bytes 221216 | tf_op jit(solution)/shard_map/ppermute | solution.py:491
  250.1 7.4 %unpack.3 = (f32[1536,768]{1,0:T(8,128)}, f32[384,3072]{1,0:T(8,128)}, f32[384,768]{1,0:T(8,128)}, f32[384]{0:T(512)}, f32[384]{0:T(512)}, /*index=5*/f32[384]{0...) custom-call(s32[2]{0:T(128)} %pad_add_fusion.side_ref.meta_ref, ...), custom_call_target="tpu_custom_call" | custom-call | bytes 5373960 | tf_op jit(solution)/shard_map/unpack/pallas_call | solution.py:70
  260.4 3.9 %unpack.2 = (f32[384,2304]{1,0:T(8,128)}, f32[384]{0:T(512)}, f32[384]{0:T(512)}, f32[384]{0:T(512)}, f32[384]{0:T(512)}) custom-call(s32[2]{0:T(128)} %pad_add_fusion.side_ref.meta_ref, bf16[8,232,128]{2,1,0:T(8,128)(2,1)} %copy-done.5, bf16[8,232,128]{2,1,0:T(8,128)(2,1)} %copy-done.18, bf16[8,216,128]{2,1,0:T(8,128)(2,1)} %copy-done.6, ...), custom_call_target="tpu_custom_call" | custom-call | bytes 1835016 | tf_op jit(solution)/shard_map/unpack/pallas_call | solution.py:70
  (198 shorter events, 45.2 us)
Async XLA Ops:
  6.1 53.6 %collective-permute-start.3 = (bf16[384,3072]{1,0:T(8,128)(2,1)}, bf16[384,3072]{1,0:T(8,128)(2,1)}, u32[]{:S(2)}, u32[]{:S(2)}) collective-permute-start(bf16[384,3072]{1,0:T(8,128)(2,1)} %refs_2_.2), channel_id=1, source_target_pairs={{0,1},{1,0},{2,3},{3,2},{4,5},{5,4},{6,7},{7,6},{8,9},{9,8},{10,11... | collective-permute-start | bytes 7077896 | tf_op jit(solution)/shard_map/ppermute | solution.py:453
  6.5 53.2 %collective-permute-start.4 = (bf16[1536,768]{1,0:T(8,128)(2,1)}, bf16[1536,768]{1,0:T(8,128)(2,1)}, u32[]{:S(2)}, u32[]{:S(2)}) collective-permute-start(bf16[1536,768]{1,0:T(8,128)(2,1)} %refs_4_.2), channel_id=1, source_target_pairs={{0,1},{1,0},{2,3},{3,2},{4,5},{5,4},{6,7},{7,6},{8,9},{9,8},{10,11... | collective-permute-start | bytes 7077896 | tf_op jit(solution)/shard_map/ppermute | solution.py:453
  11.4 28.3 %all-to-all-start = ((bf16[16,192,128]{2,1,0:T(8,128)(2,1)}), bf16[16,192,128]{2,1,0:T(8,128)(2,1)S(1)}, u32[]{:S(2)}, u32[]{:S(2)}) async-start(bf16[16,192,128]{2,1,0:T(8,128)(2,1)} %get-tuple-element.135), calls=%async_computation | async-start | bytes 1572864 | tf_op jit(solution)/shard_map/all_to_all | solution.py:694
  19.7 31.5 %collective-permute-start.2 = (bf16[384,768]{1,0:T(8,128)(2,1)S(1)}, bf16[384,768]{1,0:T(8,128)(2,1)S(1)}, u32[]{:S(2)}, u32[]{:S(2)}) collective-permute-start(bf16[384,768]{1,0:T(8,128)(2,1)S(1)} %copy-done.15), channel_id=1, source_target_pairs={{0,1},{1,0},{2,3},{3,2},{4,5},{5,4},{6,7},{7,6},{8,9},{9,8},{10,11... | collective-permute-start | bytes 1769480 | tf_op jit(solution)/shard_map/ppermute | solution.py:453
  46.3 13.4 %all-to-all-start.1 = ((bf16[16,64,128]{2,1,0:T(8,128)(2,1)}), bf16[16,64,128]{2,1,0:T(8,128)(2,1)S(1)}, u32[]{:S(2)}, u32[]{:S(2)}) async-start(bf16[16,64,128]{2,1,0:T(8,128)(2,1)} %get-tuple-element.136.att_ref), calls=%async_computation.1 | async-start | bytes 524288 | tf_op jit(solution)/shard_map/all_to_all | solution.py:702
  72.2 14.7 %all-to-all-start.2 = ((bf16[16,64,128]{2,1,0:T(8,128)(2,1)}), bf16[16,64,128]{2,1,0:T(8,128)(2,1)S(1)}, u32[]{:S(2)}, u32[]{:S(2)}) async-start(bf16[16,64,128]{2,1,0:T(8,128)(2,1)} %get-tuple-element.158), calls=%async_computation.2 | async-start | bytes 524288 | tf_op jit(solution)/shard_map/all_to_all | solution.py:723
  86.9 33.2 %collective-permute-start.12 = (bf16[8,448,128]{2,1,0:T(8,128)(2,1)}, bf16[8,448,128]{2,1,0:T(8,128)(2,1)S(1)}, u32[]{:S(2)}, u32[]{:S(2)}) collective-permute-start(bf16[8,448,128]{2,1,0:T(8,128)(2,1)} %get-tuple-element.165), channel_id=1, source_target_pairs={{0,2},{2,0},{4,6},{6,4},{8,10},{10,8},{12,14},{14,12},{16,18},{18,... | collective-permute-start | bytes 2752520 | tf_op jit(solution)/shard_map/ppermute | solution.py:491
  88.8 25.1 %collective-permute-start.13 = (bf16[8,432,128]{2,1,0:T(8,128)(2,1)}, bf16[8,432,128]{2,1,0:T(8,128)(2,1)}, u32[]{:S(2)}, u32[]{:S(2)}) collective-permute-start(bf16[8,432,128]{2,1,0:T(8,128)(2,1)} %get-tuple-element.166), channel_id=1, source_target_pairs={{0,4},{2,6},{4,0},{6,2},{8,12},{10,14},{12,8},{14,10},{16,20},{18,... | collective-permute-start | bytes 2654216 | tf_op jit(solution)/shard_map/ppermute | solution.py:491
  90.3 29.7 %collective-permute-start.14 = (bf16[8,432,128]{2,1,0:T(8,128)(2,1)}, bf16[8,432,128]{2,1,0:T(8,128)(2,1)}, u32[]{:S(2)}, u32[]{:S(2)}) collective-permute-start(bf16[8,432,128]{2,1,0:T(8,128)(2,1)} %get-tuple-element.167), channel_id=1, source_target_pairs={{0,8},{2,10},{4,12},{6,14},{8,0},{10,2},{12,4},{14,6},{16,24},{18,... | collective-permute-start | bytes 2654216 | tf_op jit(solution)/shard_map/ppermute | solution.py:491
  101.0 33.0 %all-to-all-start.3 = ((bf16[16,192,128]{2,1,0:T(8,128)(2,1)}), bf16[16,192,128]{2,1,0:T(8,128)(2,1)S(1)}, u32[]{:S(2)}, u32[]{:S(2)}) async-start(bf16[16,192,128]{2,1,0:T(8,128)(2,1)} %attend_back.1), calls=%async_computation.3 | async-start | bytes 1572864 | tf_op jit(solution)/shard_map/all_to_all | solution.py:746
  122.2 11.8 %collective-permute-start.15 = (bf16[4,448,128]{2,1,0:T(8,128)(2,1)S(1)}, bf16[4,448,128]{2,1,0:T(8,128)(2,1)S(1)}, u32[]{:S(2)}, u32[]{:S(2)}) collective-permute-start(bf16[4,448,128]{2,1,0:T(8,128)(2,1)S(1)} %get-tuple-element.174), channel_id=1, source_target_pairs={{0,4},{2,6},{4,0},{6,2},{8,12},{10,14},{12,8},{14,10},{16,20},{18,... | collective-permute-start | bytes 1376264 | tf_op jit(solution)/shard_map/ppermute | solution.py:491
  122.2 11.7 %collective-permute-start.16 = (bf16[4,432,128]{2,1,0:T(8,128)(2,1)S(1)}, bf16[4,432,128]{2,1,0:T(8,128)(2,1)S(1)}, u32[]{:S(2)}, u32[]{:S(2)}) collective-permute-start(bf16[4,432,128]{2,1,0:T(8,128)(2,1)S(1)} %get-tuple-element.175), channel_id=1, source_target_pairs={{0,8},{2,10},{4,12},{6,14},{8,0},{10,2},{12,4},{14,6},{16,24},{18,... | collective-permute-start | bytes 1327112 | tf_op jit(solution)/shard_map/ppermute | solution.py:491
  122.3 11.6 %collective-permute-start.17 = (bf16[4,432,128]{2,1,0:T(8,128)(2,1)S(1)}, bf16[4,432,128]{2,1,0:T(8,128)(2,1)S(1)}, u32[]{:S(2)}, u32[]{:S(2)}) collective-permute-start(bf16[4,432,128]{2,1,0:T(8,128)(2,1)S(1)} %get-tuple-element.176), channel_id=1, source_target_pairs={{0,2},{2,0},{4,6},{6,4},{8,10},{10,8},{12,14},{14,12},{16,18},{18,... | collective-permute-start | bytes 1327112 | tf_op jit(solution)/shard_map/ppermute | solution.py:491
  141.9 9.5 %collective-permute-start.21 = (bf16[2,448,128]{2,1,0:T(8,128)(2,1)S(1)}, bf16[2,448,128]{2,1,0:T(8,128)(2,1)S(1)}, u32[]{:S(2)}, u32[]{:S(2)}) collective-permute-start(bf16[2,448,128]{2,1,0:T(8,128)(2,1)S(1)} %get-tuple-element.195), channel_id=1, source_target_pairs={{0,8},{2,10},{4,12},{6,14},{8,0},{10,2},{12,4},{14,6},{16,24},{18,... | collective-permute-start | bytes 688136 | tf_op jit(solution)/shard_map/ppermute | solution.py:491
  147.9 13.1 %collective-permute-start.25 = (bf16[8,232,128]{2,1,0:T(8,128)(2,1)}, bf16[8,232,128]{2,1,0:T(8,128)(2,1)S(1)}, u32[]{:S(2)}, u32[]{:S(2)}) collective-permute-start(bf16[8,232,128]{2,1,0:T(8,128)(2,1)} %get-tuple-element.203), channel_id=1, source_target_pairs={{0,2},{2,0},{4,6},{6,4},{8,10},{10,8},{12,14},{14,12},{16,18},{18,... | collective-permute-start | bytes 1425416 | tf_op jit(solution)/shard_map/ppermute | solution.py:491
  149.4 11.5 %collective-permute-start.26 = (bf16[8,216,128]{2,1,0:T(8,128)(2,1)}, bf16[8,216,128]{2,1,0:T(8,128)(2,1)S(1)}, u32[]{:S(2)}, u32[]{:S(2)}) collective-permute-start(bf16[8,216,128]{2,1,0:T(8,128)(2,1)} %get-tuple-element.204), channel_id=1, source_target_pairs={{0,4},{2,6},{4,0},{6,2},{8,12},{10,14},{12,8},{14,10},{16,20},{18,... | collective-permute-start | bytes 1327112 | tf_op jit(solution)/shard_map/ppermute | solution.py:491
  151.6 16.6 %collective-permute-start.24 = (bf16[1,1312,128]{2,1,0:T(8,128)(2,1)S(1)}, bf16[1,1312,128]{2,1,0:T(8,128)(2,1)S(1)}, u32[]{:S(2)}, u32[]{:S(2)}) collective-permute-start(bf16[1,1312,128]{2,1,0:T(8,128)(2,1)S(1)} %pad_maximum_fusion.8), channel_id=1, source_target_pairs={{0,16},{2,18},{4,20},{6,22},{8,24},{10,26},{12,28},{14,30},{16,0},... | collective-permute-start | bytes 1007624 | tf_op jit(solution)/shard_map/ppermute | solution.py:491
  169.2 16.8 %collective-permute-start.27 = (bf16[1,1312,128]{2,1,0:T(8,128)(2,1)S(1)}, bf16[1,1312,128]{2,1,0:T(8,128)(2,1)S(1)}, u32[]{:S(2)}, u32[]{:S(2)}) collective-permute-start(bf16[1,1312,128]{2,1,0:T(8,128)(2,1)S(1)} %pad_maximum_fusion.9), channel_id=1, source_target_pairs={{0,16},{2,18},{4,20},{6,22},{8,24},{10,26},{12,28},{14,30},{16,0},... | collective-permute-start | bytes 1007624 | tf_op jit(solution)/shard_map/ppermute | solution.py:491
  186.2 8.5 %collective-permute-start.30 = (bf16[2,448,128]{2,1,0:T(8,128)(2,1)S(1)}, bf16[2,448,128]{2,1,0:T(8,128)(2,1)S(1)}, u32[]{:S(2)}, u32[]{:S(2)}) collective-permute-start(bf16[2,448,128]{2,1,0:T(8,128)(2,1)S(1)} %pad_maximum_fusion.11), channel_id=1, source_target_pairs={{0,8},{2,10},{4,12},{6,14},{8,0},{10,2},{12,4},{14,6},{16,24},{18,... | collective-permute-start | bytes 688136 | tf_op jit(solution)/shard_map/ppermute | solution.py:491
  186.3 8.9 %collective-permute-start.33 = (bf16[2,432,128]{2,1,0:T(8,128)(2,1)S(1)}, bf16[2,432,128]{2,1,0:T(8,128)(2,1)S(1)}, u32[]{:S(2)}, u32[]{:S(2)}) collective-permute-start(bf16[2,432,128]{2,1,0:T(8,128)(2,1)S(1)} %pad_maximum_fusion.14), channel_id=1, source_target_pairs={{0,4},{2,6},{4,0},{6,2},{8,12},{10,14},{12,8},{14,10},{16,20},{18,... | collective-permute-start | bytes 663560 | tf_op jit(solution)/shard_map/ppermute | solution.py:491
  189.0 11.3 %collective-permute-start.31 = (bf16[2,448,128]{2,1,0:T(8,128)(2,1)S(1)}, bf16[2,448,128]{2,1,0:T(8,128)(2,1)S(1)}, u32[]{:S(2)}, u32[]{:S(2)}) collective-permute-start(bf16[2,448,128]{2,1,0:T(8,128)(2,1)S(1)} %pad_maximum_fusion.12), channel_id=1, source_target_pairs={{0,8},{2,10},{4,12},{6,14},{8,0},{10,2},{12,4},{14,6},{16,24},{18,... | collective-permute-start | bytes 688136 | tf_op jit(solution)/shard_map/ppermute | solution.py:491
  202.6 19.6 %collective-permute-start.38 = (bf16[4,432,128]{2,1,0:T(8,128)(2,1)S(1)}, bf16[4,432,128]{2,1,0:T(8,128)(2,1)S(1)}, u32[]{:S(2)}, u32[]{:S(2)}) collective-permute-start(bf16[4,432,128]{2,1,0:T(8,128)(2,1)S(1)} %pad_maximum_fusion.6), channel_id=1, source_target_pairs={{0,2},{2,0},{4,6},{6,4},{8,10},{10,8},{12,14},{14,12},{16,18},{18,... | collective-permute-start | bytes 1327112 | tf_op jit(solution)/shard_map/ppermute | solution.py:491
  204.1 18.2 %collective-permute-start.36 = (bf16[4,448,128]{2,1,0:T(8,128)(2,1)S(1)}, bf16[4,448,128]{2,1,0:T(8,128)(2,1)S(1)}, u32[]{:S(2)}, u32[]{:S(2)}) collective-permute-start(bf16[4,448,128]{2,1,0:T(8,128)(2,1)S(1)} %pad_maximum_fusion.4), channel_id=1, source_target_pairs={{0,4},{2,6},{4,0},{6,2},{8,12},{10,14},{12,8},{14,10},{16,20},{18,... | collective-permute-start | bytes 1376264 | tf_op jit(solution)/shard_map/ppermute | solution.py:491
  205.7 16.6 %collective-permute-start.37 = (bf16[4,432,128]{2,1,0:T(8,128)(2,1)S(1)}, bf16[4,432,128]{2,1,0:T(8,128)(2,1)S(1)}, u32[]{:S(2)}, u32[]{:S(2)}) collective-permute-start(bf16[4,432,128]{2,1,0:T(8,128)(2,1)S(1)} %pad_maximum_fusion.5), channel_id=1, source_target_pairs={{0,8},{2,10},{4,12},{6,14},{8,0},{10,2},{12,4},{14,6},{16,24},{18,... | collective-permute-start | bytes 1327112 | tf_op jit(solution)/shard_map/ppermute | solution.py:491
  208.6 13.6 %collective-permute-start.39 = (bf16[2,448,128]{2,1,0:T(8,128)(2,1)S(1)}, bf16[2,448,128]{2,1,0:T(8,128)(2,1)S(1)}, u32[]{:S(2)}, u32[]{:S(2)}) collective-permute-start(bf16[2,448,128]{2,1,0:T(8,128)(2,1)S(1)} %maximum_maximum_fusion), channel_id=1, source_target_pairs={{0,8},{2,10},{4,12},{6,14},{8,0},{10,2},{12,4},{14,6},{16,24},{18,... | collective-permute-start | bytes 688136 | tf_op jit(solution)/shard_map/ppermute | solution.py:491
  222.4 26.2 %collective-permute-start.42 = (bf16[8,432,128]{2,1,0:T(8,128)(2,1)S(1)}, bf16[8,432,128]{2,1,0:T(8,128)(2,1)S(1)}, u32[]{:S(2)}, u32[]{:S(2)}) collective-permute-start(bf16[8,432,128]{2,1,0:T(8,128)(2,1)S(1)} %pad_maximum_fusion.2.refs_4_), channel_id=1, source_target_pairs={{0,8},{2,10},{4,12},{6,14},{8,0},{10,2},{12,4},{14,6},{16,24},{18,... | collective-permute-start | bytes 2654216 | tf_op jit(solution)/shard_map/ppermute | solution.py:491
  222.6 26.0 %collective-permute-start.40 = (bf16[8,448,128]{2,1,0:T(8,128)(2,1)S(1)}, bf16[8,448,128]{2,1,0:T(8,128)(2,1)S(1)}, u32[]{:S(2)}, u32[]{:S(2)}) collective-permute-start(bf16[8,448,128]{2,1,0:T(8,128)(2,1)S(1)} %pad_maximum_fusion.refs_0_), channel_id=1, source_target_pairs={{0,2},{2,0},{4,6},{6,4},{8,10},{10,8},{12,14},{14,12},{16,18},{18,... | collective-permute-start | bytes 2752520 | tf_op jit(solution)/shard_map/ppermute | solution.py:491
  223.7 24.9 %collective-permute-start.41 = (bf16[8,432,128]{2,1,0:T(8,128)(2,1)S(1)}, bf16[8,432,128]{2,1,0:T(8,128)(2,1)S(1)}, u32[]{:S(2)}, u32[]{:S(2)}) collective-permute-start(bf16[8,432,128]{2,1,0:T(8,128)(2,1)S(1)} %pad_maximum_fusion.1.refs_2_), channel_id=1, source_target_pairs={{0,4},{2,6},{4,0},{6,2},{8,12},{10,14},{12,8},{14,10},{16,20},{18,... | collective-permute-start | bytes 2654216 | tf_op jit(solution)/shard_map/ppermute | solution.py:491
  224.6 24.0 %collective-permute-start.43 = (bf16[4,232,128]{2,1,0:T(8,128)(2,1)S(1)}, bf16[4,232,128]{2,1,0:T(8,128)(2,1)S(1)}, u32[]{:S(2)}, u32[]{:S(2)}) collective-permute-start(bf16[4,232,128]{2,1,0:T(8,128)(2,1)S(1)} %pad_maximum_fusion.10), channel_id=1, source_target_pairs={{0,4},{2,6},{4,0},{6,2},{8,12},{10,14},{12,8},{14,10},{16,20},{18,... | collective-permute-start | bytes 712712 | tf_op jit(solution)/shard_map/ppermute | solution.py:491
  226.0 22.0 %collective-permute-start.44 = (bf16[4,216,128]{2,1,0:T(8,128)(2,1)S(1)}, bf16[4,216,128]{2,1,0:T(8,128)(2,1)S(1)}, u32[]{:S(2)}, u32[]{:S(2)}) collective-permute-start(bf16[4,216,128]{2,1,0:T(8,128)(2,1)S(1)} %pad_maximum_fusion.15), channel_id=1, source_target_pairs={{0,2},{2,0},{4,6},{6,4},{8,10},{10,8},{12,14},{14,12},{16,18},{18,... | collective-permute-start | bytes 663560 | tf_op jit(solution)/shard_map/ppermute | solution.py:491
  248.7 10.2 %collective-permute-start.45 = (bf16[8,232,128]{2,1,0:T(8,128)(2,1)S(1)}, bf16[8,232,128]{2,1,0:T(8,128)(2,1)S(1)}, u32[]{:S(2)}, u32[]{:S(2)}) collective-permute-start(bf16[8,232,128]{2,1,0:T(8,128)(2,1)S(1)} %pad_maximum_fusion.3.refs_0_), channel_id=1, source_target_pairs={{0,2},{2,0},{4,6},{6,4},{8,10},{10,8},{12,14},{14,12},{16,18},{18,... | collective-permute-start | bytes 1425416 | tf_op jit(solution)/shard_map/ppermute | solution.py:491
  249.7 9.2 %collective-permute-start.46 = (bf16[8,216,128]{2,1,0:T(8,128)(2,1)S(1)}, bf16[8,216,128]{2,1,0:T(8,128)(2,1)S(1)}, u32[]{:S(2)}, u32[]{:S(2)}) collective-permute-start(bf16[8,216,128]{2,1,0:T(8,128)(2,1)S(1)} %pad_maximum_fusion.7.refs_2_), channel_id=1, source_target_pairs={{0,4},{2,6},{4,0},{6,2},{8,12},{10,14},{12,8},{14,10},{16,20},{18,... | collective-permute-start | bytes 1327112 | tf_op jit(solution)/shard_map/ppermute | solution.py:491
  (55 other events, 326.1 us)

commit v6 on v5

--- a/solution.py
+++ b/solution.py
@@ -61,7 +61,7 @@
     return own, other
 
 
-def call(kernel, outs, scratch, name, flops, *args, smem=1, away=0, away_outs=0):
+def call(kernel, outs, scratch, name, flops, *args, smem=1, away=0, away_outs=0, limit=56):
     vmem = pl.BlockSpec(memory_space=pltpu.VMEM)
     anywhere = pl.BlockSpec(memory_space=pl.ANY)
     specs = [pl.BlockSpec(memory_space=pltpu.SMEM)] * smem
@@ -73,7 +73,7 @@
         in_specs=specs,
         out_specs=[anywhere] * away_outs + [vmem] * (len(outs) - away_outs),
         scratch_shapes=[pltpu.VMEM(*s) if isinstance(s, tuple) else s for s in scratch],
-        compiler_params=pltpu.CompilerParams(vmem_limit_bytes=56 * MIB),
+        compiler_params=pltpu.CompilerParams(vmem_limit_bytes=limit * MIB),
         cost_estimate=pl.CostEstimate(flops=flops, bytes_accessed=moved, transcendentals=0),
         name=name,
     )(*args)
@@ -426,11 +426,11 @@
             )
             copy.start()
             copies.append(copy)
-    each = lines[0].shape[0] // LANES
-    for q in range(len(lines) * each):
-        lines[q // each][q % each * LANES : (q % each + 1) * LANES] = extra[
-            q // LINES, q % LINES, :
-        ]
+    q = 0
+    for line in lines:
+        for start in range(0, line.shape[0], LANES):
+            line[start : start + LANES] = extra[q // LINES, q % LINES, :]
+            q += 1
     for copy in copies:
         copy.wait()
 
@@ -627,14 +627,16 @@
         near_far = [part for pair in zip(flow.keeps, flow.fars) for part in pair]
         outs = call(
             functools.partial(unpack_kernel, paired, parts),
-            [(s, F32) for s in shapes] + [((each,), F32)] * vectors,
+            [(s, F32) for s in shapes] + [((n * each,), F32) for n in vectors],
             [((parts, r, c // parts), F32) for r, c in shapes]
             + [((count, LINES, LANES), F32), pltpu.SemaphoreType.DMA((parts, len(shapes)))],
-            "unpack", 0, meta, *near_far, away_outs=len(shapes),
+            "unpack", 0, meta, *near_far, away_outs=len(shapes), limit=24,
         )
         return outs[: len(shapes)], outs[len(shapes) :]
     weights, extra = plain_unpack(flow.keeps, flow.fars, shapes, index, count, parts)
-    return weights, list(extra.reshape(-1)[: vectors * each].reshape(vectors, each))
+    ends = [sum(vectors[: k + 1]) * each for k in range(len(vectors))]
+    flat = extra.reshape(-1)
+    return weights, [flat[end - n * each : end] for end, n in zip(ends, vectors)]
 
 
 def body(
@@ -667,7 +669,6 @@
         (mine,) = call(
             stack_kernel, [((12, each), BF16)], [], "stack", 0, *vectors, expand_bias, smem=0
         )
-        mine, qkv_weight = lax.optimization_barrier((mine, qkv_weight))
         vec = mine, swap_side(mine)
     else:
         lines = lax.all_gather(jnp.stack(vectors), "fsdp", axis=1, tiled=True)
@@ -697,7 +698,7 @@
         [((count, HD, rows), BF16), ((1, length), F32)],
         [((HD, length), BF16), ((length, HD), BF16), ((HD, length), BF16), ((HD, length), BF16)],
         "attend", 2 * length * length * HD,
-        slots, qkv_here,
+        slots, qkv_here, limit=32,
     )
     att_here = lax.all_to_all(att_send, "ctx", 0, 0, tiled=True)
     (
@@ -741,7 +742,7 @@
             ((HD, length), F32),
         ],
         "attend_back", 5 * length * length * HD,
-        slots, qkv_here, att_send, grad_here, log_total,
+        slots, qkv_here, att_send, grad_here, log_total, limit=32,
     )
     dqkv_here = lax.all_to_all(dqkv_send, "ctx", 0, 0, tiled=True)
     early.keeps, early.sends, _ = lax.optimization_barrier(
@@ -767,17 +768,17 @@
     while not early.over():
         advance(early, count, late, 1 + (2 * early.bits - 1 > early.step >= 2 * early.bits - 3))
     (grad_shrink, grad_expand, grad_mix), sums = unpack(
-        early, ((4 * each, width), (each, ff), (each, width)), early_kinds, 8, meta, index,
+        early, ((4 * each, width), (each, ff), (each, width)), early_kinds, (1, 1, 1, 1, 4), meta, index,
         group, count,
     )
     while not late.over():
         advance(late, count)
     (grad_qkv,), late_sums = unpack(
-        late, ((each, 3 * width),), (False,), 4, meta, index, group, count
+        late, ((each, 3 * width),), (False,), (1,) * 4, meta, index, group, count
     )
     return (
         result[None], input_grad[None], late_sums[0], late_sums[1], grad_qkv, late_sums[2],
-        late_sums[3], grad_mix, sums[0], sums[1], sums[2], grad_expand, jnp.concatenate(sums[4:8]),
+        late_sums[3], grad_mix, sums[0], sums[1], sums[2], grad_expand, sums[4],
         grad_shrink, sums[3],
     )
 

time: 265 us -> 260 us (0.981)
  Pallas kernels: 57.5 us -> 54 us
    pallas_call x10, Pallas kernels: 57.5 us -> 54 us  [call(): pl.pallas_call(kernel, out_shape=[jax.ShapeDtypeStruct(s, d) for s, d in...]
    ppermute x32, waiting for transfers between devices: 103 us -> 106 us  [swap_bit(): return lax.ppermute(part, 'ctx', [(d, d ^ 1 << bit) for d in range(count)])]
    unnamed x72 -> x50, local copies, waits for them, and re-layouts: 5.77 us -> 3.36 us
  transfers between devices with their start and end apart: 51 -> 51, of which waited for: 24 -> 26; matrix products, arithmetic and copies ran while one was open for 2% -> 2% of each run, Pallas kernels for 14% -> 14%
where the time goes in v6:
time: 260 us; the launch traced here: 259 us
  waiting for transfers between devices  139 us (53%)
  starting transfers between devices  56.5 us (22%)
  Pallas kernels  54 us (21%)
  other arithmetic  4.67 us (2%)
  local copies, waits for them, and re-layouts  3.42 us (1%)
    ppermute x32, waiting for transfers between devices, swap_bit(): return lax.ppermute(part, 'ctx', [(d, d ^ 1 << bit) for d in range(count)])  106 us
    pallas_call x10, Pallas kernels, call(): pl.pallas_call(kernel, out_shape=[jax.ShapeDtypeStruct(s, d) for s, d in...  54 us
    ppermute x32, starting transfers between devices, swap_bit(): return lax.ppermute(part, 'ctx', [(d, d ^ 1 << bit) for d in range(count)])  32.1 us
    all_to_all x1, waiting for transfers between devices, body(): qkv_here = lax.all_to_all(qkv_send, 'ctx', 0, 0, tiled=True)  19.8 us
    all_to_all x1, waiting for transfers between devices, body(): att_here = lax.all_to_all(att_send, 'ctx', 0, 0, tiled=True)  8.48 us
    all_to_all x1, starting transfers between devices, body(): qkv_here = lax.all_to_all(qkv_send, 'ctx', 0, 0, tiled=True)  8.23 us
  transfers between devices with their start and end apart: 51, of which 26 were waited for; matrix products, arithmetic and copies ran while one was open for 2% of the time, Pallas kernels for 14%

profile of v6, /device:TPU:0, one launch (start us, length us, event | category | flops | bytes accessed | tf_op | source)
XLA Modules:
  0.0 259.3 jit_solution(8096126001504354699)
XLA Ops:
  2.7 2.1 collective-permute-done.theirs_ref
  5.9 4.1 %project.1 = (bf16[128,768]{1,0:T(8,128)(2,1)}, bf16[16,192,128]{2,1,0:T(8,128)(2,1)}) custom-call(s32[2]{0:T(128)} %pad_add_fusion.side_ref.meta_ref, bf16[128,768]{1,0:T(8,128)(2,1)} %bitcast.7, bf16[12,384]{1,0:T(8,128)(2,1)} %stack.13.mine_ref, bf16[12,384]{1,0:T(8,128)(2,1)} %copy-done.11, bf16[384,2304]{1,0:T(8,128)(2,1)} %own_ref.1, ...), custom_call_target="tpu_custom_call" | custom-call | flops 452984832 | bytes 3753992 | tf_op jit(solution)/shard_map/project/pallas_call | solution.py:70
  10.1 8.2 %all-to-all-start = ((bf16[16,192,128]{2,1,0:T(8,128)(2,1)}), bf16[16,192,128]{2,1,0:T(8,128)(2,1)S(1)}, u32[]{:S(2)}, u32[]{:S(2)}) async-start(bf16[16,192,128]{2,1,0:T(8,128)(2,1)} %get-tuple-element.128), calls=%async_computation | async-start | bytes 1572864 | tf_op jit(solution)/shard_map/all_to_all | solution.py:695
  18.5 19.8 %all-to-all-done.in_ref = bf16[16,192,128]{2,1,0:T(8,128)(2,1)S(1)} async-done(((bf16[16,192,128]{2,1,0:T(8,128)(2,1)}), bf16[16,192,128]{2,1,0:T(8,128)(2,1)S(1)}, u32[]{:S(2)}, u32[]{:S(2)}) %all-to-all-start) | async-done | bytes 786464 | tf_op jit(solution)/shard_map/all_to_all | solution.py:695
  38.3 5.3 %attend.1 = (bf16[16,64,128]{2,1,0:T(8,128)(2,1)}, f32[1,2048]{1,0:T(1,128)S(1)}) custom-call(s32[16]{0:T(128)S(1)} %select_reduce_fusion.slot_ref, bf16[16,192,128]{2,1,0:T(8,128)(2,1)S(1)} %all-to-all-done.in_ref), custom_call_target="tpu_custom_call" | custom-call | flops 536870912 | bytes 786496 | tf_op jit(solution)/shard_map/attend/pallas_call | solution.py:70
  43.6 4.9 %all-to-all-start.1 = ((bf16[16,64,128]{2,1,0:T(8,128)(2,1)}), bf16[16,64,128]{2,1,0:T(8,128)(2,1)S(1)}, u32[]{:S(2)}, u32[]{:S(2)}) async-start(bf16[16,64,128]{2,1,0:T(8,128)(2,1)} %get-tuple-element.129.att_ref), calls=%async_computation.1 | async-start | bytes 524288 | tf_op jit(solution)/shard_map/all_to_all | solution.py:703
  48.6 8.5 %all-to-all-done.1.att_in = bf16[16,64,128]{2,1,0:T(8,128)(2,1)S(1)} async-done(((bf16[16,64,128]{2,1,0:T(8,128)(2,1)}), bf16[16,64,128]{2,1,0:T(8,128)(2,1)S(1)}, u32[]{:S(2)}, u32[]{:S(2)}) %all-to-all-start.1) | async-done | bytes 262176 | tf_op jit(solution)/shard_map/all_to_all | solution.py:703
  57.8 11.2 %middle.1 = (bf16[128,768]{1,0:T(8,128)(2,1)}, f32[128,768]{1,0:T(8,128)}, bf16[16,64,128]{2,1,0:T(8,128)(2,1)}, f32[8,384]{1,0:T(8,128)}, f32[8,384]{1,0:T(8,12...) custom-call(s32[2]{0:T(128)} %pad_add_fusion.side_ref.meta_ref, ...), custom_call_target="tpu_custom_call" | custom-call | flops 2717908992 | bytes 11487240 | tf_op jit(solution)/shard_map/middle/pallas_call | solution.py:70
  69.5 3.8 %all-to-all-start.2 = ((bf16[16,64,128]{2,1,0:T(8,128)(2,1)}), bf16[16,64,128]{2,1,0:T(8,128)(2,1)S(1)}, u32[]{:S(2)}, u32[]{:S(2)}) async-start(bf16[16,64,128]{2,1,0:T(8,128)(2,1)} %get-tuple-element.151), calls=%async_computation.2 | async-start | bytes 524288 | tf_op jit(solution)/shard_map/all_to_all | solution.py:724
  77.8 6.4 %pack.2 = (bf16[8,448,128]{2,1,0:T(8,128)(2,1)}, bf16[8,448,128]{2,1,0:T(8,128)(2,1)}, bf16[8,432,128]{2,1,0:T(8,128)(2,1)}, bf16[8,432,128]{2,1,0:T(8,128)(2,1)...) custom-call(s32[2]{0:T(128)} %pad_add_fusion.side_ref.meta_ref, ...), custom_call_target="tpu_custom_call" | custom-call | flops 1358954496 | bytes 3563528 | tf_op jit(solution)/shard_map/pack/pallas_call | solution.py:70
  84.2 2.0 collective-permute-start.12
  89.1 8.9 %attend_back.1 = bf16[16,192,128]{2,1,0:T(8,128)(2,1)} custom-call(s32[16]{0:T(128)S(1)} %select_reduce_fusion.slot_ref, bf16[16,192,128]{2,1,0:T(8,128)(2,1)S(1)} %all-to-all-done.in_ref, bf16[16,64,128]{2,1,0:T(8,128)(2,1)} %get-tuple-element.129.att_ref, bf16[16,64,128]{2,1,0:T(8,128)(2,1)S(1)} %all-to-all-done.2.grad_ref, ...), custom_call_target="tpu_custom_call" | custom-call | flops 1342177280 | bytes 1318976 | tf_op jit(solution)/shard_map/attend_back/pallas_call | solution.py:70
  98.1 3.9 %all-to-all-start.3 = ((bf16[16,192,128]{2,1,0:T(8,128)(2,1)}), bf16[16,192,128]{2,1,0:T(8,128)(2,1)S(1)}, u32[]{:S(2)}, u32[]{:S(2)}) async-start(bf16[16,192,128]{2,1,0:T(8,128)(2,1)} %attend_back.1), calls=%async_computation.3 | async-start | bytes 1572864 | tf_op jit(solution)/shard_map/all_to_all | solution.py:747
  102.0 9.3 %collective-permute-done.13 = bf16[8,432,128]{2,1,0:T(8,128)(2,1)} collective-permute-done((bf16[8,432,128]{2,1,0:T(8,128)(2,1)}, bf16[8,432,128]{2,1,0:T(8,128)(2,1)}, u32[]{:S(2)}, u32[]{:S(2)}) %collective-permute-start.13) | collective-permute-done | bytes 884768 | tf_op jit(solution)/shard_map/ppermute | solution.py:491
  111.3 6.1 %collective-permute-done.14 = bf16[8,432,128]{2,1,0:T(8,128)(2,1)} collective-permute-done((bf16[8,432,128]{2,1,0:T(8,128)(2,1)}, bf16[8,432,128]{2,1,0:T(8,128)(2,1)}, u32[]{:S(2)}, u32[]{:S(2)}) %collective-permute-start.14) | collective-permute-done | bytes 884768 | tf_op jit(solution)/shard_map/ppermute | solution.py:491
  119.8 11.6 %collective-permute-done.16 = bf16[4,432,128]{2,1,0:T(8,128)(2,1)S(1)} collective-permute-done((bf16[4,432,128]{2,1,0:T(8,128)(2,1)S(1)}, bf16[4,432,128]{2,1,0:T(8,128)(2,1)S(1)}, u32[]{:S(2)}, u32[]{:S(2)}) %collective-permute-start.16) | collective-permute-done | bytes 442400 | tf_op jit(solution)/shard_map/ppermute | solution.py:491
  132.2 4.8 %finish.1 = (f32[128,768]{1,0:T(8,128)}, f32[4,384]{1,0:T(4,128)}, f32[4,384]{1,0:T(4,128)}, bf16[128,2304]{1,0:T(8,128)(2,1)}, bf16[128,384]{1,0:T(8,128)(2,1)}, /*index=5*/bf16[128,384]{1,0:T(8,128)(2,1)}) custom-call(s32[2]{0:T(128)} %pad_add_fusion.side_ref.meta_ref, bf16[16,192,128]{2,1,0:T(8,128)(2,1)} %copy-done.2, bf16[128,768]{1,0:T(8,128)(2,1)} %bitcast.9, ...), custom_call_target="tpu_custom_call" | custom-call | flops 452984832 | bytes 5130248 | tf_op jit(solution)/shard_map/finish/pallas_call | solution.py:70
  142.0 3.3 %pack.3 = (bf16[8,232,128]{2,1,0:T(8,128)(2,1)}, bf16[8,232,128]{2,1,0:T(8,128)(2,1)}, bf16[8,216,128]{2,1,0:T(8,128)(2,1)}, bf16[8,216,128]{2,1,0:T(8,128)(2,1)}) custom-call(s32[2]{0:T(128)} %pad_add_fusion.side_ref.meta_ref, bf16[128,384]{1,0:T(8,128)(2,1)} %get-tuple-element.180.refs_0_, bf16[128,384]{1,0:T(8,128)(2,1)} %copy-done.18, ...), custom_call_target="tpu_custom_call" | custom-call | flops 452984832 | bytes 1388552 | tf_op jit(solution)/shard_map/pack/pallas_call | solution.py:70
  148.9 2.5 collective-permute-start.24
  151.3 6.9 %collective-permute-done.26 = bf16[8,216,128]{2,1,0:T(8,128)(2,1)S(1)} collective-permute-done((bf16[8,216,128]{2,1,0:T(8,128)(2,1)}, bf16[8,216,128]{2,1,0:T(8,128)(2,1)S(1)}, u32[]{:S(2)}, u32[]{:S(2)}) %collective-permute-start.26) | collective-permute-done | bytes 442400 | tf_op jit(solution)/shard_map/ppermute | solution.py:491
  158.4 7.2 %collective-permute-done.24 = bf16[1,1312,128]{2,1,0:T(8,128)(2,1)S(1)} collective-permute-done((bf16[1,1312,128]{2,1,0:T(8,128)(2,1)S(1)}, bf16[1,1312,128]{2,1,0:T(8,128)(2,1)S(1)}, u32[]{:S(2)}, u32[]{:S(2)}) %collective-permute-start.24) | collective-permute-done | bytes 335904 | tf_op jit(solution)/shard_map/ppermute | solution.py:491
  168.2 5.5 %collective-permute-done.29 = bf16[4,216,128]{2,1,0:T(8,128)(2,1)S(1)} collective-permute-done((bf16[4,216,128]{2,1,0:T(8,128)(2,1)S(1)}, bf16[4,216,128]{2,1,0:T(8,128)(2,1)S(1)}, u32[]{:S(2)}, u32[]{:S(2)}) %collective-permute-start.29) | collective-permute-done | bytes 221216 | tf_op jit(solution)/shard_map/ppermute | solution.py:491
  173.7 9.6 %collective-permute-done.27 = bf16[1,1312,128]{2,1,0:T(8,128)(2,1)S(1)} collective-permute-done((bf16[1,1312,128]{2,1,0:T(8,128)(2,1)S(1)}, bf16[1,1312,128]{2,1,0:T(8,128)(2,1)S(1)}, u32[]{:S(2)}, u32[]{:S(2)}) %collective-permute-start.27) | collective-permute-done | bytes 335904 | tf_op jit(solution)/shard_map/ppermute | solution.py:491
  186.4 2.1 collective-permute-start.31
  188.5 3.6 %collective-permute-done.30 = bf16[2,448,128]{2,1,0:T(8,128)(2,1)S(1)} collective-permute-done((bf16[2,448,128]{2,1,0:T(8,128)(2,1)S(1)}, bf16[2,448,128]{2,1,0:T(8,128)(2,1)S(1)}, u32[]{:S(2)}, u32[]{:S(2)}) %collective-permute-start.30) | collective-permute-done | bytes 229408 | tf_op jit(solution)/shard_map/ppermute | solution.py:491
  192.6 5.1 %collective-permute-done.31 = bf16[2,448,128]{2,1,0:T(8,128)(2,1)S(1)} collective-permute-done((bf16[2,448,128]{2,1,0:T(8,128)(2,1)S(1)}, bf16[2,448,128]{2,1,0:T(8,128)(2,1)S(1)}, u32[]{:S(2)}, u32[]{:S(2)}) %collective-permute-start.31) | collective-permute-done | bytes 229408 | tf_op jit(solution)/shard_map/ppermute | solution.py:491
  203.1 2.4 collective-permute-start.37
  206.1 13.6 %collective-permute-done.39 = bf16[2,448,128]{2,1,0:T(8,128)(2,1)S(1)} collective-permute-done((bf16[2,448,128]{2,1,0:T(8,128)(2,1)S(1)}, bf16[2,448,128]{2,1,0:T(8,128)(2,1)S(1)}, u32[]{:S(2)}, u32[]{:S(2)}) %collective-permute-start.39) | collective-permute-done | bytes 229408 | tf_op jit(solution)/shard_map/ppermute | solution.py:491
  224.4 20.8 %collective-permute-done.44 = bf16[4,216,128]{2,1,0:T(8,128)(2,1)S(1)} collective-permute-done((bf16[4,216,128]{2,1,0:T(8,128)(2,1)S(1)}, bf16[4,216,128]{2,1,0:T(8,128)(2,1)S(1)}, u32[]{:S(2)}, u32[]{:S(2)}) %collective-permute-start.44) | collective-permute-done | bytes 221216 | tf_op jit(solution)/shard_map/ppermute | solution.py:491
  247.4 5.5 %unpack.3 = (f32[1536,768]{1,0:T(8,128)}, f32[384,3072]{1,0:T(8,128)}, f32[384,768]{1,0:T(8,128)}, f32[384]{0:T(512)}, f32[384]{0:T(512)}, /*index=5*/f32[384]{0:T(512)}, f32[384]{0:T(512)}, f32[1536]{0:T(1024)}) custom-call(s32[2]{0:T(128)S(1)} %copy-done, bf16[8,448,128]{2,1,0:T(8,128)(2,1)S(1)} %pad_maximum_fusion.refs_0_, ...), custom_call_target="tpu_custom_call" | custom-call | bytes 5373960 | tf_op jit(solution)/shard_map/unpack/pallas_call | solution.py:70
  252.8 3.1 %collective-permute-done.46.refs_3_ = bf16[8,216,128]{2,1,0:T(8,128)(2,1)S(1)} collective-permute-done((bf16[8,216,128]{2,1,0:T(8,128)(2,1)S(1)}, bf16[8,216,128]{2,1,0:T(8,128)(2,1)S(1)}, u32[]{:S(2)}, u32[]{:S(2)}) %collective-permute-start.46) | collective-permute-done | bytes 442400 | tf_op jit(solution)/shard_map/ppermute | solution.py:491
  256.1 3.0 %unpack.2 = (f32[384,2304]{1,0:T(8,128)}, f32[384]{0:T(512)}, f32[384]{0:T(512)}, f32[384]{0:T(512)}, f32[384]{0:T(512)}) custom-call(s32[2]{0:T(128)S(1)} %copy-done, bf16[8,232,128]{2,1,0:T(8,128)(2,1)S(1)} %pad_maximum_fusion.3.refs_0_, bf16[8,232,128]{2,1,0:T(8,128)(2,1)S(1)} %collective-permute-done.45.refs_1_, ...), custom_call_target="tpu_custom_call" | custom-call | bytes 1835016 | tf_op jit(solution)/shard_map/unpack/pallas_call | solution.py:70
  (175 shorter events, 42.7 us)
Async XLA Ops:
  4.7 52.4 %collective-permute-start.3 = (bf16[384,3072]{1,0:T(8,128)(2,1)}, bf16[384,3072]{1,0:T(8,128)(2,1)}, u32[]{:S(2)}, u32[]{:S(2)}) collective-permute-start(bf16[384,3072]{1,0:T(8,128)(2,1)} %refs_2_.2), channel_id=1, source_target_pairs={{0,1},{1,0},{2,3},{3,2},{4,5},{5,4},{6,7},{7,6},{8,9},{9,8},{10,11... | collective-permute-start | bytes 7077896 | tf_op jit(solution)/shard_map/ppermute | solution.py:453
  5.2 51.9 %collective-permute-start.4 = (bf16[1536,768]{1,0:T(8,128)(2,1)}, bf16[1536,768]{1,0:T(8,128)(2,1)}, u32[]{:S(2)}, u32[]{:S(2)}) collective-permute-start(bf16[1536,768]{1,0:T(8,128)(2,1)} %refs_4_.2), channel_id=1, source_target_pairs={{0,1},{1,0},{2,3},{3,2},{4,5},{5,4},{6,7},{7,6},{8,9},{9,8},{10,11... | collective-permute-start | bytes 7077896 | tf_op jit(solution)/shard_map/ppermute | solution.py:453
  10.1 28.2 %all-to-all-start = ((bf16[16,192,128]{2,1,0:T(8,128)(2,1)}), bf16[16,192,128]{2,1,0:T(8,128)(2,1)S(1)}, u32[]{:S(2)}, u32[]{:S(2)}) async-start(bf16[16,192,128]{2,1,0:T(8,128)(2,1)} %get-tuple-element.128), calls=%async_computation | async-start | bytes 1572864 | tf_op jit(solution)/shard_map/all_to_all | solution.py:695
  18.3 30.3 %collective-permute-start.2 = (bf16[384,768]{1,0:T(8,128)(2,1)S(1)}, bf16[384,768]{1,0:T(8,128)(2,1)S(1)}, u32[]{:S(2)}, u32[]{:S(2)}) collective-permute-start(bf16[384,768]{1,0:T(8,128)(2,1)S(1)} %copy-done.7), channel_id=1, source_target_pairs={{0,1},{1,0},{2,3},{3,2},{4,5},{5,4},{6,7},{7,6},{8,9},{9,8},{10,11... | collective-permute-start | bytes 1769480 | tf_op jit(solution)/shard_map/ppermute | solution.py:453
  43.6 13.5 %all-to-all-start.1 = ((bf16[16,64,128]{2,1,0:T(8,128)(2,1)}), bf16[16,64,128]{2,1,0:T(8,128)(2,1)S(1)}, u32[]{:S(2)}, u32[]{:S(2)}) async-start(bf16[16,64,128]{2,1,0:T(8,128)(2,1)} %get-tuple-element.129.att_ref), calls=%async_computation.1 | async-start | bytes 524288 | tf_op jit(solution)/shard_map/all_to_all | solution.py:703
  69.5 14.7 %all-to-all-start.2 = ((bf16[16,64,128]{2,1,0:T(8,128)(2,1)}), bf16[16,64,128]{2,1,0:T(8,128)(2,1)S(1)}, u32[]{:S(2)}, u32[]{:S(2)}) async-start(bf16[16,64,128]{2,1,0:T(8,128)(2,1)} %get-tuple-element.151), calls=%async_computation.2 | async-start | bytes 524288 | tf_op jit(solution)/shard_map/all_to_all | solution.py:724
  84.2 33.2 %collective-permute-start.12 = (bf16[8,448,128]{2,1,0:T(8,128)(2,1)}, bf16[8,448,128]{2,1,0:T(8,128)(2,1)S(1)}, u32[]{:S(2)}, u32[]{:S(2)}) collective-permute-start(bf16[8,448,128]{2,1,0:T(8,128)(2,1)} %get-tuple-element.158), channel_id=1, source_target_pairs={{0,2},{2,0},{4,6},{6,4},{8,10},{10,8},{12,14},{14,12},{16,18},{18,... | collective-permute-start | bytes 2752520 | tf_op jit(solution)/shard_map/ppermute | solution.py:491
  86.2 25.1 %collective-permute-start.13 = (bf16[8,432,128]{2,1,0:T(8,128)(2,1)}, bf16[8,432,128]{2,1,0:T(8,128)(2,1)}, u32[]{:S(2)}, u32[]{:S(2)}) collective-permute-start(bf16[8,432,128]{2,1,0:T(8,128)(2,1)} %get-tuple-element.159), channel_id=1, source_target_pairs={{0,4},{2,6},{4,0},{6,2},{8,12},{10,14},{12,8},{14,10},{16,20},{18,... | collective-permute-start | bytes 2654216 | tf_op jit(solution)/shard_map/ppermute | solution.py:491
  87.7 29.7 %collective-permute-start.14 = (bf16[8,432,128]{2,1,0:T(8,128)(2,1)}, bf16[8,432,128]{2,1,0:T(8,128)(2,1)}, u32[]{:S(2)}, u32[]{:S(2)}) collective-permute-start(bf16[8,432,128]{2,1,0:T(8,128)(2,1)} %get-tuple-element.160), channel_id=1, source_target_pairs={{0,8},{2,10},{4,12},{6,14},{8,0},{10,2},{12,4},{14,6},{16,24},{18,... | collective-permute-start | bytes 2654216 | tf_op jit(solution)/shard_map/ppermute | solution.py:491
  98.1 33.3 %all-to-all-start.3 = ((bf16[16,192,128]{2,1,0:T(8,128)(2,1)}), bf16[16,192,128]{2,1,0:T(8,128)(2,1)S(1)}, u32[]{:S(2)}, u32[]{:S(2)}) async-start(bf16[16,192,128]{2,1,0:T(8,128)(2,1)} %attend_back.1), calls=%async_computation.3 | async-start | bytes 1572864 | tf_op jit(solution)/shard_map/all_to_all | solution.py:747
  119.5 11.8 %collective-permute-start.15 = (bf16[4,448,128]{2,1,0:T(8,128)(2,1)S(1)}, bf16[4,448,128]{2,1,0:T(8,128)(2,1)S(1)}, u32[]{:S(2)}, u32[]{:S(2)}) collective-permute-start(bf16[4,448,128]{2,1,0:T(8,128)(2,1)S(1)} %get-tuple-element.167), channel_id=1, source_target_pairs={{0,4},{2,6},{4,0},{6,2},{8,12},{10,14},{12,8},{14,10},{16,20},{18,... | collective-permute-start | bytes 1376264 | tf_op jit(solution)/shard_map/ppermute | solution.py:491
  119.6 11.7 %collective-permute-start.16 = (bf16[4,432,128]{2,1,0:T(8,128)(2,1)S(1)}, bf16[4,432,128]{2,1,0:T(8,128)(2,1)S(1)}, u32[]{:S(2)}, u32[]{:S(2)}) collective-permute-start(bf16[4,432,128]{2,1,0:T(8,128)(2,1)S(1)} %get-tuple-element.168), channel_id=1, source_target_pairs={{0,8},{2,10},{4,12},{6,14},{8,0},{10,2},{12,4},{14,6},{16,24},{18,... | collective-permute-start | bytes 1327112 | tf_op jit(solution)/shard_map/ppermute | solution.py:491
  119.7 11.6 %collective-permute-start.17 = (bf16[4,432,128]{2,1,0:T(8,128)(2,1)S(1)}, bf16[4,432,128]{2,1,0:T(8,128)(2,1)S(1)}, u32[]{:S(2)}, u32[]{:S(2)}) collective-permute-start(bf16[4,432,128]{2,1,0:T(8,128)(2,1)S(1)} %get-tuple-element.169), channel_id=1, source_target_pairs={{0,2},{2,0},{4,6},{6,4},{8,10},{10,8},{12,14},{14,12},{16,18},{18,... | collective-permute-start | bytes 1327112 | tf_op jit(solution)/shard_map/ppermute | solution.py:491
  139.3 9.4 %collective-permute-start.21 = (bf16[2,448,128]{2,1,0:T(8,128)(2,1)S(1)}, bf16[2,448,128]{2,1,0:T(8,128)(2,1)S(1)}, u32[]{:S(2)}, u32[]{:S(2)}) collective-permute-start(bf16[2,448,128]{2,1,0:T(8,128)(2,1)S(1)} %get-tuple-element.188), channel_id=1, source_target_pairs={{0,8},{2,10},{4,12},{6,14},{8,0},{10,2},{12,4},{14,6},{16,24},{18,... | collective-permute-start | bytes 688136 | tf_op jit(solution)/shard_map/ppermute | solution.py:491
  145.3 13.1 %collective-permute-start.25 = (bf16[8,232,128]{2,1,0:T(8,128)(2,1)}, bf16[8,232,128]{2,1,0:T(8,128)(2,1)S(1)}, u32[]{:S(2)}, u32[]{:S(2)}) collective-permute-start(bf16[8,232,128]{2,1,0:T(8,128)(2,1)} %get-tuple-element.196), channel_id=1, source_target_pairs={{0,2},{2,0},{4,6},{6,4},{8,10},{10,8},{12,14},{14,12},{16,18},{18,... | collective-permute-start | bytes 1425416 | tf_op jit(solution)/shard_map/ppermute | solution.py:491
  146.8 11.5 %collective-permute-start.26 = (bf16[8,216,128]{2,1,0:T(8,128)(2,1)}, bf16[8,216,128]{2,1,0:T(8,128)(2,1)S(1)}, u32[]{:S(2)}, u32[]{:S(2)}) collective-permute-start(bf16[8,216,128]{2,1,0:T(8,128)(2,1)} %get-tuple-element.197), channel_id=1, source_target_pairs={{0,4},{2,6},{4,0},{6,2},{8,12},{10,14},{12,8},{14,10},{16,20},{18,... | collective-permute-start | bytes 1327112 | tf_op jit(solution)/shard_map/ppermute | solution.py:491
  148.9 16.7 %collective-permute-start.24 = (bf16[1,1312,128]{2,1,0:T(8,128)(2,1)S(1)}, bf16[1,1312,128]{2,1,0:T(8,128)(2,1)S(1)}, u32[]{:S(2)}, u32[]{:S(2)}) collective-permute-start(bf16[1,1312,128]{2,1,0:T(8,128)(2,1)S(1)} %pad_maximum_fusion.8), channel_id=1, source_target_pairs={{0,16},{2,18},{4,20},{6,22},{8,24},{10,26},{12,28},{14,30},{16,0},... | collective-permute-start | bytes 1007624 | tf_op jit(solution)/shard_map/ppermute | solution.py:491
  166.5 16.8 %collective-permute-start.27 = (bf16[1,1312,128]{2,1,0:T(8,128)(2,1)S(1)}, bf16[1,1312,128]{2,1,0:T(8,128)(2,1)S(1)}, u32[]{:S(2)}, u32[]{:S(2)}) collective-permute-start(bf16[1,1312,128]{2,1,0:T(8,128)(2,1)S(1)} %pad_maximum_fusion.9), channel_id=1, source_target_pairs={{0,16},{2,18},{4,20},{6,22},{8,24},{10,26},{12,28},{14,30},{16,0},... | collective-permute-start | bytes 1007624 | tf_op jit(solution)/shard_map/ppermute | solution.py:491
  183.5 8.5 %collective-permute-start.30 = (bf16[2,448,128]{2,1,0:T(8,128)(2,1)S(1)}, bf16[2,448,128]{2,1,0:T(8,128)(2,1)S(1)}, u32[]{:S(2)}, u32[]{:S(2)}) collective-permute-start(bf16[2,448,128]{2,1,0:T(8,128)(2,1)S(1)} %pad_maximum_fusion.11), channel_id=1, source_target_pairs={{0,8},{2,10},{4,12},{6,14},{8,0},{10,2},{12,4},{14,6},{16,24},{18,... | collective-permute-start | bytes 688136 | tf_op jit(solution)/shard_map/ppermute | solution.py:491
  183.7 8.9 %collective-permute-start.33 = (bf16[2,432,128]{2,1,0:T(8,128)(2,1)S(1)}, bf16[2,432,128]{2,1,0:T(8,128)(2,1)S(1)}, u32[]{:S(2)}, u32[]{:S(2)}) collective-permute-start(bf16[2,432,128]{2,1,0:T(8,128)(2,1)S(1)} %pad_maximum_fusion.14), channel_id=1, source_target_pairs={{0,4},{2,6},{4,0},{6,2},{8,12},{10,14},{12,8},{14,10},{16,20},{18,... | collective-permute-start | bytes 663560 | tf_op jit(solution)/shard_map/ppermute | solution.py:491
  186.4 11.3 %collective-permute-start.31 = (bf16[2,448,128]{2,1,0:T(8,128)(2,1)S(1)}, bf16[2,448,128]{2,1,0:T(8,128)(2,1)S(1)}, u32[]{:S(2)}, u32[]{:S(2)}) collective-permute-start(bf16[2,448,128]{2,1,0:T(8,128)(2,1)S(1)} %pad_maximum_fusion.12), channel_id=1, source_target_pairs={{0,8},{2,10},{4,12},{6,14},{8,0},{10,2},{12,4},{14,6},{16,24},{18,... | collective-permute-start | bytes 688136 | tf_op jit(solution)/shard_map/ppermute | solution.py:491
  200.0 19.6 %collective-permute-start.38 = (bf16[4,432,128]{2,1,0:T(8,128)(2,1)S(1)}, bf16[4,432,128]{2,1,0:T(8,128)(2,1)S(1)}, u32[]{:S(2)}, u32[]{:S(2)}) collective-permute-start(bf16[4,432,128]{2,1,0:T(8,128)(2,1)S(1)} %pad_maximum_fusion.6), channel_id=1, source_target_pairs={{0,2},{2,0},{4,6},{6,4},{8,10},{10,8},{12,14},{14,12},{16,18},{18,... | collective-permute-start | bytes 1327112 | tf_op jit(solution)/shard_map/ppermute | solution.py:491
  201.4 18.2 %collective-permute-start.36 = (bf16[4,448,128]{2,1,0:T(8,128)(2,1)S(1)}, bf16[4,448,128]{2,1,0:T(8,128)(2,1)S(1)}, u32[]{:S(2)}, u32[]{:S(2)}) collective-permute-start(bf16[4,448,128]{2,1,0:T(8,128)(2,1)S(1)} %pad_maximum_fusion.4), channel_id=1, source_target_pairs={{0,4},{2,6},{4,0},{6,2},{8,12},{10,14},{12,8},{14,10},{16,20},{18,... | collective-permute-start | bytes 1376264 | tf_op jit(solution)/shard_map/ppermute | solution.py:491
  203.1 16.6 %collective-permute-start.37 = (bf16[4,432,128]{2,1,0:T(8,128)(2,1)S(1)}, bf16[4,432,128]{2,1,0:T(8,128)(2,1)S(1)}, u32[]{:S(2)}, u32[]{:S(2)}) collective-permute-start(bf16[4,432,128]{2,1,0:T(8,128)(2,1)S(1)} %pad_maximum_fusion.5), channel_id=1, source_target_pairs={{0,8},{2,10},{4,12},{6,14},{8,0},{10,2},{12,4},{14,6},{16,24},{18,... | collective-permute-start | bytes 1327112 | tf_op jit(solution)/shard_map/ppermute | solution.py:491
  206.0 13.7 %collective-permute-start.39 = (bf16[2,448,128]{2,1,0:T(8,128)(2,1)S(1)}, bf16[2,448,128]{2,1,0:T(8,128)(2,1)S(1)}, u32[]{:S(2)}, u32[]{:S(2)}) collective-permute-start(bf16[2,448,128]{2,1,0:T(8,128)(2,1)S(1)} %maximum_maximum_fusion), channel_id=1, source_target_pairs={{0,8},{2,10},{4,12},{6,14},{8,0},{10,2},{12,4},{14,6},{16,24},{18,... | collective-permute-start | bytes 688136 | tf_op jit(solution)/shard_map/ppermute | solution.py:491
  219.7 26.2 %collective-permute-start.42 = (bf16[8,432,128]{2,1,0:T(8,128)(2,1)S(1)}, bf16[8,432,128]{2,1,0:T(8,128)(2,1)S(1)}, u32[]{:S(2)}, u32[]{:S(2)}) collective-permute-start(bf16[8,432,128]{2,1,0:T(8,128)(2,1)S(1)} %pad_maximum_fusion.2.refs_4_), channel_id=1, source_target_pairs={{0,8},{2,10},{4,12},{6,14},{8,0},{10,2},{12,4},{14,6},{16,24},{18,... | collective-permute-start | bytes 2654216 | tf_op jit(solution)/shard_map/ppermute | solution.py:491
  219.9 26.0 %collective-permute-start.40 = (bf16[8,448,128]{2,1,0:T(8,128)(2,1)S(1)}, bf16[8,448,128]{2,1,0:T(8,128)(2,1)S(1)}, u32[]{:S(2)}, u32[]{:S(2)}) collective-permute-start(bf16[8,448,128]{2,1,0:T(8,128)(2,1)S(1)} %pad_maximum_fusion.refs_0_), channel_id=1, source_target_pairs={{0,2},{2,0},{4,6},{6,4},{8,10},{10,8},{12,14},{14,12},{16,18},{18,... | collective-permute-start | bytes 2752520 | tf_op jit(solution)/shard_map/ppermute | solution.py:491
  221.1 24.9 %collective-permute-start.41 = (bf16[8,432,128]{2,1,0:T(8,128)(2,1)S(1)}, bf16[8,432,128]{2,1,0:T(8,128)(2,1)S(1)}, u32[]{:S(2)}, u32[]{:S(2)}) collective-permute-start(bf16[8,432,128]{2,1,0:T(8,128)(2,1)S(1)} %pad_maximum_fusion.1.refs_2_), channel_id=1, source_target_pairs={{0,4},{2,6},{4,0},{6,2},{8,12},{10,14},{12,8},{14,10},{16,20},{18,... | collective-permute-start | bytes 2654216 | tf_op jit(solution)/shard_map/ppermute | solution.py:491
  221.9 24.0 %collective-permute-start.43 = (bf16[4,232,128]{2,1,0:T(8,128)(2,1)S(1)}, bf16[4,232,128]{2,1,0:T(8,128)(2,1)S(1)}, u32[]{:S(2)}, u32[]{:S(2)}) collective-permute-start(bf16[4,232,128]{2,1,0:T(8,128)(2,1)S(1)} %pad_maximum_fusion.10), channel_id=1, source_target_pairs={{0,4},{2,6},{4,0},{6,2},{8,12},{10,14},{12,8},{14,10},{16,20},{18,... | collective-permute-start | bytes 712712 | tf_op jit(solution)/shard_map/ppermute | solution.py:491
  223.3 22.0 %collective-permute-start.44 = (bf16[4,216,128]{2,1,0:T(8,128)(2,1)S(1)}, bf16[4,216,128]{2,1,0:T(8,128)(2,1)S(1)}, u32[]{:S(2)}, u32[]{:S(2)}) collective-permute-start(bf16[4,216,128]{2,1,0:T(8,128)(2,1)S(1)} %pad_maximum_fusion.15), channel_id=1, source_target_pairs={{0,2},{2,0},{4,6},{6,4},{8,10},{10,8},{12,14},{14,12},{16,18},{18,... | collective-permute-start | bytes 663560 | tf_op jit(solution)/shard_map/ppermute | solution.py:491
  246.0 10.1 %collective-permute-start.45 = (bf16[8,232,128]{2,1,0:T(8,128)(2,1)S(1)}, bf16[8,232,128]{2,1,0:T(8,128)(2,1)S(1)}, u32[]{:S(2)}, u32[]{:S(2)}) collective-permute-start(bf16[8,232,128]{2,1,0:T(8,128)(2,1)S(1)} %pad_maximum_fusion.3.refs_0_), channel_id=1, source_target_pairs={{0,2},{2,0},{4,6},{6,4},{8,10},{10,8},{12,14},{14,12},{16,18},{18,... | collective-permute-start | bytes 1425416 | tf_op jit(solution)/shard_map/ppermute | solution.py:491
  247.0 8.9 %collective-permute-start.46 = (bf16[8,216,128]{2,1,0:T(8,128)(2,1)S(1)}, bf16[8,216,128]{2,1,0:T(8,128)(2,1)S(1)}, u32[]{:S(2)}, u32[]{:S(2)}) collective-permute-start(bf16[8,216,128]{2,1,0:T(8,128)(2,1)S(1)} %pad_maximum_fusion.7.refs_2_), channel_id=1, source_target_pairs={{0,4},{2,6},{4,0},{6,2},{8,12},{10,14},{12,8},{14,10},{16,20},{18,... | collective-permute-start | bytes 1327112 | tf_op jit(solution)/shard_map/ppermute | solution.py:491
  (44 other events, 267.0 us)

commit v7 on v6

--- a/solution.py
+++ b/solution.py
@@ -610,7 +610,7 @@
             functools.partial(pack_kernel, paired, parts), outs,
             [((2 * rows, a.shape[1]), BF16) for a in args[:-2:2]]
             + [((count, block, LANES), kind), ((count, LINES, LANES), F32)],
-            "pack", 4 * rows * size, meta, *args,
+            "pack", 4 * rows * size, meta, *args, limit=24 if parts == 2 else 56,
         )
         return Flow(flows[::2], flows[1::2], count)
     extra = sums_over_group(keep_sums, send_sums, group).reshape(-1, LANES)
@@ -766,7 +766,7 @@
     advance(early, count)
     late = pack(pairs, sums, args, (False,), 2, meta, index, group, count)
     while not early.over():
-        advance(early, count, late, 1 + (2 * early.bits - 1 > early.step >= 2 * early.bits - 3))
+        advance(early, count, late, 1 + (2 * early.bits - 2 > early.step >= 2 * early.bits - 4))
     (grad_shrink, grad_expand, grad_mix), sums = unpack(
         early, ((4 * each, width), (each, ff), (each, width)), early_kinds, (1, 1, 1, 1, 4), meta, index,
         group, count,

time: 260 us -> 257 us (0.988)
  transfers between devices with their start and end apart: 51 -> 51, of which waited for: 26 -> 25; matrix products, arithmetic and copies ran while one was open for 2% -> 2% of each run, Pallas kernels for 14% -> 13%
where the time goes in v7:
time: 257 us; the launch traced here: 256 us
  waiting for transfers between devices  138 us (54%)
  starting transfers between devices  56.6 us (22%)
  Pallas kernels  52.1 us (20%)
  other arithmetic  4.66 us (2%)
  local copies, waits for them, and re-layouts  3.39 us (1%)
    ppermute x32, waiting for transfers between devices, swap_bit(): return lax.ppermute(part, 'ctx', [(d, d ^ 1 << bit) for d in range(count)])  105 us
    pallas_call x10, Pallas kernels, call(): pl.pallas_call(kernel, out_shape=[jax.ShapeDtypeStruct(s, d) for s, d in...  52.1 us
    ppermute x32, starting transfers between devices, swap_bit(): return lax.ppermute(part, 'ctx', [(d, d ^ 1 << bit) for d in range(count)])  32.2 us
    all_to_all x1, waiting for transfers between devices, body(): qkv_here = lax.all_to_all(qkv_send, 'ctx', 0, 0, tiled=True)  19.8 us
    all_to_all x1, waiting for transfers between devices, body(): att_here = lax.all_to_all(att_send, 'ctx', 0, 0, tiled=True)  8.48 us
    all_to_all x1, starting transfers between devices, body(): qkv_here = lax.all_to_all(qkv_send, 'ctx', 0, 0, tiled=True)  8.23 us
  transfers between devices with their start and end apart: 51, of which 25 were waited for; matrix products, arithmetic and copies ran while one was open for 2% of the time, Pallas kernels for 13%

profile of v7, /device:TPU:0, one launch (start us, length us, event | category | flops | bytes accessed | tf_op | source)
XLA Modules:
  0.0 256.0 jit_solution(1674576697021946352)
XLA Ops:
  2.7 2.1 collective-permute-done.theirs_ref
  5.9 4.1 %project.1 = (bf16[128,768]{1,0:T(8,128)(2,1)}, bf16[16,192,128]{2,1,0:T(8,128)(2,1)}) custom-call(s32[2]{0:T(128)} %pad_add_fusion.side_ref.meta_ref, bf16[128,768]{1,0:T(8,128)(2,1)} %bitcast.7, bf16[12,384]{1,0:T(8,128)(2,1)} %stack.13.mine_ref, bf16[12,384]{1,0:T(8,128)(2,1)} %copy-done.12, bf16[384,2304]{1,0:T(8,128)(2,1)} %own_ref.1, ...), custom_call_target="tpu_custom_call" | custom-call | flops 452984832 | bytes 3753992 | tf_op jit(solution)/shard_map/project/pallas_call | solution.py:70
  10.1 8.2 %all-to-all-start = ((bf16[16,192,128]{2,1,0:T(8,128)(2,1)}), bf16[16,192,128]{2,1,0:T(8,128)(2,1)S(1)}, u32[]{:S(2)}, u32[]{:S(2)}) async-start(bf16[16,192,128]{2,1,0:T(8,128)(2,1)} %get-tuple-element.129), calls=%async_computation | async-start | bytes 1572864 | tf_op jit(solution)/shard_map/all_to_all | solution.py:695
  18.5 19.8 %all-to-all-done.in_ref = bf16[16,192,128]{2,1,0:T(8,128)(2,1)S(1)} async-done(((bf16[16,192,128]{2,1,0:T(8,128)(2,1)}), bf16[16,192,128]{2,1,0:T(8,128)(2,1)S(1)}, u32[]{:S(2)}, u32[]{:S(2)}) %all-to-all-start) | async-done | bytes 786464 | tf_op jit(solution)/shard_map/all_to_all | solution.py:695
  38.3 5.3 %attend.1 = (bf16[16,64,128]{2,1,0:T(8,128)(2,1)}, f32[1,2048]{1,0:T(1,128)S(1)}) custom-call(s32[16]{0:T(128)S(1)} %select_reduce_fusion.slot_ref, bf16[16,192,128]{2,1,0:T(8,128)(2,1)S(1)} %all-to-all-done.in_ref), custom_call_target="tpu_custom_call" | custom-call | flops 536870912 | bytes 786496 | tf_op jit(solution)/shard_map/attend/pallas_call | solution.py:70
  43.6 4.9 %all-to-all-start.1 = ((bf16[16,64,128]{2,1,0:T(8,128)(2,1)}), bf16[16,64,128]{2,1,0:T(8,128)(2,1)S(1)}, u32[]{:S(2)}, u32[]{:S(2)}) async-start(bf16[16,64,128]{2,1,0:T(8,128)(2,1)} %get-tuple-element.130.att_ref), calls=%async_computation.1 | async-start | bytes 524288 | tf_op jit(solution)/shard_map/all_to_all | solution.py:703
  48.6 8.5 %all-to-all-done.1.att_in = bf16[16,64,128]{2,1,0:T(8,128)(2,1)S(1)} async-done(((bf16[16,64,128]{2,1,0:T(8,128)(2,1)}), bf16[16,64,128]{2,1,0:T(8,128)(2,1)S(1)}, u32[]{:S(2)}, u32[]{:S(2)}) %all-to-all-start.1) | async-done | bytes 262176 | tf_op jit(solution)/shard_map/all_to_all | solution.py:703
  57.8 11.2 %middle.1 = (bf16[128,768]{1,0:T(8,128)(2,1)}, f32[128,768]{1,0:T(8,128)}, bf16[16,64,128]{2,1,0:T(8,128)(2,1)}, f32[8,384]{1,0:T(8,128)}, f32[8,384]{1,0:T(8,12...) custom-call(s32[2]{0:T(128)} %pad_add_fusion.side_ref.meta_ref, ...), custom_call_target="tpu_custom_call" | custom-call | flops 2717908992 | bytes 11487240 | tf_op jit(solution)/shard_map/middle/pallas_call | solution.py:70
  69.5 3.8 %all-to-all-start.2 = ((bf16[16,64,128]{2,1,0:T(8,128)(2,1)}), bf16[16,64,128]{2,1,0:T(8,128)(2,1)S(1)}, u32[]{:S(2)}, u32[]{:S(2)}) async-start(bf16[16,64,128]{2,1,0:T(8,128)(2,1)} %get-tuple-element.152), calls=%async_computation.2 | async-start | bytes 524288 | tf_op jit(solution)/shard_map/all_to_all | solution.py:724
  77.8 6.4 %pack.2 = (bf16[8,448,128]{2,1,0:T(8,128)(2,1)}, bf16[8,448,128]{2,1,0:T(8,128)(2,1)}, bf16[8,432,128]{2,1,0:T(8,128)(2,1)}, bf16[8,432,128]{2,1,0:T(8,128)(2,1)...) custom-call(s32[2]{0:T(128)} %pad_add_fusion.side_ref.meta_ref, ...), custom_call_target="tpu_custom_call" | custom-call | flops 1358954496 | bytes 3563528 | tf_op jit(solution)/shard_map/pack/pallas_call | solution.py:70
  84.3 2.0 collective-permute-start.12
  89.2 8.9 %attend_back.1 = bf16[16,192,128]{2,1,0:T(8,128)(2,1)} custom-call(s32[16]{0:T(128)S(1)} %select_reduce_fusion.slot_ref, bf16[16,192,128]{2,1,0:T(8,128)(2,1)S(1)} %all-to-all-done.in_ref, bf16[16,64,128]{2,1,0:T(8,128)(2,1)} %get-tuple-element.130.att_ref, bf16[16,64,128]{2,1,0:T(8,128)(2,1)S(1)} %all-to-all-done.2.grad_ref, ...), custom_call_target="tpu_custom_call" | custom-call | flops 1342177280 | bytes 1318976 | tf_op jit(solution)/shard_map/attend_back/pallas_call | solution.py:70
  98.1 3.9 %all-to-all-start.3 = ((bf16[16,192,128]{2,1,0:T(8,128)(2,1)}), bf16[16,192,128]{2,1,0:T(8,128)(2,1)S(1)}, u32[]{:S(2)}, u32[]{:S(2)}) async-start(bf16[16,192,128]{2,1,0:T(8,128)(2,1)} %attend_back.1), calls=%async_computation.3 | async-start | bytes 1572864 | tf_op jit(solution)/shard_map/all_to_all | solution.py:747
  102.0 9.3 %collective-permute-done.13 = bf16[8,432,128]{2,1,0:T(8,128)(2,1)} collective-permute-done((bf16[8,432,128]{2,1,0:T(8,128)(2,1)}, bf16[8,432,128]{2,1,0:T(8,128)(2,1)}, u32[]{:S(2)}, u32[]{:S(2)}) %collective-permute-start.13) | collective-permute-done | bytes 884768 | tf_op jit(solution)/shard_map/ppermute | solution.py:491
  111.3 6.1 %collective-permute-done.14 = bf16[8,432,128]{2,1,0:T(8,128)(2,1)} collective-permute-done((bf16[8,432,128]{2,1,0:T(8,128)(2,1)}, bf16[8,432,128]{2,1,0:T(8,128)(2,1)}, u32[]{:S(2)}, u32[]{:S(2)}) %collective-permute-start.14) | collective-permute-done | bytes 884768 | tf_op jit(solution)/shard_map/ppermute | solution.py:491
  117.7 1.9 add_convert_fusion.2
  119.8 11.6 %collective-permute-done.16 = bf16[4,432,128]{2,1,0:T(8,128)(2,1)S(1)} collective-permute-done((bf16[4,432,128]{2,1,0:T(8,128)(2,1)S(1)}, bf16[4,432,128]{2,1,0:T(8,128)(2,1)S(1)}, u32[]{:S(2)}, u32[]{:S(2)}) %collective-permute-start.16) | collective-permute-done | bytes 442400 | tf_op jit(solution)/shard_map/ppermute | solution.py:491
  132.3 4.8 %finish.1 = (f32[128,768]{1,0:T(8,128)}, f32[4,384]{1,0:T(4,128)}, f32[4,384]{1,0:T(4,128)}, bf16[128,2304]{1,0:T(8,128)(2,1)}, bf16[128,384]{1,0:T(8,128)(2,1)}, /*index=5*/bf16[128,384]{1,0:T(8,128)(2,1)}) custom-call(s32[2]{0:T(128)} %pad_add_fusion.side_ref.meta_ref, bf16[16,192,128]{2,1,0:T(8,128)(2,1)} %copy-done.5, bf16[128,768]{1,0:T(8,128)(2,1)} %bitcast.9, ...), custom_call_target="tpu_custom_call" | custom-call | flops 452984832 | bytes 5130248 | tf_op jit(solution)/shard_map/finish/pallas_call | solution.py:70
  146.4 2.7 %collective-permute-done.22 = bf16[2,432,128]{2,1,0:T(8,128)(2,1)S(1)} collective-permute-done((bf16[2,432,128]{2,1,0:T(8,128)(2,1)S(1)}, bf16[2,432,128]{2,1,0:T(8,128)(2,1)S(1)}, u32[]{:S(2)}, u32[]{:S(2)}) %collective-permute-start.22) | collective-permute-done | bytes 221216 | tf_op jit(solution)/shard_map/ppermute | solution.py:491
  149.9 2.4 collective-permute-start.24
  152.3 5.6 %collective-permute-done.26 = bf16[8,216,128]{2,1,0:T(8,128)(2,1)S(1)} collective-permute-done((bf16[8,216,128]{2,1,0:T(8,128)(2,1)S(1)}, bf16[8,216,128]{2,1,0:T(8,128)(2,1)S(1)}, u32[]{:S(2)}, u32[]{:S(2)}) %collective-permute-start.26) | collective-permute-done | bytes 442400 | tf_op jit(solution)/shard_map/ppermute | solution.py:491
  158.3 7.0 %collective-permute-done.24 = bf16[1,1312,128]{2,1,0:T(8,128)(2,1)S(1)} collective-permute-done((bf16[1,1312,128]{2,1,0:T(8,128)(2,1)S(1)}, bf16[1,1312,128]{2,1,0:T(8,128)(2,1)S(1)}, u32[]{:S(2)}, u32[]{:S(2)}) %collective-permute-start.24) | collective-permute-done | bytes 335904 | tf_op jit(solution)/shard_map/ppermute | solution.py:491
  168.0 5.4 %collective-permute-done.28 = bf16[4,216,128]{2,1,0:T(8,128)(2,1)S(1)} collective-permute-done((bf16[4,216,128]{2,1,0:T(8,128)(2,1)S(1)}, bf16[4,216,128]{2,1,0:T(8,128)(2,1)S(1)}, u32[]{:S(2)}, u32[]{:S(2)}) %collective-permute-start.28) | collective-permute-done | bytes 221216 | tf_op jit(solution)/shard_map/ppermute | solution.py:491
  173.6 10.6 %collective-permute-done.29 = bf16[1,1312,128]{2,1,0:T(8,128)(2,1)S(1)} collective-permute-done((bf16[1,1312,128]{2,1,0:T(8,128)(2,1)S(1)}, bf16[1,1312,128]{2,1,0:T(8,128)(2,1)S(1)}, u32[]{:S(2)}, u32[]{:S(2)}) %collective-permute-start.29) | collective-permute-done | bytes 335904 | tf_op jit(solution)/shard_map/ppermute | solution.py:491
  184.2 2.7 %collective-permute-done.30 = bf16[2,448,128]{2,1,0:T(8,128)(2,1)S(1)} collective-permute-done((bf16[2,448,128]{2,1,0:T(8,128)(2,1)S(1)}, bf16[2,448,128]{2,1,0:T(8,128)(2,1)S(1)}, u32[]{:S(2)}, u32[]{:S(2)}) %collective-permute-start.30) | collective-permute-done | bytes 229408 | tf_op jit(solution)/shard_map/ppermute | solution.py:491
  194.6 5.6 %collective-permute-done.32 = bf16[2,448,128]{2,1,0:T(8,128)(2,1)S(1)} collective-permute-done((bf16[2,448,128]{2,1,0:T(8,128)(2,1)S(1)}, bf16[2,448,128]{2,1,0:T(8,128)(2,1)S(1)}, u32[]{:S(2)}, u32[]{:S(2)}) %collective-permute-start.32) | collective-permute-done | bytes 229408 | tf_op jit(solution)/shard_map/ppermute | solution.py:491
  200.3 2.1 collective-permute-start.38
  203.7 2.1 collective-permute-start.39
  205.8 12.9 %collective-permute-done.39 = bf16[2,448,128]{2,1,0:T(8,128)(2,1)S(1)} collective-permute-done((bf16[2,448,128]{2,1,0:T(8,128)(2,1)S(1)}, bf16[2,448,128]{2,1,0:T(8,128)(2,1)S(1)}, u32[]{:S(2)}, u32[]{:S(2)}) %collective-permute-start.39) | collective-permute-done | bytes 229408 | tf_op jit(solution)/shard_map/ppermute | solution.py:491
  223.5 19.6 %collective-permute-done.44 = bf16[4,216,128]{2,1,0:T(8,128)(2,1)S(1)} collective-permute-done((bf16[4,216,128]{2,1,0:T(8,128)(2,1)S(1)}, bf16[4,216,128]{2,1,0:T(8,128)(2,1)S(1)}, u32[]{:S(2)}, u32[]{:S(2)}) %collective-permute-start.44) | collective-permute-done | bytes 221216 | tf_op jit(solution)/shard_map/ppermute | solution.py:491
  245.7 5.5 %unpack.3 = (f32[1536,768]{1,0:T(8,128)}, f32[384,3072]{1,0:T(8,128)}, f32[384,768]{1,0:T(8,128)}, f32[384]{0:T(512)}, f32[384]{0:T(512)}, /*index=5*/f32[384]{0:T(512)}, f32[384]{0:T(512)}, f32[1536]{0:T(1024)}) custom-call(s32[2]{0:T(128)S(1)} %copy-done, bf16[8,448,128]{2,1,0:T(8,128)(2,1)S(1)} %pad_maximum_fusion.refs_0_, ...), custom_call_target="tpu_custom_call" | custom-call | bytes 5373960 | tf_op jit(solution)/shard_map/unpack/pallas_call | solution.py:70
  252.7 3.0 %unpack.2 = (f32[384,2304]{1,0:T(8,128)}, f32[384]{0:T(512)}, f32[384]{0:T(512)}, f32[384]{0:T(512)}, f32[384]{0:T(512)}) custom-call(s32[2]{0:T(128)S(1)} %copy-done, bf16[8,232,128]{2,1,0:T(8,128)(2,1)S(1)} %pad_maximum_fusion.3.refs_0_, bf16[8,232,128]{2,1,0:T(8,128)(2,1)S(1)} %collective-permute-done.45.refs_1_, ...), custom_call_target="tpu_custom_call" | custom-call | bytes 1835016 | tf_op jit(solution)/shard_map/unpack/pallas_call | solution.py:70
  (171 shorter events, 44.5 us)
Async XLA Ops:
  4.7 52.4 %collective-permute-start.3 = (bf16[384,3072]{1,0:T(8,128)(2,1)}, bf16[384,3072]{1,0:T(8,128)(2,1)}, u32[]{:S(2)}, u32[]{:S(2)}) collective-permute-start(bf16[384,3072]{1,0:T(8,128)(2,1)} %refs_2_.2), channel_id=1, source_target_pairs={{0,1},{1,0},{2,3},{3,2},{4,5},{5,4},{6,7},{7,6},{8,9},{9,8},{10,11... | collective-permute-start | bytes 7077896 | tf_op jit(solution)/shard_map/ppermute | solution.py:453
  5.2 51.9 %collective-permute-start.4 = (bf16[1536,768]{1,0:T(8,128)(2,1)}, bf16[1536,768]{1,0:T(8,128)(2,1)}, u32[]{:S(2)}, u32[]{:S(2)}) collective-permute-start(bf16[1536,768]{1,0:T(8,128)(2,1)} %refs_4_.2), channel_id=1, source_target_pairs={{0,1},{1,0},{2,3},{3,2},{4,5},{5,4},{6,7},{7,6},{8,9},{9,8},{10,11... | collective-permute-start | bytes 7077896 | tf_op jit(solution)/shard_map/ppermute | solution.py:453
  10.1 28.2 %all-to-all-start = ((bf16[16,192,128]{2,1,0:T(8,128)(2,1)}), bf16[16,192,128]{2,1,0:T(8,128)(2,1)S(1)}, u32[]{:S(2)}, u32[]{:S(2)}) async-start(bf16[16,192,128]{2,1,0:T(8,128)(2,1)} %get-tuple-element.129), calls=%async_computation | async-start | bytes 1572864 | tf_op jit(solution)/shard_map/all_to_all | solution.py:695
  18.3 30.3 %collective-permute-start.2 = (bf16[384,768]{1,0:T(8,128)(2,1)S(1)}, bf16[384,768]{1,0:T(8,128)(2,1)S(1)}, u32[]{:S(2)}, u32[]{:S(2)}) collective-permute-start(bf16[384,768]{1,0:T(8,128)(2,1)S(1)} %copy-done.10), channel_id=1, source_target_pairs={{0,1},{1,0},{2,3},{3,2},{4,5},{5,4},{6,7},{7,6},{8,9},{9,8},{10,11... | collective-permute-start | bytes 1769480 | tf_op jit(solution)/shard_map/ppermute | solution.py:453
  43.6 13.5 %all-to-all-start.1 = ((bf16[16,64,128]{2,1,0:T(8,128)(2,1)}), bf16[16,64,128]{2,1,0:T(8,128)(2,1)S(1)}, u32[]{:S(2)}, u32[]{:S(2)}) async-start(bf16[16,64,128]{2,1,0:T(8,128)(2,1)} %get-tuple-element.130.att_ref), calls=%async_computation.1 | async-start | bytes 524288 | tf_op jit(solution)/shard_map/all_to_all | solution.py:703
  69.5 14.7 %all-to-all-start.2 = ((bf16[16,64,128]{2,1,0:T(8,128)(2,1)}), bf16[16,64,128]{2,1,0:T(8,128)(2,1)S(1)}, u32[]{:S(2)}, u32[]{:S(2)}) async-start(bf16[16,64,128]{2,1,0:T(8,128)(2,1)} %get-tuple-element.152), calls=%async_computation.2 | async-start | bytes 524288 | tf_op jit(solution)/shard_map/all_to_all | solution.py:724
  84.3 33.2 %collective-permute-start.12 = (bf16[8,448,128]{2,1,0:T(8,128)(2,1)}, bf16[8,448,128]{2,1,0:T(8,128)(2,1)S(1)}, u32[]{:S(2)}, u32[]{:S(2)}) collective-permute-start(bf16[8,448,128]{2,1,0:T(8,128)(2,1)} %get-tuple-element.159), channel_id=1, source_target_pairs={{0,2},{2,0},{4,6},{6,4},{8,10},{10,8},{12,14},{14,12},{16,18},{18,... | collective-permute-start | bytes 2752520 | tf_op jit(solution)/shard_map/ppermute | solution.py:491
  86.2 25.1 %collective-permute-start.13 = (bf16[8,432,128]{2,1,0:T(8,128)(2,1)}, bf16[8,432,128]{2,1,0:T(8,128)(2,1)}, u32[]{:S(2)}, u32[]{:S(2)}) collective-permute-start(bf16[8,432,128]{2,1,0:T(8,128)(2,1)} %get-tuple-element.160), channel_id=1, source_target_pairs={{0,4},{2,6},{4,0},{6,2},{8,12},{10,14},{12,8},{14,10},{16,20},{18,... | collective-permute-start | bytes 2654216 | tf_op jit(solution)/shard_map/ppermute | solution.py:491
  87.7 29.7 %collective-permute-start.14 = (bf16[8,432,128]{2,1,0:T(8,128)(2,1)}, bf16[8,432,128]{2,1,0:T(8,128)(2,1)}, u32[]{:S(2)}, u32[]{:S(2)}) collective-permute-start(bf16[8,432,128]{2,1,0:T(8,128)(2,1)} %get-tuple-element.161), channel_id=1, source_target_pairs={{0,8},{2,10},{4,12},{6,14},{8,0},{10,2},{12,4},{14,6},{16,24},{18,... | collective-permute-start | bytes 2654216 | tf_op jit(solution)/shard_map/ppermute | solution.py:491
  98.1 33.3 %all-to-all-start.3 = ((bf16[16,192,128]{2,1,0:T(8,128)(2,1)}), bf16[16,192,128]{2,1,0:T(8,128)(2,1)S(1)}, u32[]{:S(2)}, u32[]{:S(2)}) async-start(bf16[16,192,128]{2,1,0:T(8,128)(2,1)} %attend_back.1), calls=%async_computation.3 | async-start | bytes 1572864 | tf_op jit(solution)/shard_map/all_to_all | solution.py:747
  119.6 11.8 %collective-permute-start.15 = (bf16[4,448,128]{2,1,0:T(8,128)(2,1)S(1)}, bf16[4,448,128]{2,1,0:T(8,128)(2,1)S(1)}, u32[]{:S(2)}, u32[]{:S(2)}) collective-permute-start(bf16[4,448,128]{2,1,0:T(8,128)(2,1)S(1)} %get-tuple-element.168), channel_id=1, source_target_pairs={{0,4},{2,6},{4,0},{6,2},{8,12},{10,14},{12,8},{14,10},{16,20},{18,... | collective-permute-start | bytes 1376264 | tf_op jit(solution)/shard_map/ppermute | solution.py:491
  119.7 11.7 %collective-permute-start.16 = (bf16[4,432,128]{2,1,0:T(8,128)(2,1)S(1)}, bf16[4,432,128]{2,1,0:T(8,128)(2,1)S(1)}, u32[]{:S(2)}, u32[]{:S(2)}) collective-permute-start(bf16[4,432,128]{2,1,0:T(8,128)(2,1)S(1)} %get-tuple-element.169), channel_id=1, source_target_pairs={{0,8},{2,10},{4,12},{6,14},{8,0},{10,2},{12,4},{14,6},{16,24},{18,... | collective-permute-start | bytes 1327112 | tf_op jit(solution)/shard_map/ppermute | solution.py:491
  119.7 11.6 %collective-permute-start.17 = (bf16[4,432,128]{2,1,0:T(8,128)(2,1)S(1)}, bf16[4,432,128]{2,1,0:T(8,128)(2,1)S(1)}, u32[]{:S(2)}, u32[]{:S(2)}) collective-permute-start(bf16[4,432,128]{2,1,0:T(8,128)(2,1)S(1)} %get-tuple-element.170), channel_id=1, source_target_pairs={{0,2},{2,0},{4,6},{6,4},{8,10},{10,8},{12,14},{14,12},{16,18},{18,... | collective-permute-start | bytes 1327112 | tf_op jit(solution)/shard_map/ppermute | solution.py:491
  139.4 10.4 %collective-permute-start.21 = (bf16[2,448,128]{2,1,0:T(8,128)(2,1)S(1)}, bf16[2,448,128]{2,1,0:T(8,128)(2,1)S(1)}, u32[]{:S(2)}, u32[]{:S(2)}) collective-permute-start(bf16[2,448,128]{2,1,0:T(8,128)(2,1)S(1)} %get-tuple-element.189), channel_id=1, source_target_pairs={{0,8},{2,10},{4,12},{6,14},{8,0},{10,2},{12,4},{14,6},{16,24},{18,... | collective-permute-start | bytes 688136 | tf_op jit(solution)/shard_map/ppermute | solution.py:491
  141.4 8.3 %collective-permute-start.23 = (bf16[2,432,128]{2,1,0:T(8,128)(2,1)S(1)}, bf16[2,432,128]{2,1,0:T(8,128)(2,1)S(1)}, u32[]{:S(2)}, u32[]{:S(2)}) collective-permute-start(bf16[2,432,128]{2,1,0:T(8,128)(2,1)S(1)} %get-tuple-element.191), channel_id=1, source_target_pairs={{0,4},{2,6},{4,0},{6,2},{8,12},{10,14},{12,8},{14,10},{16,20},{18,... | collective-permute-start | bytes 663560 | tf_op jit(solution)/shard_map/ppermute | solution.py:491
  143.5 14.8 %collective-permute-start.25 = (bf16[8,232,128]{2,1,0:T(8,128)(2,1)S(1)}, bf16[8,232,128]{2,1,0:T(8,128)(2,1)S(1)}, u32[]{:S(2)}, u32[]{:S(2)}) collective-permute-start(bf16[8,232,128]{2,1,0:T(8,128)(2,1)S(1)} %get-tuple-element.197), channel_id=1, source_target_pairs={{0,2},{2,0},{4,6},{6,4},{8,10},{10,8},{12,14},{14,12},{16,18},{18,... | collective-permute-start | bytes 1425416 | tf_op jit(solution)/shard_map/ppermute | solution.py:491
  145.0 12.9 %collective-permute-start.26 = (bf16[8,216,128]{2,1,0:T(8,128)(2,1)S(1)}, bf16[8,216,128]{2,1,0:T(8,128)(2,1)S(1)}, u32[]{:S(2)}, u32[]{:S(2)}) collective-permute-start(bf16[8,216,128]{2,1,0:T(8,128)(2,1)S(1)} %get-tuple-element.198), channel_id=1, source_target_pairs={{0,4},{2,6},{4,0},{6,2},{8,12},{10,14},{12,8},{14,10},{16,20},{18,... | collective-permute-start | bytes 1327112 | tf_op jit(solution)/shard_map/ppermute | solution.py:491
  149.9 15.4 %collective-permute-start.24 = (bf16[1,1312,128]{2,1,0:T(8,128)(2,1)S(1)}, bf16[1,1312,128]{2,1,0:T(8,128)(2,1)S(1)}, u32[]{:S(2)}, u32[]{:S(2)}) collective-permute-start(bf16[1,1312,128]{2,1,0:T(8,128)(2,1)S(1)} %pad_maximum_fusion.8), channel_id=1, source_target_pairs={{0,16},{2,18},{4,20},{6,22},{8,24},{10,26},{12,28},{14,30},{16,0},... | collective-permute-start | bytes 1007624 | tf_op jit(solution)/shard_map/ppermute | solution.py:491
  167.9 16.3 %collective-permute-start.29 = (bf16[1,1312,128]{2,1,0:T(8,128)(2,1)S(1)}, bf16[1,1312,128]{2,1,0:T(8,128)(2,1)S(1)}, u32[]{:S(2)}, u32[]{:S(2)}) collective-permute-start(bf16[1,1312,128]{2,1,0:T(8,128)(2,1)S(1)} %pad_maximum_fusion.9), channel_id=1, source_target_pairs={{0,16},{2,18},{4,20},{6,22},{8,24},{10,26},{12,28},{14,30},{16,0},... | collective-permute-start | bytes 1007624 | tf_op jit(solution)/shard_map/ppermute | solution.py:491
  173.5 13.4 %collective-permute-start.30 = (bf16[2,448,128]{2,1,0:T(8,128)(2,1)S(1)}, bf16[2,448,128]{2,1,0:T(8,128)(2,1)S(1)}, u32[]{:S(2)}, u32[]{:S(2)}) collective-permute-start(bf16[2,448,128]{2,1,0:T(8,128)(2,1)S(1)} %pad_maximum_fusion.11), channel_id=1, source_target_pairs={{0,8},{2,10},{4,12},{6,14},{8,0},{10,2},{12,4},{14,6},{16,24},{18,... | collective-permute-start | bytes 688136 | tf_op jit(solution)/shard_map/ppermute | solution.py:491
  190.2 10.0 %collective-permute-start.32 = (bf16[2,448,128]{2,1,0:T(8,128)(2,1)S(1)}, bf16[2,448,128]{2,1,0:T(8,128)(2,1)S(1)}, u32[]{:S(2)}, u32[]{:S(2)}) collective-permute-start(bf16[2,448,128]{2,1,0:T(8,128)(2,1)S(1)} %pad_maximum_fusion.12), channel_id=1, source_target_pairs={{0,8},{2,10},{4,12},{6,14},{8,0},{10,2},{12,4},{14,6},{16,24},{18,... | collective-permute-start | bytes 688136 | tf_op jit(solution)/shard_map/ppermute | solution.py:491
  200.3 18.4 %collective-permute-start.38 = (bf16[4,432,128]{2,1,0:T(8,128)(2,1)S(1)}, bf16[4,432,128]{2,1,0:T(8,128)(2,1)S(1)}, u32[]{:S(2)}, u32[]{:S(2)}) collective-permute-start(bf16[4,432,128]{2,1,0:T(8,128)(2,1)S(1)} %pad_maximum_fusion.6), channel_id=1, source_target_pairs={{0,2},{2,0},{4,6},{6,4},{8,10},{10,8},{12,14},{14,12},{16,18},{18,... | collective-permute-start | bytes 1327112 | tf_op jit(solution)/shard_map/ppermute | solution.py:491
  202.4 16.3 %collective-permute-start.36 = (bf16[4,448,128]{2,1,0:T(8,128)(2,1)S(1)}, bf16[4,448,128]{2,1,0:T(8,128)(2,1)S(1)}, u32[]{:S(2)}, u32[]{:S(2)}) collective-permute-start(bf16[4,448,128]{2,1,0:T(8,128)(2,1)S(1)} %pad_maximum_fusion.4), channel_id=1, source_target_pairs={{0,4},{2,6},{4,0},{6,2},{8,12},{10,14},{12,8},{14,10},{16,20},{18,... | collective-permute-start | bytes 1376264 | tf_op jit(solution)/shard_map/ppermute | solution.py:491
  203.6 15.1 %collective-permute-start.37 = (bf16[4,432,128]{2,1,0:T(8,128)(2,1)S(1)}, bf16[4,432,128]{2,1,0:T(8,128)(2,1)S(1)}, u32[]{:S(2)}, u32[]{:S(2)}) collective-permute-start(bf16[4,432,128]{2,1,0:T(8,128)(2,1)S(1)} %pad_maximum_fusion.5), channel_id=1, source_target_pairs={{0,8},{2,10},{4,12},{6,14},{8,0},{10,2},{12,4},{14,6},{16,24},{18,... | collective-permute-start | bytes 1327112 | tf_op jit(solution)/shard_map/ppermute | solution.py:491
  203.7 15.0 %collective-permute-start.39 = (bf16[2,448,128]{2,1,0:T(8,128)(2,1)S(1)}, bf16[2,448,128]{2,1,0:T(8,128)(2,1)S(1)}, u32[]{:S(2)}, u32[]{:S(2)}) collective-permute-start(bf16[2,448,128]{2,1,0:T(8,128)(2,1)S(1)} %maximum_maximum_fusion), channel_id=1, source_target_pairs={{0,8},{2,10},{4,12},{6,14},{8,0},{10,2},{12,4},{14,6},{16,24},{18,... | collective-permute-start | bytes 688136 | tf_op jit(solution)/shard_map/ppermute | solution.py:491
  218.8 24.2 %collective-permute-start.42 = (bf16[8,432,128]{2,1,0:T(8,128)(2,1)S(1)}, bf16[8,432,128]{2,1,0:T(8,128)(2,1)S(1)}, u32[]{:S(2)}, u32[]{:S(2)}) collective-permute-start(bf16[8,432,128]{2,1,0:T(8,128)(2,1)S(1)} %pad_maximum_fusion.2.refs_4_), channel_id=1, source_target_pairs={{0,8},{2,10},{4,12},{6,14},{8,0},{10,2},{12,4},{14,6},{16,24},{18,... | collective-permute-start | bytes 2654216 | tf_op jit(solution)/shard_map/ppermute | solution.py:491
  219.0 24.1 %collective-permute-start.40 = (bf16[8,448,128]{2,1,0:T(8,128)(2,1)S(1)}, bf16[8,448,128]{2,1,0:T(8,128)(2,1)S(1)}, u32[]{:S(2)}, u32[]{:S(2)}) collective-permute-start(bf16[8,448,128]{2,1,0:T(8,128)(2,1)S(1)} %pad_maximum_fusion.refs_0_), channel_id=1, source_target_pairs={{0,2},{2,0},{4,6},{6,4},{8,10},{10,8},{12,14},{14,12},{16,18},{18,... | collective-permute-start | bytes 2752520 | tf_op jit(solution)/shard_map/ppermute | solution.py:491
  220.0 23.1 %collective-permute-start.41 = (bf16[8,432,128]{2,1,0:T(8,128)(2,1)S(1)}, bf16[8,432,128]{2,1,0:T(8,128)(2,1)S(1)}, u32[]{:S(2)}, u32[]{:S(2)}) collective-permute-start(bf16[8,432,128]{2,1,0:T(8,128)(2,1)S(1)} %pad_maximum_fusion.1.refs_2_), channel_id=1, source_target_pairs={{0,4},{2,6},{4,0},{6,2},{8,12},{10,14},{12,8},{14,10},{16,20},{18,... | collective-permute-start | bytes 2654216 | tf_op jit(solution)/shard_map/ppermute | solution.py:491
  220.6 22.5 %collective-permute-start.43 = (bf16[4,232,128]{2,1,0:T(8,128)(2,1)S(1)}, bf16[4,232,128]{2,1,0:T(8,128)(2,1)S(1)}, u32[]{:S(2)}, u32[]{:S(2)}) collective-permute-start(bf16[4,232,128]{2,1,0:T(8,128)(2,1)S(1)} %pad_maximum_fusion.10), channel_id=1, source_target_pairs={{0,4},{2,6},{4,0},{6,2},{8,12},{10,14},{12,8},{14,10},{16,20},{18,... | collective-permute-start | bytes 712712 | tf_op jit(solution)/shard_map/ppermute | solution.py:491
  222.2 20.8 %collective-permute-start.44 = (bf16[4,216,128]{2,1,0:T(8,128)(2,1)S(1)}, bf16[4,216,128]{2,1,0:T(8,128)(2,1)S(1)}, u32[]{:S(2)}, u32[]{:S(2)}) collective-permute-start(bf16[4,216,128]{2,1,0:T(8,128)(2,1)S(1)} %pad_maximum_fusion.15), channel_id=1, source_target_pairs={{0,2},{2,0},{4,6},{6,4},{8,10},{10,8},{12,14},{14,12},{16,18},{18,... | collective-permute-start | bytes 663560 | tf_op jit(solution)/shard_map/ppermute | solution.py:491
  243.1 9.6 %collective-permute-start.45 = (bf16[8,232,128]{2,1,0:T(8,128)(2,1)S(1)}, bf16[8,232,128]{2,1,0:T(8,128)(2,1)S(1)}, u32[]{:S(2)}, u32[]{:S(2)}) collective-permute-start(bf16[8,232,128]{2,1,0:T(8,128)(2,1)S(1)} %pad_maximum_fusion.3.refs_0_), channel_id=1, source_target_pairs={{0,2},{2,0},{4,6},{6,4},{8,10},{10,8},{12,14},{14,12},{16,18},{18,... | collective-permute-start | bytes 1425416 | tf_op jit(solution)/shard_map/ppermute | solution.py:491
  244.4 8.4 %collective-permute-start.46 = (bf16[8,216,128]{2,1,0:T(8,128)(2,1)S(1)}, bf16[8,216,128]{2,1,0:T(8,128)(2,1)S(1)}, u32[]{:S(2)}, u32[]{:S(2)}) collective-permute-start(bf16[8,216,128]{2,1,0:T(8,128)(2,1)S(1)} %pad_maximum_fusion.7.refs_2_), channel_id=1, source_target_pairs={{0,4},{2,6},{4,0},{6,2},{8,12},{10,14},{12,8},{14,10},{16,20},{18,... | collective-permute-start | bytes 1327112 | tf_op jit(solution)/shard_map/ppermute | solution.py:491
  (42 other events, 210.5 us)
